TPU v7x, 512 devices: a whole 4x4x16 slice. The times are simulated.
512 devices in a mesh: inst: 16 (over y_lo, x, core), sector: 32 (over y_hi, z).
Axes of the slice: x: 4, y: 4 (y_hi: 2, y_lo: 2; y = y_hi * 2 + y_lo), z: 16, core: 2. Of those that a mesh axis runs over, the one named last changes fastest.
Arguments:
- lam_init: float32 [16, 512, 32, 128], P('inst', 'sector'), may hold values from -6 to 6
- rhs: float32 [16, 512, 32, 128], P('inst', 'sector'), may hold values from -6 to 6
- relax: float32 [16, 512, 128], P('inst', 'sector'), may hold values from 0.15 to 0.6
- cond: float32 [512, 128], P('sector'), may hold values from 0.05 to 0.4
- jac: bfloat16 [16, 512, 6, 128, 128], P('inst', 'sector'), may hold values from -0.21875 to 0.21875
- rotor_jac: bfloat16 [16, 128, 128, 128], P('inst', 'sector'), may hold values from -0.5 to 0.5
- cols: int32 [512, 6], P('sector'), may hold values from 0 to 17
- rotor_shift: int32 [16, 128], P('inst', 'sector'), may hold values from 0 to 1
- owned: int32 [32], P('sector'), may hold values from 1 to 12, 288 in all
Outputs:
- adjoint: float32 [16, 512, 32, 128], P('inst', 'sector')
All inputs are finite; a program needn't handle non-finite values. No bound on the sum of `owned` on one device may be relied on, other than what follows from the above.
Results may differ from a plain program's by a relative error of at most 0.002.
Values may be sent and summed in bfloat16 or wider, within the bound.
No kernel may reach another device: no remote copies, remote signals or barrier semaphores. Data moves between devices by JAX's collectives and lax.ppermute only.
A program may use at most 64 MiB of HBM per device.

v0:
```python
import jax
import jax.numpy as jnp
from jax import lax
from jax.sharding import PartitionSpec as P

NT = 16
SWEEPS = 2


def padded(cells, sides, width):
    for axis, dim in sides:
        count = lax.axis_size(axis)
        head = lax.slice_in_dim(cells, 0, width, axis=dim)
        tail = lax.slice_in_dim(cells, cells.shape[dim] - width, cells.shape[dim], axis=dim)
        cells = jnp.concatenate(
            [
                lax.ppermute(tail, axis, [(i, (i + 1) % count) for i in range(count)]),
                cells,
                lax.ppermute(head, axis, [((i + 1) % count, i) for i in range(count)]),
            ],
            axis=dim,
        )
    return cells


def shifted(block, axis, distance):
    devices = range(lax.axis_size(axis))
    route = [((i - distance) % len(devices), i) for i in devices]
    return lax.ppermute(block, axis, route)


def spectral_matrix():
    index = jnp.arange(NT)
    offset = index[:, None] - index[None, :]
    angle = jnp.pi * offset.astype(jnp.float32) / NT
    safe_sin = jnp.where(offset == 0, jnp.float32(1.0), jnp.sin(angle))
    parity = jnp.where(offset % 2 == 0, jnp.float32(1.0), jnp.float32(-1.0))
    deriv = jnp.where(offset == 0, jnp.float32(0.0), 0.5 * parity * jnp.cos(angle) / safe_sin)
    return deriv + jnp.float32(2.0) / NT


def shards(lam_init, rhs, relax, cond, jac, rotor_jac, cols, rotor_shift, owned):
    local_inst = lam_init.shape[0]
    rows = lam_init.shape[1]
    rotor_rows = rotor_jac.shape[1]
    dspec = spectral_matrix()
    first_inst = lax.axis_index("inst") * local_inst
    row = jnp.arange(rows)
    live = ((row >= rows - rotor_rows) | (row < owned[0])).astype(jnp.float32)[None, :, None, None]
    lam = lam_init * live
    moving = rotor_shift.astype(jnp.float32)[:, :, None, None]
    relax_wide = relax[:, :, None, :]
    cond_wide = cond[None, :, None, :]
    for sweep in range(SWEEPS):
        lam_b = lam.astype(jnp.bfloat16)
        lam_h = padded(lam_b, (("sector", 1),), 1)
        picked = lam_h[:, cols]
        stator = jnp.einsum("tnkri,tnkio->tnro", picked, jac, preferred_element_type=jnp.float32)
        records = jnp.einsum(
            "tjri,tjio->tjro",
            lam_b[:, rows - rotor_rows :],
            rotor_jac,
            preferred_element_type=jnp.float32,
        )
        arrived = shifted((records * moving).astype(jnp.bfloat16), "sector", 1).astype(jnp.float32)
        rotor = records * (1.0 - moving) + arrived
        rotor_full = jnp.concatenate(
            [jnp.zeros((local_inst, rows - rotor_rows) + rotor.shape[2:], jnp.float32), rotor],
            axis=1,
        )
        weighted = lam * cond_wide
        piece = lax.all_gather(weighted, "inst", axis=0, tiled=True)
        coef = lax.dynamic_slice(dspec, (0, first_inst), (piece.shape[0], local_inst))
        spec = jnp.zeros_like(weighted) + jnp.einsum(
            "jt,jnrc->tnrc", coef, piece, precision=lax.Precision.HIGHEST
        )
        resid = rhs - (stator + rotor_full + spec)
        lam = lam + relax_wide * resid * live
    return lam


def solution(mesh):
    return jax.shard_map(
        shards,
        mesh=mesh,
        in_specs=(
            P("inst", "sector", None, None),
            P("inst", "sector", None, None),
            P("inst", "sector", None),
            P("sector", None),
            P("inst", "sector", None, None, None),
            P("inst", "sector", None, None),
            P("sector", None),
            P("inst", "sector"),
            P("sector"),
        ),
        out_specs=P("inst", "sector", None, None),
        check_vma=False,
    )
```

profile of v0, /device:TPU:1, one launch (start us, length us, event | category | flops | bytes accessed | tf_op | source)
XLA Modules:
  0.0 128.8 jit_solution(6784059207675336559)
XLA Ops:
  7.4 1.9 %multiply_convert_fusion = (bf16[1,16,32,128]{3,2,1,0:T(8,128)(2,1)S(1)}, f32[1,16,32,128]{3,2,1,0:T(8,128)}) fusion(f32[1,16,32,128]{3,2,1,0:T(8,128)} %param.9, f32[16]{0:T(128)S(1)} %or_convert_fusion, f32[16,128]{1,0:T(8,128)} %param.12), kind=kLoop, calls=%fused_computation.15 | loop fusion | flops 196608 | bytes 663616 | tf_op jit(solution)/shard_map/convert_element_type | solution.py:55
  9.3 0.7 convert_bitcast_fusion
  10.0 1.1 fusion.16
  11.1 0.7 fusion.18
  11.7 4.4 %collective-permute-start.2 = (bf16[1,4,32,128]{3,2,1,0:T(8,128)(2,1)}, bf16[1,4,32,128]{3,2,1,0:T(8,128)(2,1)S(1)}, u32[]{:S(2)}, u32[]{:S(2)}) collective-permute-start(bf16[1,4,32,128]{3,2,1,0:T(8,128)(2,1)} %fusion.18), channel_id=1, source_target_pairs={{31,0},{0,1},{1,2},{2,3},{3,4},{4,5},{5,6},{6,7},{7,8},{8,9},{9,10... | collective-permute-start | bytes 98312 | tf_op jit(solution)/shard_map/ppermute | solution.py:29
  16.1 12.1 %collective-permute-start.1 = (bf16[1,1,32,128]{3,2,1,0:T(8,128)(2,1)S(1)}, bf16[1,1,32,128]{3,2,1,0:T(8,128)(2,1)S(1)}, u32[]{:S(2)}, u32[]{:S(2)}) collective-permute-start(bf16[1,1,32,128]{3,2,1,0:T(8,128)(2,1)S(1)} %get-tuple-element.12), channel_id=1, source_target_pairs={{1,0},{2,1},{3,2},{4,3},{5,4},{6,5},{7,6},{8,7},{9,8},{10,9},{11,1... | collective-permute-start | bytes 24584 | tf_op jit(solution)/shard_map/ppermute | solution.py:19
  28.3 1.9 %collective-permute-start = (bf16[1,1,32,128]{3,2,1,0:T(8,128)(2,1)S(1)}, bf16[1,1,32,128]{3,2,1,0:T(8,128)(2,1)}, u32[]{:S(2)}, u32[]{:S(2)}) collective-permute-start(bf16[1,1,32,128]{3,2,1,0:T(8,128)(2,1)S(1)} %get-tuple-element.11), channel_id=1, source_target_pairs={{0,1},{1,2},{2,3},{3,4},{4,5},{5,6},{6,7},{7,8},{8,9},{9,10},{10,1... | collective-permute-start | bytes 24584 | tf_op jit(solution)/shard_map/ppermute | solution.py:17
  30.2 0.7 compare_select_fusion
  31.0 0.1 reshape.75
  31.1 1.2 broadcast_subtract_fusion
  32.3 0.6 copy-done.15
  32.9 3.6 %collective-permute-done = bf16[1,1,32,128]{3,2,1,0:T(8,128)(2,1)} collective-permute-done((bf16[1,1,32,128]{3,2,1,0:T(8,128)(2,1)S(1)}, bf16[1,1,32,128]{3,2,1,0:T(8,128)(2,1)}, u32[]{:S(2)}, u32[]{:S(2)}) %collective-permute-start) | collective-permute-done | bytes 8224 | tf_op jit(solution)/shard_map/ppermute | solution.py:17
  36.5 0.7 maximum_bitcast_fusion
  37.2 1.6 %gather_fusion = bf16[96,32,128]{2,1,0:T(8,128)(2,1)} fusion(bf16[18,32,128]{2,1,0:T(8,128)(2,1)S(1)} %maximum_bitcast_fusion, s32[1024]{0:T(1024)S(1)} %pad_clamp_fusion), kind=kCustom, calls=%fused_computation | custom fusion | bytes 1573248 | tf_op jit(solution)/shard_map/gather | solution.py:57
  38.8 1.3 %bitcast_add_fusion.1 = f32[1,4,32,128]{3,2,1,0:T(8,128)} fusion(bf16[1,4,32,128]{3,2,1,0:T(8,128)(2,1)S(1)} %collective-permute-done.2, f32[4,32,128]{2,1,0:T(8,128)S(1)} %fusion.16, f32[4]{0:T(128)} %broadcast_subtract_fusion), kind=kLoop, calls=%fused_computation.24 | loop fusion | flops 49152 | bytes 163856 | tf_op jit(solution)/shard_map/add | solution.py:66
  40.1 20.2 %all-gather.3.cloned.1.call-done = f32[16,16,32,128]{3,2,1,0:T(8,128)} async-done(((f32[1,16,32,128]{3,2,1,0:T(8,128)}), f32[16,16,32,128]{3,2,1,0:T(8,128)}) %all-gather.3.cloned.1.call-update) | async-done | bytes 4194320 | tf_op jit(solution)/shard_map/all_gather | solution.py:72
  60.4 6.5 %fusion.2 = f32[1,16,32,128]{3,0,2,1:T(1,128)S(1)} fusion(f32[16,16,32,128]{3,2,1,0:T(8,128)} %all-gather.3.cloned.1.call-done, f32[16,16]{0,1:T(8,128)S(1)} %get-tuple-element.14, s32[]{:T(128)S(6)} %select_n.31, pred[16,16]{0,1:T(8,128)(4,1)S(1)} %fusion.21, s32[16,16]{0,1:T(8,128)S(1)} %get-tuple-element.13), kind=kOutput, calls=%fused_computation.4 | convolution fusion | flops 12583056 | bytes 4457988 | tf_op jit(solution)/shard_map/jt,jnrc->tnrc/dot_general | solution.py:74
  67.0 0.7 fusion.32
  67.7 0.7 broadcast_multiply_fusion
  68.5 7.7 %collective-permute-start.4 = (bf16[1,1,32,128]{3,2,1,0:T(8,128)(2,1)S(1)}, bf16[1,1,32,128]{3,2,1,0:T(8,128)(2,1)S(1)}, u32[]{:S(2)}, u32[]{:S(2)}) collective-permute-start(bf16[1,1,32,128]{3,2,1,0:T(8,128)(2,1)S(1)} %get-tuple-element.10), channel_id=1, source_target_pairs={{1,0},{2,1},{3,2},{4,3},{5,4},{6,5},{7,6},{8,7},{9,8},{10,9},{11,1... | collective-permute-start | bytes 24584 | tf_op jit(solution)/shard_map/ppermute | solution.py:19
  76.3 1.9 %collective-permute-start.3 = (bf16[1,1,32,128]{3,2,1,0:T(8,128)(2,1)S(1)}, bf16[1,1,32,128]{3,2,1,0:T(8,128)(2,1)S(1)}, u32[]{:S(2)}, u32[]{:S(2)}) collective-permute-start(bf16[1,1,32,128]{3,2,1,0:T(8,128)(2,1)S(1)} %get-tuple-element.9), channel_id=1, source_target_pairs={{0,1},{1,2},{2,3},{3,4},{4,5},{5,6},{6,7},{7,8},{8,9},{9,10},{10,1... | collective-permute-start | bytes 24584 | tf_op jit(solution)/shard_map/ppermute | solution.py:17
  78.2 1.1 fusion.14
  79.2 1.4 %fusion.19 = bf16[1,4,32,128]{3,2,1,0:T(8,128)(2,1)} fusion(f32[4,32,128]{2,1,0:T(8,128)S(1)} %fusion.14, f32[4]{0:T(128)} %copy-done.20), kind=kLoop, calls=%fused_computation.28 | loop fusion | flops 32768 | bytes 98320 | tf_op jit(solution)/shard_map/convert_element_type | solution.py:65
  80.6 1.9 %collective-permute-start.5 = (bf16[1,4,32,128]{3,2,1,0:T(8,128)(2,1)}, bf16[1,4,32,128]{3,2,1,0:T(8,128)(2,1)}, u32[]{:S(2)}, u32[]{:S(2)}) collective-permute-start(bf16[1,4,32,128]{3,2,1,0:T(8,128)(2,1)} %fusion.19), channel_id=1, source_target_pairs={{31,0},{0,1},{1,2},{2,3},{3,4},{4,5},{5,6},{6,7},{7,8},{8,9},{9,10... | collective-permute-start | bytes 98312 | tf_op jit(solution)/shard_map/ppermute | solution.py:29
  82.5 1.7 %collective-permute-done.3 = bf16[1,1,32,128]{3,2,1,0:T(8,128)(2,1)S(1)} collective-permute-done((bf16[1,1,32,128]{3,2,1,0:T(8,128)(2,1)S(1)}, bf16[1,1,32,128]{3,2,1,0:T(8,128)(2,1)S(1)}, u32[]{:S(2)}, u32[]{:S(2)}) %collective-permute-start.3) | collective-permute-done | bytes 8224 | tf_op jit(solution)/shard_map/ppermute | solution.py:17
  84.3 0.9 maximum_bitcast_fusion.1
  85.2 1.7 %gather_fusion.1 = bf16[96,32,128]{2,1,0:T(8,128)(2,1)} fusion(bf16[18,32,128]{2,1,0:T(8,128)(2,1)S(1)} %maximum_bitcast_fusion.1, s32[1024]{0:T(1024)} %copy-done.9), kind=kCustom, calls=%fused_computation.1 | custom fusion | bytes 1573248 | tf_op jit(solution)/shard_map/gather | solution.py:57
  86.9 2.4 %collective-permute-done.5 = bf16[1,4,32,128]{3,2,1,0:T(8,128)(2,1)} collective-permute-done((bf16[1,4,32,128]{3,2,1,0:T(8,128)(2,1)}, bf16[1,4,32,128]{3,2,1,0:T(8,128)(2,1)}, u32[]{:S(2)}, u32[]{:S(2)}) %collective-permute-start.5) | collective-permute-done | bytes 32800 | tf_op jit(solution)/shard_map/ppermute | solution.py:29
  89.3 0.9 bitcast_add_fusion
  90.2 23.8 %all-gather.5.cloned.1.call-done = f32[16,16,32,128]{3,2,1,0:T(8,128)} async-done(((f32[1,16,32,128]{3,2,1,0:T(8,128)}), f32[16,16,32,128]{3,2,1,0:T(8,128)}) %all-gather.5.cloned.1.call-update) | async-done | bytes 4194320 | tf_op jit(solution)/shard_map/all_gather | solution.py:72
  114.0 6.5 %fusion = f32[1,16,32,128]{3,0,2,1:T(1,128)S(1)} fusion(f32[16,16,32,128]{3,2,1,0:T(8,128)} %all-gather.5.cloned.1.call-done, f32[16,16]{0,1:T(8,128)} %copy-done.14, s32[]{:T(128)S(6)} %select_n.31, pred[16,16]{0,1:T(8,128)(4,1)} %copy-done.16, s32[16,16]{0,1:T(8,128)} %copy-done.13), kind=kOutput, calls=%fused_computation.2 | convolution fusion | flops 12583056 | bytes 4457988 | tf_op jit(solution)/shard_map/jt,jnrc->tnrc/dot_general | solution.py:74
  120.5 1.4 %multiply_add_fusion = f32[1,16,32,128]{3,2,1,0:T(8,128)} fusion(f32[1,16,32,128]{3,2,1,0:T(8,128)S(1)} %get-tuple-element.6, f32[1,16,32,128]{3,2,1,0:T(8,128)S(1)} %copy-done.5, f32[1,16,32,128]{3,2,1,0:T(8,128)S(1)} %bitcast.74, f32[1,4,32,128]{3,2,1,0:T(8,128)S(1)} %bitcast_add_fusion, f32[16,128]{1,0:T(8,128)S(1)} %bitcast.77, f32[16]{0:T(128)S(1)} %copy-done.19, ...), kind=kOutput, calls=%fused_computation.12 | convolution fusion | flops 101056512 | bytes 5054528 | tf_op jit(solution)/shard_map/tnkri,tnkio->tnro/dot_general | solution.py:58
  (55 shorter events, 0.3 us)
Async XLA Ops:
  6.5 60.4 %copy-start = (bf16[1,16,6,128,128]{4,3,2,1,0:T(8,128)(2,1)S(1)}, bf16[1,16,6,128,128]{4,3,2,1,0:T(8,128)(2,1)}, u32[]{:S(2)}) copy-start(bf16[1,16,6,128,128]{4,3,2,1,0:T(8,128)(2,1)} %param.13) | copy-start | bytes 9437188
  6.5 60.4 %copy-start.11 = (f32[1,16,128]{2,1,0:T(8,128)S(1)}, f32[1,16,128]{2,1,0:T(8,128)}, u32[]{:S(2)}) copy-start(f32[1,16,128]{2,1,0:T(8,128)} %param.11) | copy-start | bytes 24580
  6.5 53.8 %all-gather.3.cloned.1.call-start = ((), (), s32[]{:S(2)}) async-start(), calls=%async_computation | async-start | bytes 4456448 | tf_op jit(solution)/shard_map/all_gather | solution.py:72
  7.4 2.7 %copy-start.17 = (f32[16]{0:T(128)}, f32[16]{0:T(128)S(1)}, u32[]{:S(2)}) copy-start(f32[16]{0:T(128)S(1)} %or_convert_fusion) | copy-start | bytes 196
  9.3 104.7 %all-gather.5.cloned.1.call-start = ((), (), s32[]{:S(2)}) async-start(), calls=%async_computation.1 | async-start | bytes 4456448 | tf_op jit(solution)/shard_map/all_gather | solution.py:72
  10.0 6.1 %copy-start.20 = (f32[4]{0:T(128)}, f32[4]{0:T(128)S(1)}, u32[]{:S(2)}) copy-start(f32[4]{0:T(128)S(1)} %convert_bitcast_fusion) | copy-start | bytes 52
  11.7 27.1 %collective-permute-start.2 = (bf16[1,4,32,128]{3,2,1,0:T(8,128)(2,1)}, bf16[1,4,32,128]{3,2,1,0:T(8,128)(2,1)S(1)}, u32[]{:S(2)}, u32[]{:S(2)}) collective-permute-start(bf16[1,4,32,128]{3,2,1,0:T(8,128)(2,1)} %fusion.18), channel_id=1, source_target_pairs={{31,0},{0,1},{1,2},{2,3},{3,4},{4,5},{5,6},{6,7},{7,8},{8,9},{9,10... | collective-permute-start | bytes 98312 | tf_op jit(solution)/shard_map/ppermute | solution.py:29
  16.1 16.2 %collective-permute-start.1 = (bf16[1,1,32,128]{3,2,1,0:T(8,128)(2,1)S(1)}, bf16[1,1,32,128]{3,2,1,0:T(8,128)(2,1)S(1)}, u32[]{:S(2)}, u32[]{:S(2)}) collective-permute-start(bf16[1,1,32,128]{3,2,1,0:T(8,128)(2,1)S(1)} %get-tuple-element.12), channel_id=1, source_target_pairs={{1,0},{2,1},{3,2},{4,3},{5,4},{6,5},{7,6},{8,7},{9,8},{10,9},{11,1... | collective-permute-start | bytes 24584 | tf_op jit(solution)/shard_map/ppermute | solution.py:19
  28.3 8.2 %collective-permute-start = (bf16[1,1,32,128]{3,2,1,0:T(8,128)(2,1)S(1)}, bf16[1,1,32,128]{3,2,1,0:T(8,128)(2,1)}, u32[]{:S(2)}, u32[]{:S(2)}) collective-permute-start(bf16[1,1,32,128]{3,2,1,0:T(8,128)(2,1)S(1)} %get-tuple-element.11), channel_id=1, source_target_pairs={{0,1},{1,2},{2,3},{3,4},{4,5},{5,6},{6,7},{7,8},{8,9},{9,10},{10,1... | collective-permute-start | bytes 24584 | tf_op jit(solution)/shard_map/ppermute | solution.py:17
  31.1 35.9 %copy-start.9 = (s32[1024]{0:T(1024)}, s32[1024]{0:T(1024)S(1)}, u32[]{:S(2)}) copy-start(s32[1024]{0:T(1024)S(1)} %pad_clamp_fusion) | copy-start | bytes 12292
  31.1 35.8 %copy-start.13 = (s32[16,16]{0,1:T(8,128)}, s32[16,16]{0,1:T(8,128)S(1)}, u32[]{:S(2)}) copy-start(s32[16,16]{0,1:T(8,128)S(1)} %get-tuple-element.13) | copy-start | bytes 3076
  31.1 36.6 %copy-start.14 = (f32[16,16]{0,1:T(8,128)}, f32[16,16]{0,1:T(8,128)S(1)}, u32[]{:S(2)}) copy-start(f32[16,16]{0,1:T(8,128)S(1)} %get-tuple-element.14) | copy-start | bytes 3076
  32.3 34.7 %copy-start.16 = (pred[16,16]{0,1:T(8,128)(4,1)}, pred[16,16]{0,1:T(8,128)(4,1)S(1)}, u32[]{:S(2)}) copy-start(pred[16,16]{0,1:T(8,128)(4,1)S(1)} %fusion.21) | copy-start | bytes 772
  32.3 0.6 copy-start.15
  60.4 6.6 %copy-start.2 = (bf16[96,32,128]{2,1,0:T(8,128)(2,1)S(1)}, bf16[96,32,128]{2,1,0:T(8,128)(2,1)}, u32[]{:S(2)}) copy-start(bf16[96,32,128]{2,1,0:T(8,128)(2,1)} %gather_fusion) | copy-start | bytes 2359300
  60.4 6.6 %copy-start.3 = (f32[1,16,32,128]{3,2,1,0:T(8,128)S(1)}, f32[1,16,32,128]{3,2,1,0:T(8,128)}, u32[]{:S(2)}) copy-start(f32[1,16,32,128]{3,2,1,0:T(8,128)} %param.9) | copy-start | bytes 786436
  60.4 6.6 %copy-start.4 = (f32[1,16,32,128]{3,2,1,0:T(8,128)S(1)}, f32[1,16,32,128]{3,2,1,0:T(8,128)}, u32[]{:S(2)}) copy-start(f32[1,16,32,128]{3,2,1,0:T(8,128)} %param.10) | copy-start | bytes 786436
  60.4 6.7 %copy-start.8 = (f32[1,4,32,128]{3,2,1,0:T(8,128)S(1)}, f32[1,4,32,128]{3,2,1,0:T(8,128)}, u32[]{:S(2)}) copy-start(f32[1,4,32,128]{3,2,1,0:T(8,128)} %bitcast_add_fusion.1) | copy-start | bytes 196612
  60.4 6.7 %copy-start.18 = (f32[16]{0:T(128)S(1)}, f32[16]{0:T(128)}, u32[]{:S(2)}) copy-start(f32[16]{0:T(128)} %copy-done.17) | copy-start | bytes 196
  60.4 7.4 %copy-start.10 = (f32[16,128]{1,0:T(8,128)S(1)}, f32[16,128]{1,0:T(8,128)}, u32[]{:S(2)}) copy-start(f32[16,128]{1,0:T(8,128)} %param.12) | copy-start | bytes 24580
  67.7 14.8 %copy-start.6 = (bf16[1,16,32,128]{3,2,1,0:T(8,128)(2,1)}, bf16[1,16,32,128]{3,2,1,0:T(8,128)(2,1)S(1)}, u32[]{:S(2)}) copy-start(bf16[1,16,32,128]{3,2,1,0:T(8,128)(2,1)S(1)} %get-tuple-element.5) | copy-start | bytes 393220
  68.5 14.0 %collective-permute-start.4 = (bf16[1,1,32,128]{3,2,1,0:T(8,128)(2,1)S(1)}, bf16[1,1,32,128]{3,2,1,0:T(8,128)(2,1)S(1)}, u32[]{:S(2)}, u32[]{:S(2)}) collective-permute-start(bf16[1,1,32,128]{3,2,1,0:T(8,128)(2,1)S(1)} %get-tuple-element.10), channel_id=1, source_target_pairs={{1,0},{2,1},{3,2},{4,3},{5,4},{6,5},{7,6},{8,7},{9,8},{10,9},{11,1... | collective-permute-start | bytes 24584 | tf_op jit(solution)/shard_map/ppermute | solution.py:19
  76.3 8.0 %collective-permute-start.3 = (bf16[1,1,32,128]{3,2,1,0:T(8,128)(2,1)S(1)}, bf16[1,1,32,128]{3,2,1,0:T(8,128)(2,1)S(1)}, u32[]{:S(2)}, u32[]{:S(2)}) collective-permute-start(bf16[1,1,32,128]{3,2,1,0:T(8,128)(2,1)S(1)} %get-tuple-element.9), channel_id=1, source_target_pairs={{0,1},{1,2},{2,3},{3,4},{4,5},{5,6},{6,7},{7,8},{8,9},{9,10},{10,1... | collective-permute-start | bytes 24584 | tf_op jit(solution)/shard_map/ppermute | solution.py:17
  79.2 5.0 %copy-start.7 = (f32[4,32,128]{2,1,0:T(8,128)}, f32[4,32,128]{2,1,0:T(8,128)S(1)}, u32[]{:S(2)}) copy-start(f32[4,32,128]{2,1,0:T(8,128)S(1)} %fusion.14) | copy-start | bytes 196612
  80.6 8.7 %collective-permute-start.5 = (bf16[1,4,32,128]{3,2,1,0:T(8,128)(2,1)}, bf16[1,4,32,128]{3,2,1,0:T(8,128)(2,1)}, u32[]{:S(2)}, u32[]{:S(2)}) collective-permute-start(bf16[1,4,32,128]{3,2,1,0:T(8,128)(2,1)} %fusion.19), channel_id=1, source_target_pairs={{31,0},{0,1},{1,2},{2,3},{3,4},{4,5},{5,6},{6,7},{7,8},{8,9},{9,10... | collective-permute-start | bytes 98312 | tf_op jit(solution)/shard_map/ppermute | solution.py:29
  86.9 33.6 %copy-start.12 = (f32[1,16,128]{2,1,0:T(8,128)S(1)}, f32[1,16,128]{2,1,0:T(8,128)}, u32[]{:S(2)}) copy-start(f32[1,16,128]{2,1,0:T(8,128)} %param.11) | copy-start | bytes 24580
  86.9 33.6 %copy-start.19 = (f32[16]{0:T(128)S(1)}, f32[16]{0:T(128)}, u32[]{:S(2)}) copy-start(f32[16]{0:T(128)} %copy-done.17) | copy-start | bytes 196
  114.0 6.6 %copy-start.1 = (bf16[96,32,128]{2,1,0:T(8,128)(2,1)S(1)}, bf16[96,32,128]{2,1,0:T(8,128)(2,1)}, u32[]{:S(2)}) copy-start(bf16[96,32,128]{2,1,0:T(8,128)(2,1)} %gather_fusion.1) | copy-start | bytes 2359300
  114.0 6.6 %copy-start.5 = (f32[1,16,32,128]{3,2,1,0:T(8,128)S(1)}, f32[1,16,32,128]{3,2,1,0:T(8,128)}, u32[]{:S(2)}) copy-start(f32[1,16,32,128]{3,2,1,0:T(8,128)} %param.10) | copy-start | bytes 786436
Sparse Core Ops, SparseCore 0:
  9.5 50.8 all-gather.2
  68.6 45.2 all-gather.4
where the time goes:
time: 129 us
  waiting for transfers between devices  51.7 us (40%)
  starting transfers between devices  30 us (23%)
  matrix products  17.2 us (13%)
  between operations  14.6 us (11%)
  other arithmetic  11.1 us (9%)
  local copies, waits for them, and re-layouts  4.14 us (3%)
    all_gather x2, waiting for transfers between devices, shards(): piece = lax.all_gather(weighted, 'inst', axis=0, tiled=True)  44 us
    ppermute x2, starting transfers between devices, padded(): lax.ppermute(head, axis, [((i + 1) % count, i) for i in range(count)])  19.9 us
    dot_general x2, matrix products, shards(): jnp.einsum('jt,jnrc->tnrc', coef, piece, precision=lax.Precision.HIGHEST)  13.1 us
    ppermute x2, starting transfers between devices, shifted(): return lax.ppermute(block, axis, route)  6.27 us
    ppermute x2, waiting for transfers between devices, padded(): lax.ppermute(tail, axis, [(i, (i + 1) % count) for i in range(count)])  5.31 us
    ppermute x2, starting transfers between devices, padded(): lax.ppermute(tail, axis, [(i, (i + 1) % count) for i in range(count)])  3.84 us
    gather x2, local copies, waits for them, and re-layouts, shards(): picked = lam_h[:, cols]  3.29 us
  transfers between devices with their start and end apart: 8, of which 5 were waited for; matrix products, arithmetic and copies ran while one was open for 11% of the time, Pallas kernels for 0%

commit v1 on v0

--- a/solution.py
+++ b/solution.py
@@ -39,6 +39,39 @@
     return deriv + jnp.float32(2.0) / NT
 
 
+def column_of(s, dx):
+    return (s // 8) * 8 + (((s // 2) % 4 + dx) % 4) * 2 + s % 2
+
+
+def routed(block, dest):
+    return lax.ppermute(block, "inst", [(s, dest(s)) for s in range(lax.axis_size("inst"))])
+
+
+def instance_mix(weighted, dspec):
+    i = lax.axis_index("inst")
+    mate = routed(weighted, lambda s: s ^ 1)
+    across = routed(weighted, lambda s: s ^ 8)
+    diagonal = routed(across, lambda s: s ^ 1)
+    members = jnp.stack([i, i ^ 1, i ^ 8, i ^ 9])
+    values = (weighted, mate, across, diagonal)
+
+    def partial(target):
+        coef = dspec[members, target]
+        return sum(coef[k] * values[k] for k in range(4))
+
+    half = weighted.shape[1] // 2
+    far = partial(column_of(i, 2))
+    ahead = routed(far[:, :half], lambda s: column_of(s, 1))
+    behind = routed(far[:, half:], lambda s: column_of(s, 3))
+    up = partial(column_of(i, 1))
+    up = up.at[:, :half].add(ahead)
+    down = partial(column_of(i, 3))
+    down = down.at[:, half:].add(behind)
+    from_below = routed(up, lambda s: column_of(s, 1))
+    from_above = routed(down, lambda s: column_of(s, 3))
+    return partial(i) + from_below + from_above
+
+
 def shards(lam_init, rhs, relax, cond, jac, rotor_jac, cols, rotor_shift, owned):
     local_inst = lam_init.shape[0]
     rows = lam_init.shape[1]
@@ -69,11 +102,7 @@
             axis=1,
         )
         weighted = lam * cond_wide
-        piece = lax.all_gather(weighted, "inst", axis=0, tiled=True)
-        coef = lax.dynamic_slice(dspec, (0, first_inst), (piece.shape[0], local_inst))
-        spec = jnp.zeros_like(weighted) + jnp.einsum(
-            "jt,jnrc->tnrc", coef, piece, precision=lax.Precision.HIGHEST
-        )
+        spec = instance_mix(weighted, dspec)
         resid = rhs - (stator + rotor_full + spec)
         lam = lam + relax_wide * resid * live
     return lam

time: 129 us -> 146 us (1.13)
  starting transfers between devices: 30 us -> 71.9 us
  waiting for transfers between devices: 51.7 us -> 11.4 us
  other arithmetic: 11.1 us -> 39.6 us
  matrix products: 17.2 us -> 3.77 us
  between operations: 14.6 us -> 1.58 us
  local copies, waits for them, and re-layouts: 4.14 us -> 16.5 us
    ppermute x0 -> x14, starting transfers between devices: none -> 47.7 us  [routed(): lax.ppermute(block, 'inst', [(s, dest(s)) for s in range(lax.axis_size('i...]
    all_gather x2 -> x0, waiting for transfers between devices: 44 us -> none  [shards(): piece = lax.all_gather(weighted, 'inst', axis=0, tiled=True)]
    add x0 -> x4, other arithmetic: none -> 21.5 us  [the longest x2 18.2 us: partial(): return sum((coef[k] * values[k] for k in range(4)))]
    dot_general x2 -> x0, matrix products: 13.1 us -> none  [shards(): jnp.einsum('jt,jnrc->tnrc', coef, piece, precision=lax.Precision.HIGHEST)]
    ppermute x0 -> x14, waiting for transfers between devices: none -> 11.4 us  [routed(): lax.ppermute(block, 'inst', [(s, dest(s)) for s in range(lax.axis_size('i...]
    slice x0 -> x6, local copies, waits for them, and re-layouts: none -> 7.19 us  [the longest x4 5.76 us: partial(): return sum((coef[k] * values[k] for k in range(4)))]
    scatter-add x0 -> x4, other arithmetic: none -> 5.87 us  [the longest x2 3.35 us: instance_mix(): down = down.at[:, half:].add(behind)]
    ppermute x2, waiting for transfers between devices: 5.31 us -> 0.01 us  [padded(): lax.ppermute(tail, axis, [(i, (i + 1) % count) for i in range(count)])]
  transfers between devices with their start and end apart: 8 -> 20, of which waited for: 5 -> 4; matrix products, arithmetic and copies ran while one was open for 11% -> 28% of each run, Pallas kernels for 0% -> 0%
where the time goes in v1:
time: 146 us; the launch traced here: 145 us
  starting transfers between devices  71.9 us (49%)
  other arithmetic  39.6 us (27%)
  local copies, waits for them, and re-layouts  16.5 us (11%)
  waiting for transfers between devices  11.4 us (8%)
  matrix products  3.77 us (3%)
  between operations  1.58 us (1%)
    ppermute x14, starting transfers between devices, routed(): lax.ppermute(block, 'inst', [(s, dest(s)) for s in range(lax.axis_size('i...  47.7 us
    add x2, other arithmetic, partial(): return sum((coef[k] * values[k] for k in range(4)))  18.2 us
    ppermute x2, starting transfers between devices, padded(): lax.ppermute(head, axis, [((i + 1) % count, i) for i in range(count)])  16.3 us
    ppermute x14, waiting for transfers between devices, routed(): lax.ppermute(block, 'inst', [(s, dest(s)) for s in range(lax.axis_size('i...  11.4 us
    slice x4, local copies, waits for them, and re-layouts, partial(): return sum((coef[k] * values[k] for k in range(4)))  5.76 us
    gather x4, local copies, waits for them, and re-layouts, partial(): coef = dspec[members, target]  5.03 us
    ppermute x2, starting transfers between devices, padded(): lax.ppermute(tail, axis, [(i, (i + 1) % count) for i in range(count)])  3.96 us
    ppermute x2, starting transfers between devices, shifted(): return lax.ppermute(block, axis, route)  3.82 us
  transfers between devices with their start and end apart: 20, of which 4 were waited for; matrix products, arithmetic and copies ran while one was open for 28% of the time, Pallas kernels for 0%

profile of v1, /device:TPU:1, one launch (start us, length us, event | category | flops | bytes accessed | tf_op | source)
XLA Modules:
  0.0 144.7 jit_solution(2927873514929235220)
XLA Ops:
  1.3 1.7 %multiply_multiply_fusion = f32[1,16,32,128]{3,2,1,0:T(8,128)} fusion(f32[1,16,32,128]{3,2,1,0:T(8,128)} %param.17, f32[16,128]{1,0:T(8,128)} %param.20, f32[16]{0:T(128)S(1)} %or_convert_fusion), kind=kLoop, calls=%fused_computation.20 | loop fusion | flops 131072 | bytes 532544 | tf_op jit(solution)/shard_map/mul | solution.py:104
  3.0 8.8 %collective-permute-start.3 = (f32[1,16,32,128]{3,2,1,0:T(8,128)}, f32[1,16,32,128]{3,2,1,0:T(8,128)}, u32[]{:S(2)}, u32[]{:S(2)}) collective-permute-start(f32[1,16,32,128]{3,2,1,0:T(8,128)} %multiply_multiply_fusion), channel_id=1, source_target_pairs={{0,32},{32,0},{64,96},{96,64},{128,160},{160,128},{192,224},{224,1... | collective-permute-start | bytes 786440 | tf_op jit(solution)/shard_map/ppermute | solution.py:47
  11.8 1.9 %collective-permute-start.4 = (f32[1,16,32,128]{3,2,1,0:T(8,128)}, f32[1,16,32,128]{3,2,1,0:T(8,128)}, u32[]{:S(2)}, u32[]{:S(2)}) collective-permute-start(f32[1,16,32,128]{3,2,1,0:T(8,128)} %multiply_multiply_fusion), channel_id=1, source_target_pairs={{0,256},{32,288},{64,320},{96,352},{128,384},{160,416},{192,448},{... | collective-permute-start | bytes 786440 | tf_op jit(solution)/shard_map/ppermute | solution.py:47
  27.4 1.9 %collective-permute-start.5 = (f32[1,16,32,128]{3,2,1,0:T(8,128)}, f32[1,16,32,128]{3,2,1,0:T(8,128)S(1)}, u32[]{:S(2)}, u32[]{:S(2)}) collective-permute-start(f32[1,16,32,128]{3,2,1,0:T(8,128)} %collective-permute-done.4), channel_id=1, source_target_pairs={{0,32},{32,0},{64,96},{96,64},{128,160},{160,128},{192,224},{224,1... | collective-permute-start | bytes 786440 | tf_op jit(solution)/shard_map/ppermute | solution.py:47
  31.0 9.6 %multiply_add_fusion.7 = (f32[1,16,32,128]{3,2,1,0:T(8,128)}, f32[1,16,32,128]{3,2,1,0:T(8,128)}, f32[1,16,32,128]{3,2,1,0:T(8,128)S(1)}, bf16[1,16,32,128]{3,2,1,0:T(8,128)(2,1)S(1)}) fusion(f32[1,16,32,128]{3,2,1,0:T(8,128)S(1)} %collective-permute-done.5, f32[1,16,32,128]{3,2,1,0:T(8,128)} %collective-permute-done.4, ...), kind=kLoop, calls=%fused_computation.19 | loop fusion | flops 1572864 | bytes 1974384 | tf_op jit(solution)/shard_map/add | solution.py:60
  40.7 2.0 %collective-permute-start = (bf16[1,1,32,128]{3,2,1,0:T(8,128)(2,1)S(1)}, bf16[1,1,32,128]{3,2,1,0:T(8,128)(2,1)S(1)}, u32[]{:S(2)}, u32[]{:S(2)}) collective-permute-start(bf16[1,1,32,128]{3,2,1,0:T(8,128)(2,1)S(1)} %get-tuple-element.70), channel_id=1, source_target_pairs={{0,1},{1,2},{2,3},{3,4},{4,5},{5,6},{6,7},{7,8},{8,9},{9,10},{10,1... | collective-permute-start | bytes 24584 | tf_op jit(solution)/shard_map/ppermute | solution.py:17
  42.7 9.4 %collective-permute-start.1 = (bf16[1,1,32,128]{3,2,1,0:T(8,128)(2,1)S(1)}, bf16[1,1,32,128]{3,2,1,0:T(8,128)(2,1)S(1)}, u32[]{:S(2)}, u32[]{:S(2)}) collective-permute-start(bf16[1,1,32,128]{3,2,1,0:T(8,128)(2,1)S(1)} %get-tuple-element.71), channel_id=1, source_target_pairs={{1,0},{2,1},{3,2},{4,3},{5,4},{6,5},{7,6},{8,7},{9,8},{10,9},{11,1... | collective-permute-start | bytes 24584 | tf_op jit(solution)/shard_map/ppermute | solution.py:19
  53.0 4.4 %collective-permute-start.8 = (f32[1,8,32,128]{3,2,1,0:T(8,128)}, f32[1,8,32,128]{3,2,1,0:T(8,128)}, u32[]{:S(2)}, u32[]{:S(2)}) collective-permute-start(f32[1,8,32,128]{3,2,1,0:T(8,128)} %get-tuple-element.67), channel_id=1, source_target_pairs={{0,192},{32,224},{64,0},{96,32},{128,64},{160,96},{192,128},{224,1... | collective-permute-start | bytes 393224 | tf_op jit(solution)/shard_map/ppermute | solution.py:47
  58.1 1.9 %collective-permute-start.2 = (bf16[1,4,32,128]{3,2,1,0:T(8,128)(2,1)}, bf16[1,4,32,128]{3,2,1,0:T(8,128)(2,1)}, u32[]{:S(2)}, u32[]{:S(2)}) collective-permute-start(bf16[1,4,32,128]{3,2,1,0:T(8,128)(2,1)} %fusion.18), channel_id=1, source_target_pairs={{31,0},{0,1},{1,2},{2,3},{3,4},{4,5},{5,6},{6,7},{7,8},{8,9},{9,10... | collective-permute-start | bytes 98312 | tf_op jit(solution)/shard_map/ppermute | solution.py:29
  60.0 1.9 %collective-permute-start.6 = (f32[1,8,32,128]{3,2,1,0:T(8,128)}, f32[1,8,32,128]{3,2,1,0:T(8,128)}, u32[]{:S(2)}, u32[]{:S(2)}) collective-permute-start(f32[1,8,32,128]{3,2,1,0:T(8,128)} %get-tuple-element.66), channel_id=1, source_target_pairs={{0,64},{32,96},{64,128},{96,160},{128,192},{160,224},{192,0},{224,... | collective-permute-start | bytes 393224 | tf_op jit(solution)/shard_map/ppermute | solution.py:47
  62.0 1.7 %gather_fusion = bf16[96,32,128]{2,1,0:T(8,128)(2,1)} fusion(bf16[18,32,128]{2,1,0:T(8,128)(2,1)S(1)} %maximum_bitcast_fusion, s32[1024]{0:T(1024)} %pad_clamp_fusion), kind=kCustom, calls=%fused_computation | custom fusion | bytes 1573248 | tf_op jit(solution)/shard_map/gather | solution.py:90
  63.8 1.7 %fusion.12 = f32[1,16,32,128]{3,2,1,0:T(8,128)} fusion(f32[1,16,32,128]{3,2,1,0:T(8,128)} %get-tuple-element.58, f32[1,8,32,128]{3,2,1,0:T(8,128)} %collective-permute-done.8), kind=kLoop, calls=%fused_computation.29 | loop fusion | flops 32768 | bytes 393216 | tf_op jit(solution)/shard_map/scatter-add | solution.py:69
  65.5 4.6 %collective-permute-start.9 = (f32[1,16,32,128]{3,2,1,0:T(8,128)}, f32[1,16,32,128]{3,2,1,0:T(8,128)S(1)}, u32[]{:S(2)}, u32[]{:S(2)}) collective-permute-start(f32[1,16,32,128]{3,2,1,0:T(8,128)} %fusion.12), channel_id=1, source_target_pairs={{0,192},{32,224},{64,0},{96,32},{128,64},{160,96},{192,128},{224,1... | collective-permute-start | bytes 786440 | tf_op jit(solution)/shard_map/ppermute | solution.py:47
  71.0 1.9 %collective-permute-start.7 = (f32[1,16,32,128]{3,2,1,0:T(8,128)S(1)}, f32[1,16,32,128]{3,2,1,0:T(8,128)S(1)}, u32[]{:S(2)}, u32[]{:S(2)}) collective-permute-start(f32[1,16,32,128]{3,2,1,0:T(8,128)S(1)} %fusion.13), channel_id=1, source_target_pairs={{0,64},{32,96},{64,128},{96,160},{128,192},{160,224},{192,0},{224,... | collective-permute-start | bytes 786440 | tf_op jit(solution)/shard_map/ppermute | solution.py:47
  73.0 1.8 %fusion.4 = f32[1,16,32,128]{3,2,1,0:T(8,128)S(1)} fusion(bf16[16,6,32,128]{3,2,1,0:T(8,128)(2,1)} %bitcast.80, bf16[1,16,6,128,128]{4,3,2,1,0:T(8,128)(2,1)S(1)} %copy-done), kind=kOutput, calls=%fused_computation.10 | convolution fusion | flops 100663296 | bytes 4194304 | tf_op jit(solution)/shard_map/tnkri,tnkio->tnro/dot_general | solution.py:91
  75.6 4.9 %collective-permute-done.7 = f32[1,16,32,128]{3,2,1,0:T(8,128)S(1)} collective-permute-done((f32[1,16,32,128]{3,2,1,0:T(8,128)S(1)}, f32[1,16,32,128]{3,2,1,0:T(8,128)S(1)}, u32[]{:S(2)}, u32[]{:S(2)}) %collective-permute-start.7) | collective-permute-done | bytes 262176 | tf_op jit(solution)/shard_map/ppermute | solution.py:47
  80.6 3.7 %fusion.28 = (bf16[1,16,32,128]{3,2,1,0:T(8,128)(2,1)S(1)}, f32[1,16,32,128]{3,2,1,0:T(8,128)S(1)}) fusion(f32[1,16,32,128]{3,2,1,0:T(8,128)S(1)} %copy-done.3, f32[1,16,32,128]{3,2,1,0:T(8,128)S(1)} %collective-permute-done.9, f32[1,16,32,128]{3,2,1,0:T(8,128)S(1)} %collective-permute-done.7, f32[1,16,32,128]{3,2,1,0:T(8,128)S(1)} %copy-done.6, ...), kind=kLoop, calls=%fused_computation.68 | loop fusion | flops 1179648 | bytes 2572368 | tf_op jit(solution)/shard_map/convert_element_type | solution.py:88
  84.3 1.9 %collective-permute-start.14 = (f32[1,16,32,128]{3,2,1,0:T(8,128)S(1)}, f32[1,16,32,128]{3,2,1,0:T(8,128)S(1)}, u32[]{:S(2)}, u32[]{:S(2)}) collective-permute-start(f32[1,16,32,128]{3,2,1,0:T(8,128)S(1)} %broadcast_multiply_fusion), channel_id=1, source_target_pairs={{0,256},{32,288},{64,320},{96,352},{128,384},{160,416},{192,448},{... | collective-permute-start | bytes 786440 | tf_op jit(solution)/shard_map/ppermute | solution.py:47
  86.2 4.4 %collective-permute-start.13 = (f32[1,16,32,128]{3,2,1,0:T(8,128)S(1)}, f32[1,16,32,128]{3,2,1,0:T(8,128)S(1)}, u32[]{:S(2)}, u32[]{:S(2)}) collective-permute-start(f32[1,16,32,128]{3,2,1,0:T(8,128)S(1)} %broadcast_multiply_fusion), channel_id=1, source_target_pairs={{0,32},{32,0},{64,96},{96,64},{128,160},{160,128},{192,224},{224,1... | collective-permute-start | bytes 786440 | tf_op jit(solution)/shard_map/ppermute | solution.py:47
  91.4 5.4 %collective-permute-start.15 = (f32[1,16,32,128]{3,2,1,0:T(8,128)S(1)}, f32[1,16,32,128]{3,2,1,0:T(8,128)S(1)}, u32[]{:S(2)}, u32[]{:S(2)}) collective-permute-start(f32[1,16,32,128]{3,2,1,0:T(8,128)S(1)} %collective-permute-done.14), channel_id=1, source_target_pairs={{0,32},{32,0},{64,96},{96,64},{128,160},{160,128},{192,224},{224,1... | collective-permute-start | bytes 786440 | tf_op jit(solution)/shard_map/ppermute | solution.py:47
  96.8 1.9 %collective-permute-start.10 = (bf16[1,1,32,128]{3,2,1,0:T(8,128)(2,1)S(1)}, bf16[1,1,32,128]{3,2,1,0:T(8,128)(2,1)S(1)}, u32[]{:S(2)}, u32[]{:S(2)}) collective-permute-start(bf16[1,1,32,128]{3,2,1,0:T(8,128)(2,1)S(1)} %get-tuple-element.68), channel_id=1, source_target_pairs={{0,1},{1,2},{2,3},{3,4},{4,5},{5,6},{6,7},{7,8},{8,9},{9,10},{10,1... | collective-permute-start | bytes 24584 | tf_op jit(solution)/shard_map/ppermute | solution.py:17
  98.7 7.0 %collective-permute-start.11 = (bf16[1,1,32,128]{3,2,1,0:T(8,128)(2,1)S(1)}, bf16[1,1,32,128]{3,2,1,0:T(8,128)(2,1)S(1)}, u32[]{:S(2)}, u32[]{:S(2)}) collective-permute-start(bf16[1,1,32,128]{3,2,1,0:T(8,128)(2,1)S(1)} %get-tuple-element.69), channel_id=1, source_target_pairs={{1,0},{2,1},{3,2},{4,3},{5,4},{6,5},{7,6},{8,7},{9,8},{10,9},{11,1... | collective-permute-start | bytes 24584 | tf_op jit(solution)/shard_map/ppermute | solution.py:19
  105.9 8.5 %multiply_add_fusion.3 = (f32[1,16,32,128]{3,2,1,0:T(8,128)}, f32[1,16,32,128]{3,2,1,0:T(8,128)}, f32[1,16,32,128]{3,2,1,0:T(8,128)S(1)}) fusion(f32[1,16,32,128]{3,2,1,0:T(8,128)S(1)} %collective-permute-done.15, f32[1,16,32,128]{3,2,1,0:T(8,128)S(1)} %collective-permute-done.14, f32[1,16,32,128]{3,2,1,0:T(8,128)S(1)} %collective-permute-done.13, ...), kind=kLoop, calls=%fused_computation.15 | loop fusion | flops 1441792 | bytes 1843248 | tf_op jit(solution)/shard_map/add | solution.py:60
  115.1 1.9 %collective-permute-start.18 = (f32[1,8,32,128]{3,2,1,0:T(8,128)}, f32[1,8,32,128]{3,2,1,0:T(8,128)}, u32[]{:S(2)}, u32[]{:S(2)}) collective-permute-start(f32[1,8,32,128]{3,2,1,0:T(8,128)} %get-tuple-element.65), channel_id=1, source_target_pairs={{0,192},{32,224},{64,0},{96,32},{128,64},{160,96},{192,128},{224,1... | collective-permute-start | bytes 393224 | tf_op jit(solution)/shard_map/ppermute | solution.py:47
  117.7 1.9 %collective-permute-start.12 = (bf16[1,4,32,128]{3,2,1,0:T(8,128)(2,1)}, bf16[1,4,32,128]{3,2,1,0:T(8,128)(2,1)}, u32[]{:S(2)}, u32[]{:S(2)}) collective-permute-start(bf16[1,4,32,128]{3,2,1,0:T(8,128)(2,1)} %fusion.19), channel_id=1, source_target_pairs={{31,0},{0,1},{1,2},{2,3},{3,4},{4,5},{5,6},{6,7},{7,8},{8,9},{9,10... | collective-permute-start | bytes 98312 | tf_op jit(solution)/shard_map/ppermute | solution.py:29
  119.7 1.7 %gather_fusion.5 = bf16[96,32,128]{2,1,0:T(8,128)(2,1)} fusion(bf16[18,32,128]{2,1,0:T(8,128)(2,1)S(1)} %maximum_bitcast_fusion.1, s32[1024]{0:T(1024)} %pad_clamp_fusion), kind=kCustom, calls=%fused_computation.5 | custom fusion | bytes 1573248 | tf_op jit(solution)/shard_map/gather | solution.py:90
  121.5 3.5 %collective-permute-start.16 = (f32[1,8,32,128]{3,2,1,0:T(8,128)}, f32[1,8,32,128]{3,2,1,0:T(8,128)S(1)}, u32[]{:S(2)}, u32[]{:S(2)}) collective-permute-start(f32[1,8,32,128]{3,2,1,0:T(8,128)} %get-tuple-element.64), channel_id=1, source_target_pairs={{0,64},{32,96},{64,128},{96,160},{128,192},{160,224},{192,0},{224,... | collective-permute-start | bytes 393224 | tf_op jit(solution)/shard_map/ppermute | solution.py:47
  126.7 3.1 %collective-permute-start.19 = (f32[1,16,32,128]{3,2,1,0:T(8,128)}, f32[1,16,32,128]{3,2,1,0:T(8,128)S(1)}, u32[]{:S(2)}, u32[]{:S(2)}) collective-permute-start(f32[1,16,32,128]{3,2,1,0:T(8,128)} %fusion.10), channel_id=1, source_target_pairs={{0,192},{32,224},{64,0},{96,32},{128,64},{160,96},{192,128},{224,1... | collective-permute-start | bytes 786440 | tf_op jit(solution)/shard_map/ppermute | solution.py:47
  131.4 2.1 %collective-permute-start.17 = (f32[1,16,32,128]{3,2,1,0:T(8,128)}, f32[1,16,32,128]{3,2,1,0:T(8,128)S(1)}, u32[]{:S(2)}, u32[]{:S(2)}) collective-permute-start(f32[1,16,32,128]{3,2,1,0:T(8,128)} %fusion.11), channel_id=1, source_target_pairs={{0,64},{32,96},{64,128},{96,160},{128,192},{160,224},{192,0},{224,... | collective-permute-start | bytes 786440 | tf_op jit(solution)/shard_map/ppermute | solution.py:47
  133.6 1.7 %fusion.7 = f32[1,16,32,128]{3,2,1,0:T(8,128)S(1)} fusion(bf16[16,6,32,128]{3,2,1,0:T(8,128)(2,1)} %bitcast.79, bf16[1,16,6,128,128]{4,3,2,1,0:T(8,128)(2,1)S(1)} %copy-done), kind=kOutput, calls=%fused_computation.11 | convolution fusion | flops 100663296 | bytes 4194304 | tf_op jit(solution)/shard_map/tnkri,tnkio->tnro/dot_general | solution.py:91
  136.2 5.2 %collective-permute-done.17 = f32[1,16,32,128]{3,2,1,0:T(8,128)S(1)} collective-permute-done((f32[1,16,32,128]{3,2,1,0:T(8,128)}, f32[1,16,32,128]{3,2,1,0:T(8,128)S(1)}, u32[]{:S(2)}, u32[]{:S(2)}) %collective-permute-start.17) | collective-permute-done | bytes 262176 | tf_op jit(solution)/shard_map/ppermute | solution.py:47
  141.4 3.3 %multiply_add_fusion = f32[1,16,32,128]{3,2,1,0:T(8,128)} fusion(f32[1,16,32,128]{3,2,1,0:T(8,128)S(1)} %get-tuple-element.54, f32[1,16,32,128]{3,2,1,0:T(8,128)S(1)} %copy-done.4, f32[1,16,32,128]{3,2,1,0:T(8,128)S(1)} %collective-permute-done.19, f32[1,16,32,128]{3,2,1,0:T(8,128)S(1)} %collective-permute-done.17, f32[1,16,32,128]{3,2,1,0:T(8,128)S(1)} %copy-done.12, ...), kind=kLoop, calls=%fused_computation.12 | loop fusion | flops 1048576 | bytes 2441296 | tf_op jit(solution)/shard_map/add | solution.py:107
  (114 shorter events, 25.7 us)
Async XLA Ops:
  0.0 73.0 %copy-start = (bf16[1,16,6,128,128]{4,3,2,1,0:T(8,128)(2,1)S(1)}, bf16[1,16,6,128,128]{4,3,2,1,0:T(8,128)(2,1)}, u32[]{:S(2)}) copy-start(bf16[1,16,6,128,128]{4,3,2,1,0:T(8,128)(2,1)} %param.21) | copy-start | bytes 9437188
  0.0 31.0 %copy-start.1 = (f32[1,16,32,128]{3,2,1,0:T(8,128)S(1)}, f32[1,16,32,128]{3,2,1,0:T(8,128)}, u32[]{:S(2)}) copy-start(f32[1,16,32,128]{3,2,1,0:T(8,128)} %param.17) | copy-start | bytes 786436
  0.0 52.1 %copy-start.18 = (bf16[1,4,128,128]{3,2,1,0:T(8,128)(2,1)S(1)}, bf16[1,4,128,128]{3,2,1,0:T(8,128)(2,1)}, u32[]{:S(2)}) copy-start(bf16[1,4,128,128]{3,2,1,0:T(8,128)(2,1)} %param.22) | copy-start | bytes 393220
  3.0 27.5 %collective-permute-start.3 = (f32[1,16,32,128]{3,2,1,0:T(8,128)}, f32[1,16,32,128]{3,2,1,0:T(8,128)}, u32[]{:S(2)}, u32[]{:S(2)}) collective-permute-start(f32[1,16,32,128]{3,2,1,0:T(8,128)} %multiply_multiply_fusion), channel_id=1, source_target_pairs={{0,32},{32,0},{64,96},{96,64},{128,160},{160,128},{192,224},{224,1... | collective-permute-start | bytes 786440 | tf_op jit(solution)/shard_map/ppermute | solution.py:47
  11.8 15.6 %collective-permute-start.4 = (f32[1,16,32,128]{3,2,1,0:T(8,128)}, f32[1,16,32,128]{3,2,1,0:T(8,128)}, u32[]{:S(2)}, u32[]{:S(2)}) collective-permute-start(f32[1,16,32,128]{3,2,1,0:T(8,128)} %multiply_multiply_fusion), channel_id=1, source_target_pairs={{0,256},{32,288},{64,320},{96,352},{128,384},{160,416},{192,448},{... | collective-permute-start | bytes 786440 | tf_op jit(solution)/shard_map/ppermute | solution.py:47
  27.4 3.6 %collective-permute-start.5 = (f32[1,16,32,128]{3,2,1,0:T(8,128)}, f32[1,16,32,128]{3,2,1,0:T(8,128)S(1)}, u32[]{:S(2)}, u32[]{:S(2)}) collective-permute-start(f32[1,16,32,128]{3,2,1,0:T(8,128)} %collective-permute-done.4), channel_id=1, source_target_pairs={{0,32},{32,0},{64,96},{96,64},{128,160},{160,128},{192,224},{224,1... | collective-permute-start | bytes 786440 | tf_op jit(solution)/shard_map/ppermute | solution.py:47
  30.6 31.4 %copy-start.29 = (f32[4]{0:T(128)}, f32[4]{0:T(128)S(1)}, u32[]{:S(2)}) copy-start(f32[4]{0:T(128)S(1)} %convert_bitcast_fusion) | copy-start | bytes 52
  31.0 30.9 %copy-start.5 = (f32[1,16,32,128]{3,2,1,0:T(8,128)}, f32[1,16,32,128]{3,2,1,0:T(8,128)S(1)}, u32[]{:S(2)}) copy-start(f32[1,16,32,128]{3,2,1,0:T(8,128)S(1)} %collective-permute-done.5) | copy-start | bytes 786436
  40.7 29.4 %copy-start.13 = (f32[1,16,32,128]{3,2,1,0:T(8,128)S(1)}, f32[1,16,32,128]{3,2,1,0:T(8,128)}, u32[]{:S(2)}) copy-start(f32[1,16,32,128]{3,2,1,0:T(8,128)} %get-tuple-element.57) | copy-start | bytes 786436
  40.7 21.2 %collective-permute-start = (bf16[1,1,32,128]{3,2,1,0:T(8,128)(2,1)S(1)}, bf16[1,1,32,128]{3,2,1,0:T(8,128)(2,1)S(1)}, u32[]{:S(2)}, u32[]{:S(2)}) collective-permute-start(bf16[1,1,32,128]{3,2,1,0:T(8,128)(2,1)S(1)} %get-tuple-element.70), channel_id=1, source_target_pairs={{0,1},{1,2},{2,3},{3,4},{4,5},{5,6},{6,7},{7,8},{8,9},{9,10},{10,1... | collective-permute-start | bytes 24584 | tf_op jit(solution)/shard_map/ppermute | solution.py:17
  42.7 19.2 %collective-permute-start.1 = (bf16[1,1,32,128]{3,2,1,0:T(8,128)(2,1)S(1)}, bf16[1,1,32,128]{3,2,1,0:T(8,128)(2,1)S(1)}, u32[]{:S(2)}, u32[]{:S(2)}) collective-permute-start(bf16[1,1,32,128]{3,2,1,0:T(8,128)(2,1)S(1)} %get-tuple-element.71), channel_id=1, source_target_pairs={{1,0},{2,1},{3,2},{4,3},{5,4},{6,5},{7,6},{8,7},{9,8},{10,9},{11,1... | collective-permute-start | bytes 24584 | tf_op jit(solution)/shard_map/ppermute | solution.py:19
  53.0 10.8 %collective-permute-start.8 = (f32[1,8,32,128]{3,2,1,0:T(8,128)}, f32[1,8,32,128]{3,2,1,0:T(8,128)}, u32[]{:S(2)}, u32[]{:S(2)}) collective-permute-start(f32[1,8,32,128]{3,2,1,0:T(8,128)} %get-tuple-element.67), channel_id=1, source_target_pairs={{0,192},{32,224},{64,0},{96,32},{128,64},{160,96},{192,128},{224,1... | collective-permute-start | bytes 393224 | tf_op jit(solution)/shard_map/ppermute | solution.py:47
  58.1 16.7 %collective-permute-start.2 = (bf16[1,4,32,128]{3,2,1,0:T(8,128)(2,1)}, bf16[1,4,32,128]{3,2,1,0:T(8,128)(2,1)}, u32[]{:S(2)}, u32[]{:S(2)}) collective-permute-start(bf16[1,4,32,128]{3,2,1,0:T(8,128)(2,1)} %fusion.18), channel_id=1, source_target_pairs={{31,0},{0,1},{1,2},{2,3},{3,4},{4,5},{5,6},{6,7},{7,8},{8,9},{9,10... | collective-permute-start | bytes 98312 | tf_op jit(solution)/shard_map/ppermute | solution.py:29
  60.0 10.1 %collective-permute-start.6 = (f32[1,8,32,128]{3,2,1,0:T(8,128)}, f32[1,8,32,128]{3,2,1,0:T(8,128)}, u32[]{:S(2)}, u32[]{:S(2)}) collective-permute-start(f32[1,8,32,128]{3,2,1,0:T(8,128)} %get-tuple-element.66), channel_id=1, source_target_pairs={{0,64},{32,96},{64,128},{96,160},{128,192},{160,224},{192,0},{224,... | collective-permute-start | bytes 393224 | tf_op jit(solution)/shard_map/ppermute | solution.py:47
  65.5 10.1 %collective-permute-start.9 = (f32[1,16,32,128]{3,2,1,0:T(8,128)}, f32[1,16,32,128]{3,2,1,0:T(8,128)S(1)}, u32[]{:S(2)}, u32[]{:S(2)}) collective-permute-start(f32[1,16,32,128]{3,2,1,0:T(8,128)} %fusion.12), channel_id=1, source_target_pairs={{0,192},{32,224},{64,0},{96,32},{128,64},{160,96},{192,128},{224,1... | collective-permute-start | bytes 786440 | tf_op jit(solution)/shard_map/ppermute | solution.py:47
  71.0 9.5 %collective-permute-start.7 = (f32[1,16,32,128]{3,2,1,0:T(8,128)S(1)}, f32[1,16,32,128]{3,2,1,0:T(8,128)S(1)}, u32[]{:S(2)}, u32[]{:S(2)}) collective-permute-start(f32[1,16,32,128]{3,2,1,0:T(8,128)S(1)} %fusion.13), channel_id=1, source_target_pairs={{0,64},{32,96},{64,128},{96,160},{128,192},{160,224},{192,0},{224,... | collective-permute-start | bytes 786440 | tf_op jit(solution)/shard_map/ppermute | solution.py:47
  73.0 32.7 %copy-start.19 = (bf16[1,4,128,128]{3,2,1,0:T(8,128)(2,1)S(1)}, bf16[1,4,128,128]{3,2,1,0:T(8,128)(2,1)}, u32[]{:S(2)}) copy-start(bf16[1,4,128,128]{3,2,1,0:T(8,128)(2,1)} %param.22) | copy-start | bytes 393220
  74.7 42.3 %copy-start.30 = (f32[4]{0:T(128)S(1)}, f32[4]{0:T(128)}, u32[]{:S(2)}) copy-start(f32[4]{0:T(128)} %copy-done.29) | copy-start | bytes 52
  84.3 7.1 %collective-permute-start.14 = (f32[1,16,32,128]{3,2,1,0:T(8,128)S(1)}, f32[1,16,32,128]{3,2,1,0:T(8,128)S(1)}, u32[]{:S(2)}, u32[]{:S(2)}) collective-permute-start(f32[1,16,32,128]{3,2,1,0:T(8,128)S(1)} %broadcast_multiply_fusion), channel_id=1, source_target_pairs={{0,256},{32,288},{64,320},{96,352},{128,384},{160,416},{192,448},{... | collective-permute-start | bytes 786440 | tf_op jit(solution)/shard_map/ppermute | solution.py:47
  86.2 19.7 %collective-permute-start.13 = (f32[1,16,32,128]{3,2,1,0:T(8,128)S(1)}, f32[1,16,32,128]{3,2,1,0:T(8,128)S(1)}, u32[]{:S(2)}, u32[]{:S(2)}) collective-permute-start(f32[1,16,32,128]{3,2,1,0:T(8,128)S(1)} %broadcast_multiply_fusion), channel_id=1, source_target_pairs={{0,32},{32,0},{64,96},{96,64},{128,160},{160,128},{192,224},{224,1... | collective-permute-start | bytes 786440 | tf_op jit(solution)/shard_map/ppermute | solution.py:47
  91.4 28.3 %copy-start.7 = (f32[1,16,32,128]{3,2,1,0:T(8,128)}, f32[1,16,32,128]{3,2,1,0:T(8,128)S(1)}, u32[]{:S(2)}) copy-start(f32[1,16,32,128]{3,2,1,0:T(8,128)S(1)} %collective-permute-done.14) | copy-start | bytes 786436
  91.4 14.5 %collective-permute-start.15 = (f32[1,16,32,128]{3,2,1,0:T(8,128)S(1)}, f32[1,16,32,128]{3,2,1,0:T(8,128)S(1)}, u32[]{:S(2)}, u32[]{:S(2)}) collective-permute-start(f32[1,16,32,128]{3,2,1,0:T(8,128)S(1)} %collective-permute-done.14), channel_id=1, source_target_pairs={{0,32},{32,0},{64,96},{96,64},{128,160},{160,128},{192,224},{224,1... | collective-permute-start | bytes 786440 | tf_op jit(solution)/shard_map/ppermute | solution.py:47
  96.8 22.9 %collective-permute-start.10 = (bf16[1,1,32,128]{3,2,1,0:T(8,128)(2,1)S(1)}, bf16[1,1,32,128]{3,2,1,0:T(8,128)(2,1)S(1)}, u32[]{:S(2)}, u32[]{:S(2)}) collective-permute-start(bf16[1,1,32,128]{3,2,1,0:T(8,128)(2,1)S(1)} %get-tuple-element.68), channel_id=1, source_target_pairs={{0,1},{1,2},{2,3},{3,4},{4,5},{5,6},{6,7},{7,8},{8,9},{9,10},{10,1... | collective-permute-start | bytes 24584 | tf_op jit(solution)/shard_map/ppermute | solution.py:17
  98.7 21.0 %collective-permute-start.11 = (bf16[1,1,32,128]{3,2,1,0:T(8,128)(2,1)S(1)}, bf16[1,1,32,128]{3,2,1,0:T(8,128)(2,1)S(1)}, u32[]{:S(2)}, u32[]{:S(2)}) collective-permute-start(bf16[1,1,32,128]{3,2,1,0:T(8,128)(2,1)S(1)} %get-tuple-element.69), channel_id=1, source_target_pairs={{1,0},{2,1},{3,2},{4,3},{5,4},{6,5},{7,6},{8,7},{9,8},{10,9},{11,1... | collective-permute-start | bytes 24584 | tf_op jit(solution)/shard_map/ppermute | solution.py:19
  115.1 9.9 %collective-permute-start.18 = (f32[1,8,32,128]{3,2,1,0:T(8,128)}, f32[1,8,32,128]{3,2,1,0:T(8,128)}, u32[]{:S(2)}, u32[]{:S(2)}) collective-permute-start(f32[1,8,32,128]{3,2,1,0:T(8,128)} %get-tuple-element.65), channel_id=1, source_target_pairs={{0,192},{32,224},{64,0},{96,32},{128,64},{160,96},{192,128},{224,1... | collective-permute-start | bytes 393224 | tf_op jit(solution)/shard_map/ppermute | solution.py:47
  117.7 17.6 %collective-permute-start.12 = (bf16[1,4,32,128]{3,2,1,0:T(8,128)(2,1)}, bf16[1,4,32,128]{3,2,1,0:T(8,128)(2,1)}, u32[]{:S(2)}, u32[]{:S(2)}) collective-permute-start(bf16[1,4,32,128]{3,2,1,0:T(8,128)(2,1)} %fusion.19), channel_id=1, source_target_pairs={{31,0},{0,1},{1,2},{2,3},{3,4},{4,5},{5,6},{6,7},{7,8},{8,9},{9,10... | collective-permute-start | bytes 98312 | tf_op jit(solution)/shard_map/ppermute | solution.py:29
  121.5 19.9 %copy-start.4 = (f32[1,16,32,128]{3,2,1,0:T(8,128)S(1)}, f32[1,16,32,128]{3,2,1,0:T(8,128)}, u32[]{:S(2)}) copy-start(f32[1,16,32,128]{3,2,1,0:T(8,128)} %param.18) | copy-start | bytes 786436
  121.5 19.9 %copy-start.8 = (f32[1,16,32,128]{3,2,1,0:T(8,128)S(1)}, f32[1,16,32,128]{3,2,1,0:T(8,128)}, u32[]{:S(2)}) copy-start(f32[1,16,32,128]{3,2,1,0:T(8,128)} %copy-done.7) | copy-start | bytes 786436
  121.5 19.9 %copy-start.10 = (f32[1,16,32,128]{3,2,1,0:T(8,128)S(1)}, f32[1,16,32,128]{3,2,1,0:T(8,128)}, u32[]{:S(2)}) copy-start(f32[1,16,32,128]{3,2,1,0:T(8,128)} %copy-done.9) | copy-start | bytes 786436
  121.5 8.3 %collective-permute-start.16 = (f32[1,8,32,128]{3,2,1,0:T(8,128)}, f32[1,8,32,128]{3,2,1,0:T(8,128)S(1)}, u32[]{:S(2)}, u32[]{:S(2)}) collective-permute-start(f32[1,8,32,128]{3,2,1,0:T(8,128)} %get-tuple-element.64), channel_id=1, source_target_pairs={{0,64},{32,96},{64,128},{96,160},{128,192},{160,224},{192,0},{224,... | collective-permute-start | bytes 393224 | tf_op jit(solution)/shard_map/ppermute | solution.py:47
  126.7 9.5 %collective-permute-start.19 = (f32[1,16,32,128]{3,2,1,0:T(8,128)}, f32[1,16,32,128]{3,2,1,0:T(8,128)S(1)}, u32[]{:S(2)}, u32[]{:S(2)}) collective-permute-start(f32[1,16,32,128]{3,2,1,0:T(8,128)} %fusion.10), channel_id=1, source_target_pairs={{0,192},{32,224},{64,0},{96,32},{128,64},{160,96},{192,128},{224,1... | collective-permute-start | bytes 786440 | tf_op jit(solution)/shard_map/ppermute | solution.py:47
  131.4 10.0 %collective-permute-start.17 = (f32[1,16,32,128]{3,2,1,0:T(8,128)}, f32[1,16,32,128]{3,2,1,0:T(8,128)S(1)}, u32[]{:S(2)}, u32[]{:S(2)}) collective-permute-start(f32[1,16,32,128]{3,2,1,0:T(8,128)} %fusion.11), channel_id=1, source_target_pairs={{0,64},{32,96},{64,128},{96,160},{128,192},{160,224},{192,0},{224,... | collective-permute-start | bytes 786440 | tf_op jit(solution)/shard_map/ppermute | solution.py:47
  (19 other events, 281.7 us)

commit v2 on v0

--- a/solution.py
+++ b/solution.py
@@ -1,5 +1,8 @@
 import jax
 import jax.numpy as jnp
+import numpy as np
+from jax.experimental import pallas as pl
+from jax.experimental.pallas import tpu as pltpu
 from jax import lax
 from jax.sharding import PartitionSpec as P
 
@@ -39,6 +42,70 @@
     return deriv + jnp.float32(2.0) / NT
 
 
+def column_of(s, dx):
+    return (s // 8) * 8 + (((s // 2) % 4 + dx) % 4) * 2 + s % 2
+
+
+def routed(block, dest):
+    return lax.ppermute(block, "inst", [(s, dest(s)) for s in range(lax.axis_size("inst"))])
+
+
+def coefficient_table():
+    index = np.arange(NT)
+    offset = index[:, None] - index[None, :]
+    angle = np.pi * offset / NT
+    safe_sin = np.where(offset == 0, 1.0, np.sin(angle))
+    parity = np.where(offset % 2 == 0, 1.0, -1.0)
+    deriv = np.where(offset == 0, 0.0, 0.5 * parity * np.cos(angle) / safe_sin)
+    dspec = deriv + 2.0 / NT
+    table = np.zeros((NT, 16), np.float64)
+    for s in range(NT):
+        members = [s, s ^ 1, s ^ 8, s ^ 9]
+        targets = [s, column_of(s, 2), column_of(s, 1), column_of(s, 3)]
+        table[s] = [dspec[m, t] for t in targets for m in members]
+    return table.astype(np.float32)
+
+
+def mix_kernel(coef_ref, a_ref, b_ref, c_ref, d_ref, own_ref, far_ref, up_ref, down_ref):
+    values = (a_ref[...], b_ref[...], c_ref[...], d_ref[...])
+    for slot, out in enumerate((own_ref, far_ref, up_ref, down_ref)):
+        acc = coef_ref[slot * 4] * values[0]
+        for m in range(1, 4):
+            acc = acc + coef_ref[slot * 4 + m] * values[m]
+        out[...] = acc
+
+
+def partial_sums(coef, values):
+    rows = values[0].shape[0]
+    block = 128
+    spec = pl.BlockSpec((block, values[0].shape[1]), lambda r: (r, 0))
+    return pl.pallas_call(
+        mix_kernel,
+        grid=(rows // block,),
+        in_specs=[pl.BlockSpec(memory_space=pltpu.SMEM)] + [spec] * 4,
+        out_specs=[spec] * 4,
+        out_shape=[jax.ShapeDtypeStruct(values[0].shape, jnp.float32)] * 4,
+    )(coef, *values)
+
+
+def instance_mix(weighted):
+    i = lax.axis_index("inst")
+    shape = weighted.shape
+    flat = weighted.reshape(-1, shape[-1])
+    across = routed(flat, lambda s: s ^ 8)
+    pair = routed(jnp.stack([flat, across]), lambda s: s ^ 1)
+    coef = lax.dynamic_slice_in_dim(jnp.asarray(coefficient_table()), i, 1).reshape(-1)
+    own, far, up, down = partial_sums(coef, (flat, pair[0], across, pair[1]))
+    half = flat.shape[0] // 2
+    ahead = routed(far[:half], lambda s: column_of(s, 1))
+    behind = routed(far[half:], lambda s: column_of(s, 3))
+    up = up + jnp.concatenate([ahead, jnp.zeros_like(behind)])
+    down = down + jnp.concatenate([jnp.zeros_like(ahead), behind])
+    from_below = routed(up, lambda s: column_of(s, 1))
+    from_above = routed(down, lambda s: column_of(s, 3))
+    return (own + from_below + from_above).reshape(shape)
+
+
 def shards(lam_init, rhs, relax, cond, jac, rotor_jac, cols, rotor_shift, owned):
     local_inst = lam_init.shape[0]
     rows = lam_init.shape[1]
@@ -69,11 +136,7 @@
             axis=1,
         )
         weighted = lam * cond_wide
-        piece = lax.all_gather(weighted, "inst", axis=0, tiled=True)
-        coef = lax.dynamic_slice(dspec, (0, first_inst), (piece.shape[0], local_inst))
-        spec = jnp.zeros_like(weighted) + jnp.einsum(
-            "jt,jnrc->tnrc", coef, piece, precision=lax.Precision.HIGHEST
-        )
+        spec = instance_mix(weighted)
         resid = rhs - (stator + rotor_full + spec)
         lam = lam + relax_wide * resid * live
     return lam

time: 129 us -> 127 us (0.984)
  starting transfers between devices: 30 us -> 65.9 us
  waiting for transfers between devices: 51.7 us -> 17.1 us
  between operations: 14.6 us -> 1.37 us
  matrix products: 17.2 us -> 4.64 us
  local copies, waits for them, and re-layouts: 4.14 us -> 13.4 us
  Pallas kernels: 0 us -> 6.77 us
  other arithmetic: 11.1 us -> 16.5 us
    all_gather x2 -> x0, waiting for transfers between devices: 44 us -> none  [shards(): piece = lax.all_gather(weighted, 'inst', axis=0, tiled=True)]
    ppermute x0 -> x12, starting transfers between devices: none -> 37.6 us  [routed(): lax.ppermute(block, 'inst', [(s, dest(s)) for s in range(lax.axis_size('i...]
    ppermute x0 -> x12, waiting for transfers between devices: none -> 17.1 us  [routed(): lax.ppermute(block, 'inst', [(s, dest(s)) for s in range(lax.axis_size('i...]
    dot_general x2 -> x0, matrix products: 13.1 us -> none  [shards(): jnp.einsum('jt,jnrc->tnrc', coef, piece, precision=lax.Precision.HIGHEST)]
    pallas_call x0 -> x2, Pallas kernels: none -> 6.77 us  [partial_sums(): pl.pallas_call(mix_kernel, grid=(rows // block,), in_specs=[pl.BlockSpec(...]
    ppermute x2, waiting for transfers between devices: 5.31 us -> 0.01 us  [padded(): lax.ppermute(tail, axis, [(i, (i + 1) % count) for i in range(count)])]
    add x0 -> x7, other arithmetic: none -> 4.81 us  [the longest x2 1.98 us: instance_mix(): down = down + jnp.concatenate([jnp.zeros_like(ahead), behind])]
    slice x0 -> x2, local copies, waits for them, and re-layouts: none -> 3.36 us  [instance_mix(): ahead = routed(far[:half], lambda s: column_of(s, 1))]
  transfers between devices with their start and end apart: 8 -> 18, of which waited for: 5 -> 5; matrix products, arithmetic and copies ran while one was open for 11% -> 25% of each run, Pallas kernels for 0% -> 5%
where the time goes in v2:
time: 127 us; the launch traced here: 126 us
  starting transfers between devices  65.9 us (52%)
  waiting for transfers between devices  17.1 us (13%)
  other arithmetic  16.5 us (13%)
  local copies, waits for them, and re-layouts  13.4 us (11%)
  Pallas kernels  6.77 us (5%)
  matrix products  4.64 us (4%)
  between operations  1.37 us (1%)
    ppermute x12, starting transfers between devices, routed(): lax.ppermute(block, 'inst', [(s, dest(s)) for s in range(lax.axis_size('i...  37.6 us
    ppermute x2, starting transfers between devices, padded(): lax.ppermute(head, axis, [((i + 1) % count, i) for i in range(count)])  20.7 us
    ppermute x12, waiting for transfers between devices, routed(): lax.ppermute(block, 'inst', [(s, dest(s)) for s in range(lax.axis_size('i...  17.1 us
    pallas_call x2, Pallas kernels, partial_sums(): pl.pallas_call(mix_kernel, grid=(rows // block,), in_specs=[pl.BlockSpec(...  6.77 us
    ppermute x2, starting transfers between devices, padded(): lax.ppermute(tail, axis, [(i, (i + 1) % count) for i in range(count)])  3.84 us
    ppermute x2, starting transfers between devices, shifted(): return lax.ppermute(block, axis, route)  3.82 us
    dot_general x2, matrix products, shards(): jnp.einsum('tnkri,tnkio->tnro', picked, jac, preferred_element_type=jnp.f...  3.44 us
    gather x2, local copies, waits for them, and re-layouts, shards(): picked = lam_h[:, cols]  3.37 us
  transfers between devices with their start and end apart: 18, of which 5 were waited for; matrix products, arithmetic and copies ran while one was open for 25% of the time, Pallas kernels for 5%

profile of v2, /device:TPU:1, one launch (start us, length us, event | category | flops | bytes accessed | tf_op | source)
XLA Modules:
  0.0 125.7 jit_solution(7304759653910432499)
XLA Ops:
  2.0 4.0 %collective-permute-start.3 = (f32[512,128]{1,0:T(8,128)S(1)}, f32[512,128]{1,0:T(8,128)}, u32[]{:S(2)}, u32[]{:S(2)}) collective-permute-start(f32[512,128]{1,0:T(8,128)S(1)} %bitcast.71), channel_id=1, source_target_pairs={{0,256},{32,288},{64,320},{96,352},{128,384},{160,416},{192,448},{... | collective-permute-start | bytes 786440 | tf_op jit(solution)/shard_map/ppermute | solution.py:50
  6.7 13.4 %collective-permute-start.1 = (bf16[1,1,32,128]{3,2,1,0:T(8,128)(2,1)}, bf16[1,1,32,128]{3,2,1,0:T(8,128)(2,1)}, u32[]{:S(2)}, u32[]{:S(2)}) collective-permute-start(bf16[1,1,32,128]{3,2,1,0:T(8,128)(2,1)} %get-tuple-element.36), channel_id=1, source_target_pairs={{1,0},{2,1},{3,2},{4,3},{5,4},{6,5},{7,6},{8,7},{9,8},{10,9},{11,1... | collective-permute-start | bytes 24584 | tf_op jit(solution)/shard_map/ppermute | solution.py:22
  20.2 1.9 %collective-permute-start = (bf16[1,1,32,128]{3,2,1,0:T(8,128)(2,1)}, bf16[1,1,32,128]{3,2,1,0:T(8,128)(2,1)}, u32[]{:S(2)}, u32[]{:S(2)}) collective-permute-start(bf16[1,1,32,128]{3,2,1,0:T(8,128)(2,1)} %get-tuple-element.35), channel_id=1, source_target_pairs={{0,1},{1,2},{2,3},{3,4},{4,5},{5,6},{6,7},{7,8},{8,9},{9,10},{10,1... | collective-permute-start | bytes 24584 | tf_op jit(solution)/shard_map/ppermute | solution.py:20
  24.5 1.9 %collective-permute-start.2 = (bf16[1,4,32,128]{3,2,1,0:T(8,128)(2,1)}, bf16[1,4,32,128]{3,2,1,0:T(8,128)(2,1)}, u32[]{:S(2)}, u32[]{:S(2)}) collective-permute-start(bf16[1,4,32,128]{3,2,1,0:T(8,128)(2,1)} %fusion.14), channel_id=1, source_target_pairs={{31,0},{0,1},{1,2},{2,3},{3,4},{4,5},{5,6},{6,7},{7,8},{8,9},{9,10... | collective-permute-start | bytes 98312 | tf_op jit(solution)/shard_map/ppermute | solution.py:32
  26.4 1.8 %pad_maximum_fusion = f32[2,512,128]{2,1,0:T(8,128)} fusion(f32[1,512,128]{2,1,0:T(8,128)} %bitcast.16, f32[1,512,128]{2,1,0:T(8,128)S(1)} %bitcast.72), kind=kLoop, calls=%fused_computation.8 | loop fusion | flops 131072 | bytes 1048576 | tf_op jit(solution)/shard_map/stack | solution.py:96
  28.2 3.1 %collective-permute-start.4 = (f32[2,512,128]{2,1,0:T(8,128)}, f32[2,512,128]{2,1,0:T(8,128)}, u32[]{:S(2)}, u32[]{:S(2)}) collective-permute-start(f32[2,512,128]{2,1,0:T(8,128)} %pad_maximum_fusion), channel_id=1, source_target_pairs={{0,32},{32,0},{64,96},{96,64},{128,160},{160,128},{192,224},{224,1... | collective-permute-start | bytes 1572872 | tf_op jit(solution)/shard_map/ppermute | solution.py:50
  32.8 1.3 %dynamic-slice_bitcast_fusion.coef_ref = f32[16]{0:T(128)} fusion(f32[16,16]{1,0:T(8,128)} %constant.22.clone, s32[]{:T(128)S(6)} %select_n.9), kind=kLoop, calls=%fused_computation.42 | loop fusion | bytes 132 | tf_op jit(solution)/shard_map/reshape | solution.py:97
  35.3 1.9 %slice_bitcast_fusion.2 = (f32[512,128]{1,0:T(8,128)}, f32[512,128]{1,0:T(8,128)}) fusion(f32[2,512,128]{2,1,0:T(8,128)} %collective-permute-done.4), kind=kLoop, calls=%fused_computation.12 | loop fusion | bytes 1048576 | tf_op jit(solution)/shard_map/squeeze | solution.py:98
  37.2 3.4 %shard_map.109 = (f32[512,128]{1,0:T(8,128)}, f32[512,128]{1,0:T(8,128)}, f32[512,128]{1,0:T(8,128)}, f32[512,128]{1,0:T(8,128)}) custom-call(f32[16]{0:T(128)} %dynamic-slice_bitcast_fusion.coef_ref, f32[512,128]{1,0:T(8,128)} %bitcast.73, f32[512,128]{1,0:T(8,128)} %get-tuple-element.26.b_ref, f32[512,128]{1,0:T(8,128)} %collective-permute-done.3.c_ref, ...), custom_call_target="tpu_custom_call" | custom-call | tf_op jit(solution)/shard_map/pallas_call | solution.py:82
  40.6 1.7 %fusion.18 = (f32[256,128]{1,0:T(8,128)}, f32[256,128]{1,0:T(8,128)}) fusion(f32[512,128]{1,0:T(8,128)} %get-tuple-element.15), kind=kLoop, calls=%fused_computation.47 | loop fusion | bytes 524288 | tf_op jit(solution)/shard_map/slice | solution.py:100
  42.2 4.4 %collective-permute-start.7 = (f32[256,128]{1,0:T(8,128)}, f32[256,128]{1,0:T(8,128)S(1)}, u32[]{:S(2)}, u32[]{:S(2)}) collective-permute-start(f32[256,128]{1,0:T(8,128)} %get-tuple-element.32), channel_id=1, source_target_pairs={{0,192},{32,224},{64,0},{96,32},{128,64},{160,96},{192,128},{224,1... | collective-permute-start | bytes 393224 | tf_op jit(solution)/shard_map/ppermute | solution.py:50
  48.6 1.7 %gather_fusion = bf16[96,32,128]{2,1,0:T(8,128)(2,1)} fusion(bf16[18,32,128]{2,1,0:T(8,128)(2,1)S(1)} %maximum_bitcast_fusion, s32[1024]{0:T(1024)} %pad_clamp_fusion), kind=kCustom, calls=%fused_computation | custom fusion | bytes 1573248 | tf_op jit(solution)/shard_map/gather | solution.py:124
  50.3 2.0 %collective-permute-start.5 = (f32[256,128]{1,0:T(8,128)}, f32[256,128]{1,0:T(8,128)S(1)}, u32[]{:S(2)}, u32[]{:S(2)}) collective-permute-start(f32[256,128]{1,0:T(8,128)} %get-tuple-element.31), channel_id=1, source_target_pairs={{0,64},{32,96},{64,128},{96,160},{128,192},{160,224},{192,0},{224,... | collective-permute-start | bytes 393224 | tf_op jit(solution)/shard_map/ppermute | solution.py:50
  53.4 4.7 %collective-permute-start.8 = (f32[512,128]{1,0:T(8,128)S(1)}, f32[512,128]{1,0:T(8,128)S(1)}, u32[]{:S(2)}, u32[]{:S(2)}) collective-permute-start(f32[512,128]{1,0:T(8,128)S(1)} %pad_add_fusion.2), channel_id=1, source_target_pairs={{0,192},{32,224},{64,0},{96,32},{128,64},{160,96},{192,128},{224,1... | collective-permute-start | bytes 786440 | tf_op jit(solution)/shard_map/ppermute | solution.py:50
  59.5 1.9 %collective-permute-start.6 = (f32[512,128]{1,0:T(8,128)S(1)}, f32[512,128]{1,0:T(8,128)S(1)}, u32[]{:S(2)}, u32[]{:S(2)}) collective-permute-start(f32[512,128]{1,0:T(8,128)S(1)} %pad_add_fusion.3), channel_id=1, source_target_pairs={{0,64},{32,96},{64,128},{96,160},{128,192},{160,224},{192,0},{224,... | collective-permute-start | bytes 786440 | tf_op jit(solution)/shard_map/ppermute | solution.py:50
  61.5 1.7 %fusion.4 = f32[1,16,32,128]{3,2,1,0:T(8,128)S(1)} fusion(bf16[16,6,32,128]{3,2,1,0:T(8,128)(2,1)} %bitcast.70, bf16[1,16,6,128,128]{4,3,2,1,0:T(8,128)(2,1)S(1)} %copy-done), kind=kOutput, calls=%fused_computation.6 | convolution fusion | flops 100663296 | bytes 4194304 | tf_op jit(solution)/shard_map/tnkri,tnkio->tnro/dot_general | solution.py:125
  64.1 5.2 %collective-permute-done.6 = f32[512,128]{1,0:T(8,128)S(1)} collective-permute-done((f32[512,128]{1,0:T(8,128)S(1)}, f32[512,128]{1,0:T(8,128)S(1)}, u32[]{:S(2)}, u32[]{:S(2)}) %collective-permute-start.6) | collective-permute-done | bytes 262176 | tf_op jit(solution)/shard_map/ppermute | solution.py:50
  69.6 1.9 %collective-permute-start.12 = (f32[512,128]{1,0:T(8,128)S(1)}, f32[512,128]{1,0:T(8,128)S(1)}, u32[]{:S(2)}, u32[]{:S(2)}) collective-permute-start(f32[512,128]{1,0:T(8,128)S(1)} %bitcast.74), channel_id=1, source_target_pairs={{0,256},{32,288},{64,320},{96,352},{128,384},{160,416},{192,448},{... | collective-permute-start | bytes 786440 | tf_op jit(solution)/shard_map/ppermute | solution.py:50
  71.5 5.7 %collective-permute-done.12.c_ref = f32[512,128]{1,0:T(8,128)S(1)} collective-permute-done((f32[512,128]{1,0:T(8,128)S(1)}, f32[512,128]{1,0:T(8,128)S(1)}, u32[]{:S(2)}, u32[]{:S(2)}) %collective-permute-start.12) | collective-permute-done | bytes 262176 | tf_op jit(solution)/shard_map/ppermute | solution.py:50
  78.0 4.9 %collective-permute-start.13 = (f32[2,512,128]{2,1,0:T(8,128)S(1)}, f32[2,512,128]{2,1,0:T(8,128)S(1)}, u32[]{:S(2)}, u32[]{:S(2)}) collective-permute-start(f32[2,512,128]{2,1,0:T(8,128)S(1)} %pad_maximum_fusion.1), channel_id=1, source_target_pairs={{0,32},{32,0},{64,96},{96,64},{128,160},{160,128},{192,224},{224,1... | collective-permute-start | bytes 1572872 | tf_op jit(solution)/shard_map/ppermute | solution.py:50
  82.8 7.3 %collective-permute-start.10 = (bf16[1,1,32,128]{3,2,1,0:T(8,128)(2,1)S(1)}, bf16[1,1,32,128]{3,2,1,0:T(8,128)(2,1)S(1)}, u32[]{:S(2)}, u32[]{:S(2)}) collective-permute-start(bf16[1,1,32,128]{3,2,1,0:T(8,128)(2,1)S(1)} %get-tuple-element.34), channel_id=1, source_target_pairs={{1,0},{2,1},{3,2},{4,3},{5,4},{6,5},{7,6},{8,7},{9,8},{10,9},{11,1... | collective-permute-start | bytes 24584 | tf_op jit(solution)/shard_map/ppermute | solution.py:22
  90.1 1.9 %collective-permute-start.9 = (bf16[1,1,32,128]{3,2,1,0:T(8,128)(2,1)S(1)}, bf16[1,1,32,128]{3,2,1,0:T(8,128)(2,1)}, u32[]{:S(2)}, u32[]{:S(2)}) collective-permute-start(bf16[1,1,32,128]{3,2,1,0:T(8,128)(2,1)S(1)} %get-tuple-element.33), channel_id=1, source_target_pairs={{0,1},{1,2},{2,3},{3,4},{4,5},{5,6},{6,7},{7,8},{8,9},{9,10},{10,1... | collective-permute-start | bytes 24584 | tf_op jit(solution)/shard_map/ppermute | solution.py:20
  93.0 3.4 %shard_map.110 = (f32[512,128]{1,0:T(8,128)}, f32[512,128]{1,0:T(8,128)}, f32[512,128]{1,0:T(8,128)}, f32[512,128]{1,0:T(8,128)}) custom-call(f32[16]{0:T(128)} %dynamic-slice_bitcast_fusion.coef_ref, f32[512,128]{1,0:T(8,128)} %bitcast.76, f32[512,128]{1,0:T(8,128)} %get-tuple-element.24.b_ref, f32[512,128]{1,0:T(8,128)} %copy-done.6, ...), custom_call_target="tpu_custom_call" | custom-call | tf_op jit(solution)/shard_map/pallas_call | solution.py:82
  96.4 1.7 %fusion.17 = (f32[256,128]{1,0:T(8,128)}, f32[256,128]{1,0:T(8,128)}) fusion(f32[512,128]{1,0:T(8,128)} %get-tuple-element.19), kind=kLoop, calls=%fused_computation.46 | loop fusion | bytes 524288 | tf_op jit(solution)/shard_map/slice | solution.py:100
  98.1 1.9 %collective-permute-start.16 = (f32[256,128]{1,0:T(8,128)}, f32[256,128]{1,0:T(8,128)}, u32[]{:S(2)}, u32[]{:S(2)}) collective-permute-start(f32[256,128]{1,0:T(8,128)} %get-tuple-element.30), channel_id=1, source_target_pairs={{0,192},{32,224},{64,0},{96,32},{128,64},{160,96},{192,128},{224,1... | collective-permute-start | bytes 393224 | tf_op jit(solution)/shard_map/ppermute | solution.py:50
  100.7 1.9 %collective-permute-start.11 = (bf16[1,4,32,128]{3,2,1,0:T(8,128)(2,1)}, bf16[1,4,32,128]{3,2,1,0:T(8,128)(2,1)}, u32[]{:S(2)}, u32[]{:S(2)}) collective-permute-start(bf16[1,4,32,128]{3,2,1,0:T(8,128)(2,1)} %fusion.15), channel_id=1, source_target_pairs={{31,0},{0,1},{1,2},{2,3},{3,4},{4,5},{5,6},{6,7},{7,8},{8,9},{9,10... | collective-permute-start | bytes 98312 | tf_op jit(solution)/shard_map/ppermute | solution.py:32
  104.2 1.7 %gather_fusion.1 = bf16[96,32,128]{2,1,0:T(8,128)(2,1)} fusion(bf16[18,32,128]{2,1,0:T(8,128)(2,1)S(1)} %maximum_bitcast_fusion.1, s32[1024]{0:T(1024)} %pad_clamp_fusion), kind=kCustom, calls=%fused_computation.1 | custom fusion | bytes 1573248 | tf_op jit(solution)/shard_map/gather | solution.py:124
  105.9 3.5 %collective-permute-start.14 = (f32[256,128]{1,0:T(8,128)}, f32[256,128]{1,0:T(8,128)S(1)}, u32[]{:S(2)}, u32[]{:S(2)}) collective-permute-start(f32[256,128]{1,0:T(8,128)} %get-tuple-element.29), channel_id=1, source_target_pairs={{0,64},{32,96},{64,128},{96,160},{128,192},{160,224},{192,0},{224,... | collective-permute-start | bytes 393224 | tf_op jit(solution)/shard_map/ppermute | solution.py:50
  110.4 3.3 %collective-permute-start.17 = (f32[512,128]{1,0:T(8,128)S(1)}, f32[512,128]{1,0:T(8,128)S(1)}, u32[]{:S(2)}, u32[]{:S(2)}) collective-permute-start(f32[512,128]{1,0:T(8,128)S(1)} %pad_add_fusion), channel_id=1, source_target_pairs={{0,192},{32,224},{64,0},{96,32},{128,64},{160,96},{192,128},{224,1... | collective-permute-start | bytes 786440 | tf_op jit(solution)/shard_map/ppermute | solution.py:50
  115.1 1.9 %collective-permute-start.15 = (f32[512,128]{1,0:T(8,128)S(1)}, f32[512,128]{1,0:T(8,128)S(1)}, u32[]{:S(2)}, u32[]{:S(2)}) collective-permute-start(f32[512,128]{1,0:T(8,128)S(1)} %pad_add_fusion.1), channel_id=1, source_target_pairs={{0,64},{32,96},{64,128},{96,160},{128,192},{160,224},{192,0},{224,... | collective-permute-start | bytes 786440 | tf_op jit(solution)/shard_map/ppermute | solution.py:50
  117.0 1.7 %fusion.7 = f32[1,16,32,128]{3,2,1,0:T(8,128)S(1)} fusion(bf16[16,6,32,128]{3,2,1,0:T(8,128)(2,1)} %bitcast.69, bf16[1,16,6,128,128]{4,3,2,1,0:T(8,128)(2,1)S(1)} %copy-done), kind=kOutput, calls=%fused_computation.7 | convolution fusion | flops 100663296 | bytes 4194304 | tf_op jit(solution)/shard_map/tnkri,tnkio->tnro/dot_general | solution.py:125
  119.6 5.3 %collective-permute-done.15 = f32[512,128]{1,0:T(8,128)S(1)} collective-permute-done((f32[512,128]{1,0:T(8,128)S(1)}, f32[512,128]{1,0:T(8,128)S(1)}, u32[]{:S(2)}, u32[]{:S(2)}) %collective-permute-start.15) | collective-permute-done | bytes 262176 | tf_op jit(solution)/shard_map/ppermute | solution.py:50
  (96 shorter events, 20.4 us)
Async XLA Ops:
  0.0 61.5 %copy-start = (bf16[1,16,6,128,128]{4,3,2,1,0:T(8,128)(2,1)S(1)}, bf16[1,16,6,128,128]{4,3,2,1,0:T(8,128)(2,1)}, u32[]{:S(2)}) copy-start(bf16[1,16,6,128,128]{4,3,2,1,0:T(8,128)(2,1)} %param.15) | copy-start | bytes 9437188
  0.8 19.3 %copy-start.19 = (f32[16]{0:T(128)}, f32[16]{0:T(128)S(1)}, u32[]{:S(2)}) copy-start(f32[16]{0:T(128)S(1)} %or_convert_fusion) | copy-start | bytes 196
  2.0 35.1 %copy-start.1 = (f32[1,16,32,128]{3,2,1,0:T(8,128)}, f32[1,16,32,128]{3,2,1,0:T(8,128)S(1)}, u32[]{:S(2)}) copy-start(f32[1,16,32,128]{3,2,1,0:T(8,128)S(1)} %get-tuple-element.28) | copy-start | bytes 786436
  2.0 24.4 %collective-permute-start.3 = (f32[512,128]{1,0:T(8,128)S(1)}, f32[512,128]{1,0:T(8,128)}, u32[]{:S(2)}, u32[]{:S(2)}) collective-permute-start(f32[512,128]{1,0:T(8,128)S(1)} %bitcast.71), channel_id=1, source_target_pairs={{0,256},{32,288},{64,320},{96,352},{128,384},{160,416},{192,448},{... | collective-permute-start | bytes 786440 | tf_op jit(solution)/shard_map/ppermute | solution.py:50
  6.7 41.2 %collective-permute-start.1 = (bf16[1,1,32,128]{3,2,1,0:T(8,128)(2,1)}, bf16[1,1,32,128]{3,2,1,0:T(8,128)(2,1)}, u32[]{:S(2)}, u32[]{:S(2)}) collective-permute-start(bf16[1,1,32,128]{3,2,1,0:T(8,128)(2,1)} %get-tuple-element.36), channel_id=1, source_target_pairs={{1,0},{2,1},{3,2},{4,3},{5,4},{6,5},{7,6},{8,7},{9,8},{10,9},{11,1... | collective-permute-start | bytes 24584 | tf_op jit(solution)/shard_map/ppermute | solution.py:22
  20.2 27.7 %collective-permute-start = (bf16[1,1,32,128]{3,2,1,0:T(8,128)(2,1)}, bf16[1,1,32,128]{3,2,1,0:T(8,128)(2,1)}, u32[]{:S(2)}, u32[]{:S(2)}) collective-permute-start(bf16[1,1,32,128]{3,2,1,0:T(8,128)(2,1)} %get-tuple-element.35), channel_id=1, source_target_pairs={{0,1},{1,2},{2,3},{3,4},{4,5},{5,6},{6,7},{7,8},{8,9},{9,10},{10,1... | collective-permute-start | bytes 24584 | tf_op jit(solution)/shard_map/ppermute | solution.py:20
  24.5 38.7 %collective-permute-start.2 = (bf16[1,4,32,128]{3,2,1,0:T(8,128)(2,1)}, bf16[1,4,32,128]{3,2,1,0:T(8,128)(2,1)}, u32[]{:S(2)}, u32[]{:S(2)}) collective-permute-start(bf16[1,4,32,128]{3,2,1,0:T(8,128)(2,1)} %fusion.14), channel_id=1, source_target_pairs={{31,0},{0,1},{1,2},{2,3},{3,4},{4,5},{5,6},{6,7},{7,8},{8,9},{9,10... | collective-permute-start | bytes 98312 | tf_op jit(solution)/shard_map/ppermute | solution.py:32
  28.2 7.1 %collective-permute-start.4 = (f32[2,512,128]{2,1,0:T(8,128)}, f32[2,512,128]{2,1,0:T(8,128)}, u32[]{:S(2)}, u32[]{:S(2)}) collective-permute-start(f32[2,512,128]{2,1,0:T(8,128)} %pad_maximum_fusion), channel_id=1, source_target_pairs={{0,32},{32,0},{64,96},{96,64},{128,160},{160,128},{192,224},{224,1... | collective-permute-start | bytes 1572872 | tf_op jit(solution)/shard_map/ppermute | solution.py:50
  42.2 10.1 %collective-permute-start.7 = (f32[256,128]{1,0:T(8,128)}, f32[256,128]{1,0:T(8,128)S(1)}, u32[]{:S(2)}, u32[]{:S(2)}) collective-permute-start(f32[256,128]{1,0:T(8,128)} %get-tuple-element.32), channel_id=1, source_target_pairs={{0,192},{32,224},{64,0},{96,32},{128,64},{160,96},{192,128},{224,1... | collective-permute-start | bytes 393224 | tf_op jit(solution)/shard_map/ppermute | solution.py:50
  50.3 19.0 %copy-start.14 = (f32[512,128]{1,0:T(8,128)S(1)}, f32[512,128]{1,0:T(8,128)}, u32[]{:S(2)}) copy-start(f32[512,128]{1,0:T(8,128)} %get-tuple-element.13) | copy-start | bytes 786436
  50.3 8.2 %collective-permute-start.5 = (f32[256,128]{1,0:T(8,128)}, f32[256,128]{1,0:T(8,128)S(1)}, u32[]{:S(2)}, u32[]{:S(2)}) collective-permute-start(f32[256,128]{1,0:T(8,128)} %get-tuple-element.31), channel_id=1, source_target_pairs={{0,64},{32,96},{64,128},{96,160},{128,192},{160,224},{192,0},{224,... | collective-permute-start | bytes 393224 | tf_op jit(solution)/shard_map/ppermute | solution.py:50
  53.4 16.0 %copy-start.3 = (f32[1,16,32,128]{3,2,1,0:T(8,128)S(1)}, f32[1,16,32,128]{3,2,1,0:T(8,128)}, u32[]{:S(2)}) copy-start(f32[1,16,32,128]{3,2,1,0:T(8,128)} %param.12) | copy-start | bytes 786436
  53.4 16.0 %copy-start.5 = (f32[1,16,32,128]{3,2,1,0:T(8,128)S(1)}, f32[1,16,32,128]{3,2,1,0:T(8,128)}, u32[]{:S(2)}) copy-start(f32[1,16,32,128]{3,2,1,0:T(8,128)} %param.11) | copy-start | bytes 786436
  53.4 16.0 %copy-start.16 = (f32[1,16,128]{2,1,0:T(8,128)S(1)}, f32[1,16,128]{2,1,0:T(8,128)}, u32[]{:S(2)}) copy-start(f32[1,16,128]{2,1,0:T(8,128)} %param.13) | copy-start | bytes 24580
  53.4 16.0 %copy-start.20 = (f32[16]{0:T(128)S(1)}, f32[16]{0:T(128)}, u32[]{:S(2)}) copy-start(f32[16]{0:T(128)} %copy-done.19) | copy-start | bytes 196
  53.4 10.7 %collective-permute-start.8 = (f32[512,128]{1,0:T(8,128)S(1)}, f32[512,128]{1,0:T(8,128)S(1)}, u32[]{:S(2)}, u32[]{:S(2)}) collective-permute-start(f32[512,128]{1,0:T(8,128)S(1)} %pad_add_fusion.2), channel_id=1, source_target_pairs={{0,192},{32,224},{64,0},{96,32},{128,64},{160,96},{192,128},{224,1... | collective-permute-start | bytes 786440 | tf_op jit(solution)/shard_map/ppermute | solution.py:50
  59.5 9.8 %collective-permute-start.6 = (f32[512,128]{1,0:T(8,128)S(1)}, f32[512,128]{1,0:T(8,128)S(1)}, u32[]{:S(2)}, u32[]{:S(2)}) collective-permute-start(f32[512,128]{1,0:T(8,128)S(1)} %pad_add_fusion.3), channel_id=1, source_target_pairs={{0,64},{32,96},{64,128},{96,160},{128,192},{160,224},{192,0},{224,... | collective-permute-start | bytes 786440 | tf_op jit(solution)/shard_map/ppermute | solution.py:50
  63.2 28.8 %copy-start.12 = (bf16[1,4,128,128]{3,2,1,0:T(8,128)(2,1)S(1)}, bf16[1,4,128,128]{3,2,1,0:T(8,128)(2,1)}, u32[]{:S(2)}) copy-start(bf16[1,4,128,128]{3,2,1,0:T(8,128)(2,1)} %param.16) | copy-start | bytes 393220
  69.4 30.6 %copy-start.25 = (f32[4]{0:T(128)S(1)}, f32[4]{0:T(128)}, u32[]{:S(2)}) copy-start(f32[4]{0:T(128)} %copy-done.24) | copy-start | bytes 52
  69.5 22.5 %copy-start.7 = (bf16[1,16,32,128]{3,2,1,0:T(8,128)(2,1)}, bf16[1,16,32,128]{3,2,1,0:T(8,128)(2,1)S(1)}, u32[]{:S(2)}) copy-start(bf16[1,16,32,128]{3,2,1,0:T(8,128)(2,1)S(1)} %get-tuple-element.21) | copy-start | bytes 393220
  69.6 7.7 %collective-permute-start.12 = (f32[512,128]{1,0:T(8,128)S(1)}, f32[512,128]{1,0:T(8,128)S(1)}, u32[]{:S(2)}, u32[]{:S(2)}) collective-permute-start(f32[512,128]{1,0:T(8,128)S(1)} %bitcast.74), channel_id=1, source_target_pairs={{0,256},{32,288},{64,320},{96,352},{128,384},{160,416},{192,448},{... | collective-permute-start | bytes 786440 | tf_op jit(solution)/shard_map/ppermute | solution.py:50
  78.0 14.2 %collective-permute-start.13 = (f32[2,512,128]{2,1,0:T(8,128)S(1)}, f32[2,512,128]{2,1,0:T(8,128)S(1)}, u32[]{:S(2)}, u32[]{:S(2)}) collective-permute-start(f32[2,512,128]{2,1,0:T(8,128)S(1)} %pad_maximum_fusion.1), channel_id=1, source_target_pairs={{0,32},{32,0},{64,96},{96,64},{128,160},{160,128},{192,224},{224,1... | collective-permute-start | bytes 1572872 | tf_op jit(solution)/shard_map/ppermute | solution.py:50
  82.8 19.8 %collective-permute-start.10 = (bf16[1,1,32,128]{3,2,1,0:T(8,128)(2,1)S(1)}, bf16[1,1,32,128]{3,2,1,0:T(8,128)(2,1)S(1)}, u32[]{:S(2)}, u32[]{:S(2)}) collective-permute-start(bf16[1,1,32,128]{3,2,1,0:T(8,128)(2,1)S(1)} %get-tuple-element.34), channel_id=1, source_target_pairs={{1,0},{2,1},{3,2},{4,3},{5,4},{6,5},{7,6},{8,7},{9,8},{10,9},{11,1... | collective-permute-start | bytes 24584 | tf_op jit(solution)/shard_map/ppermute | solution.py:22
  90.1 13.1 %collective-permute-start.9 = (bf16[1,1,32,128]{3,2,1,0:T(8,128)(2,1)S(1)}, bf16[1,1,32,128]{3,2,1,0:T(8,128)(2,1)}, u32[]{:S(2)}, u32[]{:S(2)}) collective-permute-start(bf16[1,1,32,128]{3,2,1,0:T(8,128)(2,1)S(1)} %get-tuple-element.33), channel_id=1, source_target_pairs={{0,1},{1,2},{2,3},{3,4},{4,5},{5,6},{6,7},{7,8},{8,9},{9,10},{10,1... | collective-permute-start | bytes 24584 | tf_op jit(solution)/shard_map/ppermute | solution.py:20
  98.1 11.3 %collective-permute-start.16 = (f32[256,128]{1,0:T(8,128)}, f32[256,128]{1,0:T(8,128)}, u32[]{:S(2)}, u32[]{:S(2)}) collective-permute-start(f32[256,128]{1,0:T(8,128)} %get-tuple-element.30), channel_id=1, source_target_pairs={{0,192},{32,224},{64,0},{96,32},{128,64},{160,96},{192,128},{224,1... | collective-permute-start | bytes 393224 | tf_op jit(solution)/shard_map/ppermute | solution.py:50
  100.7 18.0 %collective-permute-start.11 = (bf16[1,4,32,128]{3,2,1,0:T(8,128)(2,1)}, bf16[1,4,32,128]{3,2,1,0:T(8,128)(2,1)}, u32[]{:S(2)}, u32[]{:S(2)}) collective-permute-start(bf16[1,4,32,128]{3,2,1,0:T(8,128)(2,1)} %fusion.15), channel_id=1, source_target_pairs={{31,0},{0,1},{1,2},{2,3},{3,4},{4,5},{5,6},{6,7},{7,8},{8,9},{9,10... | collective-permute-start | bytes 98312 | tf_op jit(solution)/shard_map/ppermute | solution.py:32
  105.9 19.0 %copy-start.13 = (f32[512,128]{1,0:T(8,128)S(1)}, f32[512,128]{1,0:T(8,128)}, u32[]{:S(2)}) copy-start(f32[512,128]{1,0:T(8,128)} %get-tuple-element.17) | copy-start | bytes 786436
  105.9 8.2 %collective-permute-start.14 = (f32[256,128]{1,0:T(8,128)}, f32[256,128]{1,0:T(8,128)S(1)}, u32[]{:S(2)}, u32[]{:S(2)}) collective-permute-start(f32[256,128]{1,0:T(8,128)} %get-tuple-element.29), channel_id=1, source_target_pairs={{0,64},{32,96},{64,128},{96,160},{128,192},{160,224},{192,0},{224,... | collective-permute-start | bytes 393224 | tf_op jit(solution)/shard_map/ppermute | solution.py:50
  110.4 14.5 %copy-start.4 = (f32[1,16,32,128]{3,2,1,0:T(8,128)S(1)}, f32[1,16,32,128]{3,2,1,0:T(8,128)}, u32[]{:S(2)}) copy-start(f32[1,16,32,128]{3,2,1,0:T(8,128)} %param.12) | copy-start | bytes 786436
  110.4 14.5 %copy-start.17 = (f32[1,16,128]{2,1,0:T(8,128)S(1)}, f32[1,16,128]{2,1,0:T(8,128)}, u32[]{:S(2)}) copy-start(f32[1,16,128]{2,1,0:T(8,128)} %param.13) | copy-start | bytes 24580
  110.4 9.2 %collective-permute-start.17 = (f32[512,128]{1,0:T(8,128)S(1)}, f32[512,128]{1,0:T(8,128)S(1)}, u32[]{:S(2)}, u32[]{:S(2)}) collective-permute-start(f32[512,128]{1,0:T(8,128)S(1)} %pad_add_fusion), channel_id=1, source_target_pairs={{0,192},{32,224},{64,0},{96,32},{128,64},{160,96},{192,128},{224,1... | collective-permute-start | bytes 786440 | tf_op jit(solution)/shard_map/ppermute | solution.py:50
  115.1 9.8 %collective-permute-start.15 = (f32[512,128]{1,0:T(8,128)S(1)}, f32[512,128]{1,0:T(8,128)S(1)}, u32[]{:S(2)}, u32[]{:S(2)}) collective-permute-start(f32[512,128]{1,0:T(8,128)S(1)} %pad_add_fusion.1), channel_id=1, source_target_pairs={{0,64},{32,96},{64,128},{96,160},{128,192},{160,224},{192,0},{224,... | collective-permute-start | bytes 786440 | tf_op jit(solution)/shard_map/ppermute | solution.py:50
  (12 other events, 95.0 us)

commit v3 on v2

--- a/solution.py
+++ b/solution.py
@@ -42,12 +42,7 @@
     return deriv + jnp.float32(2.0) / NT
 
 
-def column_of(s, dx):
-    return (s // 8) * 8 + (((s // 2) % 4 + dx) % 4) * 2 + s % 2
-
-
-def routed(block, dest):
-    return lax.ppermute(block, "inst", [(s, dest(s)) for s in range(lax.axis_size("inst"))])
+INST = ("iy", "ix", "ic")
 
 
 def coefficient_table():
@@ -60,50 +55,44 @@
     dspec = deriv + 2.0 / NT
     table = np.zeros((NT, 16), np.float64)
     for s in range(NT):
-        members = [s, s ^ 1, s ^ 8, s ^ 9]
-        targets = [s, column_of(s, 2), column_of(s, 1), column_of(s, 3)]
+        y, x, c = s // 8, (s // 2) % 4, s % 2
+        members = [(m // 2) * 8 + x * 2 + m % 2 for m in range(4)]
+        targets = [y * 8 + column * 2 + c for column in range(4)]
         table[s] = [dspec[m, t] for t in targets for m in members]
     return table.astype(np.float32)
 
 
-def mix_kernel(coef_ref, a_ref, b_ref, c_ref, d_ref, own_ref, far_ref, up_ref, down_ref):
-    values = (a_ref[...], b_ref[...], c_ref[...], d_ref[...])
-    for slot, out in enumerate((own_ref, far_ref, up_ref, down_ref)):
+def mix_kernel(coef_ref, v_ref, o_ref):
+    values = [v_ref[m] for m in range(4)]
+    for slot in range(4):
         acc = coef_ref[slot * 4] * values[0]
         for m in range(1, 4):
             acc = acc + coef_ref[slot * 4 + m] * values[m]
-        out[...] = acc
+        o_ref[slot] = acc
 
 
-def partial_sums(coef, values):
-    rows = values[0].shape[0]
+def partial_sums(coef, stacked):
+    _, rows, lanes = stacked.shape
     block = 128
-    spec = pl.BlockSpec((block, values[0].shape[1]), lambda r: (r, 0))
+    spec = pl.BlockSpec((4, block, lanes), lambda r: (0, r, 0))
     return pl.pallas_call(
         mix_kernel,
         grid=(rows // block,),
-        in_specs=[pl.BlockSpec(memory_space=pltpu.SMEM)] + [spec] * 4,
-        out_specs=[spec] * 4,
-        out_shape=[jax.ShapeDtypeStruct(values[0].shape, jnp.float32)] * 4,
-    )(coef, *values)
+        in_specs=[pl.BlockSpec(memory_space=pltpu.SMEM), spec],
+        out_specs=spec,
+        out_shape=jax.ShapeDtypeStruct(stacked.shape, jnp.float32),
+    )(coef, stacked)
 
 
 def instance_mix(weighted):
-    i = lax.axis_index("inst")
+    y, x, c = lax.axis_index("iy"), lax.axis_index("ix"), lax.axis_index("ic")
+    i = y * 8 + x * 2 + c
     shape = weighted.shape
     flat = weighted.reshape(-1, shape[-1])
-    across = routed(flat, lambda s: s ^ 8)
-    pair = routed(jnp.stack([flat, across]), lambda s: s ^ 1)
+    column = lax.all_gather(flat, ("iy", "ic"), axis=0)
     coef = lax.dynamic_slice_in_dim(jnp.asarray(coefficient_table()), i, 1).reshape(-1)
-    own, far, up, down = partial_sums(coef, (flat, pair[0], across, pair[1]))
-    half = flat.shape[0] // 2
-    ahead = routed(far[:half], lambda s: column_of(s, 1))
-    behind = routed(far[half:], lambda s: column_of(s, 3))
-    up = up + jnp.concatenate([ahead, jnp.zeros_like(behind)])
-    down = down + jnp.concatenate([jnp.zeros_like(ahead), behind])
-    from_below = routed(up, lambda s: column_of(s, 1))
-    from_above = routed(down, lambda s: column_of(s, 3))
-    return (own + from_below + from_above).reshape(shape)
+    partials = partial_sums(coef, column)
+    return lax.psum_scatter(partials, "ix", scatter_dimension=0).reshape(shape)
 
 
 def shards(lam_init, rhs, relax, cond, jac, rotor_jac, cols, rotor_shift, owned):
@@ -111,7 +100,7 @@
     rows = lam_init.shape[1]
     rotor_rows = rotor_jac.shape[1]
     dspec = spectral_matrix()
-    first_inst = lax.axis_index("inst") * local_inst
+    first_inst = 0
     row = jnp.arange(rows)
     live = ((row >= rows - rotor_rows) | (row < owned[0])).astype(jnp.float32)[None, :, None, None]
     lam = lam_init * live
@@ -143,20 +132,21 @@
 
 
 def solution(mesh):
+    fine = jax.sharding.Mesh(mesh.devices.reshape(2, 4, 2, -1), INST + ("sector",))
     return jax.shard_map(
         shards,
-        mesh=mesh,
+        mesh=fine,
         in_specs=(
-            P("inst", "sector", None, None),
-            P("inst", "sector", None, None),
-            P("inst", "sector", None),
+            P(INST, "sector", None, None),
+            P(INST, "sector", None, None),
+            P(INST, "sector", None),
             P("sector", None),
-            P("inst", "sector", None, None, None),
-            P("inst", "sector", None, None),
+            P(INST, "sector", None, None, None),
+            P(INST, "sector", None, None),
             P("sector", None),
-            P("inst", "sector"),
+            P(INST, "sector"),
             P("sector"),
         ),
-        out_specs=P("inst", "sector", None, None),
+        out_specs=P(INST, "sector", None, None),
         check_vma=False,
     )

time: 127 us -> 155 us (1.22)
  waiting for transfers between devices: 17.1 us -> 91.3 us
  starting transfers between devices: 65.9 us -> 23.5 us
  between operations: 1.37 us -> 14.2 us
  other arithmetic: 16.5 us -> 7.34 us
  local copies, waits for them, and re-layouts: 13.4 us -> 4.77 us
    all_gather x0 -> x2, waiting for transfers between devices: none -> 63 us  [instance_mix(): column = lax.all_gather(flat, ('iy', 'ic'), axis=0)]
    ppermute x12 -> x0, starting transfers between devices: 37.6 us -> none  [routed(): lax.ppermute(block, 'inst', [(s, dest(s)) for s in range(lax.axis_size('i...]
    reduce_scatter x0 -> x2, waiting for transfers between devices: none -> 18.4 us  [instance_mix(): return lax.psum_scatter(partials, 'ix', scatter_dimension=0).reshape(shape)]
    ppermute x12 -> x0, waiting for transfers between devices: 17.1 us -> none  [routed(): lax.ppermute(block, 'inst', [(s, dest(s)) for s in range(lax.axis_size('i...]
    ppermute x2, waiting for transfers between devices: 0.01 us -> 8.32 us  [padded(): lax.ppermute(tail, axis, [(i, (i + 1) % count) for i in range(count)])]
    ppermute x2, starting transfers between devices: 20.7 us -> 14.4 us  [padded(): lax.ppermute(head, axis, [((i + 1) % count, i) for i in range(count)])]
    add x7 -> x0, other arithmetic: 4.81 us -> none  [the longest x2 1.98 us: instance_mix(): down = down + jnp.concatenate([jnp.zeros_like(ahead), behind])]
    slice x2 -> x0, local copies, waits for them, and re-layouts: 3.36 us -> none  [instance_mix(): ahead = routed(far[:half], lambda s: column_of(s, 1))]
  transfers between devices with their start and end apart: 18 -> 10, of which waited for: 5 -> 7; matrix products, arithmetic and copies ran while one was open for 25% -> 7% of each run, Pallas kernels for 5% -> 0%
where the time goes in v3:
time: 155 us; the launch traced here: 154 us
  waiting for transfers between devices  91.3 us (59%)
  starting transfers between devices  23.5 us (15%)
  between operations  14.2 us (9%)
  other arithmetic  7.34 us (5%)
  Pallas kernels  6.98 us (5%)
  matrix products  5.85 us (4%)
  local copies, waits for them, and re-layouts  4.77 us (3%)
    all_gather x2, waiting for transfers between devices, instance_mix(): column = lax.all_gather(flat, ('iy', 'ic'), axis=0)  63 us
    reduce_scatter x2, waiting for transfers between devices, instance_mix(): return lax.psum_scatter(partials, 'ix', scatter_dimension=0).reshape(shape)  18.4 us
    ppermute x2, starting transfers between devices, padded(): lax.ppermute(head, axis, [((i + 1) % count, i) for i in range(count)])  14.4 us
    ppermute x2, waiting for transfers between devices, padded(): lax.ppermute(tail, axis, [(i, (i + 1) % count) for i in range(count)])  8.32 us
    pallas_call x2, Pallas kernels, partial_sums(): pl.pallas_call(mix_kernel, grid=(rows // block,), in_specs=[pl.BlockSpec(...  6.98 us
    ppermute x2, starting transfers between devices, shifted(): return lax.ppermute(block, axis, route)  5.08 us
    dot_general x2, matrix products, shards(): jnp.einsum('tnkri,tnkio->tnro', picked, jac, preferred_element_type=jnp.f...  4.65 us
    ppermute x2, starting transfers between devices, padded(): lax.ppermute(tail, axis, [(i, (i + 1) % count) for i in range(count)])  3.84 us
  transfers between devices with their start and end apart: 10, of which 7 were waited for; matrix products, arithmetic and copies ran while one was open for 7% of the time, Pallas kernels for 0%

profile of v3, /device:TPU:1, one launch (start us, length us, event | category | flops | bytes accessed | tf_op | source)
XLA Modules:
  0.0 153.9 jit_solution(4955744942598622554)
XLA Ops:
  7.4 2.0 %multiply_convert_fusion = (bf16[1,16,32,128]{3,2,1,0:T(8,128)(2,1)S(1)}, f32[1,16,32,128]{3,2,1,0:T(8,128)}) fusion(f32[1,16,32,128]{3,2,1,0:T(8,128)} %param.11, f32[16]{0:T(128)S(1)} %or_convert_fusion, f32[16,128]{1,0:T(8,128)} %param.14), kind=kLoop, calls=%fused_computation.11 | loop fusion | flops 196608 | bytes 663616 | tf_op jit(solution)/shard_map/convert_element_type | solution.py:111
  9.4 1.3 dynamic-slice_bitcast_fusion.coef_ref
  10.7 32.9 %all-gather.3.cloned.1.call-done.v_ref = f32[4,512,128]{2,1,0:T(8,128)} async-done(((f32[1,512,128]{2,1,0:T(8,128)}), f32[4,512,128]{2,1,0:T(8,128)}) %all-gather.3.cloned.1.call-update) | async-done | bytes 1048592 | tf_op jit(solution)/shard_map/all_gather | solution.py:92
  43.6 3.5 %shard_map.109 = f32[4,512,128]{2,1,0:T(8,128)} custom-call(f32[16]{0:T(128)} %dynamic-slice_bitcast_fusion.coef_ref, f32[4,512,128]{2,1,0:T(8,128)} %all-gather.3.cloned.1.call-done.v_ref), custom_call_target="tpu_custom_call" | custom-call | tf_op jit(solution)/shard_map/pallas_call | solution.py:78
  47.2 0.1 fusion.12
  47.4 0.7 fusion.14
  48.1 3.2 %collective-permute-start.2 = (bf16[1,4,32,128]{3,2,1,0:T(8,128)(2,1)}, bf16[1,4,32,128]{3,2,1,0:T(8,128)(2,1)S(1)}, u32[]{:S(2)}, u32[]{:S(2)}) collective-permute-start(bf16[1,4,32,128]{3,2,1,0:T(8,128)(2,1)} %fusion.14), channel_id=1, source_target_pairs={{31,0},{0,1},{1,2},{2,3},{3,4},{4,5},{5,6},{6,7},{7,8},{8,9},{9,10... | collective-permute-start | bytes 98312 | tf_op jit(solution)/shard_map/ppermute | solution.py:32
  51.3 6.6 %collective-permute-start.1 = (bf16[1,1,32,128]{3,2,1,0:T(8,128)(2,1)S(1)}, bf16[1,1,32,128]{3,2,1,0:T(8,128)(2,1)S(1)}, u32[]{:S(2)}, u32[]{:S(2)}) collective-permute-start(bf16[1,1,32,128]{3,2,1,0:T(8,128)(2,1)S(1)} %get-tuple-element.12), channel_id=1, source_target_pairs={{1,0},{2,1},{3,2},{4,3},{5,4},{6,5},{7,6},{8,7},{9,8},{10,9},{11,1... | collective-permute-start | bytes 24584 | tf_op jit(solution)/shard_map/ppermute | solution.py:22
  57.8 1.9 %collective-permute-start = (bf16[1,1,32,128]{3,2,1,0:T(8,128)(2,1)S(1)}, bf16[1,1,32,128]{3,2,1,0:T(8,128)(2,1)}, u32[]{:S(2)}, u32[]{:S(2)}) collective-permute-start(bf16[1,1,32,128]{3,2,1,0:T(8,128)(2,1)S(1)} %get-tuple-element.11), channel_id=1, source_target_pairs={{0,1},{1,2},{2,3},{3,4},{4,5},{5,6},{6,7},{7,8},{8,9},{9,10},{10,1... | collective-permute-start | bytes 24584 | tf_op jit(solution)/shard_map/ppermute | solution.py:20
  59.8 0.1 copy.14
  59.9 0.1 reshape.76
  60.0 5.9 %collective-permute-done = bf16[1,1,32,128]{3,2,1,0:T(8,128)(2,1)} collective-permute-done((bf16[1,1,32,128]{3,2,1,0:T(8,128)(2,1)S(1)}, bf16[1,1,32,128]{3,2,1,0:T(8,128)(2,1)}, u32[]{:S(2)}, u32[]{:S(2)}) %collective-permute-start) | collective-permute-done | bytes 8224 | tf_op jit(solution)/shard_map/ppermute | solution.py:20
  66.0 0.7 maximum_bitcast_fusion
  66.7 1.6 %gather_fusion = bf16[96,32,128]{2,1,0:T(8,128)(2,1)} fusion(bf16[18,32,128]{2,1,0:T(8,128)(2,1)S(1)} %maximum_bitcast_fusion, s32[1024]{0:T(1024)S(1)} %pad_clamp_fusion), kind=kCustom, calls=%fused_computation | custom fusion | bytes 1573248 | tf_op jit(solution)/shard_map/gather | solution.py:113
  68.3 0.7 bitcast_add_fusion.1
  69.0 8.8 %reduce-scatter.3.cloned.1.call-done = f32[1,512,128]{2,1,0:T(8,128)} async-done(((f32[4,512,128]{2,1,0:T(8,128)}), f32[1,512,128]{2,1,0:T(8,128)}) %reduce-scatter.3.cloned.1.call-update) | async-done | bytes 262160 | tf_op jit(solution)/shard_map/reduce_scatter | solution.py:95
  77.8 2.0 %fusion.16 = (bf16[1,16,32,128]{3,2,1,0:T(8,128)(2,1)S(1)}, f32[1,16,32,128]{3,2,1,0:T(8,128)S(1)}) fusion(f32[1,16,32,128]{3,2,1,0:T(8,128)} %param.12, f32[1,16,32,128]{3,2,1,0:T(8,128)} %bitcast.65, f32[1,4,32,128]{3,2,1,0:T(8,128)} %bitcast_add_fusion.1, f32[16,128]{1,0:T(8,128)S(1)} %bitcast.68, f32[1,16,32,128]{3,2,1,0:T(8,128)} %param.11, ...), kind=kOutput, calls=%fused_computation.33 | convolution fusion | flops 101187584 | bytes 5185600 | tf_op jit(solution)/shard_map/tnkri,tnkio->tnro/dot_general | solution.py:114
  79.8 0.7 broadcast_multiply_fusion
  80.6 30.0 %all-gather.5.cloned.1.call-done.v_ref = f32[4,512,128]{2,1,0:T(8,128)} async-done(((f32[1,512,128]{2,1,0:T(8,128)}), f32[4,512,128]{2,1,0:T(8,128)}) %all-gather.5.cloned.1.call-update) | async-done | bytes 1048592 | tf_op jit(solution)/shard_map/all_gather | solution.py:92
  110.7 3.5 %shard_map.110 = f32[4,512,128]{2,1,0:T(8,128)} custom-call(f32[16]{0:T(128)} %dynamic-slice_bitcast_fusion.coef_ref, f32[4,512,128]{2,1,0:T(8,128)} %all-gather.5.cloned.1.call-done.v_ref), custom_call_target="tpu_custom_call" | custom-call | tf_op jit(solution)/shard_map/pallas_call | solution.py:78
  114.2 7.8 %collective-permute-start.4 = (bf16[1,1,32,128]{3,2,1,0:T(8,128)(2,1)S(1)}, bf16[1,1,32,128]{3,2,1,0:T(8,128)(2,1)S(1)}, u32[]{:S(2)}, u32[]{:S(2)}) collective-permute-start(bf16[1,1,32,128]{3,2,1,0:T(8,128)(2,1)S(1)} %get-tuple-element.10), channel_id=1, source_target_pairs={{1,0},{2,1},{3,2},{4,3},{5,4},{6,5},{7,6},{8,7},{9,8},{10,9},{11,1... | collective-permute-start | bytes 24584 | tf_op jit(solution)/shard_map/ppermute | solution.py:22
  122.1 1.9 %collective-permute-start.3 = (bf16[1,1,32,128]{3,2,1,0:T(8,128)(2,1)S(1)}, bf16[1,1,32,128]{3,2,1,0:T(8,128)(2,1)S(1)}, u32[]{:S(2)}, u32[]{:S(2)}) collective-permute-start(bf16[1,1,32,128]{3,2,1,0:T(8,128)(2,1)S(1)} %get-tuple-element.9), channel_id=1, source_target_pairs={{0,1},{1,2},{2,3},{3,4},{4,5},{5,6},{6,7},{7,8},{8,9},{9,10},{10,1... | collective-permute-start | bytes 24584 | tf_op jit(solution)/shard_map/ppermute | solution.py:20
  124.0 1.1 fusion.10
  125.0 0.7 fusion.15
  125.7 1.9 %collective-permute-start.5 = (bf16[1,4,32,128]{3,2,1,0:T(8,128)(2,1)}, bf16[1,4,32,128]{3,2,1,0:T(8,128)(2,1)}, u32[]{:S(2)}, u32[]{:S(2)}) collective-permute-start(bf16[1,4,32,128]{3,2,1,0:T(8,128)(2,1)} %fusion.15), channel_id=1, source_target_pairs={{31,0},{0,1},{1,2},{2,3},{3,4},{4,5},{5,6},{6,7},{7,8},{8,9},{9,10... | collective-permute-start | bytes 98312 | tf_op jit(solution)/shard_map/ppermute | solution.py:32
  127.7 2.4 %collective-permute-done.3 = bf16[1,1,32,128]{3,2,1,0:T(8,128)(2,1)S(1)} collective-permute-done((bf16[1,1,32,128]{3,2,1,0:T(8,128)(2,1)S(1)}, bf16[1,1,32,128]{3,2,1,0:T(8,128)(2,1)S(1)}, u32[]{:S(2)}, u32[]{:S(2)}) %collective-permute-start.3) | collective-permute-done | bytes 8224 | tf_op jit(solution)/shard_map/ppermute | solution.py:20
  130.1 0.9 maximum_bitcast_fusion.1
  131.0 1.7 %gather_fusion.1 = bf16[96,32,128]{2,1,0:T(8,128)(2,1)} fusion(bf16[18,32,128]{2,1,0:T(8,128)(2,1)S(1)} %maximum_bitcast_fusion.1, s32[1024]{0:T(1024)} %copy-done.4), kind=kCustom, calls=%fused_computation.1 | custom fusion | bytes 1573248 | tf_op jit(solution)/shard_map/gather | solution.py:113
  132.7 1.6 %collective-permute-done.5 = bf16[1,4,32,128]{3,2,1,0:T(8,128)(2,1)} collective-permute-done((bf16[1,4,32,128]{3,2,1,0:T(8,128)(2,1)}, bf16[1,4,32,128]{3,2,1,0:T(8,128)(2,1)}, u32[]{:S(2)}, u32[]{:S(2)}) %collective-permute-start.5) | collective-permute-done | bytes 32800 | tf_op jit(solution)/shard_map/ppermute | solution.py:32
  134.3 0.9 bitcast_add_fusion
  135.2 9.6 %reduce-scatter.5.cloned.1.call-done = f32[1,512,128]{2,1,0:T(8,128)} async-done(((f32[4,512,128]{2,1,0:T(8,128)}), f32[1,512,128]{2,1,0:T(8,128)}) %reduce-scatter.5.cloned.1.call-update) | async-done | bytes 262160 | tf_op jit(solution)/shard_map/reduce_scatter | solution.py:95
  144.8 2.6 %multiply_add_fusion = f32[1,16,32,128]{3,2,1,0:T(8,128)} fusion(f32[1,16,32,128]{3,2,1,0:T(8,128)S(1)} %get-tuple-element.6, f32[1,16,32,128]{3,2,1,0:T(8,128)} %param.12, f32[1,16,32,128]{3,2,1,0:T(8,128)} %bitcast.66, f32[1,4,32,128]{3,2,1,0:T(8,128)S(1)} %bitcast_add_fusion, f32[16,128]{1,0:T(8,128)} %bitcast.67, f32[16]{0:T(128)} %copy-done.7, ...), kind=kOutput, calls=%fused_computation.8 | convolution fusion | flops 101056512 | bytes 5054528 | tf_op jit(solution)/shard_map/tnkri,tnkio->tnro/dot_general | solution.py:114
  (44 shorter events, 0.3 us)
Async XLA Ops:
  6.5 71.3 %copy-start = (bf16[1,16,6,128,128]{4,3,2,1,0:T(8,128)(2,1)S(1)}, bf16[1,16,6,128,128]{4,3,2,1,0:T(8,128)(2,1)}, u32[]{:S(2)}) copy-start(bf16[1,16,6,128,128]{4,3,2,1,0:T(8,128)(2,1)} %param.15) | copy-start | bytes 9437188
  6.5 40.7 %copy-start.12 = (s32[1,4]{1,0:T(1,128)S(1)}, s32[1,4]{1,0:T(1,128)}, u32[]{:S(2)}) copy-start(s32[1,4]{1,0:T(1,128)} %param.18) | copy-start | bytes 52
  6.5 40.7 %copy-start.3 = (bf16[1,4,128,128]{3,2,1,0:T(8,128)(2,1)S(1)}, bf16[1,4,128,128]{3,2,1,0:T(8,128)(2,1)}, u32[]{:S(2)}) copy-start(bf16[1,4,128,128]{3,2,1,0:T(8,128)(2,1)} %param.16) | copy-start | bytes 393220
  6.5 53.2 %copy-start.8 = (s32[16,6]{0,1:T(8,128)S(1)}, s32[16,6]{0,1:T(8,128)}, u32[]{:S(2)}) copy-start(s32[16,6]{0,1:T(8,128)} %param.17) | copy-start | bytes 1156
  6.5 37.1 %all-gather.3.cloned.1.call-start = ((), (), s32[]{:S(2)}) async-start(), calls=%async_computation.2 | async-start | bytes 1310720 | tf_op jit(solution)/shard_map/all_gather | solution.py:92
  7.4 52.6 %copy-start.7 = (f32[16]{0:T(128)}, f32[16]{0:T(128)S(1)}, u32[]{:S(2)}) copy-start(f32[16]{0:T(128)S(1)} %or_convert_fusion) | copy-start | bytes 196
  7.4 70.4 %copy-start.6 = (f32[1,16,128]{2,1,0:T(8,128)S(1)}, f32[1,16,128]{2,1,0:T(8,128)}, u32[]{:S(2)}) copy-start(f32[1,16,128]{2,1,0:T(8,128)} %param.13) | copy-start | bytes 24580
  9.4 68.4 %reduce-scatter.3.cloned.1.call-start = ((), (), s32[]{:S(2)}) async-start(), calls=%async_computation.3 | async-start | bytes 1310720 | tf_op jit(solution)/shard_map/reduce_scatter | solution.py:95
  47.1 63.5 %all-gather.5.cloned.1.call-start = ((), (), s32[]{:S(2)}) async-start(), calls=%async_computation.4 | async-start | bytes 1310720 | tf_op jit(solution)/shard_map/all_gather | solution.py:92
  47.2 12.8 %copy-start.9 = (f32[4]{0:T(128)}, f32[4]{0:T(128)S(1)}, u32[]{:S(2)}) copy-start(f32[4]{0:T(128)S(1)} %convert_bitcast_fusion) | copy-start | bytes 52
  48.1 20.2 %collective-permute-start.2 = (bf16[1,4,32,128]{3,2,1,0:T(8,128)(2,1)}, bf16[1,4,32,128]{3,2,1,0:T(8,128)(2,1)S(1)}, u32[]{:S(2)}, u32[]{:S(2)}) collective-permute-start(bf16[1,4,32,128]{3,2,1,0:T(8,128)(2,1)} %fusion.14), channel_id=1, source_target_pairs={{31,0},{0,1},{1,2},{2,3},{3,4},{4,5},{5,6},{6,7},{7,8},{8,9},{9,10... | collective-permute-start | bytes 98312 | tf_op jit(solution)/shard_map/ppermute | solution.py:32
  51.3 8.7 %collective-permute-start.1 = (bf16[1,1,32,128]{3,2,1,0:T(8,128)(2,1)S(1)}, bf16[1,1,32,128]{3,2,1,0:T(8,128)(2,1)S(1)}, u32[]{:S(2)}, u32[]{:S(2)}) collective-permute-start(bf16[1,1,32,128]{3,2,1,0:T(8,128)(2,1)S(1)} %get-tuple-element.12), channel_id=1, source_target_pairs={{1,0},{2,1},{3,2},{4,3},{5,4},{6,5},{7,6},{8,7},{9,8},{10,9},{11,1... | collective-permute-start | bytes 24584 | tf_op jit(solution)/shard_map/ppermute | solution.py:22
  57.8 8.1 %collective-permute-start = (bf16[1,1,32,128]{3,2,1,0:T(8,128)(2,1)S(1)}, bf16[1,1,32,128]{3,2,1,0:T(8,128)(2,1)}, u32[]{:S(2)}, u32[]{:S(2)}) collective-permute-start(bf16[1,1,32,128]{3,2,1,0:T(8,128)(2,1)S(1)} %get-tuple-element.11), channel_id=1, source_target_pairs={{0,1},{1,2},{2,3},{3,4},{4,5},{5,6},{6,7},{7,8},{8,9},{9,10},{10,1... | collective-permute-start | bytes 24584 | tf_op jit(solution)/shard_map/ppermute | solution.py:20
  60.0 17.8 %copy-start.11 = (f32[4]{0:T(128)}, f32[4]{0:T(128)S(1)}, u32[]{:S(2)}) copy-start(f32[4]{0:T(128)S(1)} %broadcast_subtract_fusion) | copy-start | bytes 52
  60.0 17.8 %copy-start.4 = (s32[1024]{0:T(1024)}, s32[1024]{0:T(1024)S(1)}, u32[]{:S(2)}) copy-start(s32[1024]{0:T(1024)S(1)} %pad_clamp_fusion) | copy-start | bytes 12292
  66.7 13.2 %copy-start.5 = (f32[16,128]{1,0:T(8,128)S(1)}, f32[16,128]{1,0:T(8,128)}, u32[]{:S(2)}) copy-start(f32[16,128]{1,0:T(8,128)} %param.14) | copy-start | bytes 24580
  79.8 47.8 %copy-start.1 = (bf16[1,16,32,128]{3,2,1,0:T(8,128)(2,1)}, bf16[1,16,32,128]{3,2,1,0:T(8,128)(2,1)S(1)}, u32[]{:S(2)}) copy-start(bf16[1,16,32,128]{3,2,1,0:T(8,128)(2,1)S(1)} %get-tuple-element.5) | copy-start | bytes 393220
  79.8 45.2 %copy-start.10 = (f32[4]{0:T(128)S(1)}, f32[4]{0:T(128)}, u32[]{:S(2)}) copy-start(f32[4]{0:T(128)} %copy-done.9) | copy-start | bytes 52
  80.6 64.2 %reduce-scatter.5.cloned.1.call-start = ((), (), s32[]{:S(2)}) async-start(), calls=%async_computation.5 | async-start | bytes 1310720 | tf_op jit(solution)/shard_map/reduce_scatter | solution.py:95
  114.2 13.4 %collective-permute-start.4 = (bf16[1,1,32,128]{3,2,1,0:T(8,128)(2,1)S(1)}, bf16[1,1,32,128]{3,2,1,0:T(8,128)(2,1)S(1)}, u32[]{:S(2)}, u32[]{:S(2)}) collective-permute-start(bf16[1,1,32,128]{3,2,1,0:T(8,128)(2,1)S(1)} %get-tuple-element.10), channel_id=1, source_target_pairs={{1,0},{2,1},{3,2},{4,3},{5,4},{6,5},{7,6},{8,7},{9,8},{10,9},{11,1... | collective-permute-start | bytes 24584 | tf_op jit(solution)/shard_map/ppermute | solution.py:22
  122.1 8.0 %collective-permute-start.3 = (bf16[1,1,32,128]{3,2,1,0:T(8,128)(2,1)S(1)}, bf16[1,1,32,128]{3,2,1,0:T(8,128)(2,1)S(1)}, u32[]{:S(2)}, u32[]{:S(2)}) collective-permute-start(bf16[1,1,32,128]{3,2,1,0:T(8,128)(2,1)S(1)} %get-tuple-element.9), channel_id=1, source_target_pairs={{0,1},{1,2},{2,3},{3,4},{4,5},{5,6},{6,7},{7,8},{8,9},{9,10},{10,1... | collective-permute-start | bytes 24584 | tf_op jit(solution)/shard_map/ppermute | solution.py:20
  125.0 5.0 %copy-start.2 = (f32[4,32,128]{2,1,0:T(8,128)}, f32[4,32,128]{2,1,0:T(8,128)S(1)}, u32[]{:S(2)}) copy-start(f32[4,32,128]{2,1,0:T(8,128)S(1)} %fusion.10) | copy-start | bytes 196612
  125.7 8.6 %collective-permute-start.5 = (bf16[1,4,32,128]{3,2,1,0:T(8,128)(2,1)}, bf16[1,4,32,128]{3,2,1,0:T(8,128)(2,1)}, u32[]{:S(2)}, u32[]{:S(2)}) collective-permute-start(bf16[1,4,32,128]{3,2,1,0:T(8,128)(2,1)} %fusion.15), channel_id=1, source_target_pairs={{31,0},{0,1},{1,2},{2,3},{3,4},{4,5},{5,6},{6,7},{7,8},{8,9},{9,10... | collective-permute-start | bytes 98312 | tf_op jit(solution)/shard_map/ppermute | solution.py:32
Sparse Core Ops, SparseCore 0:
  9.5 34.0 all-gather.2
  47.3 30.4 reduce-scatter.2
  80.7 29.9 all-gather.4
  114.3 30.4 reduce-scatter.4

commit v4 on v2

--- a/solution.py
+++ b/solution.py
@@ -96,14 +96,10 @@
     pair = routed(jnp.stack([flat, across]), lambda s: s ^ 1)
     coef = lax.dynamic_slice_in_dim(jnp.asarray(coefficient_table()), i, 1).reshape(-1)
     own, far, up, down = partial_sums(coef, (flat, pair[0], across, pair[1]))
-    half = flat.shape[0] // 2
-    ahead = routed(far[:half], lambda s: column_of(s, 1))
-    behind = routed(far[half:], lambda s: column_of(s, 3))
-    up = up + jnp.concatenate([ahead, jnp.zeros_like(behind)])
-    down = down + jnp.concatenate([jnp.zeros_like(ahead), behind])
+    from_far = routed(far, lambda s: column_of(s, 2))
     from_below = routed(up, lambda s: column_of(s, 1))
     from_above = routed(down, lambda s: column_of(s, 3))
-    return (own + from_below + from_above).reshape(shape)
+    return (own + from_far + from_below + from_above).reshape(shape)
 
 
 def shards(lam_init, rhs, relax, cond, jac, rotor_jac, cols, rotor_shift, owned):
@@ -120,16 +116,19 @@
     cond_wide = cond[None, :, None, :]
     for sweep in range(SWEEPS):
         lam_b = lam.astype(jnp.bfloat16)
-        lam_h = padded(lam_b, (("sector", 1),), 1)
-        picked = lam_h[:, cols]
-        stator = jnp.einsum("tnkri,tnkio->tnro", picked, jac, preferred_element_type=jnp.float32)
         records = jnp.einsum(
             "tjri,tjio->tjro",
             lam_b[:, rows - rotor_rows :],
             rotor_jac,
             preferred_element_type=jnp.float32,
         )
-        arrived = shifted((records * moving).astype(jnp.bfloat16), "sector", 1).astype(jnp.float32)
+        onward = jnp.concatenate([lam_b[:, rows - 1 :], (records * moving).astype(jnp.bfloat16)], axis=1)
+        onward = shifted(onward, "sector", 1)
+        head = shifted(lam_b[:, :1], "sector", -1)
+        lam_h = jnp.concatenate([onward[:, :1], lam_b, head], axis=1)
+        picked = lam_h[:, cols]
+        stator = jnp.einsum("tnkri,tnkio->tnro", picked, jac, preferred_element_type=jnp.float32)
+        arrived = onward[:, 1:].astype(jnp.float32)
         rotor = records * (1.0 - moving) + arrived
         rotor_full = jnp.concatenate(
             [jnp.zeros((local_inst, rows - rotor_rows) + rotor.shape[2:], jnp.float32), rotor],

time: 127 us -> 113 us (0.89)
  starting transfers between devices: 65.9 us -> 55.6 us
  other arithmetic: 16.5 us -> 9.3 us
  waiting for transfers between devices: 17.1 us -> 24 us
  local copies, waits for them, and re-layouts: 13.4 us -> 9.83 us
    ppermute x4 -> x0, starting transfers between devices: 24.5 us -> none  [the longest x2 20.7 us: padded(): lax.ppermute(head, axis, [((i + 1) % count, i) for i in range(count)])]
    ppermute x2 -> x4, starting transfers between devices: 3.82 us -> 24.5 us  [shifted(): return lax.ppermute(block, axis, route)]
    ppermute x12 -> x10, starting transfers between devices: 37.6 us -> 31 us  [routed(): lax.ppermute(block, 'inst', [(s, dest(s)) for s in range(lax.axis_size('i...]
    ppermute x12 -> x10, waiting for transfers between devices: 17.1 us -> 23.2 us  [routed(): lax.ppermute(block, 'inst', [(s, dest(s)) for s in range(lax.axis_size('i...]
    slice x4, local copies, waits for them, and re-layouts: 3.98 us -> 0.01 us  [the longest x2 0.01 us: shards(): lam_b[:, rows - 1:]]
    add x6 -> x2, other arithmetic: 4.01 us -> 0.1 us  [instance_mix(): return (own + from_far + from_below + from_above).reshape(shape)]
    add x2, other arithmetic: 1.7 us -> 0.15 us  [shards(): rotor = records * (1.0 - moving) + arrived]
  transfers between devices with their start and end apart: 18 -> 14, of which waited for: 5 -> 5; matrix products, arithmetic and copies ran while one was open for 25% -> 14% of each run, Pallas kernels for 5% -> 0%
where the time goes in v4:
time: 113 us; the launch traced here: 112 us
  starting transfers between devices  55.6 us (49%)
  waiting for transfers between devices  24 us (21%)
  local copies, waits for them, and re-layouts  9.83 us (9%)
  other arithmetic  9.3 us (8%)
  Pallas kernels  6.85 us (6%)
  matrix products  4.67 us (4%)
  between operations  1.32 us (1%)
    ppermute x10, starting transfers between devices, routed(): lax.ppermute(block, 'inst', [(s, dest(s)) for s in range(lax.axis_size('i...  31 us
    ppermute x4, starting transfers between devices, shifted(): return lax.ppermute(block, axis, route)  24.5 us
    ppermute x10, waiting for transfers between devices, routed(): lax.ppermute(block, 'inst', [(s, dest(s)) for s in range(lax.axis_size('i...  23.2 us
    pallas_call x2, Pallas kernels, partial_sums(): pl.pallas_call(mix_kernel, grid=(rows // block,), in_specs=[pl.BlockSpec(...  6.85 us
    squeeze x2, local copies, waits for them, and re-layouts, instance_mix(): own, far, up, down = partial_sums(coef, (flat, pair[0], across, pair[1]))  3.79 us
    dot_general x2, matrix products, shards(): jnp.einsum('tnkri,tnkio->tnro', picked, jac, preferred_element_type=jnp.f...  3.47 us
    gather x2, local copies, waits for them, and re-layouts, shards(): picked = lam_h[:, cols]  3.42 us
    another operation x2, other arithmetic, instance_mix(): pair = routed(jnp.stack([flat, across]), lambda s: s ^ 1)  2.66 us
  transfers between devices with their start and end apart: 14, of which 5 were waited for; matrix products, arithmetic and copies ran while one was open for 14% of the time, Pallas kernels for 0%

profile of v4, /device:TPU:1, one launch (start us, length us, event | category | flops | bytes accessed | tf_op | source)
XLA Modules:
  0.0 111.5 jit_solution(6626358319809988923)
XLA Ops:
  0.8 1.2 %multiply_convert_fusion = (bf16[1,16,32,128]{3,2,1,0:T(8,128)(2,1)S(1)}, f32[1,16,32,128]{3,2,1,0:T(8,128)S(1)}) fusion(f32[1,16,32,128]{3,2,1,0:T(8,128)} %param.11, f32[16]{0:T(128)S(1)} %or_convert_fusion, f32[16,128]{1,0:T(8,128)} %param.14), kind=kLoop, calls=%fused_computation.19 | loop fusion | flops 196608 | bytes 663616 | tf_op jit(solution)/shard_map/convert_element_type | solution.py:118
  2.0 4.0 %collective-permute-start.2 = (f32[512,128]{1,0:T(8,128)S(1)}, f32[512,128]{1,0:T(8,128)}, u32[]{:S(2)}, u32[]{:S(2)}) collective-permute-start(f32[512,128]{1,0:T(8,128)S(1)} %bitcast.71), channel_id=1, source_target_pairs={{0,256},{32,288},{64,320},{96,352},{128,384},{160,416},{192,448},{... | collective-permute-start | bytes 786440 | tf_op jit(solution)/shard_map/ppermute | solution.py:50
  6.1 13.5 %collective-permute-start.1 = (bf16[1,1,32,128]{3,2,1,0:T(8,128)(2,1)S(1)}, bf16[1,1,32,128]{3,2,1,0:T(8,128)(2,1)}, u32[]{:S(2)}, u32[]{:S(2)}) collective-permute-start(bf16[1,1,32,128]{3,2,1,0:T(8,128)(2,1)S(1)} %get-tuple-element.32), channel_id=1, source_target_pairs={{1,0},{2,1},{3,2},{4,3},{5,4},{6,5},{7,6},{8,7},{9,8},{10,9},{11,1... | collective-permute-start | bytes 24584 | tf_op jit(solution)/shard_map/ppermute | solution.py:32
  19.6 1.1 fusion.12
  21.8 1.9 %collective-permute-start = (bf16[1,5,32,128]{3,2,1,0:T(8,128)(2,1)S(1)}, bf16[1,5,32,128]{3,2,1,0:T(8,128)(2,1)S(1)}, u32[]{:S(2)}, u32[]{:S(2)}) collective-permute-start(bf16[1,5,32,128]{3,2,1,0:T(8,128)(2,1)S(1)} %pad_maximum_fusion.2), channel_id=1, source_target_pairs={{31,0},{0,1},{1,2},{2,3},{3,4},{4,5},{5,6},{6,7},{7,8},{8,9},{9,10... | collective-permute-start | bytes 122888 | tf_op jit(solution)/shard_map/ppermute | solution.py:32
  24.6 1.8 %pad_maximum_fusion = f32[2,512,128]{2,1,0:T(8,128)} fusion(f32[1,512,128]{2,1,0:T(8,128)} %bitcast.16, f32[1,512,128]{2,1,0:T(8,128)S(1)} %bitcast.72), kind=kLoop, calls=%fused_computation.8 | loop fusion | flops 131072 | bytes 1048576 | tf_op jit(solution)/shard_map/stack | solution.py:96
  26.4 3.1 %collective-permute-start.3 = (f32[2,512,128]{2,1,0:T(8,128)}, f32[2,512,128]{2,1,0:T(8,128)}, u32[]{:S(2)}, u32[]{:S(2)}) collective-permute-start(f32[2,512,128]{2,1,0:T(8,128)} %pad_maximum_fusion), channel_id=1, source_target_pairs={{0,32},{32,0},{64,96},{96,64},{128,160},{160,128},{192,224},{224,1... | collective-permute-start | bytes 1572872 | tf_op jit(solution)/shard_map/ppermute | solution.py:50
  30.1 1.2 %broadcast_subtract_fusion = f32[4]{0:T(128)} fusion(s32[1,4]{1,0:T(1,128)} %param.18), kind=kLoop, calls=%fused_computation.42 | loop fusion | flops 8 | bytes 32 | tf_op jit(solution)/shard_map/sub | solution.py:132
  31.3 1.3 %dynamic-slice_bitcast_fusion.coef_ref = f32[16]{0:T(128)} fusion(f32[16,16]{1,0:T(8,128)} %constant.21.clone, s32[]{:T(128)S(6)} %select_n.9), kind=kLoop, calls=%fused_computation.40 | loop fusion | bytes 132 | tf_op jit(solution)/shard_map/reshape | solution.py:97
  33.2 0.9 maximum_bitcast_fusion
  34.1 1.7 %gather_fusion = bf16[96,32,128]{2,1,0:T(8,128)(2,1)} fusion(bf16[18,32,128]{2,1,0:T(8,128)(2,1)S(1)} %maximum_bitcast_fusion, s32[1024]{0:T(1024)} %pad_clamp_fusion), kind=kCustom, calls=%fused_computation | custom fusion | bytes 1573248 | tf_op jit(solution)/shard_map/gather | solution.py:129
  35.9 1.9 %slice_bitcast_fusion.2 = (f32[512,128]{1,0:T(8,128)}, f32[512,128]{1,0:T(8,128)}) fusion(f32[2,512,128]{2,1,0:T(8,128)} %collective-permute-done.3), kind=kLoop, calls=%fused_computation.12 | loop fusion | bytes 1048576 | tf_op jit(solution)/shard_map/squeeze | solution.py:98
  37.8 3.4 %shard_map.109 = (f32[512,128]{1,0:T(8,128)}, f32[512,128]{1,0:T(8,128)}, f32[512,128]{1,0:T(8,128)}, f32[512,128]{1,0:T(8,128)}) custom-call(f32[16]{0:T(128)} %dynamic-slice_bitcast_fusion.coef_ref, f32[512,128]{1,0:T(8,128)} %bitcast.73, f32[512,128]{1,0:T(8,128)} %get-tuple-element.26.b_ref, f32[512,128]{1,0:T(8,128)} %collective-permute-done.2.c_ref, ...), custom_call_target="tpu_custom_call" | custom-call | tf_op jit(solution)/shard_map/pallas_call | solution.py:82
  41.2 4.5 %collective-permute-start.6 = (f32[512,128]{1,0:T(8,128)}, f32[512,128]{1,0:T(8,128)S(1)}, u32[]{:S(2)}, u32[]{:S(2)}) collective-permute-start(f32[512,128]{1,0:T(8,128)} %get-tuple-element.16), channel_id=1, source_target_pairs={{0,192},{32,224},{64,0},{96,32},{128,64},{160,96},{192,128},{224,1... | collective-permute-start | bytes 786440 | tf_op jit(solution)/shard_map/ppermute | solution.py:50
  45.8 1.9 %collective-permute-start.5 = (f32[512,128]{1,0:T(8,128)}, f32[512,128]{1,0:T(8,128)S(1)}, u32[]{:S(2)}, u32[]{:S(2)}) collective-permute-start(f32[512,128]{1,0:T(8,128)} %get-tuple-element.15), channel_id=1, source_target_pairs={{0,64},{32,96},{64,128},{96,160},{128,192},{160,224},{192,0},{224,... | collective-permute-start | bytes 786440 | tf_op jit(solution)/shard_map/ppermute | solution.py:50
  47.7 3.6 %collective-permute-start.4 = (f32[512,128]{1,0:T(8,128)}, f32[512,128]{1,0:T(8,128)S(1)}, u32[]{:S(2)}, u32[]{:S(2)}) collective-permute-start(f32[512,128]{1,0:T(8,128)} %get-tuple-element.14), channel_id=1, source_target_pairs={{0,128},{32,160},{64,192},{96,224},{128,0},{160,32},{192,64},{224,... | collective-permute-start | bytes 786440 | tf_op jit(solution)/shard_map/ppermute | solution.py:50
  51.4 1.8 %fusion.4 = f32[1,16,32,128]{3,2,1,0:T(8,128)S(1)} fusion(bf16[16,6,32,128]{3,2,1,0:T(8,128)(2,1)} %bitcast.70, bf16[1,16,6,128,128]{4,3,2,1,0:T(8,128)(2,1)S(1)} %copy-done), kind=kOutput, calls=%fused_computation.6 | convolution fusion | flops 100663296 | bytes 4194304 | tf_op jit(solution)/shard_map/tnkri,tnkio->tnro/dot_general | solution.py:130
  53.2 9.1 %collective-permute-done.5 = f32[512,128]{1,0:T(8,128)S(1)} collective-permute-done((f32[512,128]{1,0:T(8,128)}, f32[512,128]{1,0:T(8,128)S(1)}, u32[]{:S(2)}, u32[]{:S(2)}) %collective-permute-start.5) | collective-permute-done | bytes 262176 | tf_op jit(solution)/shard_map/ppermute | solution.py:50
  62.6 1.9 %collective-permute-start.9 = (f32[512,128]{1,0:T(8,128)S(1)}, f32[512,128]{1,0:T(8,128)S(1)}, u32[]{:S(2)}, u32[]{:S(2)}) collective-permute-start(f32[512,128]{1,0:T(8,128)S(1)} %bitcast.74), channel_id=1, source_target_pairs={{0,256},{32,288},{64,320},{96,352},{128,384},{160,416},{192,448},{... | collective-permute-start | bytes 786440 | tf_op jit(solution)/shard_map/ppermute | solution.py:50
  64.7 6.5 %collective-permute-done.9.c_ref = f32[512,128]{1,0:T(8,128)S(1)} collective-permute-done((f32[512,128]{1,0:T(8,128)S(1)}, f32[512,128]{1,0:T(8,128)S(1)}, u32[]{:S(2)}, u32[]{:S(2)}) %collective-permute-start.9) | collective-permute-done | bytes 262176 | tf_op jit(solution)/shard_map/ppermute | solution.py:50
  72.0 3.9 %collective-permute-start.10 = (f32[2,512,128]{2,1,0:T(8,128)}, f32[2,512,128]{2,1,0:T(8,128)}, u32[]{:S(2)}, u32[]{:S(2)}) collective-permute-start(f32[2,512,128]{2,1,0:T(8,128)} %pad_maximum_fusion.1), channel_id=1, source_target_pairs={{0,32},{32,0},{64,96},{96,64},{128,160},{160,128},{192,224},{224,1... | collective-permute-start | bytes 1572872 | tf_op jit(solution)/shard_map/ppermute | solution.py:50
  76.1 1.9 %collective-permute-start.7 = (bf16[1,5,32,128]{3,2,1,0:T(8,128)(2,1)S(1)}, bf16[1,5,32,128]{3,2,1,0:T(8,128)(2,1)S(1)}, u32[]{:S(2)}, u32[]{:S(2)}) collective-permute-start(bf16[1,5,32,128]{3,2,1,0:T(8,128)(2,1)S(1)} %pad_maximum_fusion.3), channel_id=1, source_target_pairs={{31,0},{0,1},{1,2},{2,3},{3,4},{4,5},{5,6},{6,7},{7,8},{8,9},{9,10... | collective-permute-start | bytes 122888 | tf_op jit(solution)/shard_map/ppermute | solution.py:32
  78.0 7.3 %collective-permute-start.8 = (bf16[1,1,32,128]{3,2,1,0:T(8,128)(2,1)S(1)}, bf16[1,1,32,128]{3,2,1,0:T(8,128)(2,1)S(1)}, u32[]{:S(2)}, u32[]{:S(2)}) collective-permute-start(bf16[1,1,32,128]{3,2,1,0:T(8,128)(2,1)S(1)} %get-tuple-element.30), channel_id=1, source_target_pairs={{1,0},{2,1},{3,2},{4,3},{5,4},{6,5},{7,6},{8,7},{9,8},{10,9},{11,1... | collective-permute-start | bytes 24584 | tf_op jit(solution)/shard_map/ppermute | solution.py:32
  86.1 1.7 %gather_fusion.1 = bf16[96,32,128]{2,1,0:T(8,128)(2,1)} fusion(bf16[18,32,128]{2,1,0:T(8,128)(2,1)S(1)} %maximum_bitcast_fusion.1, s32[1024]{0:T(1024)} %pad_clamp_fusion), kind=kCustom, calls=%fused_computation.1 | custom fusion | bytes 1573248 | tf_op jit(solution)/shard_map/gather | solution.py:129
  87.8 1.9 %slice_bitcast_fusion = (f32[512,128]{1,0:T(8,128)}, f32[512,128]{1,0:T(8,128)}) fusion(f32[2,512,128]{2,1,0:T(8,128)} %collective-permute-done.10), kind=kLoop, calls=%fused_computation.10 | loop fusion | bytes 1048576 | tf_op jit(solution)/shard_map/squeeze | solution.py:98
  89.7 3.4 %shard_map.110 = (f32[512,128]{1,0:T(8,128)}, f32[512,128]{1,0:T(8,128)}, f32[512,128]{1,0:T(8,128)}, f32[512,128]{1,0:T(8,128)}) custom-call(f32[16]{0:T(128)} %dynamic-slice_bitcast_fusion.coef_ref, f32[512,128]{1,0:T(8,128)} %bitcast.76, f32[512,128]{1,0:T(8,128)} %get-tuple-element.24.b_ref, f32[512,128]{1,0:T(8,128)} %copy-done.6, ...), custom_call_target="tpu_custom_call" | custom-call | tf_op jit(solution)/shard_map/pallas_call | solution.py:82
  93.1 2.1 %collective-permute-start.13 = (f32[512,128]{1,0:T(8,128)}, f32[512,128]{1,0:T(8,128)S(1)}, u32[]{:S(2)}, u32[]{:S(2)}) collective-permute-start(f32[512,128]{1,0:T(8,128)} %get-tuple-element.20), channel_id=1, source_target_pairs={{0,192},{32,224},{64,0},{96,32},{128,64},{160,96},{192,128},{224,1... | collective-permute-start | bytes 786440 | tf_op jit(solution)/shard_map/ppermute | solution.py:50
  95.2 3.4 %collective-permute-start.12 = (f32[512,128]{1,0:T(8,128)}, f32[512,128]{1,0:T(8,128)S(1)}, u32[]{:S(2)}, u32[]{:S(2)}) collective-permute-start(f32[512,128]{1,0:T(8,128)} %get-tuple-element.19), channel_id=1, source_target_pairs={{0,64},{32,96},{64,128},{96,160},{128,192},{160,224},{192,0},{224,... | collective-permute-start | bytes 786440 | tf_op jit(solution)/shard_map/ppermute | solution.py:50
  98.6 2.5 %collective-permute-start.11 = (f32[512,128]{1,0:T(8,128)}, f32[512,128]{1,0:T(8,128)S(1)}, u32[]{:S(2)}, u32[]{:S(2)}) collective-permute-start(f32[512,128]{1,0:T(8,128)} %get-tuple-element.18), channel_id=1, source_target_pairs={{0,128},{32,160},{64,192},{96,224},{128,0},{160,32},{192,64},{224,... | collective-permute-start | bytes 786440 | tf_op jit(solution)/shard_map/ppermute | solution.py:50
  101.1 1.7 %fusion.7 = f32[1,16,32,128]{3,2,1,0:T(8,128)S(1)} fusion(bf16[16,6,32,128]{3,2,1,0:T(8,128)(2,1)} %bitcast.69, bf16[1,16,6,128,128]{4,3,2,1,0:T(8,128)(2,1)S(1)} %copy-done), kind=kOutput, calls=%fused_computation.7 | convolution fusion | flops 100663296 | bytes 4194304 | tf_op jit(solution)/shard_map/tnkri,tnkio->tnro/dot_general | solution.py:130
  103.0 3.0 %collective-permute-done.12 = f32[512,128]{1,0:T(8,128)S(1)} collective-permute-done((f32[512,128]{1,0:T(8,128)}, f32[512,128]{1,0:T(8,128)S(1)}, u32[]{:S(2)}, u32[]{:S(2)}) %collective-permute-start.12) | collective-permute-done | bytes 262176 | tf_op jit(solution)/shard_map/ppermute | solution.py:50
  106.0 4.6 %collective-permute-done.11 = f32[512,128]{1,0:T(8,128)S(1)} collective-permute-done((f32[512,128]{1,0:T(8,128)}, f32[512,128]{1,0:T(8,128)S(1)}, u32[]{:S(2)}, u32[]{:S(2)}) %collective-permute-start.11) | collective-permute-done | bytes 262176 | tf_op jit(solution)/shard_map/ppermute | solution.py:50
  (92 shorter events, 6.5 us)
Async XLA Ops:
  0.0 51.3 %copy-start = (bf16[1,16,6,128,128]{4,3,2,1,0:T(8,128)(2,1)S(1)}, bf16[1,16,6,128,128]{4,3,2,1,0:T(8,128)(2,1)}, u32[]{:S(2)}) copy-start(bf16[1,16,6,128,128]{4,3,2,1,0:T(8,128)(2,1)} %param.15) | copy-start | bytes 9437188
  2.0 17.6 %copy-start.7 = (bf16[1,16,32,128]{3,2,1,0:T(8,128)(2,1)}, bf16[1,16,32,128]{3,2,1,0:T(8,128)(2,1)S(1)}, u32[]{:S(2)}) copy-start(bf16[1,16,32,128]{3,2,1,0:T(8,128)(2,1)S(1)} %get-tuple-element.27) | copy-start | bytes 393220
  2.0 35.7 %copy-start.1 = (f32[1,16,32,128]{3,2,1,0:T(8,128)}, f32[1,16,32,128]{3,2,1,0:T(8,128)S(1)}, u32[]{:S(2)}) copy-start(f32[1,16,32,128]{3,2,1,0:T(8,128)S(1)} %get-tuple-element.28) | copy-start | bytes 786436
  2.0 22.6 %collective-permute-start.2 = (f32[512,128]{1,0:T(8,128)S(1)}, f32[512,128]{1,0:T(8,128)}, u32[]{:S(2)}, u32[]{:S(2)}) collective-permute-start(f32[512,128]{1,0:T(8,128)S(1)} %bitcast.71), channel_id=1, source_target_pairs={{0,256},{32,288},{64,320},{96,352},{128,384},{160,416},{192,448},{... | collective-permute-start | bytes 786440 | tf_op jit(solution)/shard_map/ppermute | solution.py:50
  6.1 27.1 %collective-permute-start.1 = (bf16[1,1,32,128]{3,2,1,0:T(8,128)(2,1)S(1)}, bf16[1,1,32,128]{3,2,1,0:T(8,128)(2,1)}, u32[]{:S(2)}, u32[]{:S(2)}) collective-permute-start(bf16[1,1,32,128]{3,2,1,0:T(8,128)(2,1)S(1)} %get-tuple-element.32), channel_id=1, source_target_pairs={{1,0},{2,1},{3,2},{4,3},{5,4},{6,5},{7,6},{8,7},{9,8},{10,9},{11,1... | collective-permute-start | bytes 24584 | tf_op jit(solution)/shard_map/ppermute | solution.py:32
  21.8 10.8 %collective-permute-start = (bf16[1,5,32,128]{3,2,1,0:T(8,128)(2,1)S(1)}, bf16[1,5,32,128]{3,2,1,0:T(8,128)(2,1)S(1)}, u32[]{:S(2)}, u32[]{:S(2)}) collective-permute-start(bf16[1,5,32,128]{3,2,1,0:T(8,128)(2,1)S(1)} %pad_maximum_fusion.2), channel_id=1, source_target_pairs={{31,0},{0,1},{1,2},{2,3},{3,4},{4,5},{5,6},{6,7},{7,8},{8,9},{9,10... | collective-permute-start | bytes 122888 | tf_op jit(solution)/shard_map/ppermute | solution.py:32
  26.4 9.5 %collective-permute-start.3 = (f32[2,512,128]{2,1,0:T(8,128)}, f32[2,512,128]{2,1,0:T(8,128)}, u32[]{:S(2)}, u32[]{:S(2)}) collective-permute-start(f32[2,512,128]{2,1,0:T(8,128)} %pad_maximum_fusion), channel_id=1, source_target_pairs={{0,32},{32,0},{64,96},{96,64},{128,160},{160,128},{192,224},{224,1... | collective-permute-start | bytes 1572872 | tf_op jit(solution)/shard_map/ppermute | solution.py:50
  35.9 17.3 %copy-start.9 = (f32[4,32,128]{2,1,0:T(8,128)S(1)}, f32[4,32,128]{2,1,0:T(8,128)}, u32[]{:S(2)}) copy-start(f32[4,32,128]{2,1,0:T(8,128)} %copy-done.8) | copy-start | bytes 196612
  35.9 17.3 %copy-start.16 = (bf16[1,5,32,128]{3,2,1,0:T(8,128)(2,1)S(1)}, bf16[1,5,32,128]{3,2,1,0:T(8,128)(2,1)}, u32[]{:S(2)}) copy-start(bf16[1,5,32,128]{3,2,1,0:T(8,128)(2,1)} %copy-done.15) | copy-start | bytes 122884
  35.9 17.3 %copy-start.25 = (f32[4]{0:T(128)S(1)}, f32[4]{0:T(128)}, u32[]{:S(2)}) copy-start(f32[4]{0:T(128)} %broadcast_subtract_fusion) | copy-start | bytes 52
  37.8 24.6 %copy-start.20 = (f32[1,16,128]{2,1,0:T(8,128)S(1)}, f32[1,16,128]{2,1,0:T(8,128)}, u32[]{:S(2)}) copy-start(f32[1,16,128]{2,1,0:T(8,128)} %param.13) | copy-start | bytes 24580
  37.8 24.6 %copy-start.23 = (f32[16]{0:T(128)S(1)}, f32[16]{0:T(128)}, u32[]{:S(2)}) copy-start(f32[16]{0:T(128)} %copy-done.22) | copy-start | bytes 196
  41.2 21.1 %copy-start.14 = (f32[512,128]{1,0:T(8,128)S(1)}, f32[512,128]{1,0:T(8,128)}, u32[]{:S(2)}) copy-start(f32[512,128]{1,0:T(8,128)} %get-tuple-element.13) | copy-start | bytes 786436
  41.2 21.2 %copy-start.3 = (f32[1,16,32,128]{3,2,1,0:T(8,128)S(1)}, f32[1,16,32,128]{3,2,1,0:T(8,128)}, u32[]{:S(2)}) copy-start(f32[1,16,32,128]{3,2,1,0:T(8,128)} %param.12) | copy-start | bytes 786436
  41.2 21.2 %copy-start.5 = (f32[1,16,32,128]{3,2,1,0:T(8,128)S(1)}, f32[1,16,32,128]{3,2,1,0:T(8,128)}, u32[]{:S(2)}) copy-start(f32[1,16,32,128]{3,2,1,0:T(8,128)} %param.11) | copy-start | bytes 786436
  41.2 12.0 %collective-permute-start.6 = (f32[512,128]{1,0:T(8,128)}, f32[512,128]{1,0:T(8,128)S(1)}, u32[]{:S(2)}, u32[]{:S(2)}) collective-permute-start(f32[512,128]{1,0:T(8,128)} %get-tuple-element.16), channel_id=1, source_target_pairs={{0,192},{32,224},{64,0},{96,32},{128,64},{160,96},{192,128},{224,1... | collective-permute-start | bytes 786440 | tf_op jit(solution)/shard_map/ppermute | solution.py:50
  45.8 16.5 %collective-permute-start.5 = (f32[512,128]{1,0:T(8,128)}, f32[512,128]{1,0:T(8,128)S(1)}, u32[]{:S(2)}, u32[]{:S(2)}) collective-permute-start(f32[512,128]{1,0:T(8,128)} %get-tuple-element.15), channel_id=1, source_target_pairs={{0,64},{32,96},{64,128},{96,160},{128,192},{160,224},{192,0},{224,... | collective-permute-start | bytes 786440 | tf_op jit(solution)/shard_map/ppermute | solution.py:50
  47.7 14.6 %collective-permute-start.4 = (f32[512,128]{1,0:T(8,128)}, f32[512,128]{1,0:T(8,128)S(1)}, u32[]{:S(2)}, u32[]{:S(2)}) collective-permute-start(f32[512,128]{1,0:T(8,128)} %get-tuple-element.14), channel_id=1, source_target_pairs={{0,128},{32,160},{64,192},{96,224},{128,0},{160,32},{192,64},{224,... | collective-permute-start | bytes 786440 | tf_op jit(solution)/shard_map/ppermute | solution.py:50
  53.1 22.8 %copy-start.28 = (f32[4]{0:T(128)S(1)}, f32[4]{0:T(128)}, u32[]{:S(2)}) copy-start(f32[4]{0:T(128)} %copy-done.27) | copy-start | bytes 52
  62.6 22.8 %copy-start.2 = (f32[1,16,32,128]{3,2,1,0:T(8,128)}, f32[1,16,32,128]{3,2,1,0:T(8,128)S(1)}, u32[]{:S(2)}) copy-start(f32[1,16,32,128]{3,2,1,0:T(8,128)S(1)} %broadcast_multiply_fusion) | copy-start | bytes 786436
  62.6 8.6 %collective-permute-start.9 = (f32[512,128]{1,0:T(8,128)S(1)}, f32[512,128]{1,0:T(8,128)S(1)}, u32[]{:S(2)}, u32[]{:S(2)}) collective-permute-start(f32[512,128]{1,0:T(8,128)S(1)} %bitcast.74), channel_id=1, source_target_pairs={{0,256},{32,288},{64,320},{96,352},{128,384},{160,416},{192,448},{... | collective-permute-start | bytes 786440 | tf_op jit(solution)/shard_map/ppermute | solution.py:50
  64.7 21.4 %copy-start.10 = (f32[4,32,128]{2,1,0:T(8,128)}, f32[4,32,128]{2,1,0:T(8,128)S(1)}, u32[]{:S(2)}) copy-start(f32[4,32,128]{2,1,0:T(8,128)S(1)} %fusion.10) | copy-start | bytes 196612
  72.0 15.8 %collective-permute-start.10 = (f32[2,512,128]{2,1,0:T(8,128)}, f32[2,512,128]{2,1,0:T(8,128)}, u32[]{:S(2)}, u32[]{:S(2)}) collective-permute-start(f32[2,512,128]{2,1,0:T(8,128)} %pad_maximum_fusion.1), channel_id=1, source_target_pairs={{0,32},{32,0},{64,96},{96,64},{128,160},{160,128},{192,224},{224,1... | collective-permute-start | bytes 1572872 | tf_op jit(solution)/shard_map/ppermute | solution.py:50
  76.1 9.2 %collective-permute-start.7 = (bf16[1,5,32,128]{3,2,1,0:T(8,128)(2,1)S(1)}, bf16[1,5,32,128]{3,2,1,0:T(8,128)(2,1)S(1)}, u32[]{:S(2)}, u32[]{:S(2)}) collective-permute-start(bf16[1,5,32,128]{3,2,1,0:T(8,128)(2,1)S(1)} %pad_maximum_fusion.3), channel_id=1, source_target_pairs={{31,0},{0,1},{1,2},{2,3},{3,4},{4,5},{5,6},{6,7},{7,8},{8,9},{9,10... | collective-permute-start | bytes 122888 | tf_op jit(solution)/shard_map/ppermute | solution.py:32
  78.0 8.0 %collective-permute-start.8 = (bf16[1,1,32,128]{3,2,1,0:T(8,128)(2,1)S(1)}, bf16[1,1,32,128]{3,2,1,0:T(8,128)(2,1)S(1)}, u32[]{:S(2)}, u32[]{:S(2)}) collective-permute-start(bf16[1,1,32,128]{3,2,1,0:T(8,128)(2,1)S(1)} %get-tuple-element.30), channel_id=1, source_target_pairs={{1,0},{2,1},{3,2},{4,3},{5,4},{6,5},{7,6},{8,7},{9,8},{10,9},{11,1... | collective-permute-start | bytes 24584 | tf_op jit(solution)/shard_map/ppermute | solution.py:32
  89.7 21.0 %copy-start.21 = (f32[1,16,128]{2,1,0:T(8,128)S(1)}, f32[1,16,128]{2,1,0:T(8,128)}, u32[]{:S(2)}) copy-start(f32[1,16,128]{2,1,0:T(8,128)} %param.13) | copy-start | bytes 24580
  89.7 21.0 %copy-start.24 = (f32[16]{0:T(128)S(1)}, f32[16]{0:T(128)}, u32[]{:S(2)}) copy-start(f32[16]{0:T(128)} %copy-done.22) | copy-start | bytes 196
  93.1 17.5 %copy-start.13 = (f32[512,128]{1,0:T(8,128)S(1)}, f32[512,128]{1,0:T(8,128)}, u32[]{:S(2)}) copy-start(f32[512,128]{1,0:T(8,128)} %get-tuple-element.17) | copy-start | bytes 786436
  93.1 17.6 %copy-start.4 = (f32[1,16,32,128]{3,2,1,0:T(8,128)S(1)}, f32[1,16,32,128]{3,2,1,0:T(8,128)}, u32[]{:S(2)}) copy-start(f32[1,16,32,128]{3,2,1,0:T(8,128)} %param.12) | copy-start | bytes 786436
  93.1 9.8 %collective-permute-start.13 = (f32[512,128]{1,0:T(8,128)}, f32[512,128]{1,0:T(8,128)S(1)}, u32[]{:S(2)}, u32[]{:S(2)}) collective-permute-start(f32[512,128]{1,0:T(8,128)} %get-tuple-element.20), channel_id=1, source_target_pairs={{0,192},{32,224},{64,0},{96,32},{128,64},{160,96},{192,128},{224,1... | collective-permute-start | bytes 786440 | tf_op jit(solution)/shard_map/ppermute | solution.py:50
  95.2 10.8 %collective-permute-start.12 = (f32[512,128]{1,0:T(8,128)}, f32[512,128]{1,0:T(8,128)S(1)}, u32[]{:S(2)}, u32[]{:S(2)}) collective-permute-start(f32[512,128]{1,0:T(8,128)} %get-tuple-element.19), channel_id=1, source_target_pairs={{0,64},{32,96},{64,128},{96,160},{128,192},{160,224},{192,0},{224,... | collective-permute-start | bytes 786440 | tf_op jit(solution)/shard_map/ppermute | solution.py:50
  98.6 12.0 %collective-permute-start.11 = (f32[512,128]{1,0:T(8,128)}, f32[512,128]{1,0:T(8,128)S(1)}, u32[]{:S(2)}, u32[]{:S(2)}) collective-permute-start(f32[512,128]{1,0:T(8,128)} %get-tuple-element.18), channel_id=1, source_target_pairs={{0,128},{32,160},{64,192},{96,224},{128,0},{160,32},{192,64},{224,... | collective-permute-start | bytes 786440 | tf_op jit(solution)/shard_map/ppermute | solution.py:50
  (11 other events, 92.3 us)

commit v5 on v3

--- a/solution.py
+++ b/solution.py
@@ -45,6 +45,10 @@
 INST = ("iy", "ix", "ic")
 
 
+def routed(block, dest):
+    return lax.ppermute(block, INST, [(s, dest(s)) for s in range(NT)])
+
+
 def coefficient_table():
     index = np.arange(NT)
     offset = index[:, None] - index[None, :]
@@ -56,14 +60,14 @@
     table = np.zeros((NT, 16), np.float64)
     for s in range(NT):
         y, x, c = s // 8, (s // 2) % 4, s % 2
-        members = [(m // 2) * 8 + x * 2 + m % 2 for m in range(4)]
+        members = [s, s ^ 1, s ^ 8, s ^ 9]
         targets = [y * 8 + column * 2 + c for column in range(4)]
         table[s] = [dspec[m, t] for t in targets for m in members]
     return table.astype(np.float32)
 
 
-def mix_kernel(coef_ref, v_ref, o_ref):
-    values = [v_ref[m] for m in range(4)]
+def mix_kernel(coef_ref, own_ref, across_ref, pair_ref, o_ref):
+    values = (own_ref[...], pair_ref[0], across_ref[...], pair_ref[1])
     for slot in range(4):
         acc = coef_ref[slot * 4] * values[0]
         for m in range(1, 4):
@@ -71,28 +75,30 @@
         o_ref[slot] = acc
 
 
-def partial_sums(coef, stacked):
-    _, rows, lanes = stacked.shape
-    block = 128
-    spec = pl.BlockSpec((4, block, lanes), lambda r: (0, r, 0))
+def partial_sums(coef, own, across, pair):
+    rows, lanes = own.shape
+    block = 256
+    flat = pl.BlockSpec((block, lanes), lambda r: (r, 0))
+    stacked = pl.BlockSpec((2, block, lanes), lambda r: (0, r, 0))
     return pl.pallas_call(
         mix_kernel,
         grid=(rows // block,),
-        in_specs=[pl.BlockSpec(memory_space=pltpu.SMEM), spec],
-        out_specs=spec,
-        out_shape=jax.ShapeDtypeStruct(stacked.shape, jnp.float32),
-    )(coef, stacked)
+        in_specs=[pl.BlockSpec(memory_space=pltpu.SMEM), flat, flat, stacked],
+        out_specs=pl.BlockSpec((4, block, lanes), lambda r: (0, r, 0)),
+        out_shape=jax.ShapeDtypeStruct((4, rows, lanes), jnp.float32),
+    )(coef, own, across, pair)
 
 
 def instance_mix(weighted):
-    y, x, c = lax.axis_index("iy"), lax.axis_index("ix"), lax.axis_index("ic")
-    i = y * 8 + x * 2 + c
+    i = lax.axis_index("iy") * 8 + lax.axis_index("ix") * 2 + lax.axis_index("ic")
     shape = weighted.shape
     flat = weighted.reshape(-1, shape[-1])
-    column = lax.all_gather(flat, ("iy", "ic"), axis=0)
+    across = routed(flat, lambda s: s ^ 8)
+    pair = routed(jnp.stack([flat, across]), lambda s: s ^ 1)
     coef = lax.dynamic_slice_in_dim(jnp.asarray(coefficient_table()), i, 1).reshape(-1)
-    partials = partial_sums(coef, column)
-    return lax.psum_scatter(partials, "ix", scatter_dimension=0).reshape(shape)
+    partials = partial_sums(coef, flat, across, pair)
+    gathered = lax.all_to_all(partials, "ix", 0, 0)
+    return gathered.sum(axis=0).reshape(shape)
 
 
 def shards(lam_init, rhs, relax, cond, jac, rotor_jac, cols, rotor_shift, owned):
@@ -100,7 +106,6 @@
     rows = lam_init.shape[1]
     rotor_rows = rotor_jac.shape[1]
     dspec = spectral_matrix()
-    first_inst = 0
     row = jnp.arange(rows)
     live = ((row >= rows - rotor_rows) | (row < owned[0])).astype(jnp.float32)[None, :, None, None]
     lam = lam_init * live
@@ -109,16 +114,19 @@
     cond_wide = cond[None, :, None, :]
     for sweep in range(SWEEPS):
         lam_b = lam.astype(jnp.bfloat16)
-        lam_h = padded(lam_b, (("sector", 1),), 1)
-        picked = lam_h[:, cols]
-        stator = jnp.einsum("tnkri,tnkio->tnro", picked, jac, preferred_element_type=jnp.float32)
         records = jnp.einsum(
             "tjri,tjio->tjro",
             lam_b[:, rows - rotor_rows :],
             rotor_jac,
             preferred_element_type=jnp.float32,
         )
-        arrived = shifted((records * moving).astype(jnp.bfloat16), "sector", 1).astype(jnp.float32)
+        onward = jnp.concatenate([lam_b[:, rows - 1 :], (records * moving).astype(jnp.bfloat16)], axis=1)
+        onward = shifted(onward, "sector", 1)
+        head = shifted(lam_b[:, :1], "sector", -1)
+        lam_h = jnp.concatenate([onward[:, :1], lam_b, head], axis=1)
+        picked = lam_h[:, cols]
+        stator = jnp.einsum("tnkri,tnkio->tnro", picked, jac, preferred_element_type=jnp.float32)
+        arrived = onward[:, 1:].astype(jnp.float32)
         rotor = records * (1.0 - moving) + arrived
         rotor_full = jnp.concatenate(
             [jnp.zeros((local_inst, rows - rotor_rows) + rotor.shape[2:], jnp.float32), rotor],

time: 155 us -> 100 us (0.65)
  waiting for transfers between devices: 91.3 us -> 15.5 us
  starting transfers between devices: 23.5 us -> 45.9 us
  between operations: 14.2 us -> 1.09 us
  other arithmetic: 7.34 us -> 17.8 us
  local copies, waits for them, and re-layouts: 4.77 us -> 8.02 us
  Pallas kernels: 6.98 us -> 4.52 us
    all_gather x2 -> x0, waiting for transfers between devices: 63 us -> none  [instance_mix(): column = lax.all_gather(flat, ('iy', 'ic'), axis=0)]
    ppermute x2 -> x4, starting transfers between devices: 5.08 us -> 24.5 us  [shifted(): return lax.ppermute(block, axis, route)]
    reduce_scatter x2 -> x0, waiting for transfers between devices: 18.4 us -> none  [instance_mix(): return lax.psum_scatter(partials, 'ix', scatter_dimension=0).reshape(shape)]
    all_to_all x0 -> x2, starting transfers between devices: none -> 8.62 us  [instance_mix(): gathered = lax.all_to_all(partials, 'ix', 0, 0)]
    all_to_all x0 -> x2, waiting for transfers between devices: none -> 8.3 us  [instance_mix(): gathered = lax.all_to_all(partials, 'ix', 0, 0)]
    ppermute x4, starting transfers between devices: 18.2 us -> 12.8 us  [routed(): return lax.ppermute(block, INST, [(s, dest(s)) for s in range(NT)])]
    reduce_sum x0 -> x2, other arithmetic: none -> 4.01 us  [instance_mix(): return gathered.sum(axis=0).reshape(shape)]
    pallas_call x2, Pallas kernels: 6.98 us -> 4.52 us  [partial_sums(): pl.pallas_call(mix_kernel, grid=(rows // block,), in_specs=[pl.BlockSpec(...]
  transfers between devices with their start and end apart: 10 -> 10, of which waited for: 7 -> 4; matrix products, arithmetic and copies ran while one was open for 7% -> 22% of each run, Pallas kernels for 0% -> 2%
where the time goes in v5:
time: 100 us; the launch traced here: 98.9 us
  starting transfers between devices  45.9 us (46%)
  other arithmetic  17.8 us (18%)
  waiting for transfers between devices  15.5 us (16%)
  local copies, waits for them, and re-layouts  8.02 us (8%)
  matrix products  6.08 us (6%)
  Pallas kernels  4.52 us (5%)
  between operations  1.09 us (1%)
    ppermute x4, starting transfers between devices, shifted(): return lax.ppermute(block, axis, route)  24.5 us
    ppermute x4, starting transfers between devices, routed(): return lax.ppermute(block, INST, [(s, dest(s)) for s in range(NT)])  12.8 us
    all_to_all x2, starting transfers between devices, instance_mix(): gathered = lax.all_to_all(partials, 'ix', 0, 0)  8.62 us
    all_to_all x2, waiting for transfers between devices, instance_mix(): gathered = lax.all_to_all(partials, 'ix', 0, 0)  8.3 us
    ppermute x4, waiting for transfers between devices, routed(): return lax.ppermute(block, INST, [(s, dest(s)) for s in range(NT)])  7.01 us
    dot_general x2, matrix products, shards(): jnp.einsum('tnkri,tnkio->tnro', picked, jac, preferred_element_type=jnp.f...  4.88 us
    pallas_call x2, Pallas kernels, partial_sums(): pl.pallas_call(mix_kernel, grid=(rows // block,), in_specs=[pl.BlockSpec(...  4.52 us
    reduce_sum x2, other arithmetic, instance_mix(): return gathered.sum(axis=0).reshape(shape)  4.01 us
  transfers between devices with their start and end apart: 10, of which 4 were waited for; matrix products, arithmetic and copies ran while one was open for 22% of the time, Pallas kernels for 2%

profile of v5, /device:TPU:1, one launch (start us, length us, event | category | flops | bytes accessed | tf_op | source)
XLA Modules:
  0.0 98.9 jit_solution(7909738315974442386)
XLA Ops:
  0.8 1.2 %multiply_convert_fusion = (bf16[1,16,32,128]{3,2,1,0:T(8,128)(2,1)S(1)}, f32[1,16,32,128]{3,2,1,0:T(8,128)S(1)}) fusion(f32[1,16,32,128]{3,2,1,0:T(8,128)} %param.11, f32[16]{0:T(128)S(1)} %or_convert_fusion, f32[16,128]{1,0:T(8,128)} %param.14), kind=kLoop, calls=%fused_computation.13 | loop fusion | flops 196608 | bytes 663616 | tf_op jit(solution)/shard_map/convert_element_type | solution.py:116
  2.0 4.0 %collective-permute-start.2 = (f32[512,128]{1,0:T(8,128)S(1)}, f32[512,128]{1,0:T(8,128)}, u32[]{:S(2)}, u32[]{:S(2)}) collective-permute-start(f32[512,128]{1,0:T(8,128)S(1)} %bitcast.63), channel_id=1, source_target_pairs={{0,256},{32,288},{64,320},{96,352},{128,384},{160,416},{192,448},{... | collective-permute-start | bytes 786440 | tf_op jit(solution)/shard_map/ppermute | solution.py:49
  6.7 13.4 %collective-permute-start.1 = (bf16[1,1,32,128]{3,2,1,0:T(8,128)(2,1)}, bf16[1,1,32,128]{3,2,1,0:T(8,128)(2,1)}, u32[]{:S(2)}, u32[]{:S(2)}) collective-permute-start(bf16[1,1,32,128]{3,2,1,0:T(8,128)(2,1)} %get-tuple-element.12), channel_id=1, source_target_pairs={{1,0},{2,1},{3,2},{4,3},{5,4},{6,5},{7,6},{8,7},{9,8},{10,9},{11,1... | collective-permute-start | bytes 24584 | tf_op jit(solution)/shard_map/ppermute | solution.py:32
  20.1 1.1 %fusion.12 = f32[4,32,128]{2,1,0:T(8,128)S(1)} fusion(bf16[1,4,128,128]{3,2,1,0:T(8,128)(2,1)} %param.16, bf16[1,16,32,128]{3,2,1,0:T(8,128)(2,1)S(1)} %get-tuple-element.7), kind=kOutput, calls=%fused_computation.18 | convolution fusion | flops 4194304 | bytes 229376 | tf_op jit(solution)/shard_map/tjri,tjio->tjro/dot_general | solution.py:117
  22.6 1.9 %collective-permute-start = (bf16[1,5,32,128]{3,2,1,0:T(8,128)(2,1)}, bf16[1,5,32,128]{3,2,1,0:T(8,128)(2,1)}, u32[]{:S(2)}, u32[]{:S(2)}) collective-permute-start(bf16[1,5,32,128]{3,2,1,0:T(8,128)(2,1)} %pad_maximum_fusion.2), channel_id=1, source_target_pairs={{31,0},{0,1},{1,2},{2,3},{3,4},{4,5},{5,6},{6,7},{7,8},{8,9},{9,10... | collective-permute-start | bytes 122888 | tf_op jit(solution)/shard_map/ppermute | solution.py:32
  24.5 1.8 %pad_maximum_fusion = f32[2,512,128]{2,1,0:T(8,128)} fusion(f32[1,512,128]{2,1,0:T(8,128)} %bitcast.16, f32[1,512,128]{2,1,0:T(8,128)S(1)} %bitcast.64), kind=kLoop, calls=%fused_computation.8 | loop fusion | flops 131072 | bytes 1048576 | tf_op jit(solution)/shard_map/stack | solution.py:97
  26.3 3.1 %collective-permute-start.3 = (f32[2,512,128]{2,1,0:T(8,128)}, f32[2,512,128]{2,1,0:T(8,128)}, u32[]{:S(2)}, u32[]{:S(2)}) collective-permute-start(f32[2,512,128]{2,1,0:T(8,128)} %pad_maximum_fusion), channel_id=1, source_target_pairs={{0,32},{32,0},{64,96},{96,64},{128,160},{160,128},{192,224},{224,1... | collective-permute-start | bytes 1572872 | tf_op jit(solution)/shard_map/ppermute | solution.py:49
  30.3 1.3 %dynamic-slice_bitcast_fusion.coef_ref = f32[16]{0:T(128)} fusion(f32[16,16]{1,0:T(8,128)} %constant.36.clone, s32[]{:T(128)S(6)} %select_n.9), kind=kLoop, calls=%fused_computation.34 | loop fusion | bytes 132 | tf_op jit(solution)/shard_map/reshape | solution.py:98
  32.3 2.3 %shard_map.109 = f32[4,512,128]{2,1,0:T(8,128)} custom-call(f32[16]{0:T(128)} %dynamic-slice_bitcast_fusion.coef_ref, f32[512,128]{1,0:T(8,128)} %bitcast.65, f32[512,128]{1,0:T(8,128)} %collective-permute-done.2.across_ref, f32[2,512,128]{2,1,0:T(8,128)} %collective-permute-done.3.pair_ref), custom_call_target="tpu_custom_call" | custom-call | tf_op jit(solution)/shard_map/pallas_call | solution.py:83
  34.5 4.4 %all-to-all-start = ((f32[4,512,128]{2,1,0:T(8,128)}), f32[4,512,128]{2,1,0:T(8,128)}, u32[]{:S(2)}, u32[]{:S(2)}) async-start(f32[4,512,128]{2,1,0:T(8,128)} %shard_map.109), calls=%async_computation | async-start | bytes 2097152 | tf_op jit(solution)/shard_map/all_to_all | solution.py:100
  38.9 0.7 slice.46
  39.6 0.7 maximum_bitcast_fusion
  40.4 1.6 %gather_fusion = bf16[96,32,128]{2,1,0:T(8,128)(2,1)} fusion(bf16[18,32,128]{2,1,0:T(8,128)(2,1)S(1)} %maximum_bitcast_fusion, s32[1024]{0:T(1024)S(1)} %pad_clamp_fusion), kind=kCustom, calls=%fused_computation | custom fusion | bytes 1573248 | tf_op jit(solution)/shard_map/gather | solution.py:127
  42.0 1.5 %bitcast_add_fusion.1 = f32[1,4,32,128]{3,2,1,0:T(8,128)} fusion(f32[4,32,128]{2,1,0:T(8,128)S(1)} %copy-done.6, bf16[1,5,32,128]{3,2,1,0:T(8,128)(2,1)} %collective-permute-done, f32[4]{0:T(128)S(1)} %broadcast_subtract_fusion), kind=kLoop, calls=%fused_computation.22 | loop fusion | flops 49152 | bytes 163856 | tf_op jit(solution)/shard_map/add | solution.py:130
  43.4 2.4 %fusion.4 = f32[1,16,32,128]{3,2,1,0:T(8,128)} fusion(bf16[16,6,32,128]{3,2,1,0:T(8,128)(2,1)} %bitcast.62, bf16[1,16,6,128,128]{4,3,2,1,0:T(8,128)(2,1)S(1)} %copy-done), kind=kOutput, calls=%fused_computation.6 | convolution fusion | flops 100663296 | bytes 4194304 | tf_op jit(solution)/shard_map/tnkri,tnkio->tnro/dot_general | solution.py:128
  45.9 8.3 %all-to-all-done = f32[4,512,128]{2,1,0:T(8,128)} async-done(((f32[4,512,128]{2,1,0:T(8,128)}), f32[4,512,128]{2,1,0:T(8,128)}, u32[]{:S(2)}, u32[]{:S(2)}) %all-to-all-start) | async-done | bytes 1048608 | tf_op jit(solution)/shard_map/all_to_all | solution.py:100
  54.2 2.0 %reduce_sum.18 = f32[512,128]{1,0:T(8,128)} reduce(f32[4,512,128]{2,1,0:T(8,128)} %all-to-all-done, f32[]{:T(128)} %constant.9.clone.1), dimensions={0}, to_apply=%region_0.0 | reduce | flops 196608 | bytes 1310724 | tf_op jit(solution)/shard_map/reduce_sum | solution.py:101
  56.2 1.3 %fusion.16 = (bf16[1,16,32,128]{3,2,1,0:T(8,128)(2,1)S(1)}, f32[1,16,32,128]{3,2,1,0:T(8,128)S(1)}) fusion(f32[1,16,32,128]{3,2,1,0:T(8,128)} %param.12, f32[1,16,32,128]{3,2,1,0:T(8,128)} %bitcast.71, f32[1,16,32,128]{3,2,1,0:T(8,128)} %fusion.4, f32[1,4,32,128]{3,2,1,0:T(8,128)} %bitcast_add_fusion.1, f32[16,128]{1,0:T(8,128)S(1)} %bitcast.72, ...), kind=kLoop, calls=%fused_computation.37 | loop fusion | flops 524288 | bytes 1515584 | tf_op jit(solution)/shard_map/convert_element_type | solution.py:116
  57.6 1.9 %collective-permute-start.6 = (f32[512,128]{1,0:T(8,128)S(1)}, f32[512,128]{1,0:T(8,128)S(1)}, u32[]{:S(2)}, u32[]{:S(2)}) collective-permute-start(f32[512,128]{1,0:T(8,128)S(1)} %bitcast.66), channel_id=1, source_target_pairs={{0,256},{32,288},{64,320},{96,352},{128,384},{160,416},{192,448},{... | collective-permute-start | bytes 786440 | tf_op jit(solution)/shard_map/ppermute | solution.py:49
  59.5 6.9 %collective-permute-done.6.across_ref = f32[512,128]{1,0:T(8,128)S(1)} collective-permute-done((f32[512,128]{1,0:T(8,128)S(1)}, f32[512,128]{1,0:T(8,128)S(1)}, u32[]{:S(2)}, u32[]{:S(2)}) %collective-permute-start.6) | collective-permute-done | bytes 262176 | tf_op jit(solution)/shard_map/ppermute | solution.py:49
  67.1 3.7 %collective-permute-start.7 = (f32[2,512,128]{2,1,0:T(8,128)S(1)}, f32[2,512,128]{2,1,0:T(8,128)}, u32[]{:S(2)}, u32[]{:S(2)}) collective-permute-start(f32[2,512,128]{2,1,0:T(8,128)S(1)} %pad_maximum_fusion.1), channel_id=1, source_target_pairs={{0,32},{32,0},{64,96},{96,64},{128,160},{160,128},{192,224},{224,1... | collective-permute-start | bytes 1572872 | tf_op jit(solution)/shard_map/ppermute | solution.py:49
  71.6 0.7 fusion.15
  72.5 2.3 %shard_map.110 = f32[4,512,128]{2,1,0:T(8,128)} custom-call(f32[16]{0:T(128)} %dynamic-slice_bitcast_fusion.coef_ref, f32[512,128]{1,0:T(8,128)} %bitcast.68, f32[512,128]{1,0:T(8,128)} %copy-done.3, f32[2,512,128]{2,1,0:T(8,128)} %collective-permute-done.7.pair_ref), custom_call_target="tpu_custom_call" | custom-call | tf_op jit(solution)/shard_map/pallas_call | solution.py:83
  74.7 4.2 %all-to-all-start.1 = ((f32[4,512,128]{2,1,0:T(8,128)}), f32[4,512,128]{2,1,0:T(8,128)}, u32[]{:S(2)}, u32[]{:S(2)}) async-start(f32[4,512,128]{2,1,0:T(8,128)} %shard_map.110), calls=%async_computation.1 | async-start | bytes 2097152 | tf_op jit(solution)/shard_map/all_to_all | solution.py:100
  79.0 1.9 %collective-permute-start.4 = (bf16[1,5,32,128]{3,2,1,0:T(8,128)(2,1)S(1)}, bf16[1,5,32,128]{3,2,1,0:T(8,128)(2,1)S(1)}, u32[]{:S(2)}, u32[]{:S(2)}) collective-permute-start(bf16[1,5,32,128]{3,2,1,0:T(8,128)(2,1)S(1)} %pad_maximum_fusion.3), channel_id=1, source_target_pairs={{31,0},{0,1},{1,2},{2,3},{3,4},{4,5},{5,6},{6,7},{7,8},{8,9},{9,10... | collective-permute-start | bytes 122888 | tf_op jit(solution)/shard_map/ppermute | solution.py:32
  80.9 7.3 %collective-permute-start.5 = (bf16[1,1,32,128]{3,2,1,0:T(8,128)(2,1)S(1)}, bf16[1,1,32,128]{3,2,1,0:T(8,128)(2,1)S(1)}, u32[]{:S(2)}, u32[]{:S(2)}) collective-permute-start(bf16[1,1,32,128]{3,2,1,0:T(8,128)(2,1)S(1)} %get-tuple-element.10), channel_id=1, source_target_pairs={{1,0},{2,1},{3,2},{4,3},{5,4},{6,5},{7,6},{8,7},{9,8},{10,9},{11,1... | collective-permute-start | bytes 24584 | tf_op jit(solution)/shard_map/ppermute | solution.py:32
  89.0 0.9 maximum_bitcast_fusion.1
  89.9 1.7 %gather_fusion.1 = bf16[96,32,128]{2,1,0:T(8,128)(2,1)} fusion(bf16[18,32,128]{2,1,0:T(8,128)(2,1)S(1)} %maximum_bitcast_fusion.1, s32[1024]{0:T(1024)} %copy-done.9), kind=kCustom, calls=%fused_computation.1 | custom fusion | bytes 1573248 | tf_op jit(solution)/shard_map/gather | solution.py:127
  91.6 0.9 bitcast_add_fusion
  92.5 2.4 %fusion.7 = f32[1,16,32,128]{3,2,1,0:T(8,128)} fusion(bf16[16,6,32,128]{3,2,1,0:T(8,128)(2,1)} %bitcast.61, bf16[1,16,6,128,128]{4,3,2,1,0:T(8,128)(2,1)S(1)} %copy-done), kind=kOutput, calls=%fused_computation.7 | convolution fusion | flops 100663296 | bytes 4194304 | tf_op jit(solution)/shard_map/tnkri,tnkio->tnro/dot_general | solution.py:128
  95.0 2.0 %reduce_sum.19 = f32[512,128]{1,0:T(8,128)} reduce(f32[4,512,128]{2,1,0:T(8,128)} %all-to-all-done.1, f32[]{:T(128)} %constant.9.clone.1), dimensions={0}, to_apply=%region_1.0 | reduce | flops 196608 | bytes 1310724 | tf_op jit(solution)/shard_map/reduce_sum | solution.py:101
  97.0 1.9 %multiply_add_fusion = f32[1,16,32,128]{3,2,1,0:T(8,128)} fusion(f32[1,16,32,128]{3,2,1,0:T(8,128)S(1)} %get-tuple-element.6, f32[1,16,32,128]{3,2,1,0:T(8,128)} %param.12, f32[1,16,32,128]{3,2,1,0:T(8,128)} %bitcast.69, f32[1,16,32,128]{3,2,1,0:T(8,128)} %fusion.7, f32[1,4,32,128]{3,2,1,0:T(8,128)S(1)} %bitcast_add_fusion, f32[16,128]{1,0:T(8,128)S(1)} %bitcast.73, ...), kind=kLoop, calls=%fused_computation.10 | loop fusion | flops 393216 | bytes 1384512 | tf_op jit(solution)/shard_map/add | solution.py:138
  (60 shorter events, 5.9 us)
Async XLA Ops:
  0.0 43.4 %copy-start = (bf16[1,16,6,128,128]{4,3,2,1,0:T(8,128)(2,1)S(1)}, bf16[1,16,6,128,128]{4,3,2,1,0:T(8,128)(2,1)}, u32[]{:S(2)}) copy-start(bf16[1,16,6,128,128]{4,3,2,1,0:T(8,128)(2,1)} %param.15) | copy-start | bytes 9437188
  0.8 5.9 %copy-start.14 = (f32[16]{0:T(128)}, f32[16]{0:T(128)S(1)}, u32[]{:S(2)}) copy-start(f32[16]{0:T(128)S(1)} %or_convert_fusion) | copy-start | bytes 196
  2.0 30.2 %copy-start.1 = (f32[1,16,32,128]{3,2,1,0:T(8,128)}, f32[1,16,32,128]{3,2,1,0:T(8,128)S(1)}, u32[]{:S(2)}) copy-start(f32[1,16,32,128]{3,2,1,0:T(8,128)S(1)} %get-tuple-element.8) | copy-start | bytes 786436
  2.0 22.4 %collective-permute-start.2 = (f32[512,128]{1,0:T(8,128)S(1)}, f32[512,128]{1,0:T(8,128)}, u32[]{:S(2)}, u32[]{:S(2)}) collective-permute-start(f32[512,128]{1,0:T(8,128)S(1)} %bitcast.63), channel_id=1, source_target_pairs={{0,256},{32,288},{64,320},{96,352},{128,384},{160,416},{192,448},{... | collective-permute-start | bytes 786440 | tf_op jit(solution)/shard_map/ppermute | solution.py:49
  6.7 33.0 %collective-permute-start.1 = (bf16[1,1,32,128]{3,2,1,0:T(8,128)(2,1)}, bf16[1,1,32,128]{3,2,1,0:T(8,128)(2,1)}, u32[]{:S(2)}, u32[]{:S(2)}) collective-permute-start(bf16[1,1,32,128]{3,2,1,0:T(8,128)(2,1)} %get-tuple-element.12), channel_id=1, source_target_pairs={{1,0},{2,1},{3,2},{4,3},{5,4},{6,5},{7,6},{8,7},{9,8},{10,9},{11,1... | collective-permute-start | bytes 24584 | tf_op jit(solution)/shard_map/ppermute | solution.py:32
  21.2 0.7 copy-start.5
  21.9 0.7 copy-start.16
  22.6 16.4 %collective-permute-start = (bf16[1,5,32,128]{3,2,1,0:T(8,128)(2,1)}, bf16[1,5,32,128]{3,2,1,0:T(8,128)(2,1)}, u32[]{:S(2)}, u32[]{:S(2)}) collective-permute-start(bf16[1,5,32,128]{3,2,1,0:T(8,128)(2,1)} %pad_maximum_fusion.2), channel_id=1, source_target_pairs={{31,0},{0,1},{1,2},{2,3},{3,4},{4,5},{5,6},{6,7},{7,8},{8,9},{9,10... | collective-permute-start | bytes 122888 | tf_op jit(solution)/shard_map/ppermute | solution.py:32
  26.3 6.0 %collective-permute-start.3 = (f32[2,512,128]{2,1,0:T(8,128)}, f32[2,512,128]{2,1,0:T(8,128)}, u32[]{:S(2)}, u32[]{:S(2)}) collective-permute-start(f32[2,512,128]{2,1,0:T(8,128)} %pad_maximum_fusion), channel_id=1, source_target_pairs={{0,32},{32,0},{64,96},{96,64},{128,160},{160,128},{192,224},{224,1... | collective-permute-start | bytes 1572872 | tf_op jit(solution)/shard_map/ppermute | solution.py:49
  32.2 13.6 %copy-start.17 = (f32[4]{0:T(128)}, f32[4]{0:T(128)S(1)}, u32[]{:S(2)}) copy-start(f32[4]{0:T(128)S(1)} %broadcast_subtract_fusion) | copy-start | bytes 52
  34.5 7.4 %copy-start.6 = (f32[4,32,128]{2,1,0:T(8,128)S(1)}, f32[4,32,128]{2,1,0:T(8,128)}, u32[]{:S(2)}) copy-start(f32[4,32,128]{2,1,0:T(8,128)} %copy-done.5) | copy-start | bytes 196612
  34.5 19.6 %all-to-all-start = ((f32[4,512,128]{2,1,0:T(8,128)}), f32[4,512,128]{2,1,0:T(8,128)}, u32[]{:S(2)}, u32[]{:S(2)}) async-start(f32[4,512,128]{2,1,0:T(8,128)} %shard_map.109), calls=%async_computation | async-start | bytes 2097152 | tf_op jit(solution)/shard_map/all_to_all | solution.py:100
  38.9 17.2 %copy-start.9 = (s32[1024]{0:T(1024)}, s32[1024]{0:T(1024)S(1)}, u32[]{:S(2)}) copy-start(s32[1024]{0:T(1024)S(1)} %pad_clamp_fusion) | copy-start | bytes 12292
  41.9 14.2 %copy-start.12 = (f32[1,16,128]{2,1,0:T(8,128)S(1)}, f32[1,16,128]{2,1,0:T(8,128)}, u32[]{:S(2)}) copy-start(f32[1,16,128]{2,1,0:T(8,128)} %param.13) | copy-start | bytes 24580
  43.4 14.1 %copy-start.11 = (f32[16,128]{1,0:T(8,128)S(1)}, f32[16,128]{1,0:T(8,128)}, u32[]{:S(2)}) copy-start(f32[16,128]{1,0:T(8,128)} %param.14) | copy-start | bytes 24580
  45.9 25.0 %copy-start.8 = (bf16[1,4,128,128]{3,2,1,0:T(8,128)(2,1)S(1)}, bf16[1,4,128,128]{3,2,1,0:T(8,128)(2,1)}, u32[]{:S(2)}) copy-start(bf16[1,4,128,128]{3,2,1,0:T(8,128)(2,1)} %param.16) | copy-start | bytes 393220
  57.5 13.3 %copy-start.4 = (bf16[1,16,32,128]{3,2,1,0:T(8,128)(2,1)}, bf16[1,16,32,128]{3,2,1,0:T(8,128)(2,1)S(1)}, u32[]{:S(2)}) copy-start(bf16[1,16,32,128]{3,2,1,0:T(8,128)(2,1)S(1)} %get-tuple-element.5) | copy-start | bytes 393220
  57.6 8.9 %copy-start.2 = (f32[1,16,32,128]{3,2,1,0:T(8,128)}, f32[1,16,32,128]{3,2,1,0:T(8,128)S(1)}, u32[]{:S(2)}) copy-start(f32[1,16,32,128]{3,2,1,0:T(8,128)S(1)} %broadcast_multiply_fusion) | copy-start | bytes 786436
  57.6 8.8 %collective-permute-start.6 = (f32[512,128]{1,0:T(8,128)S(1)}, f32[512,128]{1,0:T(8,128)S(1)}, u32[]{:S(2)}, u32[]{:S(2)}) collective-permute-start(f32[512,128]{1,0:T(8,128)S(1)} %bitcast.66), channel_id=1, source_target_pairs={{0,256},{32,288},{64,320},{96,352},{128,384},{160,416},{192,448},{... | collective-permute-start | bytes 786440 | tf_op jit(solution)/shard_map/ppermute | solution.py:49
  66.4 0.7 copy-start.3
  67.1 5.3 %collective-permute-start.7 = (f32[2,512,128]{2,1,0:T(8,128)S(1)}, f32[2,512,128]{2,1,0:T(8,128)}, u32[]{:S(2)}, u32[]{:S(2)}) collective-permute-start(f32[2,512,128]{2,1,0:T(8,128)S(1)} %pad_maximum_fusion.1), channel_id=1, source_target_pairs={{0,32},{32,0},{64,96},{96,64},{128,160},{160,128},{192,224},{224,1... | collective-permute-start | bytes 1572872 | tf_op jit(solution)/shard_map/ppermute | solution.py:49
  71.0 0.6 copy-start.7
  74.7 20.2 %all-to-all-start.1 = ((f32[4,512,128]{2,1,0:T(8,128)}), f32[4,512,128]{2,1,0:T(8,128)}, u32[]{:S(2)}, u32[]{:S(2)}) async-start(f32[4,512,128]{2,1,0:T(8,128)} %shard_map.110), calls=%async_computation.1 | async-start | bytes 2097152 | tf_op jit(solution)/shard_map/all_to_all | solution.py:100
  79.0 9.2 %collective-permute-start.4 = (bf16[1,5,32,128]{3,2,1,0:T(8,128)(2,1)S(1)}, bf16[1,5,32,128]{3,2,1,0:T(8,128)(2,1)S(1)}, u32[]{:S(2)}, u32[]{:S(2)}) collective-permute-start(bf16[1,5,32,128]{3,2,1,0:T(8,128)(2,1)S(1)} %pad_maximum_fusion.3), channel_id=1, source_target_pairs={{31,0},{0,1},{1,2},{2,3},{3,4},{4,5},{5,6},{6,7},{7,8},{8,9},{9,10... | collective-permute-start | bytes 122888 | tf_op jit(solution)/shard_map/ppermute | solution.py:32
  80.9 8.0 %collective-permute-start.5 = (bf16[1,1,32,128]{3,2,1,0:T(8,128)(2,1)S(1)}, bf16[1,1,32,128]{3,2,1,0:T(8,128)(2,1)S(1)}, u32[]{:S(2)}, u32[]{:S(2)}) collective-permute-start(bf16[1,1,32,128]{3,2,1,0:T(8,128)(2,1)S(1)} %get-tuple-element.10), channel_id=1, source_target_pairs={{1,0},{2,1},{3,2},{4,3},{5,4},{6,5},{7,6},{8,7},{9,8},{10,9},{11,1... | collective-permute-start | bytes 24584 | tf_op jit(solution)/shard_map/ppermute | solution.py:32
  88.2 0.6 copy-start.10
  91.6 5.4 %copy-start.13 = (f32[1,16,128]{2,1,0:T(8,128)S(1)}, f32[1,16,128]{2,1,0:T(8,128)}, u32[]{:S(2)}) copy-start(f32[1,16,128]{2,1,0:T(8,128)} %param.13) | copy-start | bytes 24580
  91.6 5.4 %copy-start.15 = (f32[16]{0:T(128)S(1)}, f32[16]{0:T(128)}, u32[]{:S(2)}) copy-start(f32[16]{0:T(128)} %copy-done.14) | copy-start | bytes 196

commit v6 on v5

--- a/solution.py
+++ b/solution.py
@@ -66,27 +66,31 @@
     return table.astype(np.float32)
 
 
-def mix_kernel(coef_ref, own_ref, across_ref, pair_ref, o_ref):
+def mix_kernel(index_ref, coef_ref, own_ref, across_ref, pair_ref, o_ref):
+    me = index_ref[0]
     values = (own_ref[...], pair_ref[0], across_ref[...], pair_ref[1])
     for slot in range(4):
-        acc = coef_ref[slot * 4] * values[0]
+        acc = coef_ref[me, slot * 4] * values[0]
         for m in range(1, 4):
-            acc = acc + coef_ref[slot * 4 + m] * values[m]
+            acc = acc + coef_ref[me, slot * 4 + m] * values[m]
         o_ref[slot] = acc
 
 
-def partial_sums(coef, own, across, pair):
+def partial_sums(index, own, across, pair):
     rows, lanes = own.shape
     block = 256
-    flat = pl.BlockSpec((block, lanes), lambda r: (r, 0))
-    stacked = pl.BlockSpec((2, block, lanes), lambda r: (0, r, 0))
+    flat = pl.BlockSpec((block, lanes), lambda r, index: (r, 0))
+    stacked = pl.BlockSpec((2, block, lanes), lambda r, index: (0, r, 0))
     return pl.pallas_call(
         mix_kernel,
-        grid=(rows // block,),
-        in_specs=[pl.BlockSpec(memory_space=pltpu.SMEM), flat, flat, stacked],
-        out_specs=pl.BlockSpec((4, block, lanes), lambda r: (0, r, 0)),
+        grid_spec=pltpu.PrefetchScalarGridSpec(
+            num_scalar_prefetch=1,
+            grid=(rows // block,),
+            in_specs=[pl.BlockSpec(memory_space=pltpu.SMEM), flat, flat, stacked],
+            out_specs=pl.BlockSpec((4, block, lanes), lambda r, index: (0, r, 0)),
+        ),
         out_shape=jax.ShapeDtypeStruct((4, rows, lanes), jnp.float32),
-    )(coef, own, across, pair)
+    )(index, jnp.asarray(coefficient_table()), own, across, pair)
 
 
 def instance_mix(weighted):
@@ -95,10 +99,9 @@
     flat = weighted.reshape(-1, shape[-1])
     across = routed(flat, lambda s: s ^ 8)
     pair = routed(jnp.stack([flat, across]), lambda s: s ^ 1)
-    coef = lax.dynamic_slice_in_dim(jnp.asarray(coefficient_table()), i, 1).reshape(-1)
-    partials = partial_sums(coef, flat, across, pair)
+    partials = partial_sums(jnp.reshape(i, (1,)).astype(jnp.int32), flat, across, pair)
     gathered = lax.all_to_all(partials, "ix", 0, 0)
-    return gathered.sum(axis=0).reshape(shape)
+    return partials, [gathered[k].reshape(shape) for k in range(gathered.shape[0])]
 
 
 def shards(lam_init, rhs, relax, cond, jac, rotor_jac, cols, rotor_shift, owned):
@@ -114,6 +117,8 @@
     cond_wide = cond[None, :, None, :]
     for sweep in range(SWEEPS):
         lam_b = lam.astype(jnp.bfloat16)
+        weighted = lam * cond_wide
+        partials, pieces = instance_mix(weighted)
         records = jnp.einsum(
             "tjri,tjio->tjro",
             lam_b[:, rows - rotor_rows :],
@@ -121,6 +126,7 @@
             preferred_element_type=jnp.float32,
         )
         onward = jnp.concatenate([lam_b[:, rows - 1 :], (records * moving).astype(jnp.bfloat16)], axis=1)
+        onward, lam_b, _ = lax.optimization_barrier((onward, lam_b, partials))
         onward = shifted(onward, "sector", 1)
         head = shifted(lam_b[:, :1], "sector", -1)
         lam_h = jnp.concatenate([onward[:, :1], lam_b, head], axis=1)
@@ -132,8 +138,7 @@
             [jnp.zeros((local_inst, rows - rotor_rows) + rotor.shape[2:], jnp.float32), rotor],
             axis=1,
         )
-        weighted = lam * cond_wide
-        spec = instance_mix(weighted)
+        spec = pieces[0] + pieces[1] + pieces[2] + pieces[3]
         resid = rhs - (stator + rotor_full + spec)
         lam = lam + relax_wide * resid * live
     return lam

time: 100 us -> 97.1 us (0.971)
  starting transfers between devices: 45.9 us -> 49.7 us
  other arithmetic: 17.8 us -> 14.6 us
  local copies, waits for them, and re-layouts: 8.02 us -> 4.86 us
    all_to_all x2, waiting for transfers between devices: 8.3 us -> 0.01 us  [instance_mix(): gathered = lax.all_to_all(partials, 'ix', 0, 0)]
    ppermute x4, starting transfers between devices: 12.8 us -> 20.2 us  [routed(): return lax.ppermute(block, INST, [(s, dest(s)) for s in range(NT)])]
    ppermute x4, waiting for transfers between devices: 0.15 us -> 7.35 us  [shifted(): return lax.ppermute(block, axis, route)]
    reduce_sum x2 -> x0, other arithmetic: 4.01 us -> none  [instance_mix(): return gathered.sum(axis=0).reshape(shape)]
    ppermute x4, starting transfers between devices: 24.5 us -> 20.9 us  [shifted(): return lax.ppermute(block, axis, route)]
    add x0 -> x2, other arithmetic: none -> 2.51 us  [shards(): spec = pieces[0] + pieces[1] + pieces[2] + pieces[3]]
    reshape x1 -> x0, local copies, waits for them, and re-layouts: 1.29 us -> none  [instance_mix(): lax.dynamic_slice_in_dim(jnp.asarray(coefficient_table()), i, 1).reshape(-1)]
  transfers between devices with their start and end apart: 10 -> 10, of which waited for: 4 -> 6; matrix products, arithmetic and copies ran while one was open for 22% -> 17% of each run, Pallas kernels for 2% -> 0%
where the time goes in v6:
time: 97.1 us; the launch traced here: 95.4 us
  starting transfers between devices  49.7 us (51%)
  other arithmetic  14.6 us (15%)
  waiting for transfers between devices  14.6 us (15%)
  matrix products  6.06 us (6%)
  local copies, waits for them, and re-layouts  4.86 us (5%)
  Pallas kernels  4.49 us (5%)
  between operations  1.15 us (1%)
    ppermute x4, starting transfers between devices, shifted(): return lax.ppermute(block, axis, route)  20.9 us
    ppermute x4, starting transfers between devices, routed(): return lax.ppermute(block, INST, [(s, dest(s)) for s in range(NT)])  20.2 us
    all_to_all x2, starting transfers between devices, instance_mix(): gathered = lax.all_to_all(partials, 'ix', 0, 0)  8.62 us
    ppermute x4, waiting for transfers between devices, shifted(): return lax.ppermute(block, axis, route)  7.35 us
    ppermute x4, waiting for transfers between devices, routed(): return lax.ppermute(block, INST, [(s, dest(s)) for s in range(NT)])  7.24 us
    dot_general x2, matrix products, shards(): jnp.einsum('tnkri,tnkio->tnro', picked, jac, preferred_element_type=jnp.f...  4.87 us
    pallas_call x2, Pallas kernels, partial_sums(): pl.pallas_call(mix_kernel, grid_spec=pltpu.PrefetchScalarGridSpec(num_sca...  4.49 us
    gather x2, local copies, waits for them, and re-layouts, shards(): picked = lam_h[:, cols]  3.27 us
  transfers between devices with their start and end apart: 10, of which 6 were waited for; matrix products, arithmetic and copies ran while one was open for 17% of the time, Pallas kernels for 0%

profile of v6, /device:TPU:1, one launch (start us, length us, event | category | flops | bytes accessed | tf_op | source)
XLA Modules:
  0.0 95.4 jit_solution(5984707263767883780)
XLA Ops:
  0.8 1.2 %multiply_convert_fusion = (bf16[1,16,32,128]{3,2,1,0:T(8,128)(2,1)S(1)}, f32[1,16,32,128]{3,2,1,0:T(8,128)S(1)}) fusion(f32[1,16,32,128]{3,2,1,0:T(8,128)} %param.11, f32[16]{0:T(128)S(1)} %or_convert_fusion, f32[16,128]{1,0:T(8,128)} %param.14), kind=kLoop, calls=%fused_computation.19 | loop fusion | flops 196608 | bytes 663616 | tf_op jit(solution)/shard_map/convert_element_type | solution.py:119
  2.0 4.0 %collective-permute-start = (f32[512,128]{1,0:T(8,128)S(1)}, f32[512,128]{1,0:T(8,128)}, u32[]{:S(2)}, u32[]{:S(2)}) collective-permute-start(f32[512,128]{1,0:T(8,128)S(1)} %bitcast.62), channel_id=1, source_target_pairs={{0,256},{32,288},{64,320},{96,352},{128,384},{160,416},{192,448},{... | collective-permute-start | bytes 786440 | tf_op jit(solution)/shard_map/ppermute | solution.py:49
  7.6 1.1 %fusion.12 = f32[4,32,128]{2,1,0:T(8,128)S(1)} fusion(bf16[1,4,128,128]{3,2,1,0:T(8,128)(2,1)} %param.16, bf16[1,16,32,128]{3,2,1,0:T(8,128)(2,1)S(1)} %get-tuple-element.10), kind=kOutput, calls=%fused_computation.24 | convolution fusion | flops 4194304 | bytes 229376 | tf_op jit(solution)/shard_map/tjri,tjio->tjro/dot_general | solution.py:122
  8.7 1.2 %collective-permute-done.across_ref = f32[512,128]{1,0:T(8,128)} collective-permute-done((f32[512,128]{1,0:T(8,128)S(1)}, f32[512,128]{1,0:T(8,128)}, u32[]{:S(2)}, u32[]{:S(2)}) %collective-permute-start) | collective-permute-done | bytes 262176 | tf_op jit(solution)/shard_map/ppermute | solution.py:49
  9.9 1.0 %pad_maximum_fusion = f32[2,512,128]{2,1,0:T(8,128)S(1)} fusion(f32[1,512,128]{2,1,0:T(8,128)} %bitcast.9, f32[1,512,128]{2,1,0:T(8,128)S(1)} %bitcast.63), kind=kLoop, calls=%fused_computation.8 | loop fusion | flops 131072 | bytes 1048576 | tf_op jit(solution)/shard_map/stack | solution.py:101
  10.9 9.3 %collective-permute-start.1 = (f32[2,512,128]{2,1,0:T(8,128)S(1)}, f32[2,512,128]{2,1,0:T(8,128)}, u32[]{:S(2)}, u32[]{:S(2)}) collective-permute-start(f32[2,512,128]{2,1,0:T(8,128)S(1)} %pad_maximum_fusion), channel_id=1, source_target_pairs={{0,32},{32,0},{64,96},{96,64},{128,160},{160,128},{192,224},{224,1... | collective-permute-start | bytes 1572872 | tf_op jit(solution)/shard_map/ppermute | solution.py:49
  21.9 2.2 %shard_map.109 = f32[4,512,128]{2,1,0:T(8,128)} custom-call(s32[1]{0:T(128)} %bitcast.6.index_ref, f32[16,16]{1,0:T(8,128)} %constant.32.clone.coef_ref, f32[512,128]{1,0:T(8,128)} %bitcast.64, f32[512,128]{1,0:T(8,128)} %collective-permute-done.across_ref, f32[2,512,128]{2,1,0:T(8,128)} %collective-permute-done.1.pair_ref), custom_call_target="tpu_custom_call" | custom-call | tf_op jit(solution)/shard_map/pallas_call | solution.py:84
  24.1 4.4 %all-to-all-start = ((f32[4,512,128]{2,1,0:T(8,128)}), f32[4,512,128]{2,1,0:T(8,128)}, u32[]{:S(2)}, u32[]{:S(2)}) async-start(f32[4,512,128]{2,1,0:T(8,128)} %shard_map.109), calls=%async_computation | async-start | bytes 2097152 | tf_op jit(solution)/shard_map/all_to_all | solution.py:103
  28.5 10.1 %collective-permute-start.3 = (bf16[1,1,32,128]{3,2,1,0:T(8,128)(2,1)S(1)}, bf16[1,1,32,128]{3,2,1,0:T(8,128)(2,1)S(1)}, u32[]{:S(2)}, u32[]{:S(2)}) collective-permute-start(bf16[1,1,32,128]{3,2,1,0:T(8,128)(2,1)S(1)} %slice.57), channel_id=1, source_target_pairs={{1,0},{2,1},{3,2},{4,3},{5,4},{6,5},{7,6},{8,7},{9,8},{10,9},{11,1... | collective-permute-start | bytes 24584 | tf_op jit(solution)/shard_map/ppermute | solution.py:32
  38.6 1.9 %collective-permute-start.2 = (bf16[1,5,32,128]{3,2,1,0:T(8,128)(2,1)}, bf16[1,5,32,128]{3,2,1,0:T(8,128)(2,1)S(1)}, u32[]{:S(2)}, u32[]{:S(2)}) collective-permute-start(bf16[1,5,32,128]{3,2,1,0:T(8,128)(2,1)} %pad_maximum_fusion.2), channel_id=1, source_target_pairs={{31,0},{0,1},{1,2},{2,3},{3,4},{4,5},{5,6},{6,7},{7,8},{8,9},{9,10... | collective-permute-start | bytes 122888 | tf_op jit(solution)/shard_map/ppermute | solution.py:32
  40.5 6.6 %collective-permute-done.2 = bf16[1,5,32,128]{3,2,1,0:T(8,128)(2,1)S(1)} collective-permute-done((bf16[1,5,32,128]{3,2,1,0:T(8,128)(2,1)}, bf16[1,5,32,128]{3,2,1,0:T(8,128)(2,1)S(1)}, u32[]{:S(2)}, u32[]{:S(2)}) %collective-permute-start.2) | collective-permute-done | bytes 40992 | tf_op jit(solution)/shard_map/ppermute | solution.py:32
  47.2 1.6 %gather_fusion = bf16[96,32,128]{2,1,0:T(8,128)(2,1)} fusion(bf16[18,32,128]{2,1,0:T(8,128)(2,1)S(1)} %maximum_bitcast_fusion, s32[1024]{0:T(1024)S(1)} %pad_clamp_fusion), kind=kCustom, calls=%fused_computation | custom fusion | bytes 1573248 | tf_op jit(solution)/shard_map/gather | solution.py:133
  48.7 0.7 bitcast_add_fusion.1
  49.4 2.4 %fusion.4 = f32[1,16,32,128]{3,2,1,0:T(8,128)} fusion(bf16[16,6,32,128]{3,2,1,0:T(8,128)(2,1)} %bitcast.61, bf16[1,16,6,128,128]{4,3,2,1,0:T(8,128)(2,1)S(1)} %copy-done), kind=kOutput, calls=%fused_computation.6 | convolution fusion | flops 100663296 | bytes 4194304 | tf_op jit(solution)/shard_map/tnkri,tnkio->tnro/dot_general | solution.py:134
  51.9 1.3 %slice_add_fusion.3 = f32[1,512,128]{2,1,0:T(8,128)S(1)} fusion(f32[4,512,128]{2,1,0:T(8,128)} %all-to-all-done), kind=kLoop, calls=%fused_computation.13 | loop fusion | flops 196608 | bytes 1310720 | tf_op jit(solution)/shard_map/add | solution.py:141
  53.2 1.2 %fusion.16 = (bf16[1,16,32,128]{3,2,1,0:T(8,128)(2,1)S(1)}, f32[1,16,32,128]{3,2,1,0:T(8,128)S(1)}) fusion(f32[1,16,32,128]{3,2,1,0:T(8,128)} %param.12, f32[1,16,32,128]{3,2,1,0:T(8,128)S(1)} %bitcast.70, f32[1,16,32,128]{3,2,1,0:T(8,128)} %fusion.4, f32[1,4,32,128]{3,2,1,0:T(8,128)} %bitcast_add_fusion.1, f32[16,128]{1,0:T(8,128)S(1)} %bitcast.71, ...), kind=kLoop, calls=%fused_computation.42 | loop fusion | flops 524288 | bytes 1515584 | tf_op jit(solution)/shard_map/convert_element_type | solution.py:119
  54.5 2.3 %collective-permute-start.4 = (f32[512,128]{1,0:T(8,128)S(1)}, f32[512,128]{1,0:T(8,128)S(1)}, u32[]{:S(2)}, u32[]{:S(2)}) collective-permute-start(f32[512,128]{1,0:T(8,128)S(1)} %bitcast.65), channel_id=1, source_target_pairs={{0,256},{32,288},{64,320},{96,352},{128,384},{160,416},{192,448},{... | collective-permute-start | bytes 786440 | tf_op jit(solution)/shard_map/ppermute | solution.py:49
  56.8 5.6 %collective-permute-done.4.across_ref = f32[512,128]{1,0:T(8,128)S(1)} collective-permute-done((f32[512,128]{1,0:T(8,128)S(1)}, f32[512,128]{1,0:T(8,128)S(1)}, u32[]{:S(2)}, u32[]{:S(2)}) %collective-permute-start.4) | collective-permute-done | bytes 262176 | tf_op jit(solution)/shard_map/ppermute | solution.py:49
  62.4 0.7 copy-done.3
  63.1 4.6 %collective-permute-start.5 = (f32[2,512,128]{2,1,0:T(8,128)S(1)}, f32[2,512,128]{2,1,0:T(8,128)}, u32[]{:S(2)}, u32[]{:S(2)}) collective-permute-start(f32[2,512,128]{2,1,0:T(8,128)S(1)} %pad_maximum_fusion.1), channel_id=1, source_target_pairs={{0,32},{32,0},{64,96},{96,64},{128,160},{160,128},{192,224},{224,1... | collective-permute-start | bytes 1572872 | tf_op jit(solution)/shard_map/ppermute | solution.py:49
  69.4 2.2 %shard_map.110 = f32[4,512,128]{2,1,0:T(8,128)} custom-call(s32[1]{0:T(128)} %bitcast.6.index_ref, f32[16,16]{1,0:T(8,128)} %constant.32.clone.coef_ref, f32[512,128]{1,0:T(8,128)} %bitcast.67, f32[512,128]{1,0:T(8,128)} %copy-done.3, f32[2,512,128]{2,1,0:T(8,128)} %collective-permute-done.5.pair_ref), custom_call_target="tpu_custom_call" | custom-call | tf_op jit(solution)/shard_map/pallas_call | solution.py:84
  71.6 4.2 %all-to-all-start.1 = ((f32[4,512,128]{2,1,0:T(8,128)}), f32[4,512,128]{2,1,0:T(8,128)}, u32[]{:S(2)}, u32[]{:S(2)}) async-start(f32[4,512,128]{2,1,0:T(8,128)} %shard_map.110), calls=%async_computation.1 | async-start | bytes 2097152 | tf_op jit(solution)/shard_map/all_to_all | solution.py:103
  75.9 0.8 pad_maximum_fusion.3
  76.7 1.9 %collective-permute-start.6 = (bf16[1,5,32,128]{3,2,1,0:T(8,128)(2,1)S(1)}, bf16[1,5,32,128]{3,2,1,0:T(8,128)(2,1)S(1)}, u32[]{:S(2)}, u32[]{:S(2)}) collective-permute-start(bf16[1,5,32,128]{3,2,1,0:T(8,128)(2,1)S(1)} %pad_maximum_fusion.3), channel_id=1, source_target_pairs={{31,0},{0,1},{1,2},{2,3},{3,4},{4,5},{5,6},{6,7},{7,8},{8,9},{9,10... | collective-permute-start | bytes 122888 | tf_op jit(solution)/shard_map/ppermute | solution.py:32
  78.6 7.0 %collective-permute-start.7 = (bf16[1,1,32,128]{3,2,1,0:T(8,128)(2,1)S(1)}, bf16[1,1,32,128]{3,2,1,0:T(8,128)(2,1)S(1)}, u32[]{:S(2)}, u32[]{:S(2)}) collective-permute-start(bf16[1,1,32,128]{3,2,1,0:T(8,128)(2,1)S(1)} %slice.66), channel_id=1, source_target_pairs={{1,0},{2,1},{3,2},{4,3},{5,4},{6,5},{7,6},{8,7},{9,8},{10,9},{11,1... | collective-permute-start | bytes 24584 | tf_op jit(solution)/shard_map/ppermute | solution.py:32
  85.6 0.7 collective-permute-done.7
  86.4 0.9 maximum_bitcast_fusion.1
  87.3 1.7 %gather_fusion.1 = bf16[96,32,128]{2,1,0:T(8,128)(2,1)} fusion(bf16[18,32,128]{2,1,0:T(8,128)(2,1)S(1)} %maximum_bitcast_fusion.1, s32[1024]{0:T(1024)} %copy-done.9), kind=kCustom, calls=%fused_computation.1 | custom fusion | bytes 1573248 | tf_op jit(solution)/shard_map/gather | solution.py:133
  89.0 0.9 bitcast_add_fusion
  89.9 2.4 %fusion.7 = f32[1,16,32,128]{3,2,1,0:T(8,128)} fusion(bf16[16,6,32,128]{3,2,1,0:T(8,128)(2,1)} %bitcast.60, bf16[1,16,6,128,128]{4,3,2,1,0:T(8,128)(2,1)S(1)} %copy-done), kind=kOutput, calls=%fused_computation.7 | convolution fusion | flops 100663296 | bytes 4194304 | tf_op jit(solution)/shard_map/tnkri,tnkio->tnro/dot_general | solution.py:134
  92.4 1.2 %slice_add_fusion = f32[1,512,128]{2,1,0:T(8,128)S(1)} fusion(f32[4,512,128]{2,1,0:T(8,128)} %all-to-all-done.1), kind=kLoop, calls=%fused_computation.10 | loop fusion | flops 196608 | bytes 1310720 | tf_op jit(solution)/shard_map/add | solution.py:141
  93.6 1.8 %multiply_add_fusion = f32[1,16,32,128]{3,2,1,0:T(8,128)} fusion(f32[1,16,32,128]{3,2,1,0:T(8,128)S(1)} %get-tuple-element.14, f32[1,16,32,128]{3,2,1,0:T(8,128)} %param.12, f32[1,16,32,128]{3,2,1,0:T(8,128)S(1)} %bitcast.68, f32[1,16,32,128]{3,2,1,0:T(8,128)} %fusion.7, f32[1,4,32,128]{3,2,1,0:T(8,128)S(1)} %bitcast_add_fusion, f32[16,128]{1,0:T(8,128)S(1)} %bitcast.72, ...), kind=kLoop, calls=%fused_computation.16 | loop fusion | flops 393216 | bytes 1384512 | tf_op jit(solution)/shard_map/add | solution.py:143
  (63 shorter events, 5.0 us)
Async XLA Ops:
  0.0 49.4 %copy-start = (bf16[1,16,6,128,128]{4,3,2,1,0:T(8,128)(2,1)S(1)}, bf16[1,16,6,128,128]{4,3,2,1,0:T(8,128)(2,1)}, u32[]{:S(2)}) copy-start(bf16[1,16,6,128,128]{4,3,2,1,0:T(8,128)(2,1)} %param.15) | copy-start | bytes 9437188
  0.8 1.2 %copy-start.14 = (f32[16]{0:T(128)}, f32[16]{0:T(128)S(1)}, u32[]{:S(2)}) copy-start(f32[16]{0:T(128)S(1)} %or_convert_fusion) | copy-start | bytes 196
  2.0 19.8 %copy-start.1 = (f32[1,16,32,128]{3,2,1,0:T(8,128)}, f32[1,16,32,128]{3,2,1,0:T(8,128)S(1)}, u32[]{:S(2)}) copy-start(f32[1,16,32,128]{3,2,1,0:T(8,128)S(1)} %get-tuple-element.16) | copy-start | bytes 786436
  2.0 7.9 %collective-permute-start = (f32[512,128]{1,0:T(8,128)S(1)}, f32[512,128]{1,0:T(8,128)}, u32[]{:S(2)}, u32[]{:S(2)}) collective-permute-start(f32[512,128]{1,0:T(8,128)S(1)} %bitcast.62), channel_id=1, source_target_pairs={{0,256},{32,288},{64,320},{96,352},{128,384},{160,416},{192,448},{... | collective-permute-start | bytes 786440 | tf_op jit(solution)/shard_map/ppermute | solution.py:49
  7.4 41.3 %copy-start.16 = (f32[4]{0:T(128)}, f32[4]{0:T(128)S(1)}, u32[]{:S(2)}) copy-start(f32[4]{0:T(128)S(1)} %convert_bitcast_fusion) | copy-start | bytes 52
  8.7 11.5 %copy-start.5 = (f32[4,32,128]{2,1,0:T(8,128)}, f32[4,32,128]{2,1,0:T(8,128)S(1)}, u32[]{:S(2)}) copy-start(f32[4,32,128]{2,1,0:T(8,128)S(1)} %fusion.12) | copy-start | bytes 196612
  10.9 10.9 %collective-permute-start.1 = (f32[2,512,128]{2,1,0:T(8,128)S(1)}, f32[2,512,128]{2,1,0:T(8,128)}, u32[]{:S(2)}, u32[]{:S(2)}) collective-permute-start(f32[2,512,128]{2,1,0:T(8,128)S(1)} %pad_maximum_fusion), channel_id=1, source_target_pairs={{0,32},{32,0},{64,96},{96,64},{128,160},{160,128},{192,224},{224,1... | collective-permute-start | bytes 1572872 | tf_op jit(solution)/shard_map/ppermute | solution.py:49
  21.6 30.3 %copy-start.18 = (f32[4]{0:T(128)}, f32[4]{0:T(128)S(1)}, u32[]{:S(2)}) copy-start(f32[4]{0:T(128)S(1)} %broadcast_subtract_fusion) | copy-start | bytes 52
  24.1 24.6 %copy-start.6 = (f32[4,32,128]{2,1,0:T(8,128)S(1)}, f32[4,32,128]{2,1,0:T(8,128)}, u32[]{:S(2)}) copy-start(f32[4,32,128]{2,1,0:T(8,128)} %copy-done.5) | copy-start | bytes 196612
  24.1 27.8 %all-to-all-start = ((f32[4,512,128]{2,1,0:T(8,128)}), f32[4,512,128]{2,1,0:T(8,128)}, u32[]{:S(2)}, u32[]{:S(2)}) async-start(f32[4,512,128]{2,1,0:T(8,128)} %shard_map.109), calls=%async_computation | async-start | bytes 2097152 | tf_op jit(solution)/shard_map/all_to_all | solution.py:103
  28.5 18.6 %collective-permute-start.3 = (bf16[1,1,32,128]{3,2,1,0:T(8,128)(2,1)S(1)}, bf16[1,1,32,128]{3,2,1,0:T(8,128)(2,1)S(1)}, u32[]{:S(2)}, u32[]{:S(2)}) collective-permute-start(bf16[1,1,32,128]{3,2,1,0:T(8,128)(2,1)S(1)} %slice.57), channel_id=1, source_target_pairs={{1,0},{2,1},{3,2},{4,3},{5,4},{6,5},{7,6},{8,7},{9,8},{10,9},{11,1... | collective-permute-start | bytes 24584 | tf_op jit(solution)/shard_map/ppermute | solution.py:32
  38.6 8.6 %collective-permute-start.2 = (bf16[1,5,32,128]{3,2,1,0:T(8,128)(2,1)}, bf16[1,5,32,128]{3,2,1,0:T(8,128)(2,1)S(1)}, u32[]{:S(2)}, u32[]{:S(2)}) collective-permute-start(bf16[1,5,32,128]{3,2,1,0:T(8,128)(2,1)} %pad_maximum_fusion.2), channel_id=1, source_target_pairs={{31,0},{0,1},{1,2},{2,3},{3,4},{4,5},{5,6},{6,7},{7,8},{8,9},{9,10... | collective-permute-start | bytes 122888 | tf_op jit(solution)/shard_map/ppermute | solution.py:32
  40.5 12.7 %copy-start.9 = (s32[1024]{0:T(1024)}, s32[1024]{0:T(1024)S(1)}, u32[]{:S(2)}) copy-start(s32[1024]{0:T(1024)S(1)} %pad_clamp_fusion) | copy-start | bytes 12292
  48.7 4.5 %copy-start.12 = (f32[1,16,128]{2,1,0:T(8,128)S(1)}, f32[1,16,128]{2,1,0:T(8,128)}, u32[]{:S(2)}) copy-start(f32[1,16,128]{2,1,0:T(8,128)} %param.13) | copy-start | bytes 24580
  49.4 5.0 %copy-start.11 = (f32[16,128]{1,0:T(8,128)S(1)}, f32[16,128]{1,0:T(8,128)}, u32[]{:S(2)}) copy-start(f32[16,128]{1,0:T(8,128)} %param.14) | copy-start | bytes 24580
  51.9 15.9 %copy-start.8 = (bf16[1,4,128,128]{3,2,1,0:T(8,128)(2,1)S(1)}, bf16[1,4,128,128]{3,2,1,0:T(8,128)(2,1)}, u32[]{:S(2)}) copy-start(bf16[1,4,128,128]{3,2,1,0:T(8,128)(2,1)} %param.16) | copy-start | bytes 393220
  51.9 16.7 %copy-start.17 = (f32[4]{0:T(128)S(1)}, f32[4]{0:T(128)}, u32[]{:S(2)}) copy-start(f32[4]{0:T(128)} %copy-done.16) | copy-start | bytes 52
  54.4 31.2 %copy-start.4 = (bf16[1,16,32,128]{3,2,1,0:T(8,128)(2,1)}, bf16[1,16,32,128]{3,2,1,0:T(8,128)(2,1)S(1)}, u32[]{:S(2)}) copy-start(bf16[1,16,32,128]{3,2,1,0:T(8,128)(2,1)S(1)} %get-tuple-element.12) | copy-start | bytes 393220
  54.5 7.9 %copy-start.2 = (f32[1,16,32,128]{3,2,1,0:T(8,128)}, f32[1,16,32,128]{3,2,1,0:T(8,128)S(1)}, u32[]{:S(2)}) copy-start(f32[1,16,32,128]{3,2,1,0:T(8,128)S(1)} %broadcast_multiply_fusion) | copy-start | bytes 786436
  54.5 7.9 %collective-permute-start.4 = (f32[512,128]{1,0:T(8,128)S(1)}, f32[512,128]{1,0:T(8,128)S(1)}, u32[]{:S(2)}, u32[]{:S(2)}) collective-permute-start(f32[512,128]{1,0:T(8,128)S(1)} %bitcast.65), channel_id=1, source_target_pairs={{0,256},{32,288},{64,320},{96,352},{128,384},{160,416},{192,448},{... | collective-permute-start | bytes 786440 | tf_op jit(solution)/shard_map/ppermute | solution.py:49
  62.4 0.7 copy-start.3
  63.1 6.3 %collective-permute-start.5 = (f32[2,512,128]{2,1,0:T(8,128)S(1)}, f32[2,512,128]{2,1,0:T(8,128)}, u32[]{:S(2)}, u32[]{:S(2)}) collective-permute-start(f32[2,512,128]{2,1,0:T(8,128)S(1)} %pad_maximum_fusion.1), channel_id=1, source_target_pairs={{0,32},{32,0},{64,96},{96,64},{128,160},{160,128},{192,224},{224,1... | collective-permute-start | bytes 1572872 | tf_op jit(solution)/shard_map/ppermute | solution.py:49
  67.9 0.6 copy-start.7
  71.6 20.7 %all-to-all-start.1 = ((f32[4,512,128]{2,1,0:T(8,128)}), f32[4,512,128]{2,1,0:T(8,128)}, u32[]{:S(2)}, u32[]{:S(2)}) async-start(f32[4,512,128]{2,1,0:T(8,128)} %shard_map.110), calls=%async_computation.1 | async-start | bytes 2097152 | tf_op jit(solution)/shard_map/all_to_all | solution.py:103
  76.7 8.9 %collective-permute-start.6 = (bf16[1,5,32,128]{3,2,1,0:T(8,128)(2,1)S(1)}, bf16[1,5,32,128]{3,2,1,0:T(8,128)(2,1)S(1)}, u32[]{:S(2)}, u32[]{:S(2)}) collective-permute-start(bf16[1,5,32,128]{3,2,1,0:T(8,128)(2,1)S(1)} %pad_maximum_fusion.3), channel_id=1, source_target_pairs={{31,0},{0,1},{1,2},{2,3},{3,4},{4,5},{5,6},{6,7},{7,8},{8,9},{9,10... | collective-permute-start | bytes 122888 | tf_op jit(solution)/shard_map/ppermute | solution.py:32
  78.6 7.8 %collective-permute-start.7 = (bf16[1,1,32,128]{3,2,1,0:T(8,128)(2,1)S(1)}, bf16[1,1,32,128]{3,2,1,0:T(8,128)(2,1)S(1)}, u32[]{:S(2)}, u32[]{:S(2)}) collective-permute-start(bf16[1,1,32,128]{3,2,1,0:T(8,128)(2,1)S(1)} %slice.66), channel_id=1, source_target_pairs={{1,0},{2,1},{3,2},{4,3},{5,4},{6,5},{7,6},{8,7},{9,8},{10,9},{11,1... | collective-permute-start | bytes 24584 | tf_op jit(solution)/shard_map/ppermute | solution.py:32
  85.6 0.8 copy-start.10
  89.0 4.6 %copy-start.13 = (f32[1,16,128]{2,1,0:T(8,128)S(1)}, f32[1,16,128]{2,1,0:T(8,128)}, u32[]{:S(2)}) copy-start(f32[1,16,128]{2,1,0:T(8,128)} %param.13) | copy-start | bytes 24580
  89.0 4.6 %copy-start.15 = (f32[16]{0:T(128)S(1)}, f32[16]{0:T(128)}, u32[]{:S(2)}) copy-start(f32[16]{0:T(128)} %copy-done.14) | copy-start | bytes 196

commit v7 on v6

--- a/solution.py
+++ b/solution.py
@@ -49,76 +49,102 @@
     return lax.ppermute(block, INST, [(s, dest(s)) for s in range(NT)])
 
 
-def coefficient_table():
+def spectral_numpy():
     index = np.arange(NT)
     offset = index[:, None] - index[None, :]
     angle = np.pi * offset / NT
     safe_sin = np.where(offset == 0, 1.0, np.sin(angle))
     parity = np.where(offset % 2 == 0, 1.0, -1.0)
     deriv = np.where(offset == 0, 0.0, 0.5 * parity * np.cos(angle) / safe_sin)
-    dspec = deriv + 2.0 / NT
+    return deriv + 2.0 / NT
+
+
+def members_of(s):
+    return [s, s ^ 1, s ^ 8, s ^ 9]
+
+
+def targets_of(s):
+    return [(s // 8) * 8 + column * 2 + s % 2 for column in range(4)]
+
+
+def coefficient_table():
+    dspec = spectral_numpy()
     table = np.zeros((NT, 16), np.float64)
     for s in range(NT):
-        y, x, c = s // 8, (s // 2) % 4, s % 2
-        members = [s, s ^ 1, s ^ 8, s ^ 9]
-        targets = [y * 8 + column * 2 + c for column in range(4)]
-        table[s] = [dspec[m, t] for t in targets for m in members]
+        table[s] = [dspec[m, t] for t in targets_of(s) for m in members_of(s)]
     return table.astype(np.float32)
 
 
-def mix_kernel(index_ref, coef_ref, own_ref, across_ref, pair_ref, o_ref):
+def second_table():
+    dspec = spectral_numpy()
+    table = np.zeros((NT, 4, 4, 16), np.float64)
+    for s in range(NT):
+        slots = [u for t in targets_of(s) for u in members_of(t)]
+        for mv, v in enumerate(members_of(s)):
+            for k, t in enumerate(targets_of(s)):
+                table[s, mv, k] = [dspec[v, u] * dspec[u, t] for u in slots]
+    return table.astype(np.float32)
+
+
+def column_kernel(index_ref, coef_ref, own_ref, across_ref, pair_ref, o_ref):
     me = index_ref[0]
-    values = (own_ref[...], pair_ref[0], across_ref[...], pair_ref[1])
+    span = own_ref.shape[0]
+    extra = (o_ref.shape[1] - span) // 3
+    rows = span - extra
+    values = (own_ref[:rows], pair_ref[0, :rows], across_ref[:rows], pair_ref[1, :rows])
     for slot in range(4):
         acc = coef_ref[me, slot * 4] * values[0]
         for m in range(1, 4):
             acc = acc + coef_ref[me, slot * 4 + m] * values[m]
-        o_ref[slot] = acc
-
-
-def partial_sums(index, own, across, pair):
-    rows, lanes = own.shape
-    block = 256
-    flat = pl.BlockSpec((block, lanes), lambda r, index: (r, 0))
-    stacked = pl.BlockSpec((2, block, lanes), lambda r, index: (0, r, 0))
+        o_ref[slot, :rows] = acc
+        if extra:
+            o_ref[slot, rows : rows + extra] = own_ref[rows:]
+            o_ref[slot, rows + extra : rows + 2 * extra] = pair_ref[0, rows:]
+            o_ref[slot, rows + 2 * extra : rows + 3 * extra] = across_ref[rows:]
+            o_ref[slot, rows + 3 * extra : rows + 4 * extra] = pair_ref[1, rows:]
+
+
+def column_partials(index, own, across, pair, rows):
+    span, lanes = own.shape
+    extra = span - rows
     return pl.pallas_call(
-        mix_kernel,
+        column_kernel,
         grid_spec=pltpu.PrefetchScalarGridSpec(
             num_scalar_prefetch=1,
-            grid=(rows // block,),
-            in_specs=[pl.BlockSpec(memory_space=pltpu.SMEM), flat, flat, stacked],
-            out_specs=pl.BlockSpec((4, block, lanes), lambda r, index: (0, r, 0)),
+            grid=(1,),
+            in_specs=[
+                pl.BlockSpec(memory_space=pltpu.SMEM),
+                pl.BlockSpec((span, lanes), lambda r, index: (0, 0)),
+                pl.BlockSpec((span, lanes), lambda r, index: (0, 0)),
+                pl.BlockSpec((2, span, lanes), lambda r, index: (0, 0, 0)),
+            ],
+            out_specs=pl.BlockSpec((4, rows + 4 * extra, lanes), lambda r, index: (0, 0, 0)),
         ),
-        out_shape=jax.ShapeDtypeStruct((4, rows, lanes), jnp.float32),
+        out_shape=jax.ShapeDtypeStruct((4, rows + 4 * extra, lanes), jnp.float32),
     )(index, jnp.asarray(coefficient_table()), own, across, pair)
 
 
-def instance_mix(weighted):
-    i = lax.axis_index("iy") * 8 + lax.axis_index("ix") * 2 + lax.axis_index("ic")
-    shape = weighted.shape
-    flat = weighted.reshape(-1, shape[-1])
+def column_stage(flat):
     across = routed(flat, lambda s: s ^ 8)
     pair = routed(jnp.stack([flat, across]), lambda s: s ^ 1)
-    partials = partial_sums(jnp.reshape(i, (1,)).astype(jnp.int32), flat, across, pair)
-    gathered = lax.all_to_all(partials, "ix", 0, 0)
-    return partials, [gathered[k].reshape(shape) for k in range(gathered.shape[0])]
+    return across, pair
 
 
 def shards(lam_init, rhs, relax, cond, jac, rotor_jac, cols, rotor_shift, owned):
-    local_inst = lam_init.shape[0]
-    rows = lam_init.shape[1]
+    local_inst, rows, reps, lanes = lam_init.shape
     rotor_rows = rotor_jac.shape[1]
-    dspec = spectral_matrix()
+    i = lax.axis_index("iy") * 8 + lax.axis_index("ix") * 2 + lax.axis_index("ic")
+    index = jnp.reshape(i, (1,)).astype(jnp.int32)
     row = jnp.arange(rows)
-    live = ((row >= rows - rotor_rows) | (row < owned[0])).astype(jnp.float32)[None, :, None, None]
-    lam = lam_init * live
+    live_rows = ((row >= rows - rotor_rows) | (row < owned[0])).astype(jnp.float32)
+    live = live_rows[None, :, None, None]
     moving = rotor_shift.astype(jnp.float32)[:, :, None, None]
     relax_wide = relax[:, :, None, :]
     cond_wide = cond[None, :, None, :]
-    for sweep in range(SWEEPS):
+    body = rows * reps
+
+    def local_operator(lam):
         lam_b = lam.astype(jnp.bfloat16)
-        weighted = lam * cond_wide
-        partials, pieces = instance_mix(weighted)
         records = jnp.einsum(
             "tjri,tjio->tjro",
             lam_b[:, rows - rotor_rows :],
@@ -126,7 +152,6 @@
             preferred_element_type=jnp.float32,
         )
         onward = jnp.concatenate([lam_b[:, rows - 1 :], (records * moving).astype(jnp.bfloat16)], axis=1)
-        onward, lam_b, _ = lax.optimization_barrier((onward, lam_b, partials))
         onward = shifted(onward, "sector", 1)
         head = shifted(lam_b[:, :1], "sector", -1)
         lam_h = jnp.concatenate([onward[:, :1], lam_b, head], axis=1)
@@ -138,10 +163,39 @@
             [jnp.zeros((local_inst, rows - rotor_rows) + rotor.shape[2:], jnp.float32), rotor],
             axis=1,
         )
-        spec = pieces[0] + pieces[1] + pieces[2] + pieces[3]
-        resid = rhs - (stator + rotor_full + spec)
-        lam = lam + relax_wide * resid * live
-    return lam
+        return stator + rotor_full
+
+    lam0 = lam_init * live
+    w0 = (lam0 * cond_wide).reshape(body, lanes)
+    carried = jnp.concatenate([w0, relax.reshape(rows, lanes)])
+    across0, pair0 = column_stage(carried)
+    first = column_partials(index, carried, across0, pair0, body)
+    got0 = lax.all_to_all(first, "ix", 0, 0)
+
+    local0 = local_operator(lax.optimization_barrier((lam0, first))[0])
+    base = lam0 + relax_wide * (rhs - local0) * live
+    wb = (base * cond_wide).reshape(body, lanes)
+    across1, pair1 = column_stage(wb)
+    got0, across1, pair1 = lax.optimization_barrier((got0, across1, pair1))
+
+    spec0 = (got0[0, :body] + got0[1, :body] + got0[2, :body] + got0[3, :body]).reshape(lam0.shape)
+    lam1 = base - relax_wide * spec0 * live
+
+    relax_all = got0[:, body:].reshape(16, rows, lanes)
+    pairs = lax.dynamic_slice_in_dim(jnp.asarray(second_table()), i, 1)[0]
+    kernel2 = jnp.einsum("vks,snb->vknb", pairs, relax_all, precision=lax.Precision.HIGHEST)
+    kernel2 = kernel2 * live_rows[None, None, :, None] * cond[None, None]
+    w0col = jnp.stack([w0, pair0[0, :body], across0[:body], pair0[1, :body]]).reshape(4, rows, reps, lanes)
+    wbcol = jnp.stack([wb, pair1[0], across1, pair1[1]]).reshape(4, rows, reps, lanes)
+    coef = lax.dynamic_slice_in_dim(jnp.asarray(coefficient_table()), i, 1).reshape(4, 4)
+    second = jnp.einsum("km,mnrb->knrb", coef, wbcol, precision=lax.Precision.HIGHEST) - jnp.einsum(
+        "mknb,mnrb->knrb", kernel2, w0col, precision=lax.Precision.HIGHEST
+    )
+    got1 = lax.all_to_all(second.reshape(4, body, lanes), "ix", 0, 0)
+    spec1 = (got1[0] + got1[1] + got1[2] + got1[3]).reshape(lam0.shape)
+
+    local1 = local_operator(lam1)
+    return lam1 + relax_wide * (rhs - (local1 + spec1)) * live
 
 
 def solution(mesh):

time: 97.1 us -> 141 us (1.45)
  matrix products: 6.06 us -> 30.8 us
  local copies, waits for them, and re-layouts: 4.86 us -> 26.3 us
  waiting for transfers between devices: 14.6 us -> 7.1 us
  other arithmetic: 14.6 us -> 21.8 us
  Pallas kernels: 4.49 us -> 2.52 us
    dot_general x4 -> x7, matrix products: 6.06 us -> 30.8 us  [the longest x1 18.3 us: shards(): jnp.einsum('mknb,mnrb->knrb', kernel2, w0col, precision=lax.Precision.HIG...]
    dot_general x0 -> x2, local copies, waits for them, and re-layouts: none -> 8.9 us  [the longest x1 4.56 us: shards(): jnp.einsum('mknb,mnrb->knrb', kernel2, w0col, precision=lax.Precision.HIG...]
    ppermute x4, waiting for transfers between devices: 7.35 us -> 0.27 us  [shifted(): return lax.ppermute(block, axis, route)]
    another operation x2 -> x5, other arithmetic: 1.02 us -> 6.8 us  [the longest x3 3.56 us: column_stage(): pair = routed(jnp.stack([flat, across]), lambda s: s ^ 1)]
    another operation x0 -> x1, local copies, waits for them, and re-layouts: none -> 4.54 us  [shards(): jnp.stack([w0, pair0[0, :body], across0[:body], pair0[1, :body]])]
    slice x6 -> x8, local copies, waits for them, and re-layouts: 0.01 us -> 3.86 us  [the longest x1 1.85 us: shards(): pair1[0]]
    mul x2, other arithmetic: 0.68 us -> 3.21 us  [the longest x1 1.98 us: shards(): w0 = (lam0 * cond_wide).reshape(body, lanes)]
    pallas_call x2 -> x1, Pallas kernels: 4.49 us -> 2.52 us  [column_partials(): pl.pallas_call(column_kernel, grid_spec=pltpu.PrefetchScalarGridSpec(num_...]
  transfers between devices with their start and end apart: 10 -> 10, of which waited for: 6 -> 5; matrix products, arithmetic and copies ran while one was open for 17% -> 16% of each run, Pallas kernels for 0% -> 0%
where the time goes in v7:
time: 141 us; the launch traced here: 139 us
  starting transfers between devices  49 us (35%)
  matrix products  30.8 us (22%)
  local copies, waits for them, and re-layouts  26.3 us (19%)
  other arithmetic  21.8 us (15%)
  waiting for transfers between devices  7.1 us (5%)
  Pallas kernels  2.52 us (2%)
    ppermute x4, starting transfers between devices, shifted(): return lax.ppermute(block, axis, route)  21.2 us
    ppermute x4, starting transfers between devices, routed(): return lax.ppermute(block, INST, [(s, dest(s)) for s in range(NT)])  19.2 us
    dot_general x1, matrix products, shards(): jnp.einsum('mknb,mnrb->knrb', kernel2, w0col, precision=lax.Precision.HIG...  18.3 us
    ppermute x4, waiting for transfers between devices, routed(): return lax.ppermute(block, INST, [(s, dest(s)) for s in range(NT)])  6.4 us
    dot_general x2, matrix products, local_operator(): jnp.einsum('tnkri,tnkio->tnro', picked, jac, preferred_element_type=jnp.f...  5.41 us
    dot_general x1, local copies, waits for them, and re-layouts, shards(): jnp.einsum('mknb,mnrb->knrb', kernel2, w0col, precision=lax.Precision.HIG...  4.56 us
    another operation x1, local copies, waits for them, and re-layouts, shards(): jnp.stack([w0, pair0[0, :body], across0[:body], pair0[1, :body]])  4.54 us
    dot_general x1, local copies, waits for them, and re-layouts, shards(): jnp.einsum('vks,snb->vknb', pairs, relax_all, precision=lax.Precision.HIG...  4.34 us
  transfers between devices with their start and end apart: 10, of which 5 were waited for; matrix products, arithmetic and copies ran while one was open for 16% of the time, Pallas kernels for 0%

profile of v7, /device:TPU:1, one launch (start us, length us, event | category | flops | bytes accessed | tf_op | source)
XLA Modules:
  0.0 138.7 jit_solution(7591842191111067393)
XLA Ops:
  0.8 2.0 %broadcast_multiply_fusion.1 = (f32[1,16,32,128]{3,2,1,0:T(8,128)S(1)}, f32[1,16,32,128]{3,2,1,0:T(8,128)}) fusion(f32[16,128]{1,0:T(8,128)} %param.15, f32[1,16,32,128]{3,2,1,0:T(8,128)} %param.12, f32[16]{0:T(128)S(1)} %or_convert_fusion), kind=kLoop, calls=%fused_computation.36 | loop fusion | flops 131072 | bytes 794688 | tf_op jit(solution)/shard_map/mul | solution.py:169
  3.6 4.0 %collective-permute-start = (f32[528,128]{1,0:T(8,128)S(1)}, f32[528,128]{1,0:T(8,128)S(1)}, u32[]{:S(2)}, u32[]{:S(2)}) collective-permute-start(f32[528,128]{1,0:T(8,128)S(1)} %get-tuple-element.22.own_ref), channel_id=1, source_target_pairs={{0,256},{32,288},{64,320},{96,352},{128,384},{160,416},{192,448},{... | collective-permute-start | bytes 811016 | tf_op jit(solution)/shard_map/ppermute | solution.py:49
  7.6 3.8 %collective-permute-done.across_ref = f32[528,128]{1,0:T(8,128)S(1)} collective-permute-done((f32[528,128]{1,0:T(8,128)S(1)}, f32[528,128]{1,0:T(8,128)S(1)}, u32[]{:S(2)}, u32[]{:S(2)}) %collective-permute-start) | collective-permute-done | bytes 270368 | tf_op jit(solution)/shard_map/ppermute | solution.py:49
  12.4 9.3 %collective-permute-start.1 = (f32[2,528,128]{2,1,0:T(8,128)}, f32[2,528,128]{2,1,0:T(8,128)}, u32[]{:S(2)}, u32[]{:S(2)}) collective-permute-start(f32[2,528,128]{2,1,0:T(8,128)} %pad_maximum_fusion.2), channel_id=1, source_target_pairs={{0,32},{32,0},{64,96},{96,64},{128,160},{160,128},{192,224},{224,1... | collective-permute-start | bytes 1622024 | tf_op jit(solution)/shard_map/ppermute | solution.py:49
  21.6 1.3 compare_select_fusion
  22.9 1.3 copy.18
  24.3 1.3 reshape.211
  28.0 2.5 %shard_map.118 = f32[4,576,128]{2,1,0:T(8,128)} custom-call(s32[1]{0:T(128)} %bitcast.2.index_ref, f32[16,16]{1,0:T(8,128)} %constant.37.clone.coef_ref, f32[528,128]{1,0:T(8,128)} %copy-done.4, f32[528,128]{1,0:T(8,128)} %copy-done.1, f32[2,528,128]{2,1,0:T(8,128)} %collective-permute-done.1.pair_ref), custom_call_target="tpu_custom_call" | custom-call | tf_op jit(solution)/shard_map/pallas_call | solution.py:110
  32.4 1.9 %collective-permute-start.2 = (bf16[1,5,32,128]{3,2,1,0:T(8,128)(2,1)S(1)}, bf16[1,5,32,128]{3,2,1,0:T(8,128)(2,1)S(1)}, u32[]{:S(2)}, u32[]{:S(2)}) collective-permute-start(bf16[1,5,32,128]{3,2,1,0:T(8,128)(2,1)S(1)} %pad_maximum_fusion.5), channel_id=1, source_target_pairs={{31,0},{0,1},{1,2},{2,3},{3,4},{4,5},{5,6},{6,7},{7,8},{8,9},{9,10... | collective-permute-start | bytes 122888 | tf_op jit(solution)/shard_map/ppermute | solution.py:32
  34.3 10.1 %collective-permute-start.3 = (bf16[1,1,32,128]{3,2,1,0:T(8,128)(2,1)S(1)}, bf16[1,1,32,128]{3,2,1,0:T(8,128)(2,1)S(1)}, u32[]{:S(2)}, u32[]{:S(2)}) collective-permute-start(bf16[1,1,32,128]{3,2,1,0:T(8,128)(2,1)S(1)} %get-tuple-element.26), channel_id=1, source_target_pairs={{1,0},{2,1},{3,2},{4,3},{5,4},{6,5},{7,6},{8,7},{9,8},{10,9},{11,1... | collective-permute-start | bytes 24584 | tf_op jit(solution)/shard_map/ppermute | solution.py:32
  45.3 1.6 %gather_fusion = bf16[96,32,128]{2,1,0:T(8,128)(2,1)} fusion(bf16[18,32,128]{2,1,0:T(8,128)(2,1)S(1)} %maximum_bitcast_fusion, s32[1024]{0:T(1024)S(1)} %pad_clamp_fusion), kind=kCustom, calls=%fused_computation | custom fusion | bytes 1573248 | tf_op jit(solution)/shard_map/gather | solution.py:158
  47.6 2.8 %broadcast_multiply_fusion = (f32[1,16,32,128]{3,2,1,0:T(8,128)}, f32[1,16,32,128]{3,2,1,0:T(8,128)}) fusion(f32[16,128]{1,0:T(8,128)} %param.15, f32[1,16,32,128]{3,2,1,0:T(8,128)} %get-tuple-element.9, f32[16]{0:T(128)} %copy-done.12, f32[1,16,32,128]{3,2,1,0:T(8,128)} %param.13, f32[1,4,32,128]{3,2,1,0:T(8,128)S(1)} %bitcast_add_fusion.1, ...), kind=kOutput, calls=%fused_computation.35 | convolution fusion | flops 101056512 | bytes 5062720 | tf_op jit(solution)/shard_map/tnkri,tnkio->tnro/dot_general | solution.py:159
  50.3 2.3 %collective-permute-start.4 = (f32[512,128]{1,0:T(8,128)}, f32[512,128]{1,0:T(8,128)}, u32[]{:S(2)}, u32[]{:S(2)}) collective-permute-start(f32[512,128]{1,0:T(8,128)} %bitcast.17), channel_id=1, source_target_pairs={{0,256},{32,288},{64,320},{96,352},{128,384},{160,416},{192,448},{... | collective-permute-start | bytes 786440 | tf_op jit(solution)/shard_map/ppermute | solution.py:49
  52.6 4.3 %all-to-all-start = ((f32[4,576,128]{2,1,0:T(8,128)}), f32[4,576,128]{2,1,0:T(8,128)}, u32[]{:S(2)}, u32[]{:S(2)}) async-start(f32[4,576,128]{2,1,0:T(8,128)} %shard_map.118), calls=%async_computation | async-start | bytes 2359296 | tf_op jit(solution)/shard_map/all_to_all | solution.py:173
  56.9 2.6 %collective-permute-done.4 = f32[512,128]{1,0:T(8,128)} collective-permute-done((f32[512,128]{1,0:T(8,128)}, f32[512,128]{1,0:T(8,128)}, u32[]{:S(2)}, u32[]{:S(2)}) %collective-permute-start.4) | collective-permute-done | bytes 262176 | tf_op jit(solution)/shard_map/ppermute | solution.py:49
  59.5 1.9 %pad_maximum_fusion.3 = f32[2,512,128]{2,1,0:T(8,128)} fusion(f32[1,512,128]{2,1,0:T(8,128)} %bitcast.19, f32[1,512,128]{2,1,0:T(8,128)} %bitcast.18), kind=kLoop, calls=%fused_computation.18 | loop fusion | flops 131072 | bytes 1048576 | tf_op jit(solution)/shard_map/stack | solution.py:129
  61.4 3.7 %collective-permute-start.5 = (f32[2,512,128]{2,1,0:T(8,128)}, f32[2,512,128]{2,1,0:T(8,128)}, u32[]{:S(2)}, u32[]{:S(2)}) collective-permute-start(f32[2,512,128]{2,1,0:T(8,128)} %pad_maximum_fusion.3), channel_id=1, source_target_pairs={{0,32},{32,0},{64,96},{96,64},{128,160},{160,128},{192,224},{224,1... | collective-permute-start | bytes 1572872 | tf_op jit(solution)/shard_map/ppermute | solution.py:49
  67.5 2.0 %pad_maximum_fusion.1 = f32[4,16,32,128]{3,2,1,0:T(8,128)} fusion(f32[1,16,32,128]{3,2,1,0:T(8,128)S(1)} %bitcast.99, f32[1,16,32,128]{3,2,1,0:T(8,128)S(1)} %bitcast.95, f32[1,16,32,128]{3,2,1,0:T(8,128)S(1)} %bitcast.98, f32[1,16,32,128]{3,2,1,0:T(8,128)} %copy-done.3), kind=kLoop, calls=%fused_computation.15 | loop fusion | flops 786432 | bytes 2097152 | tf_op jit(solution)/shard_map/stack | solution.py:188
  69.5 4.5 %copy.20 = f32[4,16,32,128]{2,0,3,1:T(4,128)} copy(f32[4,16,32,128]{3,2,1,0:T(8,128)} %pad_maximum_fusion.1) | data formatting | bytes 2097152 | tf_op jit(solution)/shard_map/stack | solution.py:188
  77.3 1.7 %fusion.16 = f32[4,32,128]{2,1,0:T(8,128)} fusion(bf16[1,4,128,128]{3,2,1,0:T(8,128)(2,1)} %param.17, bf16[1,16,32,128]{3,2,1,0:T(8,128)(2,1)S(1)} %fusion.24), kind=kOutput, calls=%fused_computation.29 | convolution fusion | flops 4194304 | bytes 229376 | tf_op jit(solution)/shard_map/tjri,tjio->tjro/dot_general | solution.py:148
  79.0 1.8 %fusion.31 = (f32[1,512,128]{2,1,0:T(8,128)}, f32[1,512,128]{2,1,0:T(8,128)}) fusion(f32[2,512,128]{2,1,0:T(8,128)} %collective-permute-done.5), kind=kLoop, calls=%fused_computation.61 | loop fusion | bytes 1048576 | tf_op jit(solution)/shard_map/slice | solution.py:189
  80.9 1.6 %fusion.20 = f32[4,4,16,128]{3,1,2,0:T(4,128)} fusion(f32[16,16,128,1]{2,1,0,3:T(8,128)S(1)} %bitcast.100, f32[16,4,4,16]{3,2,1,0:T(4,128)} %constant.38.clone, s32[]{:T(128)S(6)} %select_n.9), kind=kOutput, calls=%fused_computation.33 | convolution fusion | flops 6291456 | bytes 270340 | tf_op jit(solution)/shard_map/vks,snb->vknb/dot_general | solution.py:186
  82.5 4.3 %copy.28 = f32[4,4,16,128]{0,1,3,2:T(4,128)} copy(f32[4,4,16,128]{3,1,2,0:T(4,128)} %fusion.20) | data formatting | bytes 262144 | tf_op jit(solution)/shard_map/vks,snb->vknb/dot_general | solution.py:186
  86.8 18.3 %fusion = f32[16,128,32,4]{2,3,1,0:T(4,128)} fusion(f32[4,16,32,128]{2,0,3,1:T(4,128)} %copy.20, f32[4,4,16,128]{0,1,3,2:T(4,128)} %copy.28, f32[16,128]{1,0:T(8,128)S(1)} %copy-done.10, f32[16]{0:T(128)} %copy-done.12), kind=kOutput, calls=%fused_computation.2 | convolution fusion | flops 12648448 | bytes 2236480 | tf_op jit(solution)/shard_map/mknb,mnrb->knrb/dot_general | solution.py:191
  105.1 4.6 %copy.21 = f32[16,128,32,4]{1,3,2,0:T(4,128)} copy(f32[16,128,32,4]{2,3,1,0:T(4,128)} %fusion) | data formatting | bytes 2097152 | tf_op jit(solution)/shard_map/mknb,mnrb->knrb/dot_general | solution.py:191
  109.7 1.3 pad_maximum_fusion
  111.0 3.6 %convolution_subtract_fusion = f32[4,16,32,128]{3,0,2,1:T(4,128)S(1)} fusion(f32[16,128,32,4]{1,3,2,0:T(4,128)} %copy.21, f32[4,16,32,128]{3,2,1,0:T(8,128)S(1)} %pad_maximum_fusion, f32[4,4,1,1]{1,0,2,3:T(4,128)S(1)} %copy-done.13), kind=kOutput, calls=%fused_computation.11 | convolution fusion | flops 12845056 | bytes 3145792 | tf_op jit(solution)/shard_map/km,mnrb->knrb/dot_general | solution.py:191
  115.6 4.2 %all-to-all-start.1 = ((f32[4,512,128]{2,1,0:T(8,128)}), f32[4,512,128]{2,1,0:T(8,128)}, u32[]{:S(2)}, u32[]{:S(2)}) async-start(f32[4,512,128]{2,1,0:T(8,128)} %copy.22), calls=%async_computation.1 | async-start | bytes 2097152 | tf_op jit(solution)/shard_map/all_to_all | solution.py:194
  120.8 1.9 %collective-permute-start.6 = (bf16[1,5,32,128]{3,2,1,0:T(8,128)(2,1)S(1)}, bf16[1,5,32,128]{3,2,1,0:T(8,128)(2,1)S(1)}, u32[]{:S(2)}, u32[]{:S(2)}) collective-permute-start(bf16[1,5,32,128]{3,2,1,0:T(8,128)(2,1)S(1)} %pad_maximum_fusion.6), channel_id=1, source_target_pairs={{31,0},{0,1},{1,2},{2,3},{3,4},{4,5},{5,6},{6,7},{7,8},{8,9},{9,10... | collective-permute-start | bytes 122888 | tf_op jit(solution)/shard_map/ppermute | solution.py:32
  122.8 7.2 %collective-permute-start.7 = (bf16[1,1,32,128]{3,2,1,0:T(8,128)(2,1)S(1)}, bf16[1,1,32,128]{3,2,1,0:T(8,128)(2,1)S(1)}, u32[]{:S(2)}, u32[]{:S(2)}) collective-permute-start(bf16[1,1,32,128]{3,2,1,0:T(8,128)(2,1)S(1)} %get-tuple-element.24), channel_id=1, source_target_pairs={{1,0},{2,1},{3,2},{4,3},{5,4},{6,5},{7,6},{8,7},{9,8},{10,9},{11,1... | collective-permute-start | bytes 24584 | tf_op jit(solution)/shard_map/ppermute | solution.py:32
  131.7 1.7 %gather_fusion.1 = bf16[96,32,128]{2,1,0:T(8,128)(2,1)} fusion(bf16[18,32,128]{2,1,0:T(8,128)(2,1)S(1)} %maximum_bitcast_fusion.1, s32[1024]{0:T(1024)} %copy-done.9), kind=kCustom, calls=%fused_computation.1 | custom fusion | bytes 1573248 | tf_op jit(solution)/shard_map/gather | solution.py:158
  136.0 2.7 %multiply_add_fusion = f32[1,16,32,128]{3,2,1,0:T(8,128)} fusion(f32[1,16,32,128]{3,2,1,0:T(8,128)} %param.13, f32[1,16,32,128]{3,2,1,0:T(8,128)S(1)} %bitcast.94, f32[1,4,32,128]{3,2,1,0:T(8,128)S(1)} %bitcast_add_fusion, f32[16,128]{1,0:T(8,128)} %bitcast.102, f32[16]{0:T(128)} %copy-done.12, f32[1,16,32,128]{3,2,1,0:T(8,128)} %get-tuple-element.14, ...), kind=kOutput, calls=%fused_computation.23 | convolution fusion | flops 101253120 | bytes 5316672 | tf_op jit(solution)/shard_map/tnkri,tnkio->tnro/dot_general | solution.py:159
  (67 shorter events, 19.3 us)
Async XLA Ops:
  0.0 47.6 %copy-start = (bf16[1,16,6,128,128]{4,3,2,1,0:T(8,128)(2,1)S(1)}, bf16[1,16,6,128,128]{4,3,2,1,0:T(8,128)(2,1)}, u32[]{:S(2)}) copy-start(bf16[1,16,6,128,128]{4,3,2,1,0:T(8,128)(2,1)} %param.16) | copy-start | bytes 9437188
  0.0 47.6 %copy-start.7 = (f32[1,16,128]{2,1,0:T(8,128)S(1)}, f32[1,16,128]{2,1,0:T(8,128)}, u32[]{:S(2)}) copy-start(f32[1,16,128]{2,1,0:T(8,128)} %param.14) | copy-start | bytes 24580
  0.0 31.5 %copy-start.6 = (bf16[1,4,128,128]{3,2,1,0:T(8,128)(2,1)S(1)}, bf16[1,4,128,128]{3,2,1,0:T(8,128)(2,1)}, u32[]{:S(2)}) copy-start(bf16[1,4,128,128]{3,2,1,0:T(8,128)(2,1)} %param.17) | copy-start | bytes 393220
  0.8 2.0 %copy-start.12 = (f32[16]{0:T(128)}, f32[16]{0:T(128)S(1)}, u32[]{:S(2)}) copy-start(f32[16]{0:T(128)S(1)} %or_convert_fusion) | copy-start | bytes 196
  2.8 8.6 %copy-start.3 = (f32[1,16,32,128]{3,2,1,0:T(8,128)}, f32[1,16,32,128]{3,2,1,0:T(8,128)S(1)}, u32[]{:S(2)}) copy-start(f32[1,16,32,128]{3,2,1,0:T(8,128)S(1)} %get-tuple-element.15) | copy-start | bytes 786436
  3.6 7.9 %copy-start.4 = (f32[528,128]{1,0:T(8,128)}, f32[528,128]{1,0:T(8,128)S(1)}, u32[]{:S(2)}) copy-start(f32[528,128]{1,0:T(8,128)S(1)} %get-tuple-element.22.own_ref) | copy-start | bytes 811012
  3.6 7.9 %collective-permute-start = (f32[528,128]{1,0:T(8,128)S(1)}, f32[528,128]{1,0:T(8,128)S(1)}, u32[]{:S(2)}, u32[]{:S(2)}) collective-permute-start(f32[528,128]{1,0:T(8,128)S(1)} %get-tuple-element.22.own_ref), channel_id=1, source_target_pairs={{0,256},{32,288},{64,320},{96,352},{128,384},{160,416},{192,448},{... | collective-permute-start | bytes 811016 | tf_op jit(solution)/shard_map/ppermute | solution.py:49
  11.4 16.6 %copy-start.1 = (f32[528,128]{1,0:T(8,128)}, f32[528,128]{1,0:T(8,128)S(1)}, u32[]{:S(2)}) copy-start(f32[528,128]{1,0:T(8,128)S(1)} %collective-permute-done.across_ref) | copy-start | bytes 811012
  12.4 15.6 %collective-permute-start.1 = (f32[2,528,128]{2,1,0:T(8,128)}, f32[2,528,128]{2,1,0:T(8,128)}, u32[]{:S(2)}, u32[]{:S(2)}) collective-permute-start(f32[2,528,128]{2,1,0:T(8,128)} %pad_maximum_fusion.2), channel_id=1, source_target_pairs={{0,32},{32,0},{64,96},{96,64},{128,160},{160,128},{192,224},{224,1... | collective-permute-start | bytes 1622024 | tf_op jit(solution)/shard_map/ppermute | solution.py:49
  32.4 12.7 %collective-permute-start.2 = (bf16[1,5,32,128]{3,2,1,0:T(8,128)(2,1)S(1)}, bf16[1,5,32,128]{3,2,1,0:T(8,128)(2,1)S(1)}, u32[]{:S(2)}, u32[]{:S(2)}) collective-permute-start(bf16[1,5,32,128]{3,2,1,0:T(8,128)(2,1)S(1)} %pad_maximum_fusion.5), channel_id=1, source_target_pairs={{31,0},{0,1},{1,2},{2,3},{3,4},{4,5},{5,6},{6,7},{7,8},{8,9},{9,10... | collective-permute-start | bytes 122888 | tf_op jit(solution)/shard_map/ppermute | solution.py:32
  34.3 10.9 %collective-permute-start.3 = (bf16[1,1,32,128]{3,2,1,0:T(8,128)(2,1)S(1)}, bf16[1,1,32,128]{3,2,1,0:T(8,128)(2,1)S(1)}, u32[]{:S(2)}, u32[]{:S(2)}) collective-permute-start(bf16[1,1,32,128]{3,2,1,0:T(8,128)(2,1)S(1)} %get-tuple-element.26), channel_id=1, source_target_pairs={{1,0},{2,1},{3,2},{4,3},{5,4},{6,5},{7,6},{8,7},{9,8},{10,9},{11,1... | collective-permute-start | bytes 24584 | tf_op jit(solution)/shard_map/ppermute | solution.py:32
  45.1 2.4 %copy-start.9 = (s32[1024]{0:T(1024)}, s32[1024]{0:T(1024)S(1)}, u32[]{:S(2)}) copy-start(s32[1024]{0:T(1024)S(1)} %pad_clamp_fusion) | copy-start | bytes 12292
  47.6 18.8 %copy-start.2 = (f32[528,128]{1,0:T(8,128)S(1)}, f32[528,128]{1,0:T(8,128)}, u32[]{:S(2)}) copy-start(f32[528,128]{1,0:T(8,128)} %copy-done.1) | copy-start | bytes 811012
  50.3 9.2 %collective-permute-start.4 = (f32[512,128]{1,0:T(8,128)}, f32[512,128]{1,0:T(8,128)}, u32[]{:S(2)}, u32[]{:S(2)}) collective-permute-start(f32[512,128]{1,0:T(8,128)} %bitcast.17), channel_id=1, source_target_pairs={{0,256},{32,288},{64,320},{96,352},{128,384},{160,416},{192,448},{... | collective-permute-start | bytes 786440 | tf_op jit(solution)/shard_map/ppermute | solution.py:49
  52.6 21.4 %all-to-all-start = ((f32[4,576,128]{2,1,0:T(8,128)}), f32[4,576,128]{2,1,0:T(8,128)}, u32[]{:S(2)}, u32[]{:S(2)}) async-start(f32[4,576,128]{2,1,0:T(8,128)} %shard_map.118), calls=%async_computation | async-start | bytes 2359296 | tf_op jit(solution)/shard_map/all_to_all | solution.py:173
  61.4 12.7 %collective-permute-start.5 = (f32[2,512,128]{2,1,0:T(8,128)}, f32[2,512,128]{2,1,0:T(8,128)}, u32[]{:S(2)}, u32[]{:S(2)}) collective-permute-start(f32[2,512,128]{2,1,0:T(8,128)} %pad_maximum_fusion.3), channel_id=1, source_target_pairs={{0,32},{32,0},{64,96},{96,64},{128,160},{160,128},{192,224},{224,1... | collective-permute-start | bytes 1572872 | tf_op jit(solution)/shard_map/ppermute | solution.py:49
  67.5 8.7 %copy-start.8 = (f32[1,16,128]{2,1,0:T(8,128)S(1)}, f32[1,16,128]{2,1,0:T(8,128)}, u32[]{:S(2)}) copy-start(f32[1,16,128]{2,1,0:T(8,128)} %param.14) | copy-start | bytes 24580
  74.1 12.8 %copy-start.10 = (f32[16,128]{1,0:T(8,128)S(1)}, f32[16,128]{1,0:T(8,128)}, u32[]{:S(2)}) copy-start(f32[16,128]{1,0:T(8,128)} %param.15) | copy-start | bytes 24580
  77.3 42.6 %copy-start.5 = (bf16[1,16,32,128]{3,2,1,0:T(8,128)(2,1)}, bf16[1,16,32,128]{3,2,1,0:T(8,128)(2,1)S(1)}, u32[]{:S(2)}) copy-start(bf16[1,16,32,128]{3,2,1,0:T(8,128)(2,1)S(1)} %fusion.24) | copy-start | bytes 393220
  105.1 5.8 %copy-start.13 = (f32[4,4,1,1]{1,0,2,3:T(4,128)S(1)}, f32[4,4,1,1]{1,0,2,3:T(4,128)}, u32[]{:S(2)}) copy-start(f32[4,4,1,1]{1,0,2,3:T(4,128)} %reshape.237) | copy-start | bytes 196
  111.0 8.9 %copy-start.14 = (f32[4]{0:T(128)S(1)}, f32[4]{0:T(128)}, u32[]{:S(2)}) copy-start(f32[4]{0:T(128)} %convert_bitcast_fusion) | copy-start | bytes 52
  115.6 19.1 %all-to-all-start.1 = ((f32[4,512,128]{2,1,0:T(8,128)}), f32[4,512,128]{2,1,0:T(8,128)}, u32[]{:S(2)}, u32[]{:S(2)}) async-start(f32[4,512,128]{2,1,0:T(8,128)} %copy.22), calls=%async_computation.1 | async-start | bytes 2097152 | tf_op jit(solution)/shard_map/all_to_all | solution.py:194
  120.8 9.2 %collective-permute-start.6 = (bf16[1,5,32,128]{3,2,1,0:T(8,128)(2,1)S(1)}, bf16[1,5,32,128]{3,2,1,0:T(8,128)(2,1)S(1)}, u32[]{:S(2)}, u32[]{:S(2)}) collective-permute-start(bf16[1,5,32,128]{3,2,1,0:T(8,128)(2,1)S(1)} %pad_maximum_fusion.6), channel_id=1, source_target_pairs={{31,0},{0,1},{1,2},{2,3},{3,4},{4,5},{5,6},{6,7},{7,8},{8,9},{9,10... | collective-permute-start | bytes 122888 | tf_op jit(solution)/shard_map/ppermute | solution.py:32
  122.8 8.0 %collective-permute-start.7 = (bf16[1,1,32,128]{3,2,1,0:T(8,128)(2,1)S(1)}, bf16[1,1,32,128]{3,2,1,0:T(8,128)(2,1)S(1)}, u32[]{:S(2)}, u32[]{:S(2)}) collective-permute-start(bf16[1,1,32,128]{3,2,1,0:T(8,128)(2,1)S(1)} %get-tuple-element.24), channel_id=1, source_target_pairs={{1,0},{2,1},{3,2},{4,3},{5,4},{6,5},{7,6},{8,7},{9,8},{10,9},{11,1... | collective-permute-start | bytes 24584 | tf_op jit(solution)/shard_map/ppermute | solution.py:32
  130.0 0.6 copy-start.11

commit v8 on v6

--- a/solution.py
+++ b/solution.py
@@ -66,9 +66,9 @@
     return table.astype(np.float32)
 
 
-def mix_kernel(index_ref, coef_ref, own_ref, across_ref, pair_ref, o_ref):
+def mix_kernel(index_ref, coef_ref, own_ref, mate_ref, across_ref, diagonal_ref, o_ref):
     me = index_ref[0]
-    values = (own_ref[...], pair_ref[0], across_ref[...], pair_ref[1])
+    values = (own_ref[...], mate_ref[...], across_ref[...], diagonal_ref[...])
     for slot in range(4):
         acc = coef_ref[me, slot * 4] * values[0]
         for m in range(1, 4):
@@ -76,49 +76,69 @@
         o_ref[slot] = acc
 
 
-def partial_sums(index, own, across, pair):
+def partial_sums(index, own, mate, across, diagonal):
     rows, lanes = own.shape
     block = 256
     flat = pl.BlockSpec((block, lanes), lambda r, index: (r, 0))
-    stacked = pl.BlockSpec((2, block, lanes), lambda r, index: (0, r, 0))
     return pl.pallas_call(
         mix_kernel,
         grid_spec=pltpu.PrefetchScalarGridSpec(
             num_scalar_prefetch=1,
             grid=(rows // block,),
-            in_specs=[pl.BlockSpec(memory_space=pltpu.SMEM), flat, flat, stacked],
+            in_specs=[pl.BlockSpec(memory_space=pltpu.SMEM), flat, flat, flat, flat],
             out_specs=pl.BlockSpec((4, block, lanes), lambda r, index: (0, r, 0)),
         ),
         out_shape=jax.ShapeDtypeStruct((4, rows, lanes), jnp.float32),
-    )(index, jnp.asarray(coefficient_table()), own, across, pair)
+    )(index, jnp.asarray(coefficient_table()), own, mate, across, diagonal)
 
 
-def instance_mix(weighted):
+def update_kernel(got_ref, base_ref, scale_ref, cond_ref, lam_ref, weighted_ref):
+    spec = (got_ref[0] + got_ref[1]) + (got_ref[2] + got_ref[3])
+    lam = base_ref[...] - scale_ref[...] * spec
+    lam_ref[...] = lam
+    weighted_ref[...] = lam * cond_ref[...]
+
+
+def updated(got, base, scale, condb):
+    rows, lanes = base.shape
+    block = 256
+    flat = pl.BlockSpec((block, lanes), lambda r: (r, 0))
+    return pl.pallas_call(
+        update_kernel,
+        grid=(rows // block,),
+        in_specs=[pl.BlockSpec((4, block, lanes), lambda r: (0, r, 0)), flat, flat, flat],
+        out_specs=[flat, flat],
+        out_shape=[jax.ShapeDtypeStruct(base.shape, jnp.float32)] * 2,
+    )(got, base, scale, condb)
+
+
+def instance_mix(flat):
     i = lax.axis_index("iy") * 8 + lax.axis_index("ix") * 2 + lax.axis_index("ic")
-    shape = weighted.shape
-    flat = weighted.reshape(-1, shape[-1])
+    mate = routed(flat, lambda s: s ^ 1)
     across = routed(flat, lambda s: s ^ 8)
-    pair = routed(jnp.stack([flat, across]), lambda s: s ^ 1)
-    partials = partial_sums(jnp.reshape(i, (1,)).astype(jnp.int32), flat, across, pair)
-    gathered = lax.all_to_all(partials, "ix", 0, 0)
-    return partials, [gathered[k].reshape(shape) for k in range(gathered.shape[0])]
+    diagonal = routed(across, lambda s: s ^ 1)
+    partials = partial_sums(jnp.reshape(i, (1,)).astype(jnp.int32), flat, mate, across, diagonal)
+    return partials, lax.all_to_all(partials, "ix", 0, 0)
 
 
 def shards(lam_init, rhs, relax, cond, jac, rotor_jac, cols, rotor_shift, owned):
     local_inst = lam_init.shape[0]
     rows = lam_init.shape[1]
     rotor_rows = rotor_jac.shape[1]
-    dspec = spectral_matrix()
+    shape = lam_init.shape
+    lanes = shape[-1]
     row = jnp.arange(rows)
     live = ((row >= rows - rotor_rows) | (row < owned[0])).astype(jnp.float32)[None, :, None, None]
     lam = lam_init * live
     moving = rotor_shift.astype(jnp.float32)[:, :, None, None]
     relax_wide = relax[:, :, None, :]
     cond_wide = cond[None, :, None, :]
+    scale = jnp.broadcast_to(relax_wide * live, shape).reshape(-1, lanes)
+    condb = jnp.broadcast_to(cond_wide, shape).reshape(-1, lanes)
+    weighted = (lam * cond_wide).reshape(-1, lanes)
     for sweep in range(SWEEPS):
         lam_b = lam.astype(jnp.bfloat16)
-        weighted = lam * cond_wide
-        partials, pieces = instance_mix(weighted)
+        partials, got = instance_mix(weighted)
         records = jnp.einsum(
             "tjri,tjio->tjro",
             lam_b[:, rows - rotor_rows :],
@@ -138,9 +158,9 @@
             [jnp.zeros((local_inst, rows - rotor_rows) + rotor.shape[2:], jnp.float32), rotor],
             axis=1,
         )
-        spec = pieces[0] + pieces[1] + pieces[2] + pieces[3]
-        resid = rhs - (stator + rotor_full + spec)
-        lam = lam + relax_wide * resid * live
+        base = lam + relax_wide * (rhs - (stator + rotor_full)) * live
+        lam_flat, weighted = updated(got, base.reshape(-1, lanes), scale, condb)
+        lam = lam_flat.reshape(shape)
     return lam
 
 

time: 97.1 us -> 94.4 us (0.972)
  waiting for transfers between devices: 14.6 us -> 4.48 us
  Pallas kernels: 4.49 us -> 8.97 us
  local copies, waits for them, and re-layouts: 4.86 us -> 6.86 us
  starting transfers between devices: 49.7 us -> 51.1 us
  other arithmetic: 14.6 us -> 13.3 us
  matrix products: 6.06 us -> 7.2 us
    ppermute x4, waiting for transfers between devices: 7.35 us -> 0.89 us  [shifted(): return lax.ppermute(block, axis, route)]
    pallas_call x0 -> x2, Pallas kernels: none -> 4.37 us  [updated(): pl.pallas_call(update_kernel, grid=(rows // block,), in_specs=[pl.BlockSp...]
    add x3 -> x0, other arithmetic: 4.34 us -> none  [the longest x2 2.51 us: shards(): spec = pieces[0] + pieces[1] + pieces[2] + pieces[3]]
    ppermute x4 -> x6, waiting for transfers between devices: 7.24 us -> 3.58 us  [routed(): return lax.ppermute(block, INST, [(s, dest(s)) for s in range(NT)])]
    ppermute x4 -> x6, starting transfers between devices: 20.2 us -> 21.7 us  [routed(): return lax.ppermute(block, INST, [(s, dest(s)) for s in range(NT)])]
    mul x1, other arithmetic: 0.02 us -> 1.36 us  [shards(): scale = jnp.broadcast_to(relax_wide * live, shape).reshape(-1, lanes)]
    another operation x2 -> x0, other arithmetic: 1.02 us -> none  [instance_mix(): pair = routed(jnp.stack([flat, across]), lambda s: s ^ 1)]
  transfers between devices with their start and end apart: 10 -> 12, of which waited for: 6 -> 3; matrix products, arithmetic and copies ran while one was open for 17% -> 24% of each run, Pallas kernels for 0% -> 0%
where the time goes in v8:
time: 94.4 us; the launch traced here: 92.9 us
  starting transfers between devices  51.1 us (54%)
  other arithmetic  13.3 us (14%)
  Pallas kernels  8.97 us (10%)
  matrix products  7.2 us (8%)
  local copies, waits for them, and re-layouts  6.86 us (7%)
  waiting for transfers between devices  4.48 us (5%)
  between operations  1.06 us (1%)
    ppermute x6, starting transfers between devices, routed(): return lax.ppermute(block, INST, [(s, dest(s)) for s in range(NT)])  21.7 us
    ppermute x4, starting transfers between devices, shifted(): return lax.ppermute(block, axis, route)  20.9 us
    all_to_all x2, starting transfers between devices, instance_mix(): return (partials, lax.all_to_all(partials, 'ix', 0, 0))  8.49 us
    dot_general x2, matrix products, shards(): jnp.einsum('tnkri,tnkio->tnro', picked, jac, preferred_element_type=jnp.f...  5.1 us
    pallas_call x2, Pallas kernels, partial_sums(): pl.pallas_call(mix_kernel, grid_spec=pltpu.PrefetchScalarGridSpec(num_sca...  4.6 us
    pallas_call x2, Pallas kernels, updated(): pl.pallas_call(update_kernel, grid=(rows // block,), in_specs=[pl.BlockSp...  4.37 us
    ppermute x6, waiting for transfers between devices, routed(): return lax.ppermute(block, INST, [(s, dest(s)) for s in range(NT)])  3.58 us
    gather x2, local copies, waits for them, and re-layouts, shards(): picked = lam_h[:, cols]  3.4 us
  transfers between devices with their start and end apart: 12, of which 3 were waited for; matrix products, arithmetic and copies ran while one was open for 24% of the time, Pallas kernels for 0%

profile of v8, /device:TPU:1, one launch (start us, length us, event | category | flops | bytes accessed | tf_op | source)
XLA Modules:
  0.0 92.9 jit_solution(12955054561097884498)
XLA Ops:
  0.8 1.9 %multiply_convert_fusion = (bf16[1,16,32,128]{3,2,1,0:T(8,128)(2,1)S(1)}, f32[1,16,32,128]{3,2,1,0:T(8,128)}) fusion(f32[1,16,32,128]{3,2,1,0:T(8,128)} %param.11, f32[16]{0:T(128)S(1)} %or_convert_fusion, f32[16,128]{1,0:T(8,128)} %param.14), kind=kLoop, calls=%fused_computation.10 | loop fusion | flops 196608 | bytes 663616 | tf_op jit(solution)/shard_map/convert_element_type | solution.py:140
  2.7 4.0 %collective-permute-start.1 = (f32[512,128]{1,0:T(8,128)}, f32[512,128]{1,0:T(8,128)}, u32[]{:S(2)}, u32[]{:S(2)}) collective-permute-start(f32[512,128]{1,0:T(8,128)} %bitcast.2.own_ref), channel_id=1, source_target_pairs={{0,256},{32,288},{64,320},{96,352},{128,384},{160,416},{192,448},{... | collective-permute-start | bytes 786440 | tf_op jit(solution)/shard_map/ppermute | solution.py:49
  6.8 6.7 %collective-permute-start = (f32[512,128]{1,0:T(8,128)}, f32[512,128]{1,0:T(8,128)}, u32[]{:S(2)}, u32[]{:S(2)}) collective-permute-start(f32[512,128]{1,0:T(8,128)} %bitcast.2.own_ref), channel_id=1, source_target_pairs={{0,32},{32,0},{64,96},{96,64},{128,160},{160,128},{192,224},{224,1... | collective-permute-start | bytes 786440 | tf_op jit(solution)/shard_map/ppermute | solution.py:49
  14.8 1.0 %fusion.12 = f32[4,32,128]{2,1,0:T(8,128)S(1)} fusion(bf16[1,4,128,128]{3,2,1,0:T(8,128)(2,1)} %param.16, bf16[1,16,32,128]{3,2,1,0:T(8,128)(2,1)S(1)} %get-tuple-element.13), kind=kOutput, calls=%fused_computation.16 | convolution fusion | flops 4194304 | bytes 229376 | tf_op jit(solution)/shard_map/tjri,tjio->tjro/dot_general | solution.py:142
  15.8 1.2 %broadcast_subtract_fusion = f32[4]{0:T(128)} fusion(s32[1,4]{1,0:T(1,128)} %param.18), kind=kLoop, calls=%fused_computation.33 | loop fusion | flops 8 | bytes 32 | tf_op jit(solution)/shard_map/sub | solution.py:156
  17.2 2.9 %collective-permute-start.2 = (f32[512,128]{1,0:T(8,128)}, f32[512,128]{1,0:T(8,128)}, u32[]{:S(2)}, u32[]{:S(2)}) collective-permute-start(f32[512,128]{1,0:T(8,128)} %collective-permute-done.1.across_ref), channel_id=1, source_target_pairs={{0,32},{32,0},{64,96},{96,64},{128,160},{160,128},{192,224},{224,1... | collective-permute-start | bytes 786440 | tf_op jit(solution)/shard_map/ppermute | solution.py:49
  20.9 1.4 %broadcast_multiply_fusion = f32[16,128]{1,0:T(8,128)} fusion(f32[16]{0:T(128)S(1)} %or_convert_fusion, f32[1,16,128]{2,1,0:T(8,128)} %param.13), kind=kLoop, calls=%fused_computation.30 | loop fusion | flops 2048 | bytes 16448 | tf_op jit(solution)/shard_map/mul | solution.py:136
  22.3 2.3 %shard_map.109 = f32[4,512,128]{2,1,0:T(8,128)} custom-call(s32[1]{0:T(128)} %bitcast.index_ref, f32[16,16]{1,0:T(8,128)} %constant.32.clone.coef_ref, f32[512,128]{1,0:T(8,128)} %bitcast.2.own_ref, f32[512,128]{1,0:T(8,128)} %collective-permute-done.mate_ref, f32[512,128]{1,0:T(8,128)} %collective-permute-done.1.across_ref, ...), custom_call_target="tpu_custom_call" | custom-call | tf_op jit(solution)/shard_map/pallas_call | solution.py:83
  24.6 4.2 %all-to-all-start = ((f32[4,512,128]{2,1,0:T(8,128)}), f32[4,512,128]{2,1,0:T(8,128)}, u32[]{:S(2)}, u32[]{:S(2)}) async-start(f32[4,512,128]{2,1,0:T(8,128)} %shard_map.109), calls=%async_computation | async-start | bytes 2097152 | tf_op jit(solution)/shard_map/all_to_all | solution.py:121
  28.8 1.9 %collective-permute-start.3 = (bf16[1,5,32,128]{3,2,1,0:T(8,128)(2,1)}, bf16[1,5,32,128]{3,2,1,0:T(8,128)(2,1)S(1)}, u32[]{:S(2)}, u32[]{:S(2)}) collective-permute-start(bf16[1,5,32,128]{3,2,1,0:T(8,128)(2,1)} %pad_maximum_fusion), channel_id=1, source_target_pairs={{31,0},{0,1},{1,2},{2,3},{3,4},{4,5},{5,6},{6,7},{7,8},{8,9},{9,10... | collective-permute-start | bytes 122888 | tf_op jit(solution)/shard_map/ppermute | solution.py:32
  30.8 10.1 %collective-permute-start.4 = (bf16[1,1,32,128]{3,2,1,0:T(8,128)(2,1)S(1)}, bf16[1,1,32,128]{3,2,1,0:T(8,128)(2,1)S(1)}, u32[]{:S(2)}, u32[]{:S(2)}) collective-permute-start(bf16[1,1,32,128]{3,2,1,0:T(8,128)(2,1)S(1)} %slice.33), channel_id=1, source_target_pairs={{1,0},{2,1},{3,2},{4,3},{5,4},{6,5},{7,6},{8,7},{9,8},{10,9},{11,1... | collective-permute-start | bytes 24584 | tf_op jit(solution)/shard_map/ppermute | solution.py:32
  42.0 0.9 maximum_bitcast_fusion
  43.0 1.7 %gather_fusion = bf16[96,32,128]{2,1,0:T(8,128)(2,1)} fusion(bf16[18,32,128]{2,1,0:T(8,128)(2,1)S(1)} %maximum_bitcast_fusion, s32[1024]{0:T(1024)} %pad_clamp_fusion), kind=kCustom, calls=%fused_computation | custom fusion | bytes 1573248 | tf_op jit(solution)/shard_map/gather | solution.py:153
  44.7 1.0 %bitcast_add_fusion.1 = f32[1,4,32,128]{3,2,1,0:T(8,128)S(1)} fusion(f32[4,32,128]{2,1,0:T(8,128)} %copy-done.4, bf16[1,5,32,128]{3,2,1,0:T(8,128)(2,1)} %copy-done.8, f32[4]{0:T(128)} %broadcast_subtract_fusion), kind=kLoop, calls=%fused_computation.19 | loop fusion | flops 49152 | bytes 163856 | tf_op jit(solution)/shard_map/add | solution.py:156
  45.7 2.6 %multiply_add_fusion.1 = f32[1,16,32,128]{3,2,1,0:T(8,128)} fusion(f32[1,16,32,128]{3,2,1,0:T(8,128)S(1)} %copy-done.1, f32[1,4,32,128]{3,2,1,0:T(8,128)S(1)} %bitcast_add_fusion.1, f32[1,16,32,128]{3,2,1,0:T(8,128)} %param.11, f32[16,128]{1,0:T(8,128)} %bitcast.74, f32[16]{0:T(128)} %copy-done.12, bf16[16,6,32,128]{3,2,1,0:T(8,128)(2,1)} %bitcast.65, ...), kind=kOutput, calls=%fused_computation.9 | convolution fusion | flops 101056512 | bytes 4792384 | tf_op jit(solution)/shard_map/tnkri,tnkio->tnro/dot_general | solution.py:154
  49.7 2.2 %shard_map.110 = (f32[512,128]{1,0:T(8,128)}, f32[512,128]{1,0:T(8,128)}) custom-call(f32[4,512,128]{2,1,0:T(8,128)} %all-to-all-done.got_ref, f32[512,128]{1,0:T(8,128)} %bitcast.71, f32[512,128]{1,0:T(8,128)} %bitcast.66, f32[512,128]{1,0:T(8,128)} %bitcast.68), custom_call_target="tpu_custom_call" | custom-call | tf_op jit(solution)/shard_map/pallas_call | solution.py:106
  51.9 2.3 %collective-permute-start.6 = (f32[512,128]{1,0:T(8,128)}, f32[512,128]{1,0:T(8,128)S(1)}, u32[]{:S(2)}, u32[]{:S(2)}) collective-permute-start(f32[512,128]{1,0:T(8,128)} %get-tuple-element.14.own_ref), channel_id=1, source_target_pairs={{0,256},{32,288},{64,320},{96,352},{128,384},{160,416},{192,448},{... | collective-permute-start | bytes 786440 | tf_op jit(solution)/shard_map/ppermute | solution.py:49
  54.2 2.6 %collective-permute-start.5 = (f32[512,128]{1,0:T(8,128)}, f32[512,128]{1,0:T(8,128)S(1)}, u32[]{:S(2)}, u32[]{:S(2)}) collective-permute-start(f32[512,128]{1,0:T(8,128)} %get-tuple-element.14.own_ref), channel_id=1, source_target_pairs={{0,32},{32,0},{64,96},{96,64},{128,160},{160,128},{192,224},{224,1... | collective-permute-start | bytes 786440 | tf_op jit(solution)/shard_map/ppermute | solution.py:49
  56.8 1.0 %convert_element_type.46 = bf16[1,16,32,128]{3,2,1,0:T(8,128)(2,1)S(1)} convert(f32[1,16,32,128]{3,2,1,0:T(8,128)} %bitcast.72) | non-fusion elementwise | flops 65536 | bytes 393216 | tf_op jit(solution)/shard_map/convert_element_type | solution.py:140
  57.8 3.6 %collective-permute-done.6.across_ref = f32[512,128]{1,0:T(8,128)S(1)} collective-permute-done((f32[512,128]{1,0:T(8,128)}, f32[512,128]{1,0:T(8,128)S(1)}, u32[]{:S(2)}, u32[]{:S(2)}) %collective-permute-start.6) | collective-permute-done | bytes 262176 | tf_op jit(solution)/shard_map/ppermute | solution.py:49
  61.4 3.2 %collective-permute-start.7 = (f32[512,128]{1,0:T(8,128)S(1)}, f32[512,128]{1,0:T(8,128)}, u32[]{:S(2)}, u32[]{:S(2)}) collective-permute-start(f32[512,128]{1,0:T(8,128)S(1)} %collective-permute-done.6.across_ref), channel_id=1, source_target_pairs={{0,32},{32,0},{64,96},{96,64},{128,160},{160,128},{192,224},{224,1... | collective-permute-start | bytes 786440 | tf_op jit(solution)/shard_map/ppermute | solution.py:49
  64.6 1.1 %fusion.10 = f32[4,32,128]{2,1,0:T(8,128)S(1)} fusion(bf16[1,4,128,128]{3,2,1,0:T(8,128)(2,1)} %param.16, bf16[1,16,32,128]{3,2,1,0:T(8,128)(2,1)S(1)} %convert_element_type.46), kind=kOutput, calls=%fused_computation.14 | convolution fusion | flops 4194304 | bytes 229376 | tf_op jit(solution)/shard_map/tjri,tjio->tjro/dot_general | solution.py:142
  67.7 2.3 %shard_map.111 = f32[4,512,128]{2,1,0:T(8,128)} custom-call(s32[1]{0:T(128)} %bitcast.index_ref, f32[16,16]{1,0:T(8,128)} %constant.32.clone.coef_ref, f32[512,128]{1,0:T(8,128)} %get-tuple-element.14.own_ref, f32[512,128]{1,0:T(8,128)} %copy-done.7, f32[512,128]{1,0:T(8,128)} %copy-done.6, f32[512,128]{1,0:T(8,128)} %collective-permute-done.7.diagonal_ref), custom_call_target="tpu_custom_call" | custom-call | tf_op jit(solution)/shard_map/pallas_call | solution.py:83
  69.9 4.2 %all-to-all-start.1 = ((f32[4,512,128]{2,1,0:T(8,128)}), f32[4,512,128]{2,1,0:T(8,128)}, u32[]{:S(2)}, u32[]{:S(2)}) async-start(f32[4,512,128]{2,1,0:T(8,128)} %shard_map.111), calls=%async_computation.1 | async-start | bytes 2097152 | tf_op jit(solution)/shard_map/all_to_all | solution.py:121
  74.2 0.8 pad_maximum_fusion.1
  75.0 1.9 %collective-permute-start.8 = (bf16[1,5,32,128]{3,2,1,0:T(8,128)(2,1)S(1)}, bf16[1,5,32,128]{3,2,1,0:T(8,128)(2,1)S(1)}, u32[]{:S(2)}, u32[]{:S(2)}) collective-permute-start(bf16[1,5,32,128]{3,2,1,0:T(8,128)(2,1)S(1)} %pad_maximum_fusion.1), channel_id=1, source_target_pairs={{31,0},{0,1},{1,2},{2,3},{3,4},{4,5},{5,6},{6,7},{7,8},{8,9},{9,10... | collective-permute-start | bytes 122888 | tf_op jit(solution)/shard_map/ppermute | solution.py:32
  76.9 7.0 %collective-permute-start.9 = (bf16[1,1,32,128]{3,2,1,0:T(8,128)(2,1)S(1)}, bf16[1,1,32,128]{3,2,1,0:T(8,128)(2,1)S(1)}, u32[]{:S(2)}, u32[]{:S(2)}) collective-permute-start(bf16[1,1,32,128]{3,2,1,0:T(8,128)(2,1)S(1)} %slice.38), channel_id=1, source_target_pairs={{1,0},{2,1},{3,2},{4,3},{5,4},{6,5},{7,6},{8,7},{9,8},{10,9},{11,1... | collective-permute-start | bytes 24584 | tf_op jit(solution)/shard_map/ppermute | solution.py:32
  84.7 0.9 maximum_bitcast_fusion.1
  85.6 1.7 %gather_fusion.1 = bf16[96,32,128]{2,1,0:T(8,128)(2,1)} fusion(bf16[18,32,128]{2,1,0:T(8,128)(2,1)S(1)} %maximum_bitcast_fusion.1, s32[1024]{0:T(1024)} %pad_clamp_fusion), kind=kCustom, calls=%fused_computation.1 | custom fusion | bytes 1573248 | tf_op jit(solution)/shard_map/gather | solution.py:153
  87.3 0.9 %bitcast_add_fusion = f32[1,4,32,128]{3,2,1,0:T(8,128)S(1)} fusion(f32[4,32,128]{2,1,0:T(8,128)} %copy-done.5, bf16[1,5,32,128]{3,2,1,0:T(8,128)(2,1)} %copy-done.9, f32[4]{0:T(128)} %broadcast_subtract_fusion), kind=kLoop, calls=%fused_computation.18 | loop fusion | flops 49152 | bytes 163856 | tf_op jit(solution)/shard_map/add | solution.py:156
  88.2 2.5 %multiply_add_fusion = f32[1,16,32,128]{3,2,1,0:T(8,128)} fusion(f32[1,16,32,128]{3,2,1,0:T(8,128)} %bitcast.73, f32[1,16,32,128]{3,2,1,0:T(8,128)S(1)} %copy-done.1, f32[1,4,32,128]{3,2,1,0:T(8,128)S(1)} %bitcast_add_fusion, f32[16,128]{1,0:T(8,128)} %bitcast.75, f32[16]{0:T(128)} %copy-done.12, bf16[16,6,32,128]{3,2,1,0:T(8,128)(2,1)} %bitcast.64, ...), kind=kOutput, calls=%fused_computation.8 | convolution fusion | flops 100990976 | bytes 4792384 | tf_op jit(solution)/shard_map/tnkri,tnkio->tnro/dot_general | solution.py:154
  90.8 2.2 %shard_map.112 = (f32[512,128]{1,0:T(8,128)}, f32[512,128]{1,0:T(8,128)}) custom-call(f32[4,512,128]{2,1,0:T(8,128)} %all-to-all-done.1.got_ref, f32[512,128]{1,0:T(8,128)} %bitcast.70, f32[512,128]{1,0:T(8,128)} %bitcast.67, f32[512,128]{1,0:T(8,128)} %bitcast.69), custom_call_target="tpu_custom_call" | custom-call | tf_op jit(solution)/shard_map/pallas_call | solution.py:106
  (58 shorter events, 7.7 us)
Async XLA Ops:
  0.0 45.6 %copy-start = (bf16[1,16,6,128,128]{4,3,2,1,0:T(8,128)(2,1)S(1)}, bf16[1,16,6,128,128]{4,3,2,1,0:T(8,128)(2,1)}, u32[]{:S(2)}) copy-start(bf16[1,16,6,128,128]{4,3,2,1,0:T(8,128)(2,1)} %param.15) | copy-start | bytes 9437188
  0.8 40.6 %copy-start.12 = (f32[16]{0:T(128)}, f32[16]{0:T(128)S(1)}, u32[]{:S(2)}) copy-start(f32[16]{0:T(128)S(1)} %or_convert_fusion) | copy-start | bytes 196
  2.7 38.7 %copy-start.3 = (bf16[1,16,32,128]{3,2,1,0:T(8,128)(2,1)}, bf16[1,16,32,128]{3,2,1,0:T(8,128)(2,1)S(1)}, u32[]{:S(2)}) copy-start(bf16[1,16,32,128]{3,2,1,0:T(8,128)(2,1)S(1)} %get-tuple-element.13) | copy-start | bytes 393220
  2.7 14.4 %collective-permute-start.1 = (f32[512,128]{1,0:T(8,128)}, f32[512,128]{1,0:T(8,128)}, u32[]{:S(2)}, u32[]{:S(2)}) collective-permute-start(f32[512,128]{1,0:T(8,128)} %bitcast.2.own_ref), channel_id=1, source_target_pairs={{0,256},{32,288},{64,320},{96,352},{128,384},{160,416},{192,448},{... | collective-permute-start | bytes 786440 | tf_op jit(solution)/shard_map/ppermute | solution.py:49
  6.8 15.5 %collective-permute-start = (f32[512,128]{1,0:T(8,128)}, f32[512,128]{1,0:T(8,128)}, u32[]{:S(2)}, u32[]{:S(2)}) collective-permute-start(f32[512,128]{1,0:T(8,128)} %bitcast.2.own_ref), channel_id=1, source_target_pairs={{0,32},{32,0},{64,96},{96,64},{128,160},{160,128},{192,224},{224,1... | collective-permute-start | bytes 786440 | tf_op jit(solution)/shard_map/ppermute | solution.py:49
  14.1 6.6 %copy-start.13 = (f32[4]{0:T(128)}, f32[4]{0:T(128)S(1)}, u32[]{:S(2)}) copy-start(f32[4]{0:T(128)S(1)} %convert_bitcast_fusion) | copy-start | bytes 52
  15.8 1.2 %copy-start.4 = (f32[4,32,128]{2,1,0:T(8,128)}, f32[4,32,128]{2,1,0:T(8,128)S(1)}, u32[]{:S(2)}) copy-start(f32[4,32,128]{2,1,0:T(8,128)S(1)} %fusion.12) | copy-start | bytes 196612
  17.2 5.1 %collective-permute-start.2 = (f32[512,128]{1,0:T(8,128)}, f32[512,128]{1,0:T(8,128)}, u32[]{:S(2)}, u32[]{:S(2)}) collective-permute-start(f32[512,128]{1,0:T(8,128)} %collective-permute-done.1.across_ref), channel_id=1, source_target_pairs={{0,32},{32,0},{64,96},{96,64},{128,160},{160,128},{192,224},{224,1... | collective-permute-start | bytes 786440 | tf_op jit(solution)/shard_map/ppermute | solution.py:49
  22.2 23.4 %copy-start.1 = (f32[1,16,32,128]{3,2,1,0:T(8,128)S(1)}, f32[1,16,32,128]{3,2,1,0:T(8,128)}, u32[]{:S(2)}) copy-start(f32[1,16,32,128]{3,2,1,0:T(8,128)} %param.12) | copy-start | bytes 786436
  24.6 23.6 %all-to-all-start = ((f32[4,512,128]{2,1,0:T(8,128)}), f32[4,512,128]{2,1,0:T(8,128)}, u32[]{:S(2)}, u32[]{:S(2)}) async-start(f32[4,512,128]{2,1,0:T(8,128)} %shard_map.109), calls=%async_computation | async-start | bytes 2097152 | tf_op jit(solution)/shard_map/all_to_all | solution.py:121
  28.8 12.6 %collective-permute-start.3 = (bf16[1,5,32,128]{3,2,1,0:T(8,128)(2,1)}, bf16[1,5,32,128]{3,2,1,0:T(8,128)(2,1)S(1)}, u32[]{:S(2)}, u32[]{:S(2)}) collective-permute-start(bf16[1,5,32,128]{3,2,1,0:T(8,128)(2,1)} %pad_maximum_fusion), channel_id=1, source_target_pairs={{31,0},{0,1},{1,2},{2,3},{3,4},{4,5},{5,6},{6,7},{7,8},{8,9},{9,10... | collective-permute-start | bytes 122888 | tf_op jit(solution)/shard_map/ppermute | solution.py:32
  30.8 10.8 %collective-permute-start.4 = (bf16[1,1,32,128]{3,2,1,0:T(8,128)(2,1)S(1)}, bf16[1,1,32,128]{3,2,1,0:T(8,128)(2,1)S(1)}, u32[]{:S(2)}, u32[]{:S(2)}) collective-permute-start(bf16[1,1,32,128]{3,2,1,0:T(8,128)(2,1)S(1)} %slice.33), channel_id=1, source_target_pairs={{1,0},{2,1},{3,2},{4,3},{5,4},{6,5},{7,6},{8,7},{9,8},{10,9},{11,1... | collective-permute-start | bytes 24584 | tf_op jit(solution)/shard_map/ppermute | solution.py:32
  41.4 0.6 copy-start.8
  44.7 3.6 %copy-start.11 = (f32[16,128]{1,0:T(8,128)S(1)}, f32[16,128]{1,0:T(8,128)}, u32[]{:S(2)}) copy-start(f32[16,128]{1,0:T(8,128)} %broadcast_multiply_fusion) | copy-start | bytes 24580
  44.7 4.3 %copy-start.10 = (f32[16,128]{1,0:T(8,128)S(1)}, f32[16,128]{1,0:T(8,128)}, u32[]{:S(2)}) copy-start(f32[16,128]{1,0:T(8,128)} %param.14) | copy-start | bytes 24580
  45.7 20.6 %copy-start.14 = (f32[4]{0:T(128)S(1)}, f32[4]{0:T(128)}, u32[]{:S(2)}) copy-start(f32[4]{0:T(128)} %copy-done.13) | copy-start | bytes 52
  51.9 9.5 %collective-permute-start.6 = (f32[512,128]{1,0:T(8,128)}, f32[512,128]{1,0:T(8,128)S(1)}, u32[]{:S(2)}, u32[]{:S(2)}) collective-permute-start(f32[512,128]{1,0:T(8,128)} %get-tuple-element.14.own_ref), channel_id=1, source_target_pairs={{0,256},{32,288},{64,320},{96,352},{128,384},{160,416},{192,448},{... | collective-permute-start | bytes 786440 | tf_op jit(solution)/shard_map/ppermute | solution.py:49
  54.2 12.8 %collective-permute-start.5 = (f32[512,128]{1,0:T(8,128)}, f32[512,128]{1,0:T(8,128)S(1)}, u32[]{:S(2)}, u32[]{:S(2)}) collective-permute-start(f32[512,128]{1,0:T(8,128)} %get-tuple-element.14.own_ref), channel_id=1, source_target_pairs={{0,32},{32,0},{64,96},{96,64},{128,160},{160,128},{192,224},{224,1... | collective-permute-start | bytes 786440 | tf_op jit(solution)/shard_map/ppermute | solution.py:49
  57.8 26.1 %copy-start.2 = (bf16[1,16,32,128]{3,2,1,0:T(8,128)(2,1)}, bf16[1,16,32,128]{3,2,1,0:T(8,128)(2,1)S(1)}, u32[]{:S(2)}) copy-start(bf16[1,16,32,128]{3,2,1,0:T(8,128)(2,1)S(1)} %convert_element_type.46) | copy-start | bytes 393220
  61.4 5.6 %copy-start.6 = (f32[512,128]{1,0:T(8,128)}, f32[512,128]{1,0:T(8,128)S(1)}, u32[]{:S(2)}) copy-start(f32[512,128]{1,0:T(8,128)S(1)} %collective-permute-done.6.across_ref) | copy-start | bytes 786436
  61.4 6.3 %collective-permute-start.7 = (f32[512,128]{1,0:T(8,128)S(1)}, f32[512,128]{1,0:T(8,128)}, u32[]{:S(2)}, u32[]{:S(2)}) collective-permute-start(f32[512,128]{1,0:T(8,128)S(1)} %collective-permute-done.6.across_ref), channel_id=1, source_target_pairs={{0,32},{32,0},{64,96},{96,64},{128,160},{160,128},{192,224},{224,1... | collective-permute-start | bytes 786440 | tf_op jit(solution)/shard_map/ppermute | solution.py:49
  65.6 0.6 copy-start.5
  67.0 0.7 copy-start.7
  69.9 20.8 %all-to-all-start.1 = ((f32[4,512,128]{2,1,0:T(8,128)}), f32[4,512,128]{2,1,0:T(8,128)}, u32[]{:S(2)}, u32[]{:S(2)}) async-start(f32[4,512,128]{2,1,0:T(8,128)} %shard_map.111), calls=%async_computation.1 | async-start | bytes 2097152 | tf_op jit(solution)/shard_map/all_to_all | solution.py:121
  75.0 8.9 %collective-permute-start.8 = (bf16[1,5,32,128]{3,2,1,0:T(8,128)(2,1)S(1)}, bf16[1,5,32,128]{3,2,1,0:T(8,128)(2,1)S(1)}, u32[]{:S(2)}, u32[]{:S(2)}) collective-permute-start(bf16[1,5,32,128]{3,2,1,0:T(8,128)(2,1)S(1)} %pad_maximum_fusion.1), channel_id=1, source_target_pairs={{31,0},{0,1},{1,2},{2,3},{3,4},{4,5},{5,6},{6,7},{7,8},{8,9},{9,10... | collective-permute-start | bytes 122888 | tf_op jit(solution)/shard_map/ppermute | solution.py:32
  76.9 7.8 %collective-permute-start.9 = (bf16[1,1,32,128]{3,2,1,0:T(8,128)(2,1)S(1)}, bf16[1,1,32,128]{3,2,1,0:T(8,128)(2,1)S(1)}, u32[]{:S(2)}, u32[]{:S(2)}) collective-permute-start(bf16[1,1,32,128]{3,2,1,0:T(8,128)(2,1)S(1)} %slice.38), channel_id=1, source_target_pairs={{1,0},{2,1},{3,2},{4,3},{5,4},{6,5},{7,6},{8,7},{9,8},{10,9},{11,1... | collective-permute-start | bytes 24584 | tf_op jit(solution)/shard_map/ppermute | solution.py:32
  83.9 0.8 copy-start.9

commit v9 on v8

--- a/solution.py
+++ b/solution.py
@@ -112,6 +112,36 @@
     )(got, base, scale, condb)
 
 
+def stator_kernel(cols_ref, halo_ref, jac_ref, out_ref):
+    group = pl.program_id(0)
+    per, width = jac_ref.shape[0], jac_ref.shape[1]
+    for j in range(per):
+        n = group * per + j
+        acc = jnp.dot(halo_ref[cols_ref[n * width]], jac_ref[j, 0], preferred_element_type=jnp.float32)
+        for k in range(1, width):
+            acc = acc + jnp.dot(halo_ref[cols_ref[n * width + k]], jac_ref[j, k], preferred_element_type=jnp.float32)
+        out_ref[j] = acc
+
+
+def stator_of(halo, jac, cols):
+    rows, width, bs, _ = jac.shape
+    span, reps, lanes = halo.shape
+    per = 4
+    return pl.pallas_call(
+        stator_kernel,
+        grid_spec=pltpu.PrefetchScalarGridSpec(
+            num_scalar_prefetch=1,
+            grid=(rows // per,),
+            in_specs=[
+                pl.BlockSpec((span, reps, lanes), lambda g, cols: (0, 0, 0)),
+                pl.BlockSpec((per, width, bs, bs), lambda g, cols: (g, 0, 0, 0)),
+            ],
+            out_specs=pl.BlockSpec((per, reps, lanes), lambda g, cols: (g, 0, 0)),
+        ),
+        out_shape=jax.ShapeDtypeStruct((rows, reps, lanes), jnp.float32),
+    )(cols.reshape(-1), halo, jac)
+
+
 def instance_mix(flat):
     i = lax.axis_index("iy") * 8 + lax.axis_index("ix") * 2 + lax.axis_index("ic")
     mate = routed(flat, lambda s: s ^ 1)
@@ -136,6 +166,7 @@
     scale = jnp.broadcast_to(relax_wide * live, shape).reshape(-1, lanes)
     condb = jnp.broadcast_to(cond_wide, shape).reshape(-1, lanes)
     weighted = (lam * cond_wide).reshape(-1, lanes)
+    scale, condb, weighted = lax.optimization_barrier((scale, condb, weighted))
     for sweep in range(SWEEPS):
         lam_b = lam.astype(jnp.bfloat16)
         partials, got = instance_mix(weighted)
@@ -150,8 +181,7 @@
         onward = shifted(onward, "sector", 1)
         head = shifted(lam_b[:, :1], "sector", -1)
         lam_h = jnp.concatenate([onward[:, :1], lam_b, head], axis=1)
-        picked = lam_h[:, cols]
-        stator = jnp.einsum("tnkri,tnkio->tnro", picked, jac, preferred_element_type=jnp.float32)
+        stator = stator_of(lam_h[0], jac[0], cols)[None]
         arrived = onward[:, 1:].astype(jnp.float32)
         rotor = records * (1.0 - moving) + arrived
         rotor_full = jnp.concatenate(

time: 94.4 us -> 97.2 us (1.030)
  Pallas kernels: 8.97 us -> 18.7 us
  matrix products: 7.2 us -> 0.29 us
  starting transfers between devices: 51.1 us -> 56 us
  other arithmetic: 13.3 us -> 8.68 us
    pallas_call x0 -> x2, Pallas kernels: none -> 9.82 us  [stator_of(): pl.pallas_call(stator_kernel, grid_spec=pltpu.PrefetchScalarGridSpec(num_...]
    dot_general x2 -> x0, matrix products: 5.1 us -> none  [shards(): jnp.einsum('tnkri,tnkio->tnro', picked, jac, preferred_element_type=jnp.f...]
    ppermute x6, starting transfers between devices: 21.7 us -> 26.4 us  [routed(): return lax.ppermute(block, INST, [(s, dest(s)) for s in range(NT)])]
    add x0 -> x2, other arithmetic: none -> 3.54 us  [shards(): base = lam + relax_wide * (rhs - (stator + rotor_full)) * live]
    gather x2 -> x0, local copies, waits for them, and re-layouts: 3.4 us -> none  [shards(): picked = lam_h[:, cols]]
    unnamed x30 -> x33, local copies, waits for them, and re-layouts: 1.83 us -> 4.2 us
    concatenate x2 -> x0, other arithmetic: 1.85 us -> none  [shards(): lam_h = jnp.concatenate([onward[:, :1], lam_b, head], axis=1)]
    dot_general x2, matrix products: 2.1 us -> 0.29 us  [shards(): jnp.einsum('tjri,tjio->tjro', lam_b[:, rows - rotor_rows:], rotor_jac, pr...]
  transfers between devices with their start and end apart: 12 -> 12, of which waited for: 3 -> 3; matrix products, arithmetic and copies ran while one was open for 24% -> 8% of each run, Pallas kernels for 0% -> 10%
where the time goes in v9:
time: 97.2 us; the launch traced here: 96 us
  starting transfers between devices  56 us (58%)
  Pallas kernels  18.7 us (19%)
  other arithmetic  8.68 us (9%)
  local copies, waits for them, and re-layouts  7.08 us (7%)
  waiting for transfers between devices  4.28 us (4%)
    ppermute x6, starting transfers between devices, routed(): return lax.ppermute(block, INST, [(s, dest(s)) for s in range(NT)])  26.4 us
    ppermute x4, starting transfers between devices, shifted(): return lax.ppermute(block, axis, route)  21.6 us
    pallas_call x2, Pallas kernels, stator_of(): pl.pallas_call(stator_kernel, grid_spec=pltpu.PrefetchScalarGridSpec(num_...  9.82 us
    all_to_all x2, starting transfers between devices, instance_mix(): return (partials, lax.all_to_all(partials, 'ix', 0, 0))  8.03 us
    pallas_call x2, Pallas kernels, partial_sums(): pl.pallas_call(mix_kernel, grid_spec=pltpu.PrefetchScalarGridSpec(num_sca...  4.51 us
    pallas_call x2, Pallas kernels, updated(): pl.pallas_call(update_kernel, grid=(rows // block,), in_specs=[pl.BlockSp...  4.35 us
    unnamed x33, local copies, waits for them, and re-layouts  4.2 us
    add x2, other arithmetic, shards(): base = lam + relax_wide * (rhs - (stator + rotor_full)) * live  3.54 us
  transfers between devices with their start and end apart: 12, of which 3 were waited for; matrix products, arithmetic and copies ran while one was open for 8% of the time, Pallas kernels for 10%

profile of v9, /device:TPU:1, one launch (start us, length us, event | category | flops | bytes accessed | tf_op | source)
XLA Modules:
  0.0 96.0 jit_solution(4768240235110032982)
XLA Ops:
  0.7 0.8 broadcast_multiply_fusion
  1.5 1.1 %multiply_convert_fusion = (bf16[1,16,32,128]{3,2,1,0:T(8,128)(2,1)S(1)}, f32[1,16,32,128]{3,2,1,0:T(8,128)S(1)}) fusion(f32[1,16,32,128]{3,2,1,0:T(8,128)} %param.11, f32[16]{0:T(128)S(1)} %or_convert_fusion, f32[16,128]{1,0:T(8,128)} %param.14), kind=kLoop, calls=%fused_computation.10 | loop fusion | flops 196608 | bytes 663616 | tf_op jit(solution)/shard_map/convert_element_type | solution.py:171
  2.5 0.8 broadcast_in_dim.29
  3.3 1.4 %broadcast_in_dim.31 = f32[16,32,128]{2,1,0:T(8,128)} broadcast(f32[16,128]{1,0:T(8,128)} %param.14), dimensions={0,2} | broadcast | bytes 270336 | tf_op jit(solution)/shard_map/broadcast_in_dim | solution.py:167
  4.7 4.0 %collective-permute-start.1 = (f32[512,128]{1,0:T(8,128)S(1)}, f32[512,128]{1,0:T(8,128)S(1)}, u32[]{:S(2)}, u32[]{:S(2)}) collective-permute-start(f32[512,128]{1,0:T(8,128)S(1)} %bitcast.66), channel_id=1, source_target_pairs={{0,256},{32,288},{64,320},{96,352},{128,384},{160,416},{192,448},{... | collective-permute-start | bytes 786440 | tf_op jit(solution)/shard_map/ppermute | solution.py:49
  8.8 6.7 %collective-permute-start = (f32[512,128]{1,0:T(8,128)S(1)}, f32[512,128]{1,0:T(8,128)S(1)}, u32[]{:S(2)}, u32[]{:S(2)}) collective-permute-start(f32[512,128]{1,0:T(8,128)S(1)} %bitcast.67), channel_id=1, source_target_pairs={{0,32},{32,0},{64,96},{96,64},{128,160},{160,128},{192,224},{224,1... | collective-permute-start | bytes 786440 | tf_op jit(solution)/shard_map/ppermute | solution.py:49
  16.3 5.5 %collective-permute-start.2 = (f32[512,128]{1,0:T(8,128)S(1)}, f32[512,128]{1,0:T(8,128)S(1)}, u32[]{:S(2)}, u32[]{:S(2)}) collective-permute-start(f32[512,128]{1,0:T(8,128)S(1)} %collective-permute-done.1.across_ref), channel_id=1, source_target_pairs={{0,32},{32,0},{64,96},{96,64},{128,160},{160,128},{192,224},{224,1... | collective-permute-start | bytes 786440 | tf_op jit(solution)/shard_map/ppermute | solution.py:49
  21.9 1.0 %collective-permute-done.2.diagonal_ref = f32[512,128]{1,0:T(8,128)S(1)} collective-permute-done((f32[512,128]{1,0:T(8,128)S(1)}, f32[512,128]{1,0:T(8,128)S(1)}, u32[]{:S(2)}, u32[]{:S(2)}) %collective-permute-start.2) | collective-permute-done | bytes 262176 | tf_op jit(solution)/shard_map/ppermute | solution.py:49
  22.9 0.7 copy-done.12
  23.6 2.3 %shard_map.109 = f32[4,512,128]{2,1,0:T(8,128)} custom-call(s32[1]{0:T(128)} %bitcast.index_ref, f32[16,16]{1,0:T(8,128)} %constant.28.clone.coef_ref, f32[512,128]{1,0:T(8,128)} %bitcast.68, f32[512,128]{1,0:T(8,128)} %copy-done.8, f32[512,128]{1,0:T(8,128)} %copy-done.7, f32[512,128]{1,0:T(8,128)} %copy-done.12), custom_call_target="tpu_custom_call" | custom-call | tf_op jit(solution)/shard_map/pallas_call | solution.py:83
  25.9 3.7 %all-to-all-start = ((f32[4,512,128]{2,1,0:T(8,128)}), f32[4,512,128]{2,1,0:T(8,128)S(1)}, u32[]{:S(2)}, u32[]{:S(2)}) async-start(f32[4,512,128]{2,1,0:T(8,128)} %shard_map.109), calls=%async_computation | async-start | bytes 2097152 | tf_op jit(solution)/shard_map/all_to_all | solution.py:151
  29.6 1.9 %collective-permute-start.3 = (bf16[1,5,32,128]{3,2,1,0:T(8,128)(2,1)S(1)}, bf16[1,5,32,128]{3,2,1,0:T(8,128)(2,1)S(1)}, u32[]{:S(2)}, u32[]{:S(2)}) collective-permute-start(bf16[1,5,32,128]{3,2,1,0:T(8,128)(2,1)S(1)} %pad_maximum_fusion), channel_id=1, source_target_pairs={{31,0},{0,1},{1,2},{2,3},{3,4},{4,5},{5,6},{6,7},{7,8},{8,9},{9,10... | collective-permute-start | bytes 122888 | tf_op jit(solution)/shard_map/ppermute | solution.py:32
  31.5 10.5 %collective-permute-start.4 = (bf16[1,1,32,128]{3,2,1,0:T(8,128)(2,1)S(1)}, bf16[1,1,32,128]{3,2,1,0:T(8,128)(2,1)S(1)}, u32[]{:S(2)}, u32[]{:S(2)}) collective-permute-start(bf16[1,1,32,128]{3,2,1,0:T(8,128)(2,1)S(1)} %slice.33), channel_id=1, source_target_pairs={{1,0},{2,1},{3,2},{4,3},{5,4},{6,5},{7,6},{8,7},{9,8},{10,9},{11,1... | collective-permute-start | bytes 24584 | tf_op jit(solution)/shard_map/ppermute | solution.py:32
  43.5 4.9 %shard_map.110 = f32[16,32,128]{2,1,0:T(8,128)} custom-call(s32[96]{0:T(128)} %reshape.99.cols_ref, bf16[18,32,128]{2,1,0:T(8,128)(2,1)} %maximum_bitcast_fusion.halo_ref, bf16[16,6,128,128]{3,2,1,0:T(8,128)(2,1)} %bitcast.60), custom_call_target="tpu_custom_call" | custom-call | tf_op jit(solution)/shard_map/pallas_call | solution.py:130
  48.6 1.8 %fusion.7 = f32[1,16,32,128]{3,2,1,0:T(8,128)} fusion(f32[1,16,32,128]{3,2,1,0:T(8,128)S(1)} %copy-done.6, f32[16,32,128]{2,1,0:T(8,128)} %shard_map.110, f32[1,4,32,128]{3,2,1,0:T(8,128)S(1)} %bitcast_add_fusion.3, f32[1,16,32,128]{3,2,1,0:T(8,128)S(1)} %copy-done.4, f32[16,128]{1,0:T(8,128)S(1)} %bitcast.73, f32[16]{0:T(128)S(1)} %or_convert_fusion), kind=kLoop, calls=%fused_computation.9 | loop fusion | flops 393216 | bytes 1122368 | tf_op jit(solution)/shard_map/add | solution.py:191
  50.3 1.0 %copy-done.2 = f32[4,512,128]{2,1,0:T(8,128)} copy-done((f32[4,512,128]{2,1,0:T(8,128)}, f32[4,512,128]{2,1,0:T(8,128)S(1)}, u32[]{:S(2)}) %copy-start.2) | copy-done | bytes 1048600
  51.3 2.2 %shard_map.111 = (f32[512,128]{1,0:T(8,128)}, f32[512,128]{1,0:T(8,128)}) custom-call(f32[4,512,128]{2,1,0:T(8,128)} %copy-done.2, f32[512,128]{1,0:T(8,128)} %bitcast.70, f32[512,128]{1,0:T(8,128)} %bitcast.62, f32[512,128]{1,0:T(8,128)} %bitcast.64), custom_call_target="tpu_custom_call" | custom-call | tf_op jit(solution)/shard_map/pallas_call | solution.py:106
  53.5 2.3 %collective-permute-start.6 = (f32[512,128]{1,0:T(8,128)}, f32[512,128]{1,0:T(8,128)S(1)}, u32[]{:S(2)}, u32[]{:S(2)}) collective-permute-start(f32[512,128]{1,0:T(8,128)} %get-tuple-element.20.own_ref), channel_id=1, source_target_pairs={{0,256},{32,288},{64,320},{96,352},{128,384},{160,416},{192,448},{... | collective-permute-start | bytes 786440 | tf_op jit(solution)/shard_map/ppermute | solution.py:49
  55.8 3.7 %collective-permute-start.5 = (f32[512,128]{1,0:T(8,128)}, f32[512,128]{1,0:T(8,128)S(1)}, u32[]{:S(2)}, u32[]{:S(2)}) collective-permute-start(f32[512,128]{1,0:T(8,128)} %get-tuple-element.20.own_ref), channel_id=1, source_target_pairs={{0,32},{32,0},{64,96},{96,64},{128,160},{160,128},{192,224},{224,1... | collective-permute-start | bytes 786440 | tf_op jit(solution)/shard_map/ppermute | solution.py:49
  59.4 2.5 %collective-permute-done.6.across_ref = f32[512,128]{1,0:T(8,128)S(1)} collective-permute-done((f32[512,128]{1,0:T(8,128)}, f32[512,128]{1,0:T(8,128)S(1)}, u32[]{:S(2)}, u32[]{:S(2)}) %collective-permute-start.6) | collective-permute-done | bytes 262176 | tf_op jit(solution)/shard_map/ppermute | solution.py:49
  61.9 4.3 %collective-permute-start.7 = (f32[512,128]{1,0:T(8,128)S(1)}, f32[512,128]{1,0:T(8,128)S(1)}, u32[]{:S(2)}, u32[]{:S(2)}) collective-permute-start(f32[512,128]{1,0:T(8,128)S(1)} %collective-permute-done.6.across_ref), channel_id=1, source_target_pairs={{0,32},{32,0},{64,96},{96,64},{128,160},{160,128},{192,224},{224,1... | collective-permute-start | bytes 786440 | tf_op jit(solution)/shard_map/ppermute | solution.py:49
  66.2 1.0 %convert_element_type.47 = bf16[1,16,32,128]{3,2,1,0:T(8,128)(2,1)S(1)} convert(f32[1,16,32,128]{3,2,1,0:T(8,128)} %bitcast.71) | non-fusion elementwise | flops 65536 | bytes 393216 | tf_op jit(solution)/shard_map/convert_element_type | solution.py:171
  68.0 0.7 copy-done.11
  68.8 2.3 %shard_map.112 = f32[4,512,128]{2,1,0:T(8,128)} custom-call(s32[1]{0:T(128)} %bitcast.index_ref, f32[16,16]{1,0:T(8,128)} %constant.28.clone.coef_ref, f32[512,128]{1,0:T(8,128)} %get-tuple-element.20.own_ref, f32[512,128]{1,0:T(8,128)} %copy-done.10, f32[512,128]{1,0:T(8,128)} %copy-done.9, f32[512,128]{1,0:T(8,128)} %copy-done.11), custom_call_target="tpu_custom_call" | custom-call | tf_op jit(solution)/shard_map/pallas_call | solution.py:83
  71.0 4.4 %all-to-all-start.1 = ((f32[4,512,128]{2,1,0:T(8,128)}), f32[4,512,128]{2,1,0:T(8,128)S(1)}, u32[]{:S(2)}, u32[]{:S(2)}) async-start(f32[4,512,128]{2,1,0:T(8,128)} %shard_map.112), calls=%async_computation.1 | async-start | bytes 2097152 | tf_op jit(solution)/shard_map/all_to_all | solution.py:151
  75.5 1.9 %collective-permute-start.8 = (bf16[1,5,32,128]{3,2,1,0:T(8,128)(2,1)S(1)}, bf16[1,5,32,128]{3,2,1,0:T(8,128)(2,1)S(1)}, u32[]{:S(2)}, u32[]{:S(2)}) collective-permute-start(bf16[1,5,32,128]{3,2,1,0:T(8,128)(2,1)S(1)} %pad_maximum_fusion.1), channel_id=1, source_target_pairs={{31,0},{0,1},{1,2},{2,3},{3,4},{4,5},{5,6},{6,7},{7,8},{8,9},{9,10... | collective-permute-start | bytes 122888 | tf_op jit(solution)/shard_map/ppermute | solution.py:32
  77.4 7.2 %collective-permute-start.9 = (bf16[1,1,32,128]{3,2,1,0:T(8,128)(2,1)S(1)}, bf16[1,1,32,128]{3,2,1,0:T(8,128)(2,1)S(1)}, u32[]{:S(2)}, u32[]{:S(2)}) collective-permute-start(bf16[1,1,32,128]{3,2,1,0:T(8,128)(2,1)S(1)} %slice.38), channel_id=1, source_target_pairs={{1,0},{2,1},{3,2},{4,3},{5,4},{6,5},{7,6},{8,7},{9,8},{10,9},{11,1... | collective-permute-start | bytes 24584 | tf_op jit(solution)/shard_map/ppermute | solution.py:32
  84.6 0.8 collective-permute-done.9
  86.0 4.9 %shard_map.113 = f32[16,32,128]{2,1,0:T(8,128)} custom-call(s32[96]{0:T(128)} %reshape.99.cols_ref, bf16[18,32,128]{2,1,0:T(8,128)(2,1)} %maximum_bitcast_fusion.1.halo_ref, bf16[16,6,128,128]{3,2,1,0:T(8,128)(2,1)} %bitcast.61), custom_call_target="tpu_custom_call" | custom-call | tf_op jit(solution)/shard_map/pallas_call | solution.py:130
  91.0 1.8 %fusion.3 = f32[1,16,32,128]{3,2,1,0:T(8,128)} fusion(f32[1,16,32,128]{3,2,1,0:T(8,128)S(1)} %bitcast.72, f32[1,16,32,128]{3,2,1,0:T(8,128)S(1)} %copy-done.6, f32[16,32,128]{2,1,0:T(8,128)} %shard_map.113, f32[1,4,32,128]{3,2,1,0:T(8,128)S(1)} %bitcast_add_fusion.2, f32[16,128]{1,0:T(8,128)S(1)} %bitcast.74, f32[16]{0:T(128)S(1)} %or_convert_fusion), kind=kLoop, calls=%fused_computation.4 | loop fusion | flops 327680 | bytes 1122368 | tf_op jit(solution)/shard_map/add | solution.py:191
  92.8 1.0 %copy-done.1 = f32[4,512,128]{2,1,0:T(8,128)} copy-done((f32[4,512,128]{2,1,0:T(8,128)}, f32[4,512,128]{2,1,0:T(8,128)S(1)}, u32[]{:S(2)}) %copy-start.1) | copy-done | bytes 1048600
  93.8 2.2 %shard_map.114 = (f32[512,128]{1,0:T(8,128)}, f32[512,128]{1,0:T(8,128)}) custom-call(f32[4,512,128]{2,1,0:T(8,128)} %copy-done.1, f32[512,128]{1,0:T(8,128)} %bitcast.69, f32[512,128]{1,0:T(8,128)} %bitcast.63, f32[512,128]{1,0:T(8,128)} %bitcast.65), custom_call_target="tpu_custom_call" | custom-call | tf_op jit(solution)/shard_map/pallas_call | solution.py:106
  (58 shorter events, 4.2 us)
Async XLA Ops:
  0.0 16.1 %copy-start = (bf16[1,4,128,128]{3,2,1,0:T(8,128)(2,1)S(1)}, bf16[1,4,128,128]{3,2,1,0:T(8,128)(2,1)}, u32[]{:S(2)}) copy-start(bf16[1,4,128,128]{3,2,1,0:T(8,128)(2,1)} %param.16) | copy-start | bytes 393220
  0.0 42.0 %copy-start.15 = (s32[1,4]{1,0:T(1,128)S(1)}, s32[1,4]{1,0:T(1,128)}, u32[]{:S(2)}) copy-start(s32[1,4]{1,0:T(1,128)} %param.18) | copy-start | bytes 52
  0.0 42.1 %copy-start.14 = (s32[16,6]{0,1:T(8,128)S(1)}, s32[16,6]{0,1:T(8,128)}, u32[]{:S(2)}) copy-start(s32[16,6]{0,1:T(8,128)} %param.17) | copy-start | bytes 1156
  2.5 20.4 %copy-start.3 = (f32[1,16,32,128]{3,2,1,0:T(8,128)}, f32[1,16,32,128]{3,2,1,0:T(8,128)S(1)}, u32[]{:S(2)}) copy-start(f32[1,16,32,128]{3,2,1,0:T(8,128)S(1)} %get-tuple-element.26) | copy-start | bytes 786436
  4.7 11.5 %collective-permute-start.1 = (f32[512,128]{1,0:T(8,128)S(1)}, f32[512,128]{1,0:T(8,128)S(1)}, u32[]{:S(2)}, u32[]{:S(2)}) collective-permute-start(f32[512,128]{1,0:T(8,128)S(1)} %bitcast.66), channel_id=1, source_target_pairs={{0,256},{32,288},{64,320},{96,352},{128,384},{160,416},{192,448},{... | collective-permute-start | bytes 786440 | tf_op jit(solution)/shard_map/ppermute | solution.py:49
  8.8 13.1 %collective-permute-start = (f32[512,128]{1,0:T(8,128)S(1)}, f32[512,128]{1,0:T(8,128)S(1)}, u32[]{:S(2)}, u32[]{:S(2)}) collective-permute-start(f32[512,128]{1,0:T(8,128)S(1)} %bitcast.67), channel_id=1, source_target_pairs={{0,32},{32,0},{64,96},{96,64},{128,160},{160,128},{192,224},{224,1... | collective-permute-start | bytes 786440 | tf_op jit(solution)/shard_map/ppermute | solution.py:49
  16.3 6.7 %copy-start.7 = (f32[512,128]{1,0:T(8,128)}, f32[512,128]{1,0:T(8,128)S(1)}, u32[]{:S(2)}) copy-start(f32[512,128]{1,0:T(8,128)S(1)} %collective-permute-done.1.across_ref) | copy-start | bytes 786436
  16.3 6.7 %collective-permute-start.2 = (f32[512,128]{1,0:T(8,128)S(1)}, f32[512,128]{1,0:T(8,128)S(1)}, u32[]{:S(2)}, u32[]{:S(2)}) collective-permute-start(f32[512,128]{1,0:T(8,128)S(1)} %collective-permute-done.1.across_ref), channel_id=1, source_target_pairs={{0,32},{32,0},{64,96},{96,64},{128,160},{160,128},{192,224},{224,1... | collective-permute-start | bytes 786440 | tf_op jit(solution)/shard_map/ppermute | solution.py:49
  21.9 1.1 %copy-start.8 = (f32[512,128]{1,0:T(8,128)}, f32[512,128]{1,0:T(8,128)S(1)}, u32[]{:S(2)}) copy-start(f32[512,128]{1,0:T(8,128)S(1)} %collective-permute-done.mate_ref) | copy-start | bytes 786436
  22.9 0.7 copy-start.12
  25.9 22.7 %copy-start.4 = (f32[1,16,32,128]{3,2,1,0:T(8,128)S(1)}, f32[1,16,32,128]{3,2,1,0:T(8,128)}, u32[]{:S(2)}) copy-start(f32[1,16,32,128]{3,2,1,0:T(8,128)} %param.11) | copy-start | bytes 786436
  25.9 22.7 %copy-start.6 = (f32[1,16,32,128]{3,2,1,0:T(8,128)S(1)}, f32[1,16,32,128]{3,2,1,0:T(8,128)}, u32[]{:S(2)}) copy-start(f32[1,16,32,128]{3,2,1,0:T(8,128)} %param.12) | copy-start | bytes 786436
  25.9 22.7 %copy-start.13 = (f32[1,16,128]{2,1,0:T(8,128)S(1)}, f32[1,16,128]{2,1,0:T(8,128)}, u32[]{:S(2)}) copy-start(f32[1,16,128]{2,1,0:T(8,128)} %param.13) | copy-start | bytes 24580
  25.9 24.4 %all-to-all-start = ((f32[4,512,128]{2,1,0:T(8,128)}), f32[4,512,128]{2,1,0:T(8,128)S(1)}, u32[]{:S(2)}, u32[]{:S(2)}) async-start(f32[4,512,128]{2,1,0:T(8,128)} %shard_map.109), calls=%async_computation | async-start | bytes 2097152 | tf_op jit(solution)/shard_map/all_to_all | solution.py:151
  29.6 13.3 %collective-permute-start.3 = (bf16[1,5,32,128]{3,2,1,0:T(8,128)(2,1)S(1)}, bf16[1,5,32,128]{3,2,1,0:T(8,128)(2,1)S(1)}, u32[]{:S(2)}, u32[]{:S(2)}) collective-permute-start(bf16[1,5,32,128]{3,2,1,0:T(8,128)(2,1)S(1)} %pad_maximum_fusion), channel_id=1, source_target_pairs={{31,0},{0,1},{1,2},{2,3},{3,4},{4,5},{5,6},{6,7},{7,8},{8,9},{9,10... | collective-permute-start | bytes 122888 | tf_op jit(solution)/shard_map/ppermute | solution.py:32
  31.5 11.3 %collective-permute-start.4 = (bf16[1,1,32,128]{3,2,1,0:T(8,128)(2,1)S(1)}, bf16[1,1,32,128]{3,2,1,0:T(8,128)(2,1)S(1)}, u32[]{:S(2)}, u32[]{:S(2)}) collective-permute-start(bf16[1,1,32,128]{3,2,1,0:T(8,128)(2,1)S(1)} %slice.33), channel_id=1, source_target_pairs={{1,0},{2,1},{3,2},{4,3},{5,4},{6,5},{7,6},{8,7},{9,8},{10,9},{11,1... | collective-permute-start | bytes 24584 | tf_op jit(solution)/shard_map/ppermute | solution.py:32
  50.3 1.0 %copy-start.2 = (f32[4,512,128]{2,1,0:T(8,128)}, f32[4,512,128]{2,1,0:T(8,128)S(1)}, u32[]{:S(2)}) copy-start(f32[4,512,128]{2,1,0:T(8,128)S(1)} %all-to-all-done.got_ref) | copy-start | bytes 3145732
  53.5 8.4 %collective-permute-start.6 = (f32[512,128]{1,0:T(8,128)}, f32[512,128]{1,0:T(8,128)S(1)}, u32[]{:S(2)}, u32[]{:S(2)}) collective-permute-start(f32[512,128]{1,0:T(8,128)} %get-tuple-element.20.own_ref), channel_id=1, source_target_pairs={{0,256},{32,288},{64,320},{96,352},{128,384},{160,416},{192,448},{... | collective-permute-start | bytes 786440 | tf_op jit(solution)/shard_map/ppermute | solution.py:49
  55.8 11.5 %collective-permute-start.5 = (f32[512,128]{1,0:T(8,128)}, f32[512,128]{1,0:T(8,128)S(1)}, u32[]{:S(2)}, u32[]{:S(2)}) collective-permute-start(f32[512,128]{1,0:T(8,128)} %get-tuple-element.20.own_ref), channel_id=1, source_target_pairs={{0,32},{32,0},{64,96},{96,64},{128,160},{160,128},{192,224},{224,1... | collective-permute-start | bytes 786440 | tf_op jit(solution)/shard_map/ppermute | solution.py:49
  61.9 5.4 %copy-start.9 = (f32[512,128]{1,0:T(8,128)}, f32[512,128]{1,0:T(8,128)S(1)}, u32[]{:S(2)}) copy-start(f32[512,128]{1,0:T(8,128)S(1)} %collective-permute-done.6.across_ref) | copy-start | bytes 786436
  61.9 5.4 %collective-permute-start.7 = (f32[512,128]{1,0:T(8,128)S(1)}, f32[512,128]{1,0:T(8,128)S(1)}, u32[]{:S(2)}, u32[]{:S(2)}) collective-permute-start(f32[512,128]{1,0:T(8,128)S(1)} %collective-permute-done.6.across_ref), channel_id=1, source_target_pairs={{0,32},{32,0},{64,96},{96,64},{128,160},{160,128},{192,224},{224,1... | collective-permute-start | bytes 786440 | tf_op jit(solution)/shard_map/ppermute | solution.py:49
  67.3 0.7 copy-start.10
  68.0 0.7 copy-start.11
  71.0 20.0 %copy-start.5 = (f32[512,128]{1,0:T(8,128)S(1)}, f32[512,128]{1,0:T(8,128)}, u32[]{:S(2)}) copy-start(f32[512,128]{1,0:T(8,128)} %get-tuple-element.21) | copy-start | bytes 786436
  71.0 21.8 %all-to-all-start.1 = ((f32[4,512,128]{2,1,0:T(8,128)}), f32[4,512,128]{2,1,0:T(8,128)S(1)}, u32[]{:S(2)}, u32[]{:S(2)}) async-start(f32[4,512,128]{2,1,0:T(8,128)} %shard_map.112), calls=%async_computation.1 | async-start | bytes 2097152 | tf_op jit(solution)/shard_map/all_to_all | solution.py:151
  75.5 9.1 %collective-permute-start.8 = (bf16[1,5,32,128]{3,2,1,0:T(8,128)(2,1)S(1)}, bf16[1,5,32,128]{3,2,1,0:T(8,128)(2,1)S(1)}, u32[]{:S(2)}, u32[]{:S(2)}) collective-permute-start(bf16[1,5,32,128]{3,2,1,0:T(8,128)(2,1)S(1)} %pad_maximum_fusion.1), channel_id=1, source_target_pairs={{31,0},{0,1},{1,2},{2,3},{3,4},{4,5},{5,6},{6,7},{7,8},{8,9},{9,10... | collective-permute-start | bytes 122888 | tf_op jit(solution)/shard_map/ppermute | solution.py:32
  77.4 8.0 %collective-permute-start.9 = (bf16[1,1,32,128]{3,2,1,0:T(8,128)(2,1)S(1)}, bf16[1,1,32,128]{3,2,1,0:T(8,128)(2,1)S(1)}, u32[]{:S(2)}, u32[]{:S(2)}) collective-permute-start(bf16[1,1,32,128]{3,2,1,0:T(8,128)(2,1)S(1)} %slice.38), channel_id=1, source_target_pairs={{1,0},{2,1},{3,2},{4,3},{5,4},{6,5},{7,6},{8,7},{9,8},{10,9},{11,1... | collective-permute-start | bytes 24584 | tf_op jit(solution)/shard_map/ppermute | solution.py:32
  92.8 1.0 %copy-start.1 = (f32[4,512,128]{2,1,0:T(8,128)}, f32[4,512,128]{2,1,0:T(8,128)S(1)}, u32[]{:S(2)}) copy-start(f32[4,512,128]{2,1,0:T(8,128)S(1)} %all-to-all-done.1.got_ref) | copy-start | bytes 3145732

commit v10 on v8

--- a/solution.py
+++ b/solution.py
@@ -136,6 +136,9 @@
     scale = jnp.broadcast_to(relax_wide * live, shape).reshape(-1, lanes)
     condb = jnp.broadcast_to(cond_wide, shape).reshape(-1, lanes)
     weighted = (lam * cond_wide).reshape(-1, lanes)
+    span = rows + 2
+    edge_mask = jnp.stack([(cols == 0), (cols == span - 1)]).astype(jnp.float32)
+    edge_jac = jnp.einsum("hnk,nkio->hnio", edge_mask, jac[0].astype(jnp.float32), precision=lax.Precision.HIGHEST)
     for sweep in range(SWEEPS):
         lam_b = lam.astype(jnp.bfloat16)
         partials, got = instance_mix(weighted)
@@ -145,13 +148,19 @@
             rotor_jac,
             preferred_element_type=jnp.float32,
         )
+        blank = jnp.zeros_like(lam_b[:, :1])
+        interior = jnp.einsum(
+            "tnkri,tnkio->tnro",
+            jnp.concatenate([blank, lam_b, blank], axis=1)[:, cols],
+            jac,
+            preferred_element_type=jnp.float32,
+        )
         onward = jnp.concatenate([lam_b[:, rows - 1 :], (records * moving).astype(jnp.bfloat16)], axis=1)
-        onward, lam_b, _ = lax.optimization_barrier((onward, lam_b, partials))
+        onward, lam_b, interior, _ = lax.optimization_barrier((onward, lam_b, interior, partials))
         onward = shifted(onward, "sector", 1)
         head = shifted(lam_b[:, :1], "sector", -1)
-        lam_h = jnp.concatenate([onward[:, :1], lam_b, head], axis=1)
-        picked = lam_h[:, cols]
-        stator = jnp.einsum("tnkri,tnkio->tnro", picked, jac, preferred_element_type=jnp.float32)
+        edges = jnp.concatenate([onward[:, :1], head], axis=1)[0].astype(jnp.float32)
+        stator = interior + jnp.einsum("hri,hnio->nro", edges, edge_jac, precision=lax.Precision.HIGHEST)[None]
         arrived = onward[:, 1:].astype(jnp.float32)
         rotor = records * (1.0 - moving) + arrived
         rotor_full = jnp.concatenate(

time: 94.4 us -> 110 us (1.17)
  matrix products: 7.2 us -> 15.8 us
  local copies, waits for them, and re-layouts: 6.86 us -> 13.7 us
  other arithmetic: 13.3 us -> 15.6 us
  waiting for transfers between devices: 4.48 us -> 2.38 us
    dot_general x2 -> x5, matrix products: 5.1 us -> 13.4 us  [the longest x2 4.9 us: shards(): jnp.einsum('hri,hnio->nro', edges, edge_jac, precision=lax.Precision.HIGH...]
    add x0 -> x2, other arithmetic: none -> 3.65 us  [shards(): base = lam + relax_wide * (rhs - (stator + rotor_full)) * live]
    ppermute x6, waiting for transfers between devices: 3.58 us -> 0.57 us  [routed(): return lax.ppermute(block, INST, [(s, dest(s)) for s in range(NT)])]
    another operation x0 -> x2, other arithmetic: none -> 2.51 us  [shards(): edge_mask = jnp.stack([cols == 0, cols == span - 1]).astype(jnp.float32)]
    slice x2, local copies, waits for them, and re-layouts: 0.01 us -> 1.4 us  [shards(): head = shifted(lam_b[:, :1], 'sector', -1)]
    another operation x0 -> x2, local copies, waits for them, and re-layouts: none -> 1.36 us  [the longest x1 1.35 us: shards(): edge_mask = jnp.stack([cols == 0, cols == span - 1]).astype(jnp.float32)]
    slice x2, local copies, waits for them, and re-layouts: 0.01 us -> 1.3 us  [shards(): lam_b[:, rows - 1:]]
    select_n x1, local copies, waits for them, and re-layouts: 0.08 us -> 1.35 us  [shards(): jnp.concatenate([blank, lam_b, blank], axis=1)[:, cols]]
  transfers between devices with their start and end apart: 12 -> 12, of which waited for: 3 -> 3; matrix products, arithmetic and copies ran while one was open for 24% -> 36% of each run, Pallas kernels for 0% -> 0%
where the time goes in v10:
time: 110 us; the launch traced here: 108 us
  starting transfers between devices  50.6 us (46%)
  matrix products  15.8 us (14%)
  other arithmetic  15.6 us (14%)
  local copies, waits for them, and re-layouts  13.7 us (12%)
  Pallas kernels  8.92 us (8%)
  waiting for transfers between devices  2.38 us (2%)
  between operations  1.13 us (1%)
    ppermute x6, starting transfers between devices, routed(): return lax.ppermute(block, INST, [(s, dest(s)) for s in range(NT)])  21.3 us
    ppermute x4, starting transfers between devices, shifted(): return lax.ppermute(block, axis, route)  20.8 us
    all_to_all x2, starting transfers between devices, instance_mix(): return (partials, lax.all_to_all(partials, 'ix', 0, 0))  8.5 us
    dot_general x2, matrix products, shards(): jnp.einsum('hri,hnio->nro', edges, edge_jac, precision=lax.Precision.HIGH...  4.9 us
    dot_general x2, matrix products, shards(): jnp.einsum('tnkri,tnkio->tnro', jnp.concatenate([blank, lam_b, blank], ax...  4.88 us
    pallas_call x2, Pallas kernels, partial_sums(): pl.pallas_call(mix_kernel, grid_spec=pltpu.PrefetchScalarGridSpec(num_sca...  4.59 us
    pallas_call x2, Pallas kernels, updated(): pl.pallas_call(update_kernel, grid=(rows // block,), in_specs=[pl.BlockSp...  4.33 us
    add x2, other arithmetic, shards(): base = lam + relax_wide * (rhs - (stator + rotor_full)) * live  3.65 us
  transfers between devices with their start and end apart: 12, of which 3 were waited for; matrix products, arithmetic and copies ran while one was open for 36% of the time, Pallas kernels for 0%

profile of v10, /device:TPU:1, one launch (start us, length us, event | category | flops | bytes accessed | tf_op | source)
XLA Modules:
  0.0 108.1 jit_solution(16276343322195552329)
XLA Ops:
  2.0 4.0 %collective-permute-start.1 = (f32[512,128]{1,0:T(8,128)S(1)}, f32[512,128]{1,0:T(8,128)}, u32[]{:S(2)}, u32[]{:S(2)}) collective-permute-start(f32[512,128]{1,0:T(8,128)S(1)} %bitcast.96), channel_id=1, source_target_pairs={{0,256},{32,288},{64,320},{96,352},{128,384},{160,416},{192,448},{... | collective-permute-start | bytes 786440 | tf_op jit(solution)/shard_map/ppermute | solution.py:49
  6.1 6.7 %collective-permute-start = (f32[512,128]{1,0:T(8,128)S(1)}, f32[512,128]{1,0:T(8,128)}, u32[]{:S(2)}, u32[]{:S(2)}) collective-permute-start(f32[512,128]{1,0:T(8,128)S(1)} %bitcast.97), channel_id=1, source_target_pairs={{0,32},{32,0},{64,96},{96,64},{128,160},{160,128},{192,224},{224,1... | collective-permute-start | bytes 786440 | tf_op jit(solution)/shard_map/ppermute | solution.py:49
  12.8 1.3 %compare_select_fusion = s32[16,6]{0,1:T(8,128)} fusion(s32[16,6]{0,1:T(8,128)} %param.17), kind=kLoop, calls=%fused_computation.43 | loop fusion | flops 288 | bytes 768 | tf_op jit(solution)/shard_map/select_n | solution.py:154
  14.1 1.3 %compare_bitcast_fusion.1 = (pred[1,16,6]{1,2,0:T(8,128)(4,1)}, pred[1,16,6]{1,2,0:T(8,128)(4,1)}) fusion(s32[16,6]{0,1:T(8,128)} %param.17), kind=kLoop, calls=%fused_computation.48 | loop fusion | flops 192 | bytes 576 | tf_op jit(solution)/shard_map/stack | solution.py:140
  15.3 1.7 %fusion.19 = f32[4,32,128]{2,1,0:T(8,128)} fusion(bf16[1,4,128,128]{3,2,1,0:T(8,128)(2,1)} %param.16, bf16[1,16,32,128]{3,2,1,0:T(8,128)(2,1)S(1)} %get-tuple-element.16), kind=kOutput, calls=%fused_computation.25 | convolution fusion | flops 4194304 | bytes 229376 | tf_op jit(solution)/shard_map/tjri,tjio->tjro/dot_general | solution.py:145
  17.6 1.3 %copy.24 = s32[16,6]{1,0:T(8,128)} copy(s32[16,6]{0,1:T(8,128)} %compare_select_fusion) | data formatting | bytes 768 | tf_op jit(solution)/shard_map/select_n | solution.py:154
  19.0 1.3 %reshape.121 = s32[96]{0:T(128)} reshape(s32[16,6]{1,0:T(8,128)} %copy.24) | data formatting | bytes 768 | tf_op jit(solution)/shard_map/broadcast_in_dim | solution.py:154
  22.8 1.4 %copy.30 = pred[2,16,6,1]{2,0,3,1:T(4,128)(4,1)} copy(pred[2,16,6,1]{1,2,0,3:T(8,128)(4,1)} %add_bitcast_fusion) | data formatting | bytes 384 | tf_op jit(solution)/shard_map/stack | solution.py:140
  24.2 1.7 %gather_fusion = bf16[96,32,128]{2,1,0:T(8,128)(2,1)} fusion(bf16[18,32,128]{2,1,0:T(8,128)(2,1)S(1)} %fusion.15, s32[1024]{0:T(1024)} %pad_clamp_fusion), kind=kCustom, calls=%fused_computation | custom fusion | bytes 1573248 | tf_op jit(solution)/shard_map/gather | solution.py:154
  25.9 2.5 %convolution_bitcast_fusion.1 = f32[1,16,32,128]{3,2,1,0:T(8,128)} fusion(bf16[16,6,32,128]{3,2,1,0:T(8,128)(2,1)} %bitcast.89, bf16[1,16,6,128,128]{4,3,2,1,0:T(8,128)(2,1)S(1)} %copy-done), kind=kOutput, calls=%fused_computation.12 | convolution fusion | flops 100663296 | bytes 4194304 | tf_op jit(solution)/shard_map/tnkri,tnkio->tnro/dot_general | solution.py:152
  28.4 3.6 %fusion.6 = f32[2,16,128,128]{3,0,2,1:T(2,128)} fusion(pred[2,16,6,1]{2,0,3,1:T(4,128)(4,1)S(1)} %copy-done.12, bf16[16,6,128,128]{3,2,1,0:T(8,128)(2,1)S(1)} %bitcast.87), kind=kOutput, calls=%fused_computation.8 | convolution fusion | flops 6291456 | bytes 5243072 | tf_op jit(solution)/shard_map/hnk,nkio->hnio/dot_general | solution.py:141
  32.7 1.9 %collective-permute-start.2 = (f32[512,128]{1,0:T(8,128)}, f32[512,128]{1,0:T(8,128)}, u32[]{:S(2)}, u32[]{:S(2)}) collective-permute-start(f32[512,128]{1,0:T(8,128)} %collective-permute-done.1.across_ref), channel_id=1, source_target_pairs={{0,32},{32,0},{64,96},{96,64},{128,160},{160,128},{192,224},{224,1... | collective-permute-start | bytes 786440 | tf_op jit(solution)/shard_map/ppermute | solution.py:49
  36.5 2.3 %shard_map.109 = f32[4,512,128]{2,1,0:T(8,128)} custom-call(s32[1]{0:T(128)} %bitcast.index_ref, f32[16,16]{1,0:T(8,128)} %constant.36.clone.coef_ref, f32[512,128]{1,0:T(8,128)} %bitcast.98, f32[512,128]{1,0:T(8,128)} %collective-permute-done.mate_ref, f32[512,128]{1,0:T(8,128)} %collective-permute-done.1.across_ref, ...), custom_call_target="tpu_custom_call" | custom-call | tf_op jit(solution)/shard_map/pallas_call | solution.py:83
  38.8 4.2 %all-to-all-start = ((f32[4,512,128]{2,1,0:T(8,128)}), f32[4,512,128]{2,1,0:T(8,128)}, u32[]{:S(2)}, u32[]{:S(2)}) async-start(f32[4,512,128]{2,1,0:T(8,128)} %shard_map.109), calls=%async_computation | async-start | bytes 2097152 | tf_op jit(solution)/shard_map/all_to_all | solution.py:121
  43.1 1.9 %collective-permute-start.3 = (bf16[1,5,32,128]{3,2,1,0:T(8,128)(2,1)}, bf16[1,5,32,128]{3,2,1,0:T(8,128)(2,1)S(1)}, u32[]{:S(2)}, u32[]{:S(2)}) collective-permute-start(bf16[1,5,32,128]{3,2,1,0:T(8,128)(2,1)} %pad_maximum_fusion.4), channel_id=1, source_target_pairs={{31,0},{0,1},{1,2},{2,3},{3,4},{4,5},{5,6},{6,7},{7,8},{8,9},{9,10... | collective-permute-start | bytes 122888 | tf_op jit(solution)/shard_map/ppermute | solution.py:32
  45.7 9.6 %collective-permute-start.4 = (bf16[1,1,32,128]{3,2,1,0:T(8,128)(2,1)S(1)}, bf16[1,1,32,128]{3,2,1,0:T(8,128)(2,1)S(1)}, u32[]{:S(2)}, u32[]{:S(2)}) collective-permute-start(bf16[1,1,32,128]{3,2,1,0:T(8,128)(2,1)S(1)} %slice.33), channel_id=1, source_target_pairs={{1,0},{2,1},{3,2},{4,3},{5,4},{6,5},{7,6},{8,7},{9,8},{10,9},{11,1... | collective-permute-start | bytes 24584 | tf_op jit(solution)/shard_map/ppermute | solution.py:32
  56.2 2.5 %fusion.9 = f32[1,16,32,128]{3,2,1,0:T(8,128)S(1)} fusion(f32[2,16,128,128]{3,0,2,1:T(2,128)} %fusion.6, bf16[1,1,32,128]{3,2,1,0:T(8,128)(2,1)S(1)} %collective-permute-done.4, bf16[1,1,32,128]{3,2,1,0:T(8,128)(2,1)S(1)} %slice.46), kind=kOutput, calls=%fused_computation.9 | convolution fusion | flops 201334784 | bytes 2375680 | tf_op jit(solution)/shard_map/hri,hnio->nro/dot_general | solution.py:163
  58.6 1.8 %multiply_add_fusion.1 = f32[1,16,32,128]{3,2,1,0:T(8,128)} fusion(f32[1,16,32,128]{3,2,1,0:T(8,128)S(1)} %copy-done.1, f32[1,4,32,128]{3,2,1,0:T(8,128)S(1)} %bitcast_add_fusion.1, f32[1,16,32,128]{3,2,1,0:T(8,128)} %convolution_bitcast_fusion.1, f32[1,16,32,128]{3,2,1,0:T(8,128)S(1)} %fusion.9, f32[1,16,32,128]{3,2,1,0:T(8,128)} %param.11, ...), kind=kLoop, calls=%fused_computation.14 | loop fusion | flops 458752 | bytes 1384512 | tf_op jit(solution)/shard_map/add | solution.py:170
  60.5 1.4 %broadcast_in_dim.12 = f32[16,32,128]{2,1,0:T(8,128)} broadcast(f32[16,128]{1,0:T(8,128)} %broadcast_multiply_fusion), dimensions={0,2} | broadcast | bytes 270336 | tf_op jit(solution)/shard_map/broadcast_in_dim | solution.py:136
  62.6 2.2 %shard_map.110 = (f32[512,128]{1,0:T(8,128)}, f32[512,128]{1,0:T(8,128)}) custom-call(f32[4,512,128]{2,1,0:T(8,128)} %all-to-all-done.got_ref, f32[512,128]{1,0:T(8,128)} %bitcast.95, f32[512,128]{1,0:T(8,128)} %bitcast.90, f32[512,128]{1,0:T(8,128)} %bitcast.92), custom_call_target="tpu_custom_call" | custom-call | tf_op jit(solution)/shard_map/pallas_call | solution.py:106
  67.2 1.9 %collective-permute-start.6 = (f32[512,128]{1,0:T(8,128)}, f32[512,128]{1,0:T(8,128)}, u32[]{:S(2)}, u32[]{:S(2)}) collective-permute-start(f32[512,128]{1,0:T(8,128)} %get-tuple-element.17.own_ref), channel_id=1, source_target_pairs={{0,256},{32,288},{64,320},{96,352},{128,384},{160,416},{192,448},{... | collective-permute-start | bytes 786440 | tf_op jit(solution)/shard_map/ppermute | solution.py:49
  69.1 3.1 %collective-permute-start.5 = (f32[512,128]{1,0:T(8,128)}, f32[512,128]{1,0:T(8,128)}, u32[]{:S(2)}, u32[]{:S(2)}) collective-permute-start(f32[512,128]{1,0:T(8,128)} %get-tuple-element.17.own_ref), channel_id=1, source_target_pairs={{0,32},{32,0},{64,96},{96,64},{128,160},{160,128},{192,224},{224,1... | collective-permute-start | bytes 786440 | tf_op jit(solution)/shard_map/ppermute | solution.py:49
  73.0 1.7 %gather_fusion.1 = bf16[96,32,128]{2,1,0:T(8,128)(2,1)} fusion(bf16[18,32,128]{2,1,0:T(8,128)(2,1)S(1)} %fusion.16, s32[1024]{0:T(1024)} %pad_clamp_fusion), kind=kCustom, calls=%fused_computation.1 | custom fusion | bytes 1573248 | tf_op jit(solution)/shard_map/gather | solution.py:154
  76.3 3.7 %collective-permute-start.7 = (f32[512,128]{1,0:T(8,128)}, f32[512,128]{1,0:T(8,128)}, u32[]{:S(2)}, u32[]{:S(2)}) collective-permute-start(f32[512,128]{1,0:T(8,128)} %collective-permute-done.6.across_ref), channel_id=1, source_target_pairs={{0,32},{32,0},{64,96},{96,64},{128,160},{160,128},{192,224},{224,1... | collective-permute-start | bytes 786440 | tf_op jit(solution)/shard_map/ppermute | solution.py:49
  80.0 2.4 %convolution_bitcast_fusion = f32[1,16,32,128]{3,2,1,0:T(8,128)} fusion(bf16[16,6,32,128]{3,2,1,0:T(8,128)(2,1)} %bitcast.88, bf16[1,16,6,128,128]{4,3,2,1,0:T(8,128)(2,1)S(1)} %copy-done), kind=kOutput, calls=%fused_computation.11 | convolution fusion | flops 100663296 | bytes 4194304 | tf_op jit(solution)/shard_map/tnkri,tnkio->tnro/dot_general | solution.py:152
  82.4 2.3 %shard_map.111 = f32[4,512,128]{2,1,0:T(8,128)} custom-call(s32[1]{0:T(128)} %bitcast.index_ref, f32[16,16]{1,0:T(8,128)} %constant.36.clone.coef_ref, f32[512,128]{1,0:T(8,128)} %get-tuple-element.17.own_ref, f32[512,128]{1,0:T(8,128)} %collective-permute-done.5.mate_ref, f32[512,128]{1,0:T(8,128)} %collective-permute-done.6.across_ref, ...), custom_call_target="tpu_custom_call" | custom-call | tf_op jit(solution)/shard_map/pallas_call | solution.py:83
  84.7 1.9 %collective-permute-start.8 = (bf16[1,5,32,128]{3,2,1,0:T(8,128)(2,1)S(1)}, bf16[1,5,32,128]{3,2,1,0:T(8,128)(2,1)}, u32[]{:S(2)}, u32[]{:S(2)}) collective-permute-start(bf16[1,5,32,128]{3,2,1,0:T(8,128)(2,1)S(1)} %pad_maximum_fusion.5), channel_id=1, source_target_pairs={{31,0},{0,1},{1,2},{2,3},{3,4},{4,5},{5,6},{6,7},{7,8},{8,9},{9,10... | collective-permute-start | bytes 122888 | tf_op jit(solution)/shard_map/ppermute | solution.py:32
  86.6 4.3 %all-to-all-start.1 = ((f32[4,512,128]{2,1,0:T(8,128)}), f32[4,512,128]{2,1,0:T(8,128)}, u32[]{:S(2)}, u32[]{:S(2)}) async-start(f32[4,512,128]{2,1,0:T(8,128)} %shard_map.111), calls=%async_computation.1 | async-start | bytes 2097152 | tf_op jit(solution)/shard_map/all_to_all | solution.py:121
  91.6 7.3 %collective-permute-start.9 = (bf16[1,1,32,128]{3,2,1,0:T(8,128)(2,1)S(1)}, bf16[1,1,32,128]{3,2,1,0:T(8,128)(2,1)S(1)}, u32[]{:S(2)}, u32[]{:S(2)}) collective-permute-start(bf16[1,1,32,128]{3,2,1,0:T(8,128)(2,1)S(1)} %slice.38), channel_id=1, source_target_pairs={{1,0},{2,1},{3,2},{4,3},{5,4},{6,5},{7,6},{8,7},{9,8},{10,9},{11,1... | collective-permute-start | bytes 24584 | tf_op jit(solution)/shard_map/ppermute | solution.py:32
  100.5 2.5 %fusion.12 = f32[1,16,32,128]{3,2,1,0:T(8,128)S(1)} fusion(f32[2,16,128,128]{3,0,2,1:T(2,128)} %fusion.6, bf16[1,1,32,128]{3,2,1,0:T(8,128)(2,1)S(1)} %collective-permute-done.9, bf16[1,1,32,128]{3,2,1,0:T(8,128)(2,1)S(1)} %slice.50), kind=kOutput, calls=%fused_computation.10 | convolution fusion | flops 201334784 | bytes 2375680 | tf_op jit(solution)/shard_map/hri,hnio->nro/dot_general | solution.py:163
  103.0 1.8 %multiply_add_fusion = f32[1,16,32,128]{3,2,1,0:T(8,128)} fusion(f32[1,16,32,128]{3,2,1,0:T(8,128)} %bitcast.100, f32[1,16,32,128]{3,2,1,0:T(8,128)S(1)} %copy-done.1, f32[1,4,32,128]{3,2,1,0:T(8,128)S(1)} %bitcast_add_fusion, f32[1,16,32,128]{3,2,1,0:T(8,128)} %convolution_bitcast_fusion, f32[1,16,32,128]{3,2,1,0:T(8,128)S(1)} %fusion.12, ...), kind=kLoop, calls=%fused_computation.13 | loop fusion | flops 393216 | bytes 1384512 | tf_op jit(solution)/shard_map/add | solution.py:170
  105.9 2.2 %shard_map.112 = (f32[512,128]{1,0:T(8,128)}, f32[512,128]{1,0:T(8,128)}) custom-call(f32[4,512,128]{2,1,0:T(8,128)} %all-to-all-done.1.got_ref, f32[512,128]{1,0:T(8,128)} %bitcast.94, f32[512,128]{1,0:T(8,128)} %bitcast.91, f32[512,128]{1,0:T(8,128)} %bitcast.93), custom_call_target="tpu_custom_call" | custom-call | tf_op jit(solution)/shard_map/pallas_call | solution.py:106
  (75 shorter events, 17.3 us)
Async XLA Ops:
  0.0 25.9 %copy-start = (bf16[1,16,6,128,128]{4,3,2,1,0:T(8,128)(2,1)S(1)}, bf16[1,16,6,128,128]{4,3,2,1,0:T(8,128)(2,1)}, u32[]{:S(2)}) copy-start(bf16[1,16,6,128,128]{4,3,2,1,0:T(8,128)(2,1)} %param.15) | copy-start | bytes 9437188
  0.8 14.5 %copy-start.13 = (f32[16]{0:T(128)}, f32[16]{0:T(128)S(1)}, u32[]{:S(2)}) copy-start(f32[16]{0:T(128)S(1)} %or_convert_fusion) | copy-start | bytes 196
  2.0 15.0 %copy-start.4 = (bf16[1,16,32,128]{3,2,1,0:T(8,128)(2,1)}, bf16[1,16,32,128]{3,2,1,0:T(8,128)(2,1)S(1)}, u32[]{:S(2)}) copy-start(bf16[1,16,32,128]{3,2,1,0:T(8,128)(2,1)S(1)} %get-tuple-element.16) | copy-start | bytes 393220
  2.0 26.3 %copy-start.2 = (f32[1,16,32,128]{3,2,1,0:T(8,128)}, f32[1,16,32,128]{3,2,1,0:T(8,128)S(1)}, u32[]{:S(2)}) copy-start(f32[1,16,32,128]{3,2,1,0:T(8,128)S(1)} %get-tuple-element.24) | copy-start | bytes 786436
  2.0 30.7 %collective-permute-start.1 = (f32[512,128]{1,0:T(8,128)S(1)}, f32[512,128]{1,0:T(8,128)}, u32[]{:S(2)}, u32[]{:S(2)}) collective-permute-start(f32[512,128]{1,0:T(8,128)S(1)} %bitcast.96), channel_id=1, source_target_pairs={{0,256},{32,288},{64,320},{96,352},{128,384},{160,416},{192,448},{... | collective-permute-start | bytes 786440 | tf_op jit(solution)/shard_map/ppermute | solution.py:49
  6.1 29.9 %collective-permute-start = (f32[512,128]{1,0:T(8,128)S(1)}, f32[512,128]{1,0:T(8,128)}, u32[]{:S(2)}, u32[]{:S(2)}) collective-permute-start(f32[512,128]{1,0:T(8,128)S(1)} %bitcast.97), channel_id=1, source_target_pairs={{0,32},{32,0},{64,96},{96,64},{128,160},{160,128},{192,224},{224,1... | collective-permute-start | bytes 786440 | tf_op jit(solution)/shard_map/ppermute | solution.py:49
  17.0 0.6 copy-start.10
  25.9 2.5 %copy-start.12 = (pred[2,16,6,1]{2,0,3,1:T(4,128)(4,1)S(1)}, pred[2,16,6,1]{2,0,3,1:T(4,128)(4,1)}, u32[]{:S(2)}) copy-start(pred[2,16,6,1]{2,0,3,1:T(4,128)(4,1)} %copy.30) | copy-start | bytes 580
  28.3 3.6 %copy-start.18 = (s32[1,4]{1,0:T(1,128)S(1)}, s32[1,4]{1,0:T(1,128)}, u32[]{:S(2)}) copy-start(s32[1,4]{1,0:T(1,128)} %param.18) | copy-start | bytes 52
  28.3 4.3 %copy-start.5 = (f32[4,32,128]{2,1,0:T(8,128)S(1)}, f32[4,32,128]{2,1,0:T(8,128)}, u32[]{:S(2)}) copy-start(f32[4,32,128]{2,1,0:T(8,128)} %fusion.19) | copy-start | bytes 196612
  28.4 6.9 %copy-start.8 = (f32[1,16,128]{2,1,0:T(8,128)S(1)}, f32[1,16,128]{2,1,0:T(8,128)}, u32[]{:S(2)}) copy-start(f32[1,16,128]{2,1,0:T(8,128)} %param.13) | copy-start | bytes 24580
  28.4 6.9 %copy-start.14 = (f32[16]{0:T(128)S(1)}, f32[16]{0:T(128)}, u32[]{:S(2)}) copy-start(f32[16]{0:T(128)} %copy-done.13) | copy-start | bytes 196
  32.0 6.9 %copy-start.15 = (f32[4]{0:T(128)}, f32[4]{0:T(128)S(1)}, u32[]{:S(2)}) copy-start(f32[4]{0:T(128)S(1)} %convert_bitcast_fusion) | copy-start | bytes 52
  32.7 3.8 %collective-permute-start.2 = (f32[512,128]{1,0:T(8,128)}, f32[512,128]{1,0:T(8,128)}, u32[]{:S(2)}, u32[]{:S(2)}) collective-permute-start(f32[512,128]{1,0:T(8,128)} %collective-permute-done.1.across_ref), channel_id=1, source_target_pairs={{0,32},{32,0},{64,96},{96,64},{128,160},{160,128},{192,224},{224,1... | collective-permute-start | bytes 786440 | tf_op jit(solution)/shard_map/ppermute | solution.py:49
  36.5 22.1 %copy-start.1 = (f32[1,16,32,128]{3,2,1,0:T(8,128)S(1)}, f32[1,16,32,128]{3,2,1,0:T(8,128)}, u32[]{:S(2)}) copy-start(f32[1,16,32,128]{3,2,1,0:T(8,128)} %param.12) | copy-start | bytes 786436
  38.8 23.1 %copy-start.11 = (f32[16,128]{1,0:T(8,128)S(1)}, f32[16,128]{1,0:T(8,128)}, u32[]{:S(2)}) copy-start(f32[16,128]{1,0:T(8,128)} %param.14) | copy-start | bytes 24580
  38.8 21.6 %all-to-all-start = ((f32[4,512,128]{2,1,0:T(8,128)}), f32[4,512,128]{2,1,0:T(8,128)}, u32[]{:S(2)}, u32[]{:S(2)}) async-start(f32[4,512,128]{2,1,0:T(8,128)} %shard_map.109), calls=%async_computation | async-start | bytes 2097152 | tf_op jit(solution)/shard_map/all_to_all | solution.py:121
  43.1 12.3 %collective-permute-start.3 = (bf16[1,5,32,128]{3,2,1,0:T(8,128)(2,1)}, bf16[1,5,32,128]{3,2,1,0:T(8,128)(2,1)S(1)}, u32[]{:S(2)}, u32[]{:S(2)}) collective-permute-start(bf16[1,5,32,128]{3,2,1,0:T(8,128)(2,1)} %pad_maximum_fusion.4), channel_id=1, source_target_pairs={{31,0},{0,1},{1,2},{2,3},{3,4},{4,5},{5,6},{6,7},{7,8},{8,9},{9,10... | collective-permute-start | bytes 122888 | tf_op jit(solution)/shard_map/ppermute | solution.py:32
  45.0 10.4 %copy-start.16 = (f32[4]{0:T(128)}, f32[4]{0:T(128)S(1)}, u32[]{:S(2)}) copy-start(f32[4]{0:T(128)S(1)} %broadcast_subtract_fusion) | copy-start | bytes 52
  45.7 10.4 %collective-permute-start.4 = (bf16[1,1,32,128]{3,2,1,0:T(8,128)(2,1)S(1)}, bf16[1,1,32,128]{3,2,1,0:T(8,128)(2,1)S(1)}, u32[]{:S(2)}, u32[]{:S(2)}) collective-permute-start(bf16[1,1,32,128]{3,2,1,0:T(8,128)(2,1)S(1)} %slice.33), channel_id=1, source_target_pairs={{1,0},{2,1},{3,2},{4,3},{5,4},{6,5},{7,6},{8,7},{9,8},{10,9},{11,1... | collective-permute-start | bytes 24584 | tf_op jit(solution)/shard_map/ppermute | solution.py:32
  55.5 10.3 %copy-start.7 = (bf16[1,4,128,128]{3,2,1,0:T(8,128)(2,1)S(1)}, bf16[1,4,128,128]{3,2,1,0:T(8,128)(2,1)}, u32[]{:S(2)}) copy-start(bf16[1,4,128,128]{3,2,1,0:T(8,128)(2,1)} %param.16) | copy-start | bytes 393220
  65.8 6.4 %copy-start.3 = (bf16[1,16,32,128]{3,2,1,0:T(8,128)(2,1)}, bf16[1,16,32,128]{3,2,1,0:T(8,128)(2,1)S(1)}, u32[]{:S(2)}) copy-start(bf16[1,16,32,128]{3,2,1,0:T(8,128)(2,1)S(1)} %convert_element_type.50) | copy-start | bytes 393220
  67.2 9.1 %collective-permute-start.6 = (f32[512,128]{1,0:T(8,128)}, f32[512,128]{1,0:T(8,128)}, u32[]{:S(2)}, u32[]{:S(2)}) collective-permute-start(f32[512,128]{1,0:T(8,128)} %get-tuple-element.17.own_ref), channel_id=1, source_target_pairs={{0,256},{32,288},{64,320},{96,352},{128,384},{160,416},{192,448},{... | collective-permute-start | bytes 786440 | tf_op jit(solution)/shard_map/ppermute | solution.py:49
  69.1 13.3 %collective-permute-start.5 = (f32[512,128]{1,0:T(8,128)}, f32[512,128]{1,0:T(8,128)}, u32[]{:S(2)}, u32[]{:S(2)}) collective-permute-start(f32[512,128]{1,0:T(8,128)} %get-tuple-element.17.own_ref), channel_id=1, source_target_pairs={{0,32},{32,0},{64,96},{96,64},{128,160},{160,128},{192,224},{224,1... | collective-permute-start | bytes 786440 | tf_op jit(solution)/shard_map/ppermute | solution.py:49
  76.3 6.1 %collective-permute-start.7 = (f32[512,128]{1,0:T(8,128)}, f32[512,128]{1,0:T(8,128)}, u32[]{:S(2)}, u32[]{:S(2)}) collective-permute-start(f32[512,128]{1,0:T(8,128)} %collective-permute-done.6.across_ref), channel_id=1, source_target_pairs={{0,32},{32,0},{64,96},{96,64},{128,160},{160,128},{192,224},{224,1... | collective-permute-start | bytes 786440 | tf_op jit(solution)/shard_map/ppermute | solution.py:49
  82.4 16.5 %copy-start.6 = (f32[4,32,128]{2,1,0:T(8,128)S(1)}, f32[4,32,128]{2,1,0:T(8,128)}, u32[]{:S(2)}) copy-start(f32[4,32,128]{2,1,0:T(8,128)} %fusion.17) | copy-start | bytes 196612
  82.4 16.5 %copy-start.17 = (f32[4]{0:T(128)S(1)}, f32[4]{0:T(128)}, u32[]{:S(2)}) copy-start(f32[4]{0:T(128)} %copy-done.16) | copy-start | bytes 52
  82.4 20.5 %copy-start.9 = (f32[1,16,128]{2,1,0:T(8,128)S(1)}, f32[1,16,128]{2,1,0:T(8,128)}, u32[]{:S(2)}) copy-start(f32[1,16,128]{2,1,0:T(8,128)} %param.13) | copy-start | bytes 24580
  84.7 14.2 %collective-permute-start.8 = (bf16[1,5,32,128]{3,2,1,0:T(8,128)(2,1)S(1)}, bf16[1,5,32,128]{3,2,1,0:T(8,128)(2,1)}, u32[]{:S(2)}, u32[]{:S(2)}) collective-permute-start(bf16[1,5,32,128]{3,2,1,0:T(8,128)(2,1)S(1)} %pad_maximum_fusion.5), channel_id=1, source_target_pairs={{31,0},{0,1},{1,2},{2,3},{3,4},{4,5},{5,6},{6,7},{7,8},{8,9},{9,10... | collective-permute-start | bytes 122888 | tf_op jit(solution)/shard_map/ppermute | solution.py:32
  86.6 19.3 %all-to-all-start.1 = ((f32[4,512,128]{2,1,0:T(8,128)}), f32[4,512,128]{2,1,0:T(8,128)}, u32[]{:S(2)}, u32[]{:S(2)}) async-start(f32[4,512,128]{2,1,0:T(8,128)} %shard_map.111), calls=%async_computation.1 | async-start | bytes 2097152 | tf_op jit(solution)/shard_map/all_to_all | solution.py:121
  91.6 8.9 %collective-permute-start.9 = (bf16[1,1,32,128]{3,2,1,0:T(8,128)(2,1)S(1)}, bf16[1,1,32,128]{3,2,1,0:T(8,128)(2,1)S(1)}, u32[]{:S(2)}, u32[]{:S(2)}) collective-permute-start(bf16[1,1,32,128]{3,2,1,0:T(8,128)(2,1)S(1)} %slice.38), channel_id=1, source_target_pairs={{1,0},{2,1},{3,2},{4,3},{5,4},{6,5},{7,6},{8,7},{9,8},{10,9},{11,1... | collective-permute-start | bytes 24584 | tf_op jit(solution)/shard_map/ppermute | solution.py:32

commit v11 on v8

--- a/solution.py
+++ b/solution.py
@@ -92,24 +92,31 @@
     )(index, jnp.asarray(coefficient_table()), own, mate, across, diagonal)
 
 
-def update_kernel(got_ref, base_ref, scale_ref, cond_ref, lam_ref, weighted_ref):
+def update_kernel(got_ref, base_ref, scale_ref, cond_ref, lam_ref, *rest):
+    rows, lanes = base_ref.shape
+    groups = scale_ref.shape[0]
     spec = (got_ref[0] + got_ref[1]) + (got_ref[2] + got_ref[3])
-    lam = base_ref[...] - scale_ref[...] * spec
+    scale = jnp.broadcast_to(scale_ref[...][:, None, :], (groups, rows // groups, lanes)).reshape(rows, lanes)
+    lam = base_ref[...] - scale * spec
     lam_ref[...] = lam
-    weighted_ref[...] = lam * cond_ref[...]
+    for weighted_ref in rest:
+        cond = jnp.broadcast_to(cond_ref[...][:, None, :], (groups, rows // groups, lanes)).reshape(rows, lanes)
+        weighted_ref[...] = lam * cond
 
 
-def updated(got, base, scale, condb):
+def updated(got, base, scale, cond, outputs):
     rows, lanes = base.shape
     block = 256
+    groups = block * scale.shape[0] // rows
     flat = pl.BlockSpec((block, lanes), lambda r: (r, 0))
+    narrow = pl.BlockSpec((groups, lanes), lambda r: (r, 0))
     return pl.pallas_call(
         update_kernel,
         grid=(rows // block,),
-        in_specs=[pl.BlockSpec((4, block, lanes), lambda r: (0, r, 0)), flat, flat, flat],
-        out_specs=[flat, flat],
-        out_shape=[jax.ShapeDtypeStruct(base.shape, jnp.float32)] * 2,
-    )(got, base, scale, condb)
+        in_specs=[pl.BlockSpec((4, block, lanes), lambda r: (0, r, 0)), flat, narrow, narrow],
+        out_specs=[flat] * outputs,
+        out_shape=[jax.ShapeDtypeStruct(base.shape, jnp.float32)] * outputs,
+    )(got, base, scale, cond)
 
 
 def instance_mix(flat):
@@ -133,8 +140,7 @@
     moving = rotor_shift.astype(jnp.float32)[:, :, None, None]
     relax_wide = relax[:, :, None, :]
     cond_wide = cond[None, :, None, :]
-    scale = jnp.broadcast_to(relax_wide * live, shape).reshape(-1, lanes)
-    condb = jnp.broadcast_to(cond_wide, shape).reshape(-1, lanes)
+    scale = relax[0] * live[0, :, 0]
     weighted = (lam * cond_wide).reshape(-1, lanes)
     for sweep in range(SWEEPS):
         lam_b = lam.astype(jnp.bfloat16)
@@ -159,8 +165,9 @@
             axis=1,
         )
         base = lam + relax_wide * (rhs - (stator + rotor_full)) * live
-        lam_flat, weighted = updated(got, base.reshape(-1, lanes), scale, condb)
-        lam = lam_flat.reshape(shape)
+        fresh = updated(got, base.reshape(-1, lanes), scale, cond, 2 if sweep + 1 < SWEEPS else 1)
+        lam = fresh[0].reshape(shape)
+        weighted = fresh[-1]
     return lam
 
 

time: 94.4 us -> 92.6 us (0.981)
  local copies, waits for them, and re-layouts: 6.86 us -> 5.39 us
where the time goes in v11:
time: 92.6 us; the launch traced here: 91.2 us
  starting transfers between devices  51.1 us (55%)
  other arithmetic  13.2 us (14%)
  Pallas kernels  8.62 us (9%)
  matrix products  7.23 us (8%)
  local copies, waits for them, and re-layouts  5.39 us (6%)
  waiting for transfers between devices  4.49 us (5%)
  between operations  1.06 us (1%)
    ppermute x6, starting transfers between devices, routed(): return lax.ppermute(block, INST, [(s, dest(s)) for s in range(NT)])  21.8 us
    ppermute x4, starting transfers between devices, shifted(): return lax.ppermute(block, axis, route)  20.9 us
    all_to_all x2, starting transfers between devices, instance_mix(): return (partials, lax.all_to_all(partials, 'ix', 0, 0))  8.49 us
    dot_general x2, matrix products, shards(): jnp.einsum('tnkri,tnkio->tnro', picked, jac, preferred_element_type=jnp.f...  5.13 us
    pallas_call x2, Pallas kernels, partial_sums(): pl.pallas_call(mix_kernel, grid_spec=pltpu.PrefetchScalarGridSpec(num_sca...  4.59 us
    pallas_call x2, Pallas kernels, updated(): pl.pallas_call(update_kernel, grid=(rows // block,), in_specs=[pl.BlockSp...  4.03 us
    ppermute x6, waiting for transfers between devices, routed(): return lax.ppermute(block, INST, [(s, dest(s)) for s in range(NT)])  3.6 us
    gather x2, local copies, waits for them, and re-layouts, shards(): picked = lam_h[:, cols]  3.4 us
  transfers between devices with their start and end apart: 12, of which 3 were waited for; matrix products, arithmetic and copies ran while one was open for 24% of the time, Pallas kernels for 0%

profile of v11, /device:TPU:1, one launch (start us, length us, event | category | flops | bytes accessed | tf_op | source)
XLA Modules:
  0.0 91.2 jit_solution(1710414942385168851)
XLA Ops:
  0.8 1.9 %multiply_convert_fusion = (bf16[1,16,32,128]{3,2,1,0:T(8,128)(2,1)S(1)}, f32[1,16,32,128]{3,2,1,0:T(8,128)}) fusion(f32[1,16,32,128]{3,2,1,0:T(8,128)} %param.11, f32[16]{0:T(128)S(1)} %or_convert_fusion, f32[16,128]{1,0:T(8,128)} %cond_ref.3), kind=kLoop, calls=%fused_computation.10 | loop fusion | flops 196608 | bytes 663616 | tf_op jit(solution)/shard_map/convert_element_type | solution.py:146
  2.7 4.0 %collective-permute-start.1 = (f32[512,128]{1,0:T(8,128)}, f32[512,128]{1,0:T(8,128)}, u32[]{:S(2)}, u32[]{:S(2)}) collective-permute-start(f32[512,128]{1,0:T(8,128)} %bitcast.2.own_ref), channel_id=1, source_target_pairs={{0,256},{32,288},{64,320},{96,352},{128,384},{160,416},{192,448},{... | collective-permute-start | bytes 786440 | tf_op jit(solution)/shard_map/ppermute | solution.py:49
  6.8 6.7 %collective-permute-start = (f32[512,128]{1,0:T(8,128)}, f32[512,128]{1,0:T(8,128)}, u32[]{:S(2)}, u32[]{:S(2)}) collective-permute-start(f32[512,128]{1,0:T(8,128)} %bitcast.2.own_ref), channel_id=1, source_target_pairs={{0,32},{32,0},{64,96},{96,64},{128,160},{160,128},{192,224},{224,1... | collective-permute-start | bytes 786440 | tf_op jit(solution)/shard_map/ppermute | solution.py:49
  14.8 1.0 %fusion.12 = f32[4,32,128]{2,1,0:T(8,128)S(1)} fusion(bf16[1,4,128,128]{3,2,1,0:T(8,128)(2,1)} %param.16, bf16[1,16,32,128]{3,2,1,0:T(8,128)(2,1)S(1)} %get-tuple-element.12), kind=kOutput, calls=%fused_computation.16 | convolution fusion | flops 4194304 | bytes 229376 | tf_op jit(solution)/shard_map/tjri,tjio->tjro/dot_general | solution.py:148
  15.8 1.2 %broadcast_subtract_fusion = f32[4]{0:T(128)} fusion(s32[1,4]{1,0:T(1,128)} %param.18), kind=kLoop, calls=%fused_computation.33 | loop fusion | flops 8 | bytes 32 | tf_op jit(solution)/shard_map/sub | solution.py:162
  17.1 2.9 %collective-permute-start.2 = (f32[512,128]{1,0:T(8,128)}, f32[512,128]{1,0:T(8,128)}, u32[]{:S(2)}, u32[]{:S(2)}) collective-permute-start(f32[512,128]{1,0:T(8,128)} %collective-permute-done.1.across_ref), channel_id=1, source_target_pairs={{0,32},{32,0},{64,96},{96,64},{128,160},{160,128},{192,224},{224,1... | collective-permute-start | bytes 786440 | tf_op jit(solution)/shard_map/ppermute | solution.py:49
  20.9 1.4 %broadcast_multiply_fusion.scale_ref = f32[16,128]{1,0:T(8,128)} fusion(f32[16]{0:T(128)S(1)} %or_convert_fusion, f32[1,16,128]{2,1,0:T(8,128)} %param.13), kind=kLoop, calls=%fused_computation.30 | loop fusion | flops 2048 | bytes 16448 | tf_op jit(solution)/shard_map/mul | solution.py:143
  22.3 2.3 %shard_map.109 = f32[4,512,128]{2,1,0:T(8,128)} custom-call(s32[1]{0:T(128)} %bitcast.index_ref, f32[16,16]{1,0:T(8,128)} %constant.32.clone.coef_ref, f32[512,128]{1,0:T(8,128)} %bitcast.2.own_ref, f32[512,128]{1,0:T(8,128)} %collective-permute-done.mate_ref, f32[512,128]{1,0:T(8,128)} %collective-permute-done.1.across_ref, ...), custom_call_target="tpu_custom_call" | custom-call | tf_op jit(solution)/shard_map/pallas_call | solution.py:83
  24.6 4.2 %all-to-all-start = ((f32[4,512,128]{2,1,0:T(8,128)}), f32[4,512,128]{2,1,0:T(8,128)}, u32[]{:S(2)}, u32[]{:S(2)}) async-start(f32[4,512,128]{2,1,0:T(8,128)} %shard_map.109), calls=%async_computation | async-start | bytes 2097152 | tf_op jit(solution)/shard_map/all_to_all | solution.py:128
  28.8 1.9 %collective-permute-start.3 = (bf16[1,5,32,128]{3,2,1,0:T(8,128)(2,1)}, bf16[1,5,32,128]{3,2,1,0:T(8,128)(2,1)S(1)}, u32[]{:S(2)}, u32[]{:S(2)}) collective-permute-start(bf16[1,5,32,128]{3,2,1,0:T(8,128)(2,1)} %pad_maximum_fusion), channel_id=1, source_target_pairs={{31,0},{0,1},{1,2},{2,3},{3,4},{4,5},{5,6},{6,7},{7,8},{8,9},{9,10... | collective-permute-start | bytes 122888 | tf_op jit(solution)/shard_map/ppermute | solution.py:32
  30.8 10.1 %collective-permute-start.4 = (bf16[1,1,32,128]{3,2,1,0:T(8,128)(2,1)S(1)}, bf16[1,1,32,128]{3,2,1,0:T(8,128)(2,1)S(1)}, u32[]{:S(2)}, u32[]{:S(2)}) collective-permute-start(bf16[1,1,32,128]{3,2,1,0:T(8,128)(2,1)S(1)} %slice.33), channel_id=1, source_target_pairs={{1,0},{2,1},{3,2},{4,3},{5,4},{6,5},{7,6},{8,7},{9,8},{10,9},{11,1... | collective-permute-start | bytes 24584 | tf_op jit(solution)/shard_map/ppermute | solution.py:32
  42.0 0.9 %maximum_bitcast_fusion = bf16[18,32,128]{2,1,0:T(8,128)(2,1)S(1)} fusion(bf16[1,1,32,128]{3,2,1,0:T(8,128)(2,1)S(1)} %collective-permute-done.4, bf16[1,16,32,128]{3,2,1,0:T(8,128)(2,1)} %copy-done.3, bf16[1,1,32,128]{3,2,1,0:T(8,128)(2,1)S(1)} %slice.46), kind=kLoop, calls=%fused_computation.12 | loop fusion | flops 147456 | bytes 294912 | tf_op jit(solution)/shard_map/concatenate | solution.py:158
  43.0 1.7 %gather_fusion = bf16[96,32,128]{2,1,0:T(8,128)(2,1)} fusion(bf16[18,32,128]{2,1,0:T(8,128)(2,1)S(1)} %maximum_bitcast_fusion, s32[1024]{0:T(1024)} %pad_clamp_fusion), kind=kCustom, calls=%fused_computation | custom fusion | bytes 1573248 | tf_op jit(solution)/shard_map/gather | solution.py:159
  44.7 0.9 %bitcast_add_fusion.1 = f32[1,4,32,128]{3,2,1,0:T(8,128)S(1)} fusion(f32[4,32,128]{2,1,0:T(8,128)} %copy-done.4, bf16[1,5,32,128]{3,2,1,0:T(8,128)(2,1)} %copy-done.8, f32[4]{0:T(128)} %broadcast_subtract_fusion), kind=kLoop, calls=%fused_computation.19 | loop fusion | flops 49152 | bytes 163856 | tf_op jit(solution)/shard_map/add | solution.py:162
  45.6 2.6 %multiply_add_fusion.1 = f32[1,16,32,128]{3,2,1,0:T(8,128)} fusion(f32[1,16,32,128]{3,2,1,0:T(8,128)S(1)} %copy-done.1, f32[1,4,32,128]{3,2,1,0:T(8,128)S(1)} %bitcast_add_fusion.1, f32[1,16,32,128]{3,2,1,0:T(8,128)} %param.11, f32[16,128]{1,0:T(8,128)} %bitcast.68, f32[16]{0:T(128)} %copy-done.10, bf16[16,6,32,128]{3,2,1,0:T(8,128)(2,1)} %bitcast.63, ...), kind=kOutput, calls=%fused_computation.9 | convolution fusion | flops 101056512 | bytes 4792384 | tf_op jit(solution)/shard_map/tnkri,tnkio->tnro/dot_general | solution.py:160
  48.2 2.0 %shard_map.110 = (f32[512,128]{1,0:T(8,128)}, f32[512,128]{1,0:T(8,128)}) custom-call(f32[4,512,128]{2,1,0:T(8,128)} %all-to-all-done.got_ref, f32[512,128]{1,0:T(8,128)} %bitcast.67, f32[16,128]{1,0:T(8,128)} %broadcast_multiply_fusion.scale_ref, f32[16,128]{1,0:T(8,128)} %cond_ref.3), custom_call_target="tpu_custom_call" | custom-call | tf_op jit(solution)/shard_map/pallas_call | solution.py:113
  50.2 2.3 %collective-permute-start.6 = (f32[512,128]{1,0:T(8,128)}, f32[512,128]{1,0:T(8,128)S(1)}, u32[]{:S(2)}, u32[]{:S(2)}) collective-permute-start(f32[512,128]{1,0:T(8,128)} %get-tuple-element.13.own_ref), channel_id=1, source_target_pairs={{0,256},{32,288},{64,320},{96,352},{128,384},{160,416},{192,448},{... | collective-permute-start | bytes 786440 | tf_op jit(solution)/shard_map/ppermute | solution.py:49
  52.5 2.6 %collective-permute-start.5 = (f32[512,128]{1,0:T(8,128)}, f32[512,128]{1,0:T(8,128)S(1)}, u32[]{:S(2)}, u32[]{:S(2)}) collective-permute-start(f32[512,128]{1,0:T(8,128)} %get-tuple-element.13.own_ref), channel_id=1, source_target_pairs={{0,32},{32,0},{64,96},{96,64},{128,160},{160,128},{192,224},{224,1... | collective-permute-start | bytes 786440 | tf_op jit(solution)/shard_map/ppermute | solution.py:49
  55.2 1.0 %convert_element_type.52 = bf16[1,16,32,128]{3,2,1,0:T(8,128)(2,1)S(1)} convert(f32[1,16,32,128]{3,2,1,0:T(8,128)} %bitcast.65) | non-fusion elementwise | flops 65536 | bytes 393216 | tf_op jit(solution)/shard_map/convert_element_type | solution.py:146
  56.2 3.6 %collective-permute-done.6.across_ref = f32[512,128]{1,0:T(8,128)S(1)} collective-permute-done((f32[512,128]{1,0:T(8,128)}, f32[512,128]{1,0:T(8,128)S(1)}, u32[]{:S(2)}, u32[]{:S(2)}) %collective-permute-start.6) | collective-permute-done | bytes 262176 | tf_op jit(solution)/shard_map/ppermute | solution.py:49
  59.8 3.2 %collective-permute-start.7 = (f32[512,128]{1,0:T(8,128)S(1)}, f32[512,128]{1,0:T(8,128)}, u32[]{:S(2)}, u32[]{:S(2)}) collective-permute-start(f32[512,128]{1,0:T(8,128)S(1)} %collective-permute-done.6.across_ref), channel_id=1, source_target_pairs={{0,32},{32,0},{64,96},{96,64},{128,160},{160,128},{192,224},{224,1... | collective-permute-start | bytes 786440 | tf_op jit(solution)/shard_map/ppermute | solution.py:49
  63.0 1.1 %fusion.10 = f32[4,32,128]{2,1,0:T(8,128)S(1)} fusion(bf16[1,4,128,128]{3,2,1,0:T(8,128)(2,1)} %param.16, bf16[1,16,32,128]{3,2,1,0:T(8,128)(2,1)S(1)} %convert_element_type.52), kind=kOutput, calls=%fused_computation.14 | convolution fusion | flops 4194304 | bytes 229376 | tf_op jit(solution)/shard_map/tjri,tjio->tjro/dot_general | solution.py:148
  66.1 2.3 %shard_map.111 = f32[4,512,128]{2,1,0:T(8,128)} custom-call(s32[1]{0:T(128)} %bitcast.index_ref, f32[16,16]{1,0:T(8,128)} %constant.32.clone.coef_ref, f32[512,128]{1,0:T(8,128)} %get-tuple-element.13.own_ref, f32[512,128]{1,0:T(8,128)} %copy-done.7, f32[512,128]{1,0:T(8,128)} %copy-done.6, f32[512,128]{1,0:T(8,128)} %collective-permute-done.7.diagonal_ref), custom_call_target="tpu_custom_call" | custom-call | tf_op jit(solution)/shard_map/pallas_call | solution.py:83
  68.3 4.2 %all-to-all-start.1 = ((f32[4,512,128]{2,1,0:T(8,128)}), f32[4,512,128]{2,1,0:T(8,128)}, u32[]{:S(2)}, u32[]{:S(2)}) async-start(f32[4,512,128]{2,1,0:T(8,128)} %shard_map.111), calls=%async_computation.1 | async-start | bytes 2097152 | tf_op jit(solution)/shard_map/all_to_all | solution.py:128
  72.6 0.8 pad_maximum_fusion.1
  73.3 1.9 %collective-permute-start.8 = (bf16[1,5,32,128]{3,2,1,0:T(8,128)(2,1)S(1)}, bf16[1,5,32,128]{3,2,1,0:T(8,128)(2,1)S(1)}, u32[]{:S(2)}, u32[]{:S(2)}) collective-permute-start(bf16[1,5,32,128]{3,2,1,0:T(8,128)(2,1)S(1)} %pad_maximum_fusion.1), channel_id=1, source_target_pairs={{31,0},{0,1},{1,2},{2,3},{3,4},{4,5},{5,6},{6,7},{7,8},{8,9},{9,10... | collective-permute-start | bytes 122888 | tf_op jit(solution)/shard_map/ppermute | solution.py:32
  75.3 7.0 %collective-permute-start.9 = (bf16[1,1,32,128]{3,2,1,0:T(8,128)(2,1)S(1)}, bf16[1,1,32,128]{3,2,1,0:T(8,128)(2,1)S(1)}, u32[]{:S(2)}, u32[]{:S(2)}) collective-permute-start(bf16[1,1,32,128]{3,2,1,0:T(8,128)(2,1)S(1)} %slice.38), channel_id=1, source_target_pairs={{1,0},{2,1},{3,2},{4,3},{5,4},{6,5},{7,6},{8,7},{9,8},{10,9},{11,1... | collective-permute-start | bytes 24584 | tf_op jit(solution)/shard_map/ppermute | solution.py:32
  83.0 0.9 %maximum_bitcast_fusion.1 = bf16[18,32,128]{2,1,0:T(8,128)(2,1)S(1)} fusion(bf16[1,1,32,128]{3,2,1,0:T(8,128)(2,1)S(1)} %collective-permute-done.9, bf16[1,16,32,128]{3,2,1,0:T(8,128)(2,1)} %copy-done.2, bf16[1,1,32,128]{3,2,1,0:T(8,128)(2,1)S(1)} %slice.50), kind=kLoop, calls=%fused_computation.13 | loop fusion | flops 147456 | bytes 294912 | tf_op jit(solution)/shard_map/concatenate | solution.py:158
  84.0 1.7 %gather_fusion.1 = bf16[96,32,128]{2,1,0:T(8,128)(2,1)} fusion(bf16[18,32,128]{2,1,0:T(8,128)(2,1)S(1)} %maximum_bitcast_fusion.1, s32[1024]{0:T(1024)} %pad_clamp_fusion), kind=kCustom, calls=%fused_computation.1 | custom fusion | bytes 1573248 | tf_op jit(solution)/shard_map/gather | solution.py:159
  85.7 0.9 %bitcast_add_fusion = f32[1,4,32,128]{3,2,1,0:T(8,128)S(1)} fusion(f32[4,32,128]{2,1,0:T(8,128)} %copy-done.5, bf16[1,5,32,128]{3,2,1,0:T(8,128)(2,1)} %copy-done.9, f32[4]{0:T(128)} %broadcast_subtract_fusion), kind=kLoop, calls=%fused_computation.18 | loop fusion | flops 49152 | bytes 163856 | tf_op jit(solution)/shard_map/add | solution.py:162
  86.6 2.6 %multiply_add_fusion = f32[1,16,32,128]{3,2,1,0:T(8,128)} fusion(f32[1,16,32,128]{3,2,1,0:T(8,128)} %bitcast.66, f32[1,16,32,128]{3,2,1,0:T(8,128)S(1)} %copy-done.1, f32[1,4,32,128]{3,2,1,0:T(8,128)S(1)} %bitcast_add_fusion, f32[16,128]{1,0:T(8,128)} %bitcast.69, f32[16]{0:T(128)} %copy-done.10, bf16[16,6,32,128]{3,2,1,0:T(8,128)(2,1)} %bitcast.62, ...), kind=kOutput, calls=%fused_computation.8 | convolution fusion | flops 100990976 | bytes 4792384 | tf_op jit(solution)/shard_map/tnkri,tnkio->tnro/dot_general | solution.py:160
  89.2 2.0 %shard_map.112 = f32[512,128]{1,0:T(8,128)} custom-call(f32[4,512,128]{2,1,0:T(8,128)} %all-to-all-done.1.got_ref, f32[512,128]{1,0:T(8,128)} %bitcast.64, f32[16,128]{1,0:T(8,128)} %broadcast_multiply_fusion.scale_ref, f32[16,128]{1,0:T(8,128)} %cond_ref.3), custom_call_target="tpu_custom_call" | custom-call | tf_op jit(solution)/shard_map/pallas_call | solution.py:113
  (52 shorter events, 6.2 us)
Async XLA Ops:
  0.0 45.6 %copy-start = (bf16[1,16,6,128,128]{4,3,2,1,0:T(8,128)(2,1)S(1)}, bf16[1,16,6,128,128]{4,3,2,1,0:T(8,128)(2,1)}, u32[]{:S(2)}) copy-start(bf16[1,16,6,128,128]{4,3,2,1,0:T(8,128)(2,1)} %param.15) | copy-start | bytes 9437188
  0.8 40.6 %copy-start.10 = (f32[16]{0:T(128)}, f32[16]{0:T(128)S(1)}, u32[]{:S(2)}) copy-start(f32[16]{0:T(128)S(1)} %or_convert_fusion) | copy-start | bytes 196
  2.7 38.7 %copy-start.3 = (bf16[1,16,32,128]{3,2,1,0:T(8,128)(2,1)}, bf16[1,16,32,128]{3,2,1,0:T(8,128)(2,1)S(1)}, u32[]{:S(2)}) copy-start(bf16[1,16,32,128]{3,2,1,0:T(8,128)(2,1)S(1)} %get-tuple-element.12) | copy-start | bytes 393220
  2.7 14.4 %collective-permute-start.1 = (f32[512,128]{1,0:T(8,128)}, f32[512,128]{1,0:T(8,128)}, u32[]{:S(2)}, u32[]{:S(2)}) collective-permute-start(f32[512,128]{1,0:T(8,128)} %bitcast.2.own_ref), channel_id=1, source_target_pairs={{0,256},{32,288},{64,320},{96,352},{128,384},{160,416},{192,448},{... | collective-permute-start | bytes 786440 | tf_op jit(solution)/shard_map/ppermute | solution.py:49
  6.8 15.5 %collective-permute-start = (f32[512,128]{1,0:T(8,128)}, f32[512,128]{1,0:T(8,128)}, u32[]{:S(2)}, u32[]{:S(2)}) collective-permute-start(f32[512,128]{1,0:T(8,128)} %bitcast.2.own_ref), channel_id=1, source_target_pairs={{0,32},{32,0},{64,96},{96,64},{128,160},{160,128},{192,224},{224,1... | collective-permute-start | bytes 786440 | tf_op jit(solution)/shard_map/ppermute | solution.py:49
  14.1 6.6 %copy-start.11 = (f32[4]{0:T(128)}, f32[4]{0:T(128)S(1)}, u32[]{:S(2)}) copy-start(f32[4]{0:T(128)S(1)} %convert_bitcast_fusion) | copy-start | bytes 52
  15.8 1.2 %copy-start.4 = (f32[4,32,128]{2,1,0:T(8,128)}, f32[4,32,128]{2,1,0:T(8,128)S(1)}, u32[]{:S(2)}) copy-start(f32[4,32,128]{2,1,0:T(8,128)S(1)} %fusion.12) | copy-start | bytes 196612
  17.1 5.1 %collective-permute-start.2 = (f32[512,128]{1,0:T(8,128)}, f32[512,128]{1,0:T(8,128)}, u32[]{:S(2)}, u32[]{:S(2)}) collective-permute-start(f32[512,128]{1,0:T(8,128)} %collective-permute-done.1.across_ref), channel_id=1, source_target_pairs={{0,32},{32,0},{64,96},{96,64},{128,160},{160,128},{192,224},{224,1... | collective-permute-start | bytes 786440 | tf_op jit(solution)/shard_map/ppermute | solution.py:49
  22.3 23.4 %copy-start.1 = (f32[1,16,32,128]{3,2,1,0:T(8,128)S(1)}, f32[1,16,32,128]{3,2,1,0:T(8,128)}, u32[]{:S(2)}) copy-start(f32[1,16,32,128]{3,2,1,0:T(8,128)} %param.12) | copy-start | bytes 786436
  24.6 23.6 %all-to-all-start = ((f32[4,512,128]{2,1,0:T(8,128)}), f32[4,512,128]{2,1,0:T(8,128)}, u32[]{:S(2)}, u32[]{:S(2)}) async-start(f32[4,512,128]{2,1,0:T(8,128)} %shard_map.109), calls=%async_computation | async-start | bytes 2097152 | tf_op jit(solution)/shard_map/all_to_all | solution.py:128
  28.8 12.6 %collective-permute-start.3 = (bf16[1,5,32,128]{3,2,1,0:T(8,128)(2,1)}, bf16[1,5,32,128]{3,2,1,0:T(8,128)(2,1)S(1)}, u32[]{:S(2)}, u32[]{:S(2)}) collective-permute-start(bf16[1,5,32,128]{3,2,1,0:T(8,128)(2,1)} %pad_maximum_fusion), channel_id=1, source_target_pairs={{31,0},{0,1},{1,2},{2,3},{3,4},{4,5},{5,6},{6,7},{7,8},{8,9},{9,10... | collective-permute-start | bytes 122888 | tf_op jit(solution)/shard_map/ppermute | solution.py:32
  30.8 10.8 %collective-permute-start.4 = (bf16[1,1,32,128]{3,2,1,0:T(8,128)(2,1)S(1)}, bf16[1,1,32,128]{3,2,1,0:T(8,128)(2,1)S(1)}, u32[]{:S(2)}, u32[]{:S(2)}) collective-permute-start(bf16[1,1,32,128]{3,2,1,0:T(8,128)(2,1)S(1)} %slice.33), channel_id=1, source_target_pairs={{1,0},{2,1},{3,2},{4,3},{5,4},{6,5},{7,6},{8,7},{9,8},{10,9},{11,1... | collective-permute-start | bytes 24584 | tf_op jit(solution)/shard_map/ppermute | solution.py:32
  41.4 0.6 copy-start.8
  45.6 19.0 %copy-start.12 = (f32[4]{0:T(128)S(1)}, f32[4]{0:T(128)}, u32[]{:S(2)}) copy-start(f32[4]{0:T(128)} %copy-done.11) | copy-start | bytes 52
  50.2 9.5 %collective-permute-start.6 = (f32[512,128]{1,0:T(8,128)}, f32[512,128]{1,0:T(8,128)S(1)}, u32[]{:S(2)}, u32[]{:S(2)}) collective-permute-start(f32[512,128]{1,0:T(8,128)} %get-tuple-element.13.own_ref), channel_id=1, source_target_pairs={{0,256},{32,288},{64,320},{96,352},{128,384},{160,416},{192,448},{... | collective-permute-start | bytes 786440 | tf_op jit(solution)/shard_map/ppermute | solution.py:49
  52.5 12.8 %collective-permute-start.5 = (f32[512,128]{1,0:T(8,128)}, f32[512,128]{1,0:T(8,128)S(1)}, u32[]{:S(2)}, u32[]{:S(2)}) collective-permute-start(f32[512,128]{1,0:T(8,128)} %get-tuple-element.13.own_ref), channel_id=1, source_target_pairs={{0,32},{32,0},{64,96},{96,64},{128,160},{160,128},{192,224},{224,1... | collective-permute-start | bytes 786440 | tf_op jit(solution)/shard_map/ppermute | solution.py:49
  56.2 26.1 %copy-start.2 = (bf16[1,16,32,128]{3,2,1,0:T(8,128)(2,1)}, bf16[1,16,32,128]{3,2,1,0:T(8,128)(2,1)S(1)}, u32[]{:S(2)}) copy-start(bf16[1,16,32,128]{3,2,1,0:T(8,128)(2,1)S(1)} %convert_element_type.52) | copy-start | bytes 393220
  59.8 5.6 %copy-start.6 = (f32[512,128]{1,0:T(8,128)}, f32[512,128]{1,0:T(8,128)S(1)}, u32[]{:S(2)}) copy-start(f32[512,128]{1,0:T(8,128)S(1)} %collective-permute-done.6.across_ref) | copy-start | bytes 786436
  59.8 6.3 %collective-permute-start.7 = (f32[512,128]{1,0:T(8,128)S(1)}, f32[512,128]{1,0:T(8,128)}, u32[]{:S(2)}, u32[]{:S(2)}) collective-permute-start(f32[512,128]{1,0:T(8,128)S(1)} %collective-permute-done.6.across_ref), channel_id=1, source_target_pairs={{0,32},{32,0},{64,96},{96,64},{128,160},{160,128},{192,224},{224,1... | collective-permute-start | bytes 786440 | tf_op jit(solution)/shard_map/ppermute | solution.py:49
  64.0 0.6 copy-start.5
  65.3 0.7 copy-start.7
  68.3 20.8 %all-to-all-start.1 = ((f32[4,512,128]{2,1,0:T(8,128)}), f32[4,512,128]{2,1,0:T(8,128)}, u32[]{:S(2)}, u32[]{:S(2)}) async-start(f32[4,512,128]{2,1,0:T(8,128)} %shard_map.111), calls=%async_computation.1 | async-start | bytes 2097152 | tf_op jit(solution)/shard_map/all_to_all | solution.py:128
  73.3 8.9 %collective-permute-start.8 = (bf16[1,5,32,128]{3,2,1,0:T(8,128)(2,1)S(1)}, bf16[1,5,32,128]{3,2,1,0:T(8,128)(2,1)S(1)}, u32[]{:S(2)}, u32[]{:S(2)}) collective-permute-start(bf16[1,5,32,128]{3,2,1,0:T(8,128)(2,1)S(1)} %pad_maximum_fusion.1), channel_id=1, source_target_pairs={{31,0},{0,1},{1,2},{2,3},{3,4},{4,5},{5,6},{6,7},{7,8},{8,9},{9,10... | collective-permute-start | bytes 122888 | tf_op jit(solution)/shard_map/ppermute | solution.py:32
  75.3 7.8 %collective-permute-start.9 = (bf16[1,1,32,128]{3,2,1,0:T(8,128)(2,1)S(1)}, bf16[1,1,32,128]{3,2,1,0:T(8,128)(2,1)S(1)}, u32[]{:S(2)}, u32[]{:S(2)}) collective-permute-start(bf16[1,1,32,128]{3,2,1,0:T(8,128)(2,1)S(1)} %slice.38), channel_id=1, source_target_pairs={{1,0},{2,1},{3,2},{4,3},{5,4},{6,5},{7,6},{8,7},{9,8},{10,9},{11,1... | collective-permute-start | bytes 24584 | tf_op jit(solution)/shard_map/ppermute | solution.py:32
  82.3 0.8 copy-start.9

commit v12 on v11

--- a/solution.py
+++ b/solution.py
@@ -68,12 +68,20 @@
 
 def mix_kernel(index_ref, coef_ref, own_ref, mate_ref, across_ref, diagonal_ref, o_ref):
     me = index_ref[0]
-    values = (own_ref[...], mate_ref[...], across_ref[...], diagonal_ref[...])
-    for slot in range(4):
-        acc = coef_ref[me, slot * 4] * values[0]
-        for m in range(1, 4):
-            acc = acc + coef_ref[me, slot * 4 + m] * values[m]
-        o_ref[slot] = acc
+    coef = [[coef_ref[me, slot * 4 + m] for m in range(4)] for slot in range(4)]
+    chunk = 32
+
+    def step(c, carry):
+        rows = pl.ds(pl.multiple_of(c * chunk, chunk), chunk)
+        values = (own_ref[rows, :], mate_ref[rows, :], across_ref[rows, :], diagonal_ref[rows, :])
+        for slot in range(4):
+            acc = coef[slot][0] * values[0]
+            for m in range(1, 4):
+                acc = acc + coef[slot][m] * values[m]
+            o_ref[slot, rows, :] = acc
+        return carry
+
+    lax.fori_loop(0, own_ref.shape[0] // chunk, step, 0, unroll=True)
 
 
 def partial_sums(index, own, mate, across, diagonal):

time: 92.6 us -> 92.5 us (level)
  no operation moved by 1% of the time
where the time goes in v12:
time: 92.5 us; the launch traced here: 91.1 us
  starting transfers between devices  51.1 us (55%)
  other arithmetic  13.2 us (14%)
  Pallas kernels  8.6 us (9%)
  matrix products  7.23 us (8%)
  local copies, waits for them, and re-layouts  5.39 us (6%)
  waiting for transfers between devices  4.49 us (5%)
  between operations  1.06 us (1%)
    ppermute x6, starting transfers between devices, routed(): return lax.ppermute(block, INST, [(s, dest(s)) for s in range(NT)])  21.8 us
    ppermute x4, starting transfers between devices, shifted(): return lax.ppermute(block, axis, route)  20.9 us
    all_to_all x2, starting transfers between devices, instance_mix(): return (partials, lax.all_to_all(partials, 'ix', 0, 0))  8.49 us
    dot_general x2, matrix products, shards(): jnp.einsum('tnkri,tnkio->tnro', picked, jac, preferred_element_type=jnp.f...  5.13 us
    pallas_call x2, Pallas kernels, partial_sums(): pl.pallas_call(mix_kernel, grid_spec=pltpu.PrefetchScalarGridSpec(num_sca...  4.56 us
    pallas_call x2, Pallas kernels, updated(): pl.pallas_call(update_kernel, grid=(rows // block,), in_specs=[pl.BlockSp...  4.03 us
    ppermute x6, waiting for transfers between devices, routed(): return lax.ppermute(block, INST, [(s, dest(s)) for s in range(NT)])  3.6 us
    gather x2, local copies, waits for them, and re-layouts, shards(): picked = lam_h[:, cols]  3.4 us
  transfers between devices with their start and end apart: 12, of which 3 were waited for; matrix products, arithmetic and copies ran while one was open for 24% of the time, Pallas kernels for 0%

profile of v12, /device:TPU:1, one launch (start us, length us, event | category | flops | bytes accessed | tf_op | source)
XLA Modules:
  0.0 91.1 jit_solution(12353278170308981354)
XLA Ops:
  0.8 1.9 %multiply_convert_fusion = (bf16[1,16,32,128]{3,2,1,0:T(8,128)(2,1)S(1)}, f32[1,16,32,128]{3,2,1,0:T(8,128)}) fusion(f32[1,16,32,128]{3,2,1,0:T(8,128)} %param.11, f32[16]{0:T(128)S(1)} %or_convert_fusion, f32[16,128]{1,0:T(8,128)} %cond_ref.3), kind=kLoop, calls=%fused_computation.10 | loop fusion | flops 196608 | bytes 663616 | tf_op jit(solution)/shard_map/convert_element_type | solution.py:154
  2.7 4.0 %collective-permute-start.1 = (f32[512,128]{1,0:T(8,128)}, f32[512,128]{1,0:T(8,128)}, u32[]{:S(2)}, u32[]{:S(2)}) collective-permute-start(f32[512,128]{1,0:T(8,128)} %bitcast.2.own_ref), channel_id=1, source_target_pairs={{0,256},{32,288},{64,320},{96,352},{128,384},{160,416},{192,448},{... | collective-permute-start | bytes 786440 | tf_op jit(solution)/shard_map/ppermute | solution.py:49
  6.8 6.7 %collective-permute-start = (f32[512,128]{1,0:T(8,128)}, f32[512,128]{1,0:T(8,128)}, u32[]{:S(2)}, u32[]{:S(2)}) collective-permute-start(f32[512,128]{1,0:T(8,128)} %bitcast.2.own_ref), channel_id=1, source_target_pairs={{0,32},{32,0},{64,96},{96,64},{128,160},{160,128},{192,224},{224,1... | collective-permute-start | bytes 786440 | tf_op jit(solution)/shard_map/ppermute | solution.py:49
  14.8 1.0 %fusion.12 = f32[4,32,128]{2,1,0:T(8,128)S(1)} fusion(bf16[1,4,128,128]{3,2,1,0:T(8,128)(2,1)} %param.16, bf16[1,16,32,128]{3,2,1,0:T(8,128)(2,1)S(1)} %get-tuple-element.12), kind=kOutput, calls=%fused_computation.16 | convolution fusion | flops 4194304 | bytes 229376 | tf_op jit(solution)/shard_map/tjri,tjio->tjro/dot_general | solution.py:156
  15.8 1.2 %broadcast_subtract_fusion = f32[4]{0:T(128)} fusion(s32[1,4]{1,0:T(1,128)} %param.18), kind=kLoop, calls=%fused_computation.33 | loop fusion | flops 8 | bytes 32 | tf_op jit(solution)/shard_map/sub | solution.py:170
  17.1 2.9 %collective-permute-start.2 = (f32[512,128]{1,0:T(8,128)}, f32[512,128]{1,0:T(8,128)}, u32[]{:S(2)}, u32[]{:S(2)}) collective-permute-start(f32[512,128]{1,0:T(8,128)} %collective-permute-done.1.across_ref), channel_id=1, source_target_pairs={{0,32},{32,0},{64,96},{96,64},{128,160},{160,128},{192,224},{224,1... | collective-permute-start | bytes 786440 | tf_op jit(solution)/shard_map/ppermute | solution.py:49
  20.9 1.4 %broadcast_multiply_fusion.scale_ref = f32[16,128]{1,0:T(8,128)} fusion(f32[16]{0:T(128)S(1)} %or_convert_fusion, f32[1,16,128]{2,1,0:T(8,128)} %param.13), kind=kLoop, calls=%fused_computation.30 | loop fusion | flops 2048 | bytes 16448 | tf_op jit(solution)/shard_map/mul | solution.py:151
  22.3 2.3 %shard_map.109 = f32[4,512,128]{2,1,0:T(8,128)} custom-call(s32[1]{0:T(128)} %bitcast.index_ref, f32[16,16]{1,0:T(8,128)} %constant.32.clone.coef_ref, f32[512,128]{1,0:T(8,128)} %bitcast.2.own_ref, f32[512,128]{1,0:T(8,128)} %collective-permute-done.mate_ref, f32[512,128]{1,0:T(8,128)} %collective-permute-done.1.across_ref, ...), custom_call_target="tpu_custom_call" | custom-call | tf_op jit(solution)/shard_map/pallas_call | solution.py:91
  24.6 4.2 %all-to-all-start = ((f32[4,512,128]{2,1,0:T(8,128)}), f32[4,512,128]{2,1,0:T(8,128)}, u32[]{:S(2)}, u32[]{:S(2)}) async-start(f32[4,512,128]{2,1,0:T(8,128)} %shard_map.109), calls=%async_computation | async-start | bytes 2097152 | tf_op jit(solution)/shard_map/all_to_all | solution.py:136
  28.8 1.9 %collective-permute-start.3 = (bf16[1,5,32,128]{3,2,1,0:T(8,128)(2,1)}, bf16[1,5,32,128]{3,2,1,0:T(8,128)(2,1)S(1)}, u32[]{:S(2)}, u32[]{:S(2)}) collective-permute-start(bf16[1,5,32,128]{3,2,1,0:T(8,128)(2,1)} %pad_maximum_fusion), channel_id=1, source_target_pairs={{31,0},{0,1},{1,2},{2,3},{3,4},{4,5},{5,6},{6,7},{7,8},{8,9},{9,10... | collective-permute-start | bytes 122888 | tf_op jit(solution)/shard_map/ppermute | solution.py:32
  30.8 10.1 %collective-permute-start.4 = (bf16[1,1,32,128]{3,2,1,0:T(8,128)(2,1)S(1)}, bf16[1,1,32,128]{3,2,1,0:T(8,128)(2,1)S(1)}, u32[]{:S(2)}, u32[]{:S(2)}) collective-permute-start(bf16[1,1,32,128]{3,2,1,0:T(8,128)(2,1)S(1)} %slice.33), channel_id=1, source_target_pairs={{1,0},{2,1},{3,2},{4,3},{5,4},{6,5},{7,6},{8,7},{9,8},{10,9},{11,1... | collective-permute-start | bytes 24584 | tf_op jit(solution)/shard_map/ppermute | solution.py:32
  42.0 0.9 %maximum_bitcast_fusion = bf16[18,32,128]{2,1,0:T(8,128)(2,1)S(1)} fusion(bf16[1,1,32,128]{3,2,1,0:T(8,128)(2,1)S(1)} %collective-permute-done.4, bf16[1,16,32,128]{3,2,1,0:T(8,128)(2,1)} %copy-done.3, bf16[1,1,32,128]{3,2,1,0:T(8,128)(2,1)S(1)} %slice.46), kind=kLoop, calls=%fused_computation.12 | loop fusion | flops 147456 | bytes 294912 | tf_op jit(solution)/shard_map/concatenate | solution.py:166
  43.0 1.7 %gather_fusion = bf16[96,32,128]{2,1,0:T(8,128)(2,1)} fusion(bf16[18,32,128]{2,1,0:T(8,128)(2,1)S(1)} %maximum_bitcast_fusion, s32[1024]{0:T(1024)} %pad_clamp_fusion), kind=kCustom, calls=%fused_computation | custom fusion | bytes 1573248 | tf_op jit(solution)/shard_map/gather | solution.py:167
  44.7 0.9 %bitcast_add_fusion.1 = f32[1,4,32,128]{3,2,1,0:T(8,128)S(1)} fusion(f32[4,32,128]{2,1,0:T(8,128)} %copy-done.4, bf16[1,5,32,128]{3,2,1,0:T(8,128)(2,1)} %copy-done.8, f32[4]{0:T(128)} %broadcast_subtract_fusion), kind=kLoop, calls=%fused_computation.19 | loop fusion | flops 49152 | bytes 163856 | tf_op jit(solution)/shard_map/add | solution.py:170
  45.6 2.6 %multiply_add_fusion.1 = f32[1,16,32,128]{3,2,1,0:T(8,128)} fusion(f32[1,16,32,128]{3,2,1,0:T(8,128)S(1)} %copy-done.1, f32[1,4,32,128]{3,2,1,0:T(8,128)S(1)} %bitcast_add_fusion.1, f32[1,16,32,128]{3,2,1,0:T(8,128)} %param.11, f32[16,128]{1,0:T(8,128)} %bitcast.68, f32[16]{0:T(128)} %copy-done.10, bf16[16,6,32,128]{3,2,1,0:T(8,128)(2,1)} %bitcast.63, ...), kind=kOutput, calls=%fused_computation.9 | convolution fusion | flops 101056512 | bytes 4792384 | tf_op jit(solution)/shard_map/tnkri,tnkio->tnro/dot_general | solution.py:168
  48.2 2.0 %shard_map.110 = (f32[512,128]{1,0:T(8,128)}, f32[512,128]{1,0:T(8,128)}) custom-call(f32[4,512,128]{2,1,0:T(8,128)} %all-to-all-done.got_ref, f32[512,128]{1,0:T(8,128)} %bitcast.67, f32[16,128]{1,0:T(8,128)} %broadcast_multiply_fusion.scale_ref, f32[16,128]{1,0:T(8,128)} %cond_ref.3), custom_call_target="tpu_custom_call" | custom-call | tf_op jit(solution)/shard_map/pallas_call | solution.py:121
  50.2 2.3 %collective-permute-start.6 = (f32[512,128]{1,0:T(8,128)}, f32[512,128]{1,0:T(8,128)S(1)}, u32[]{:S(2)}, u32[]{:S(2)}) collective-permute-start(f32[512,128]{1,0:T(8,128)} %get-tuple-element.13.own_ref), channel_id=1, source_target_pairs={{0,256},{32,288},{64,320},{96,352},{128,384},{160,416},{192,448},{... | collective-permute-start | bytes 786440 | tf_op jit(solution)/shard_map/ppermute | solution.py:49
  52.5 2.6 %collective-permute-start.5 = (f32[512,128]{1,0:T(8,128)}, f32[512,128]{1,0:T(8,128)S(1)}, u32[]{:S(2)}, u32[]{:S(2)}) collective-permute-start(f32[512,128]{1,0:T(8,128)} %get-tuple-element.13.own_ref), channel_id=1, source_target_pairs={{0,32},{32,0},{64,96},{96,64},{128,160},{160,128},{192,224},{224,1... | collective-permute-start | bytes 786440 | tf_op jit(solution)/shard_map/ppermute | solution.py:49
  55.2 1.0 %convert_element_type.52 = bf16[1,16,32,128]{3,2,1,0:T(8,128)(2,1)S(1)} convert(f32[1,16,32,128]{3,2,1,0:T(8,128)} %bitcast.65) | non-fusion elementwise | flops 65536 | bytes 393216 | tf_op jit(solution)/shard_map/convert_element_type | solution.py:154
  56.2 3.6 %collective-permute-done.6.across_ref = f32[512,128]{1,0:T(8,128)S(1)} collective-permute-done((f32[512,128]{1,0:T(8,128)}, f32[512,128]{1,0:T(8,128)S(1)}, u32[]{:S(2)}, u32[]{:S(2)}) %collective-permute-start.6) | collective-permute-done | bytes 262176 | tf_op jit(solution)/shard_map/ppermute | solution.py:49
  59.8 3.2 %collective-permute-start.7 = (f32[512,128]{1,0:T(8,128)S(1)}, f32[512,128]{1,0:T(8,128)}, u32[]{:S(2)}, u32[]{:S(2)}) collective-permute-start(f32[512,128]{1,0:T(8,128)S(1)} %collective-permute-done.6.across_ref), channel_id=1, source_target_pairs={{0,32},{32,0},{64,96},{96,64},{128,160},{160,128},{192,224},{224,1... | collective-permute-start | bytes 786440 | tf_op jit(solution)/shard_map/ppermute | solution.py:49
  63.0 1.1 %fusion.10 = f32[4,32,128]{2,1,0:T(8,128)S(1)} fusion(bf16[1,4,128,128]{3,2,1,0:T(8,128)(2,1)} %param.16, bf16[1,16,32,128]{3,2,1,0:T(8,128)(2,1)S(1)} %convert_element_type.52), kind=kOutput, calls=%fused_computation.14 | convolution fusion | flops 4194304 | bytes 229376 | tf_op jit(solution)/shard_map/tjri,tjio->tjro/dot_general | solution.py:156
  66.0 2.3 %shard_map.111 = f32[4,512,128]{2,1,0:T(8,128)} custom-call(s32[1]{0:T(128)} %bitcast.index_ref, f32[16,16]{1,0:T(8,128)} %constant.32.clone.coef_ref, f32[512,128]{1,0:T(8,128)} %get-tuple-element.13.own_ref, f32[512,128]{1,0:T(8,128)} %copy-done.7, f32[512,128]{1,0:T(8,128)} %copy-done.6, f32[512,128]{1,0:T(8,128)} %collective-permute-done.7.diagonal_ref), custom_call_target="tpu_custom_call" | custom-call | tf_op jit(solution)/shard_map/pallas_call | solution.py:91
  68.3 4.2 %all-to-all-start.1 = ((f32[4,512,128]{2,1,0:T(8,128)}), f32[4,512,128]{2,1,0:T(8,128)}, u32[]{:S(2)}, u32[]{:S(2)}) async-start(f32[4,512,128]{2,1,0:T(8,128)} %shard_map.111), calls=%async_computation.1 | async-start | bytes 2097152 | tf_op jit(solution)/shard_map/all_to_all | solution.py:136
  72.6 0.8 pad_maximum_fusion.1
  73.3 1.9 %collective-permute-start.8 = (bf16[1,5,32,128]{3,2,1,0:T(8,128)(2,1)S(1)}, bf16[1,5,32,128]{3,2,1,0:T(8,128)(2,1)S(1)}, u32[]{:S(2)}, u32[]{:S(2)}) collective-permute-start(bf16[1,5,32,128]{3,2,1,0:T(8,128)(2,1)S(1)} %pad_maximum_fusion.1), channel_id=1, source_target_pairs={{31,0},{0,1},{1,2},{2,3},{3,4},{4,5},{5,6},{6,7},{7,8},{8,9},{9,10... | collective-permute-start | bytes 122888 | tf_op jit(solution)/shard_map/ppermute | solution.py:32
  75.2 7.0 %collective-permute-start.9 = (bf16[1,1,32,128]{3,2,1,0:T(8,128)(2,1)S(1)}, bf16[1,1,32,128]{3,2,1,0:T(8,128)(2,1)S(1)}, u32[]{:S(2)}, u32[]{:S(2)}) collective-permute-start(bf16[1,1,32,128]{3,2,1,0:T(8,128)(2,1)S(1)} %slice.38), channel_id=1, source_target_pairs={{1,0},{2,1},{3,2},{4,3},{5,4},{6,5},{7,6},{8,7},{9,8},{10,9},{11,1... | collective-permute-start | bytes 24584 | tf_op jit(solution)/shard_map/ppermute | solution.py:32
  83.0 0.9 %maximum_bitcast_fusion.1 = bf16[18,32,128]{2,1,0:T(8,128)(2,1)S(1)} fusion(bf16[1,1,32,128]{3,2,1,0:T(8,128)(2,1)S(1)} %collective-permute-done.9, bf16[1,16,32,128]{3,2,1,0:T(8,128)(2,1)} %copy-done.2, bf16[1,1,32,128]{3,2,1,0:T(8,128)(2,1)S(1)} %slice.50), kind=kLoop, calls=%fused_computation.13 | loop fusion | flops 147456 | bytes 294912 | tf_op jit(solution)/shard_map/concatenate | solution.py:166
  83.9 1.7 %gather_fusion.1 = bf16[96,32,128]{2,1,0:T(8,128)(2,1)} fusion(bf16[18,32,128]{2,1,0:T(8,128)(2,1)S(1)} %maximum_bitcast_fusion.1, s32[1024]{0:T(1024)} %pad_clamp_fusion), kind=kCustom, calls=%fused_computation.1 | custom fusion | bytes 1573248 | tf_op jit(solution)/shard_map/gather | solution.py:167
  85.6 0.9 %bitcast_add_fusion = f32[1,4,32,128]{3,2,1,0:T(8,128)S(1)} fusion(f32[4,32,128]{2,1,0:T(8,128)} %copy-done.5, bf16[1,5,32,128]{3,2,1,0:T(8,128)(2,1)} %copy-done.9, f32[4]{0:T(128)} %broadcast_subtract_fusion), kind=kLoop, calls=%fused_computation.18 | loop fusion | flops 49152 | bytes 163856 | tf_op jit(solution)/shard_map/add | solution.py:170
  86.6 2.6 %multiply_add_fusion = f32[1,16,32,128]{3,2,1,0:T(8,128)} fusion(f32[1,16,32,128]{3,2,1,0:T(8,128)} %bitcast.66, f32[1,16,32,128]{3,2,1,0:T(8,128)S(1)} %copy-done.1, f32[1,4,32,128]{3,2,1,0:T(8,128)S(1)} %bitcast_add_fusion, f32[16,128]{1,0:T(8,128)} %bitcast.69, f32[16]{0:T(128)} %copy-done.10, bf16[16,6,32,128]{3,2,1,0:T(8,128)(2,1)} %bitcast.62, ...), kind=kOutput, calls=%fused_computation.8 | convolution fusion | flops 100990976 | bytes 4792384 | tf_op jit(solution)/shard_map/tnkri,tnkio->tnro/dot_general | solution.py:168
  89.1 2.0 %shard_map.112 = f32[512,128]{1,0:T(8,128)} custom-call(f32[4,512,128]{2,1,0:T(8,128)} %all-to-all-done.1.got_ref, f32[512,128]{1,0:T(8,128)} %bitcast.64, f32[16,128]{1,0:T(8,128)} %broadcast_multiply_fusion.scale_ref, f32[16,128]{1,0:T(8,128)} %cond_ref.3), custom_call_target="tpu_custom_call" | custom-call | tf_op jit(solution)/shard_map/pallas_call | solution.py:121
  (52 shorter events, 6.2 us)
Async XLA Ops:
  0.0 45.6 %copy-start = (bf16[1,16,6,128,128]{4,3,2,1,0:T(8,128)(2,1)S(1)}, bf16[1,16,6,128,128]{4,3,2,1,0:T(8,128)(2,1)}, u32[]{:S(2)}) copy-start(bf16[1,16,6,128,128]{4,3,2,1,0:T(8,128)(2,1)} %param.15) | copy-start | bytes 9437188
  0.8 40.6 %copy-start.10 = (f32[16]{0:T(128)}, f32[16]{0:T(128)S(1)}, u32[]{:S(2)}) copy-start(f32[16]{0:T(128)S(1)} %or_convert_fusion) | copy-start | bytes 196
  2.7 38.7 %copy-start.3 = (bf16[1,16,32,128]{3,2,1,0:T(8,128)(2,1)}, bf16[1,16,32,128]{3,2,1,0:T(8,128)(2,1)S(1)}, u32[]{:S(2)}) copy-start(bf16[1,16,32,128]{3,2,1,0:T(8,128)(2,1)S(1)} %get-tuple-element.12) | copy-start | bytes 393220
  2.7 14.4 %collective-permute-start.1 = (f32[512,128]{1,0:T(8,128)}, f32[512,128]{1,0:T(8,128)}, u32[]{:S(2)}, u32[]{:S(2)}) collective-permute-start(f32[512,128]{1,0:T(8,128)} %bitcast.2.own_ref), channel_id=1, source_target_pairs={{0,256},{32,288},{64,320},{96,352},{128,384},{160,416},{192,448},{... | collective-permute-start | bytes 786440 | tf_op jit(solution)/shard_map/ppermute | solution.py:49
  6.8 15.5 %collective-permute-start = (f32[512,128]{1,0:T(8,128)}, f32[512,128]{1,0:T(8,128)}, u32[]{:S(2)}, u32[]{:S(2)}) collective-permute-start(f32[512,128]{1,0:T(8,128)} %bitcast.2.own_ref), channel_id=1, source_target_pairs={{0,32},{32,0},{64,96},{96,64},{128,160},{160,128},{192,224},{224,1... | collective-permute-start | bytes 786440 | tf_op jit(solution)/shard_map/ppermute | solution.py:49
  14.1 6.6 %copy-start.11 = (f32[4]{0:T(128)}, f32[4]{0:T(128)S(1)}, u32[]{:S(2)}) copy-start(f32[4]{0:T(128)S(1)} %convert_bitcast_fusion) | copy-start | bytes 52
  15.8 1.2 %copy-start.4 = (f32[4,32,128]{2,1,0:T(8,128)}, f32[4,32,128]{2,1,0:T(8,128)S(1)}, u32[]{:S(2)}) copy-start(f32[4,32,128]{2,1,0:T(8,128)S(1)} %fusion.12) | copy-start | bytes 196612
  17.1 5.1 %collective-permute-start.2 = (f32[512,128]{1,0:T(8,128)}, f32[512,128]{1,0:T(8,128)}, u32[]{:S(2)}, u32[]{:S(2)}) collective-permute-start(f32[512,128]{1,0:T(8,128)} %collective-permute-done.1.across_ref), channel_id=1, source_target_pairs={{0,32},{32,0},{64,96},{96,64},{128,160},{160,128},{192,224},{224,1... | collective-permute-start | bytes 786440 | tf_op jit(solution)/shard_map/ppermute | solution.py:49
  22.3 23.4 %copy-start.1 = (f32[1,16,32,128]{3,2,1,0:T(8,128)S(1)}, f32[1,16,32,128]{3,2,1,0:T(8,128)}, u32[]{:S(2)}) copy-start(f32[1,16,32,128]{3,2,1,0:T(8,128)} %param.12) | copy-start | bytes 786436
  24.6 23.6 %all-to-all-start = ((f32[4,512,128]{2,1,0:T(8,128)}), f32[4,512,128]{2,1,0:T(8,128)}, u32[]{:S(2)}, u32[]{:S(2)}) async-start(f32[4,512,128]{2,1,0:T(8,128)} %shard_map.109), calls=%async_computation | async-start | bytes 2097152 | tf_op jit(solution)/shard_map/all_to_all | solution.py:136
  28.8 12.6 %collective-permute-start.3 = (bf16[1,5,32,128]{3,2,1,0:T(8,128)(2,1)}, bf16[1,5,32,128]{3,2,1,0:T(8,128)(2,1)S(1)}, u32[]{:S(2)}, u32[]{:S(2)}) collective-permute-start(bf16[1,5,32,128]{3,2,1,0:T(8,128)(2,1)} %pad_maximum_fusion), channel_id=1, source_target_pairs={{31,0},{0,1},{1,2},{2,3},{3,4},{4,5},{5,6},{6,7},{7,8},{8,9},{9,10... | collective-permute-start | bytes 122888 | tf_op jit(solution)/shard_map/ppermute | solution.py:32
  30.8 10.8 %collective-permute-start.4 = (bf16[1,1,32,128]{3,2,1,0:T(8,128)(2,1)S(1)}, bf16[1,1,32,128]{3,2,1,0:T(8,128)(2,1)S(1)}, u32[]{:S(2)}, u32[]{:S(2)}) collective-permute-start(bf16[1,1,32,128]{3,2,1,0:T(8,128)(2,1)S(1)} %slice.33), channel_id=1, source_target_pairs={{1,0},{2,1},{3,2},{4,3},{5,4},{6,5},{7,6},{8,7},{9,8},{10,9},{11,1... | collective-permute-start | bytes 24584 | tf_op jit(solution)/shard_map/ppermute | solution.py:32
  41.4 0.6 copy-start.8
  45.6 19.0 %copy-start.12 = (f32[4]{0:T(128)S(1)}, f32[4]{0:T(128)}, u32[]{:S(2)}) copy-start(f32[4]{0:T(128)} %copy-done.11) | copy-start | bytes 52
  50.2 9.5 %collective-permute-start.6 = (f32[512,128]{1,0:T(8,128)}, f32[512,128]{1,0:T(8,128)S(1)}, u32[]{:S(2)}, u32[]{:S(2)}) collective-permute-start(f32[512,128]{1,0:T(8,128)} %get-tuple-element.13.own_ref), channel_id=1, source_target_pairs={{0,256},{32,288},{64,320},{96,352},{128,384},{160,416},{192,448},{... | collective-permute-start | bytes 786440 | tf_op jit(solution)/shard_map/ppermute | solution.py:49
  52.5 12.8 %collective-permute-start.5 = (f32[512,128]{1,0:T(8,128)}, f32[512,128]{1,0:T(8,128)S(1)}, u32[]{:S(2)}, u32[]{:S(2)}) collective-permute-start(f32[512,128]{1,0:T(8,128)} %get-tuple-element.13.own_ref), channel_id=1, source_target_pairs={{0,32},{32,0},{64,96},{96,64},{128,160},{160,128},{192,224},{224,1... | collective-permute-start | bytes 786440 | tf_op jit(solution)/shard_map/ppermute | solution.py:49
  56.2 26.1 %copy-start.2 = (bf16[1,16,32,128]{3,2,1,0:T(8,128)(2,1)}, bf16[1,16,32,128]{3,2,1,0:T(8,128)(2,1)S(1)}, u32[]{:S(2)}) copy-start(bf16[1,16,32,128]{3,2,1,0:T(8,128)(2,1)S(1)} %convert_element_type.52) | copy-start | bytes 393220
  59.8 5.6 %copy-start.6 = (f32[512,128]{1,0:T(8,128)}, f32[512,128]{1,0:T(8,128)S(1)}, u32[]{:S(2)}) copy-start(f32[512,128]{1,0:T(8,128)S(1)} %collective-permute-done.6.across_ref) | copy-start | bytes 786436
  59.8 6.3 %collective-permute-start.7 = (f32[512,128]{1,0:T(8,128)S(1)}, f32[512,128]{1,0:T(8,128)}, u32[]{:S(2)}, u32[]{:S(2)}) collective-permute-start(f32[512,128]{1,0:T(8,128)S(1)} %collective-permute-done.6.across_ref), channel_id=1, source_target_pairs={{0,32},{32,0},{64,96},{96,64},{128,160},{160,128},{192,224},{224,1... | collective-permute-start | bytes 786440 | tf_op jit(solution)/shard_map/ppermute | solution.py:49
  64.0 0.6 copy-start.5
  65.3 0.7 copy-start.7
  68.3 20.8 %all-to-all-start.1 = ((f32[4,512,128]{2,1,0:T(8,128)}), f32[4,512,128]{2,1,0:T(8,128)}, u32[]{:S(2)}, u32[]{:S(2)}) async-start(f32[4,512,128]{2,1,0:T(8,128)} %shard_map.111), calls=%async_computation.1 | async-start | bytes 2097152 | tf_op jit(solution)/shard_map/all_to_all | solution.py:136
  73.3 8.9 %collective-permute-start.8 = (bf16[1,5,32,128]{3,2,1,0:T(8,128)(2,1)S(1)}, bf16[1,5,32,128]{3,2,1,0:T(8,128)(2,1)S(1)}, u32[]{:S(2)}, u32[]{:S(2)}) collective-permute-start(bf16[1,5,32,128]{3,2,1,0:T(8,128)(2,1)S(1)} %pad_maximum_fusion.1), channel_id=1, source_target_pairs={{31,0},{0,1},{1,2},{2,3},{3,4},{4,5},{5,6},{6,7},{7,8},{8,9},{9,10... | collective-permute-start | bytes 122888 | tf_op jit(solution)/shard_map/ppermute | solution.py:32
  75.2 7.8 %collective-permute-start.9 = (bf16[1,1,32,128]{3,2,1,0:T(8,128)(2,1)S(1)}, bf16[1,1,32,128]{3,2,1,0:T(8,128)(2,1)S(1)}, u32[]{:S(2)}, u32[]{:S(2)}) collective-permute-start(bf16[1,1,32,128]{3,2,1,0:T(8,128)(2,1)S(1)} %slice.38), channel_id=1, source_target_pairs={{1,0},{2,1},{3,2},{4,3},{5,4},{6,5},{7,6},{8,7},{9,8},{10,9},{11,1... | collective-permute-start | bytes 24584 | tf_op jit(solution)/shard_map/ppermute | solution.py:32
  82.2 0.8 copy-start.9

commit v13 on v12

--- a/solution.py
+++ b/solution.py
@@ -86,7 +86,7 @@
 
 def partial_sums(index, own, mate, across, diagonal):
     rows, lanes = own.shape
-    block = 256
+    block = rows
     flat = pl.BlockSpec((block, lanes), lambda r, index: (r, 0))
     return pl.pallas_call(
         mix_kernel,
@@ -114,7 +114,7 @@
 
 def updated(got, base, scale, cond, outputs):
     rows, lanes = base.shape
-    block = 256
+    block = rows
     groups = block * scale.shape[0] // rows
     flat = pl.BlockSpec((block, lanes), lambda r: (r, 0))
     narrow = pl.BlockSpec((groups, lanes), lambda r: (r, 0))

time: 92.5 us -> 93.2 us (level)
  no operation moved by 1% of the time
where the time goes in v13:
time: 93.2 us; the launch traced here: 91.7 us
  starting transfers between devices  51.1 us (55%)
  other arithmetic  13.2 us (14%)
  Pallas kernels  9.21 us (10%)
  matrix products  7.22 us (8%)
  local copies, waits for them, and re-layouts  5.39 us (6%)
  waiting for transfers between devices  4.49 us (5%)
  between operations  1.06 us (1%)
    ppermute x6, starting transfers between devices, routed(): return lax.ppermute(block, INST, [(s, dest(s)) for s in range(NT)])  21.8 us
    ppermute x4, starting transfers between devices, shifted(): return lax.ppermute(block, axis, route)  20.9 us
    all_to_all x2, starting transfers between devices, instance_mix(): return (partials, lax.all_to_all(partials, 'ix', 0, 0))  8.49 us
    dot_general x2, matrix products, shards(): jnp.einsum('tnkri,tnkio->tnro', picked, jac, preferred_element_type=jnp.f...  5.12 us
    pallas_call x2, Pallas kernels, partial_sums(): pl.pallas_call(mix_kernel, grid_spec=pltpu.PrefetchScalarGridSpec(num_sca...  4.95 us
    pallas_call x2, Pallas kernels, updated(): pl.pallas_call(update_kernel, grid=(rows // block,), in_specs=[pl.BlockSp...  4.26 us
    ppermute x6, waiting for transfers between devices, routed(): return lax.ppermute(block, INST, [(s, dest(s)) for s in range(NT)])  3.6 us
    gather x2, local copies, waits for them, and re-layouts, shards(): picked = lam_h[:, cols]  3.4 us
  transfers between devices with their start and end apart: 12, of which 3 were waited for; matrix products, arithmetic and copies ran while one was open for 24% of the time, Pallas kernels for 0%

profile of v13, /device:TPU:1, one launch (start us, length us, event | category | flops | bytes accessed | tf_op | source)
XLA Modules:
  0.0 91.7 jit_solution(10779375425225790206)
XLA Ops:
  0.8 1.9 %multiply_convert_fusion = (bf16[1,16,32,128]{3,2,1,0:T(8,128)(2,1)S(1)}, f32[1,16,32,128]{3,2,1,0:T(8,128)}) fusion(f32[1,16,32,128]{3,2,1,0:T(8,128)} %param.11, f32[16]{0:T(128)S(1)} %or_convert_fusion, f32[16,128]{1,0:T(8,128)} %cond_ref.3), kind=kLoop, calls=%fused_computation.10 | loop fusion | flops 196608 | bytes 663616 | tf_op jit(solution)/shard_map/convert_element_type | solution.py:154
  2.7 4.0 %collective-permute-start.1 = (f32[512,128]{1,0:T(8,128)}, f32[512,128]{1,0:T(8,128)}, u32[]{:S(2)}, u32[]{:S(2)}) collective-permute-start(f32[512,128]{1,0:T(8,128)} %bitcast.2.own_ref), channel_id=1, source_target_pairs={{0,256},{32,288},{64,320},{96,352},{128,384},{160,416},{192,448},{... | collective-permute-start | bytes 786440 | tf_op jit(solution)/shard_map/ppermute | solution.py:49
  6.8 6.7 %collective-permute-start = (f32[512,128]{1,0:T(8,128)}, f32[512,128]{1,0:T(8,128)}, u32[]{:S(2)}, u32[]{:S(2)}) collective-permute-start(f32[512,128]{1,0:T(8,128)} %bitcast.2.own_ref), channel_id=1, source_target_pairs={{0,32},{32,0},{64,96},{96,64},{128,160},{160,128},{192,224},{224,1... | collective-permute-start | bytes 786440 | tf_op jit(solution)/shard_map/ppermute | solution.py:49
  14.8 1.0 %fusion.12 = f32[4,32,128]{2,1,0:T(8,128)S(1)} fusion(bf16[1,4,128,128]{3,2,1,0:T(8,128)(2,1)} %param.16, bf16[1,16,32,128]{3,2,1,0:T(8,128)(2,1)S(1)} %get-tuple-element.12), kind=kOutput, calls=%fused_computation.16 | convolution fusion | flops 4194304 | bytes 229376 | tf_op jit(solution)/shard_map/tjri,tjio->tjro/dot_general | solution.py:156
  15.8 1.2 %broadcast_subtract_fusion = f32[4]{0:T(128)} fusion(s32[1,4]{1,0:T(1,128)} %param.18), kind=kLoop, calls=%fused_computation.33 | loop fusion | flops 8 | bytes 32 | tf_op jit(solution)/shard_map/sub | solution.py:170
  17.1 2.9 %collective-permute-start.2 = (f32[512,128]{1,0:T(8,128)}, f32[512,128]{1,0:T(8,128)}, u32[]{:S(2)}, u32[]{:S(2)}) collective-permute-start(f32[512,128]{1,0:T(8,128)} %collective-permute-done.1.across_ref), channel_id=1, source_target_pairs={{0,32},{32,0},{64,96},{96,64},{128,160},{160,128},{192,224},{224,1... | collective-permute-start | bytes 786440 | tf_op jit(solution)/shard_map/ppermute | solution.py:49
  20.9 1.4 %broadcast_multiply_fusion.scale_ref = f32[16,128]{1,0:T(8,128)} fusion(f32[16]{0:T(128)S(1)} %or_convert_fusion, f32[1,16,128]{2,1,0:T(8,128)} %param.13), kind=kLoop, calls=%fused_computation.30 | loop fusion | flops 2048 | bytes 16448 | tf_op jit(solution)/shard_map/mul | solution.py:151
  22.3 2.5 %shard_map.109 = f32[4,512,128]{2,1,0:T(8,128)} custom-call(s32[1]{0:T(128)} %bitcast.index_ref, f32[16,16]{1,0:T(8,128)} %constant.32.clone.coef_ref, f32[512,128]{1,0:T(8,128)} %bitcast.2.own_ref, f32[512,128]{1,0:T(8,128)} %collective-permute-done.mate_ref, f32[512,128]{1,0:T(8,128)} %collective-permute-done.1.across_ref, ...), custom_call_target="tpu_custom_call" | custom-call | tf_op jit(solution)/shard_map/pallas_call | solution.py:91
  24.8 4.2 %all-to-all-start = ((f32[4,512,128]{2,1,0:T(8,128)}), f32[4,512,128]{2,1,0:T(8,128)}, u32[]{:S(2)}, u32[]{:S(2)}) async-start(f32[4,512,128]{2,1,0:T(8,128)} %shard_map.109), calls=%async_computation | async-start | bytes 2097152 | tf_op jit(solution)/shard_map/all_to_all | solution.py:136
  29.0 1.9 %collective-permute-start.3 = (bf16[1,5,32,128]{3,2,1,0:T(8,128)(2,1)}, bf16[1,5,32,128]{3,2,1,0:T(8,128)(2,1)S(1)}, u32[]{:S(2)}, u32[]{:S(2)}) collective-permute-start(bf16[1,5,32,128]{3,2,1,0:T(8,128)(2,1)} %pad_maximum_fusion), channel_id=1, source_target_pairs={{31,0},{0,1},{1,2},{2,3},{3,4},{4,5},{5,6},{6,7},{7,8},{8,9},{9,10... | collective-permute-start | bytes 122888 | tf_op jit(solution)/shard_map/ppermute | solution.py:32
  31.0 10.1 %collective-permute-start.4 = (bf16[1,1,32,128]{3,2,1,0:T(8,128)(2,1)S(1)}, bf16[1,1,32,128]{3,2,1,0:T(8,128)(2,1)S(1)}, u32[]{:S(2)}, u32[]{:S(2)}) collective-permute-start(bf16[1,1,32,128]{3,2,1,0:T(8,128)(2,1)S(1)} %slice.33), channel_id=1, source_target_pairs={{1,0},{2,1},{3,2},{4,3},{5,4},{6,5},{7,6},{8,7},{9,8},{10,9},{11,1... | collective-permute-start | bytes 24584 | tf_op jit(solution)/shard_map/ppermute | solution.py:32
  42.2 0.9 %maximum_bitcast_fusion = bf16[18,32,128]{2,1,0:T(8,128)(2,1)S(1)} fusion(bf16[1,1,32,128]{3,2,1,0:T(8,128)(2,1)S(1)} %collective-permute-done.4, bf16[1,16,32,128]{3,2,1,0:T(8,128)(2,1)} %copy-done.3, bf16[1,1,32,128]{3,2,1,0:T(8,128)(2,1)S(1)} %slice.46), kind=kLoop, calls=%fused_computation.12 | loop fusion | flops 147456 | bytes 294912 | tf_op jit(solution)/shard_map/concatenate | solution.py:166
  43.2 1.7 %gather_fusion = bf16[96,32,128]{2,1,0:T(8,128)(2,1)} fusion(bf16[18,32,128]{2,1,0:T(8,128)(2,1)S(1)} %maximum_bitcast_fusion, s32[1024]{0:T(1024)} %pad_clamp_fusion), kind=kCustom, calls=%fused_computation | custom fusion | bytes 1573248 | tf_op jit(solution)/shard_map/gather | solution.py:167
  44.9 0.9 %bitcast_add_fusion.1 = f32[1,4,32,128]{3,2,1,0:T(8,128)S(1)} fusion(f32[4,32,128]{2,1,0:T(8,128)} %copy-done.4, bf16[1,5,32,128]{3,2,1,0:T(8,128)(2,1)} %copy-done.8, f32[4]{0:T(128)} %broadcast_subtract_fusion), kind=kLoop, calls=%fused_computation.19 | loop fusion | flops 49152 | bytes 163856 | tf_op jit(solution)/shard_map/add | solution.py:170
  45.8 2.6 %multiply_add_fusion.1 = f32[1,16,32,128]{3,2,1,0:T(8,128)} fusion(f32[1,16,32,128]{3,2,1,0:T(8,128)S(1)} %copy-done.1, f32[1,4,32,128]{3,2,1,0:T(8,128)S(1)} %bitcast_add_fusion.1, f32[1,16,32,128]{3,2,1,0:T(8,128)} %param.11, f32[16,128]{1,0:T(8,128)} %bitcast.68, f32[16]{0:T(128)} %copy-done.10, bf16[16,6,32,128]{3,2,1,0:T(8,128)(2,1)} %bitcast.63, ...), kind=kOutput, calls=%fused_computation.9 | convolution fusion | flops 101056512 | bytes 4792384 | tf_op jit(solution)/shard_map/tnkri,tnkio->tnro/dot_general | solution.py:168
  48.4 2.2 %shard_map.110 = (f32[512,128]{1,0:T(8,128)}, f32[512,128]{1,0:T(8,128)}) custom-call(f32[4,512,128]{2,1,0:T(8,128)} %all-to-all-done.got_ref, f32[512,128]{1,0:T(8,128)} %bitcast.67, f32[16,128]{1,0:T(8,128)} %broadcast_multiply_fusion.scale_ref, f32[16,128]{1,0:T(8,128)} %cond_ref.3), custom_call_target="tpu_custom_call" | custom-call | tf_op jit(solution)/shard_map/pallas_call | solution.py:121
  50.6 2.3 %collective-permute-start.6 = (f32[512,128]{1,0:T(8,128)}, f32[512,128]{1,0:T(8,128)S(1)}, u32[]{:S(2)}, u32[]{:S(2)}) collective-permute-start(f32[512,128]{1,0:T(8,128)} %get-tuple-element.13.own_ref), channel_id=1, source_target_pairs={{0,256},{32,288},{64,320},{96,352},{128,384},{160,416},{192,448},{... | collective-permute-start | bytes 786440 | tf_op jit(solution)/shard_map/ppermute | solution.py:49
  52.9 2.6 %collective-permute-start.5 = (f32[512,128]{1,0:T(8,128)}, f32[512,128]{1,0:T(8,128)S(1)}, u32[]{:S(2)}, u32[]{:S(2)}) collective-permute-start(f32[512,128]{1,0:T(8,128)} %get-tuple-element.13.own_ref), channel_id=1, source_target_pairs={{0,32},{32,0},{64,96},{96,64},{128,160},{160,128},{192,224},{224,1... | collective-permute-start | bytes 786440 | tf_op jit(solution)/shard_map/ppermute | solution.py:49
  55.5 1.0 %convert_element_type.52 = bf16[1,16,32,128]{3,2,1,0:T(8,128)(2,1)S(1)} convert(f32[1,16,32,128]{3,2,1,0:T(8,128)} %bitcast.65) | non-fusion elementwise | flops 65536 | bytes 393216 | tf_op jit(solution)/shard_map/convert_element_type | solution.py:154
  56.5 3.6 %collective-permute-done.6.across_ref = f32[512,128]{1,0:T(8,128)S(1)} collective-permute-done((f32[512,128]{1,0:T(8,128)}, f32[512,128]{1,0:T(8,128)S(1)}, u32[]{:S(2)}, u32[]{:S(2)}) %collective-permute-start.6) | collective-permute-done | bytes 262176 | tf_op jit(solution)/shard_map/ppermute | solution.py:49
  60.1 3.2 %collective-permute-start.7 = (f32[512,128]{1,0:T(8,128)S(1)}, f32[512,128]{1,0:T(8,128)}, u32[]{:S(2)}, u32[]{:S(2)}) collective-permute-start(f32[512,128]{1,0:T(8,128)S(1)} %collective-permute-done.6.across_ref), channel_id=1, source_target_pairs={{0,32},{32,0},{64,96},{96,64},{128,160},{160,128},{192,224},{224,1... | collective-permute-start | bytes 786440 | tf_op jit(solution)/shard_map/ppermute | solution.py:49
  63.3 1.1 %fusion.10 = f32[4,32,128]{2,1,0:T(8,128)S(1)} fusion(bf16[1,4,128,128]{3,2,1,0:T(8,128)(2,1)} %param.16, bf16[1,16,32,128]{3,2,1,0:T(8,128)(2,1)S(1)} %convert_element_type.52), kind=kOutput, calls=%fused_computation.14 | convolution fusion | flops 4194304 | bytes 229376 | tf_op jit(solution)/shard_map/tjri,tjio->tjro/dot_general | solution.py:156
  66.4 2.5 %shard_map.111 = f32[4,512,128]{2,1,0:T(8,128)} custom-call(s32[1]{0:T(128)} %bitcast.index_ref, f32[16,16]{1,0:T(8,128)} %constant.32.clone.coef_ref, f32[512,128]{1,0:T(8,128)} %get-tuple-element.13.own_ref, f32[512,128]{1,0:T(8,128)} %copy-done.7, f32[512,128]{1,0:T(8,128)} %copy-done.6, f32[512,128]{1,0:T(8,128)} %collective-permute-done.7.diagonal_ref), custom_call_target="tpu_custom_call" | custom-call | tf_op jit(solution)/shard_map/pallas_call | solution.py:91
  68.8 4.2 %all-to-all-start.1 = ((f32[4,512,128]{2,1,0:T(8,128)}), f32[4,512,128]{2,1,0:T(8,128)}, u32[]{:S(2)}, u32[]{:S(2)}) async-start(f32[4,512,128]{2,1,0:T(8,128)} %shard_map.111), calls=%async_computation.1 | async-start | bytes 2097152 | tf_op jit(solution)/shard_map/all_to_all | solution.py:136
  73.1 0.8 pad_maximum_fusion.1
  73.8 1.9 %collective-permute-start.8 = (bf16[1,5,32,128]{3,2,1,0:T(8,128)(2,1)S(1)}, bf16[1,5,32,128]{3,2,1,0:T(8,128)(2,1)S(1)}, u32[]{:S(2)}, u32[]{:S(2)}) collective-permute-start(bf16[1,5,32,128]{3,2,1,0:T(8,128)(2,1)S(1)} %pad_maximum_fusion.1), channel_id=1, source_target_pairs={{31,0},{0,1},{1,2},{2,3},{3,4},{4,5},{5,6},{6,7},{7,8},{8,9},{9,10... | collective-permute-start | bytes 122888 | tf_op jit(solution)/shard_map/ppermute | solution.py:32
  75.8 7.0 %collective-permute-start.9 = (bf16[1,1,32,128]{3,2,1,0:T(8,128)(2,1)S(1)}, bf16[1,1,32,128]{3,2,1,0:T(8,128)(2,1)S(1)}, u32[]{:S(2)}, u32[]{:S(2)}) collective-permute-start(bf16[1,1,32,128]{3,2,1,0:T(8,128)(2,1)S(1)} %slice.38), channel_id=1, source_target_pairs={{1,0},{2,1},{3,2},{4,3},{5,4},{6,5},{7,6},{8,7},{9,8},{10,9},{11,1... | collective-permute-start | bytes 24584 | tf_op jit(solution)/shard_map/ppermute | solution.py:32
  83.5 0.9 %maximum_bitcast_fusion.1 = bf16[18,32,128]{2,1,0:T(8,128)(2,1)S(1)} fusion(bf16[1,1,32,128]{3,2,1,0:T(8,128)(2,1)S(1)} %collective-permute-done.9, bf16[1,16,32,128]{3,2,1,0:T(8,128)(2,1)} %copy-done.2, bf16[1,1,32,128]{3,2,1,0:T(8,128)(2,1)S(1)} %slice.50), kind=kLoop, calls=%fused_computation.13 | loop fusion | flops 147456 | bytes 294912 | tf_op jit(solution)/shard_map/concatenate | solution.py:166
  84.4 1.7 %gather_fusion.1 = bf16[96,32,128]{2,1,0:T(8,128)(2,1)} fusion(bf16[18,32,128]{2,1,0:T(8,128)(2,1)S(1)} %maximum_bitcast_fusion.1, s32[1024]{0:T(1024)} %pad_clamp_fusion), kind=kCustom, calls=%fused_computation.1 | custom fusion | bytes 1573248 | tf_op jit(solution)/shard_map/gather | solution.py:167
  86.1 0.9 %bitcast_add_fusion = f32[1,4,32,128]{3,2,1,0:T(8,128)S(1)} fusion(f32[4,32,128]{2,1,0:T(8,128)} %copy-done.5, bf16[1,5,32,128]{3,2,1,0:T(8,128)(2,1)} %copy-done.9, f32[4]{0:T(128)} %broadcast_subtract_fusion), kind=kLoop, calls=%fused_computation.18 | loop fusion | flops 49152 | bytes 163856 | tf_op jit(solution)/shard_map/add | solution.py:170
  87.1 2.6 %multiply_add_fusion = f32[1,16,32,128]{3,2,1,0:T(8,128)} fusion(f32[1,16,32,128]{3,2,1,0:T(8,128)} %bitcast.66, f32[1,16,32,128]{3,2,1,0:T(8,128)S(1)} %copy-done.1, f32[1,4,32,128]{3,2,1,0:T(8,128)S(1)} %bitcast_add_fusion, f32[16,128]{1,0:T(8,128)} %bitcast.69, f32[16]{0:T(128)} %copy-done.10, bf16[16,6,32,128]{3,2,1,0:T(8,128)(2,1)} %bitcast.62, ...), kind=kOutput, calls=%fused_computation.8 | convolution fusion | flops 100990976 | bytes 4792384 | tf_op jit(solution)/shard_map/tnkri,tnkio->tnro/dot_general | solution.py:168
  89.7 2.1 %shard_map.112 = f32[512,128]{1,0:T(8,128)} custom-call(f32[4,512,128]{2,1,0:T(8,128)} %all-to-all-done.1.got_ref, f32[512,128]{1,0:T(8,128)} %bitcast.64, f32[16,128]{1,0:T(8,128)} %broadcast_multiply_fusion.scale_ref, f32[16,128]{1,0:T(8,128)} %cond_ref.3), custom_call_target="tpu_custom_call" | custom-call | tf_op jit(solution)/shard_map/pallas_call | solution.py:121
  (52 shorter events, 6.2 us)
Async XLA Ops:
  0.0 45.8 %copy-start = (bf16[1,16,6,128,128]{4,3,2,1,0:T(8,128)(2,1)S(1)}, bf16[1,16,6,128,128]{4,3,2,1,0:T(8,128)(2,1)}, u32[]{:S(2)}) copy-start(bf16[1,16,6,128,128]{4,3,2,1,0:T(8,128)(2,1)} %param.15) | copy-start | bytes 9437188
  0.8 40.8 %copy-start.10 = (f32[16]{0:T(128)}, f32[16]{0:T(128)S(1)}, u32[]{:S(2)}) copy-start(f32[16]{0:T(128)S(1)} %or_convert_fusion) | copy-start | bytes 196
  2.7 38.9 %copy-start.3 = (bf16[1,16,32,128]{3,2,1,0:T(8,128)(2,1)}, bf16[1,16,32,128]{3,2,1,0:T(8,128)(2,1)S(1)}, u32[]{:S(2)}) copy-start(bf16[1,16,32,128]{3,2,1,0:T(8,128)(2,1)S(1)} %get-tuple-element.12) | copy-start | bytes 393220
  2.7 14.4 %collective-permute-start.1 = (f32[512,128]{1,0:T(8,128)}, f32[512,128]{1,0:T(8,128)}, u32[]{:S(2)}, u32[]{:S(2)}) collective-permute-start(f32[512,128]{1,0:T(8,128)} %bitcast.2.own_ref), channel_id=1, source_target_pairs={{0,256},{32,288},{64,320},{96,352},{128,384},{160,416},{192,448},{... | collective-permute-start | bytes 786440 | tf_op jit(solution)/shard_map/ppermute | solution.py:49
  6.8 15.5 %collective-permute-start = (f32[512,128]{1,0:T(8,128)}, f32[512,128]{1,0:T(8,128)}, u32[]{:S(2)}, u32[]{:S(2)}) collective-permute-start(f32[512,128]{1,0:T(8,128)} %bitcast.2.own_ref), channel_id=1, source_target_pairs={{0,32},{32,0},{64,96},{96,64},{128,160},{160,128},{192,224},{224,1... | collective-permute-start | bytes 786440 | tf_op jit(solution)/shard_map/ppermute | solution.py:49
  14.1 6.6 %copy-start.11 = (f32[4]{0:T(128)}, f32[4]{0:T(128)S(1)}, u32[]{:S(2)}) copy-start(f32[4]{0:T(128)S(1)} %convert_bitcast_fusion) | copy-start | bytes 52
  15.8 1.2 %copy-start.4 = (f32[4,32,128]{2,1,0:T(8,128)}, f32[4,32,128]{2,1,0:T(8,128)S(1)}, u32[]{:S(2)}) copy-start(f32[4,32,128]{2,1,0:T(8,128)S(1)} %fusion.12) | copy-start | bytes 196612
  17.1 5.1 %collective-permute-start.2 = (f32[512,128]{1,0:T(8,128)}, f32[512,128]{1,0:T(8,128)}, u32[]{:S(2)}, u32[]{:S(2)}) collective-permute-start(f32[512,128]{1,0:T(8,128)} %collective-permute-done.1.across_ref), channel_id=1, source_target_pairs={{0,32},{32,0},{64,96},{96,64},{128,160},{160,128},{192,224},{224,1... | collective-permute-start | bytes 786440 | tf_op jit(solution)/shard_map/ppermute | solution.py:49
  22.3 23.5 %copy-start.1 = (f32[1,16,32,128]{3,2,1,0:T(8,128)S(1)}, f32[1,16,32,128]{3,2,1,0:T(8,128)}, u32[]{:S(2)}) copy-start(f32[1,16,32,128]{3,2,1,0:T(8,128)} %param.12) | copy-start | bytes 786436
  24.8 23.6 %all-to-all-start = ((f32[4,512,128]{2,1,0:T(8,128)}), f32[4,512,128]{2,1,0:T(8,128)}, u32[]{:S(2)}, u32[]{:S(2)}) async-start(f32[4,512,128]{2,1,0:T(8,128)} %shard_map.109), calls=%async_computation | async-start | bytes 2097152 | tf_op jit(solution)/shard_map/all_to_all | solution.py:136
  29.0 12.6 %collective-permute-start.3 = (bf16[1,5,32,128]{3,2,1,0:T(8,128)(2,1)}, bf16[1,5,32,128]{3,2,1,0:T(8,128)(2,1)S(1)}, u32[]{:S(2)}, u32[]{:S(2)}) collective-permute-start(bf16[1,5,32,128]{3,2,1,0:T(8,128)(2,1)} %pad_maximum_fusion), channel_id=1, source_target_pairs={{31,0},{0,1},{1,2},{2,3},{3,4},{4,5},{5,6},{6,7},{7,8},{8,9},{9,10... | collective-permute-start | bytes 122888 | tf_op jit(solution)/shard_map/ppermute | solution.py:32
  31.0 10.8 %collective-permute-start.4 = (bf16[1,1,32,128]{3,2,1,0:T(8,128)(2,1)S(1)}, bf16[1,1,32,128]{3,2,1,0:T(8,128)(2,1)S(1)}, u32[]{:S(2)}, u32[]{:S(2)}) collective-permute-start(bf16[1,1,32,128]{3,2,1,0:T(8,128)(2,1)S(1)} %slice.33), channel_id=1, source_target_pairs={{1,0},{2,1},{3,2},{4,3},{5,4},{6,5},{7,6},{8,7},{9,8},{10,9},{11,1... | collective-permute-start | bytes 24584 | tf_op jit(solution)/shard_map/ppermute | solution.py:32
  41.6 0.6 copy-start.8
  45.8 19.2 %copy-start.12 = (f32[4]{0:T(128)S(1)}, f32[4]{0:T(128)}, u32[]{:S(2)}) copy-start(f32[4]{0:T(128)} %copy-done.11) | copy-start | bytes 52
  50.6 9.5 %collective-permute-start.6 = (f32[512,128]{1,0:T(8,128)}, f32[512,128]{1,0:T(8,128)S(1)}, u32[]{:S(2)}, u32[]{:S(2)}) collective-permute-start(f32[512,128]{1,0:T(8,128)} %get-tuple-element.13.own_ref), channel_id=1, source_target_pairs={{0,256},{32,288},{64,320},{96,352},{128,384},{160,416},{192,448},{... | collective-permute-start | bytes 786440 | tf_op jit(solution)/shard_map/ppermute | solution.py:49
  52.9 12.8 %collective-permute-start.5 = (f32[512,128]{1,0:T(8,128)}, f32[512,128]{1,0:T(8,128)S(1)}, u32[]{:S(2)}, u32[]{:S(2)}) collective-permute-start(f32[512,128]{1,0:T(8,128)} %get-tuple-element.13.own_ref), channel_id=1, source_target_pairs={{0,32},{32,0},{64,96},{96,64},{128,160},{160,128},{192,224},{224,1... | collective-permute-start | bytes 786440 | tf_op jit(solution)/shard_map/ppermute | solution.py:49
  56.5 26.3 %copy-start.2 = (bf16[1,16,32,128]{3,2,1,0:T(8,128)(2,1)}, bf16[1,16,32,128]{3,2,1,0:T(8,128)(2,1)S(1)}, u32[]{:S(2)}) copy-start(bf16[1,16,32,128]{3,2,1,0:T(8,128)(2,1)S(1)} %convert_element_type.52) | copy-start | bytes 393220
  60.1 5.6 %copy-start.6 = (f32[512,128]{1,0:T(8,128)}, f32[512,128]{1,0:T(8,128)S(1)}, u32[]{:S(2)}) copy-start(f32[512,128]{1,0:T(8,128)S(1)} %collective-permute-done.6.across_ref) | copy-start | bytes 786436
  60.1 6.3 %collective-permute-start.7 = (f32[512,128]{1,0:T(8,128)S(1)}, f32[512,128]{1,0:T(8,128)}, u32[]{:S(2)}, u32[]{:S(2)}) collective-permute-start(f32[512,128]{1,0:T(8,128)S(1)} %collective-permute-done.6.across_ref), channel_id=1, source_target_pairs={{0,32},{32,0},{64,96},{96,64},{128,160},{160,128},{192,224},{224,1... | collective-permute-start | bytes 786440 | tf_op jit(solution)/shard_map/ppermute | solution.py:49
  64.3 0.6 copy-start.5
  65.7 0.7 copy-start.7
  68.8 20.8 %all-to-all-start.1 = ((f32[4,512,128]{2,1,0:T(8,128)}), f32[4,512,128]{2,1,0:T(8,128)}, u32[]{:S(2)}, u32[]{:S(2)}) async-start(f32[4,512,128]{2,1,0:T(8,128)} %shard_map.111), calls=%async_computation.1 | async-start | bytes 2097152 | tf_op jit(solution)/shard_map/all_to_all | solution.py:136
  73.8 8.9 %collective-permute-start.8 = (bf16[1,5,32,128]{3,2,1,0:T(8,128)(2,1)S(1)}, bf16[1,5,32,128]{3,2,1,0:T(8,128)(2,1)S(1)}, u32[]{:S(2)}, u32[]{:S(2)}) collective-permute-start(bf16[1,5,32,128]{3,2,1,0:T(8,128)(2,1)S(1)} %pad_maximum_fusion.1), channel_id=1, source_target_pairs={{31,0},{0,1},{1,2},{2,3},{3,4},{4,5},{5,6},{6,7},{7,8},{8,9},{9,10... | collective-permute-start | bytes 122888 | tf_op jit(solution)/shard_map/ppermute | solution.py:32
  75.8 7.8 %collective-permute-start.9 = (bf16[1,1,32,128]{3,2,1,0:T(8,128)(2,1)S(1)}, bf16[1,1,32,128]{3,2,1,0:T(8,128)(2,1)S(1)}, u32[]{:S(2)}, u32[]{:S(2)}) collective-permute-start(bf16[1,1,32,128]{3,2,1,0:T(8,128)(2,1)S(1)} %slice.38), channel_id=1, source_target_pairs={{1,0},{2,1},{3,2},{4,3},{5,4},{6,5},{7,6},{8,7},{9,8},{10,9},{11,1... | collective-permute-start | bytes 24584 | tf_op jit(solution)/shard_map/ppermute | solution.py:32
  82.8 0.8 copy-start.9

commit v14 on v12

--- a/solution.py
+++ b/solution.py
@@ -66,14 +66,14 @@
     return table.astype(np.float32)
 
 
-def mix_kernel(index_ref, coef_ref, own_ref, mate_ref, across_ref, diagonal_ref, o_ref):
+def mix_kernel(index_ref, coef_ref, own_ref, across_ref, pair_ref, o_ref):
     me = index_ref[0]
     coef = [[coef_ref[me, slot * 4 + m] for m in range(4)] for slot in range(4)]
     chunk = 32
 
     def step(c, carry):
         rows = pl.ds(pl.multiple_of(c * chunk, chunk), chunk)
-        values = (own_ref[rows, :], mate_ref[rows, :], across_ref[rows, :], diagonal_ref[rows, :])
+        values = (own_ref[rows, :], pair_ref[0, rows, :], across_ref[rows, :], pair_ref[1, rows, :])
         for slot in range(4):
             acc = coef[slot][0] * values[0]
             for m in range(1, 4):
@@ -84,7 +84,7 @@
     lax.fori_loop(0, own_ref.shape[0] // chunk, step, 0, unroll=True)
 
 
-def partial_sums(index, own, mate, across, diagonal):
+def partial_sums(index, own, across, pair):
     rows, lanes = own.shape
     block = 256
     flat = pl.BlockSpec((block, lanes), lambda r, index: (r, 0))
@@ -93,11 +93,11 @@
         grid_spec=pltpu.PrefetchScalarGridSpec(
             num_scalar_prefetch=1,
             grid=(rows // block,),
-            in_specs=[pl.BlockSpec(memory_space=pltpu.SMEM), flat, flat, flat, flat],
+            in_specs=[pl.BlockSpec(memory_space=pltpu.SMEM), flat, flat, pl.BlockSpec((2, block, lanes), lambda r, index: (0, r, 0))],
             out_specs=pl.BlockSpec((4, block, lanes), lambda r, index: (0, r, 0)),
         ),
         out_shape=jax.ShapeDtypeStruct((4, rows, lanes), jnp.float32),
-    )(index, jnp.asarray(coefficient_table()), own, mate, across, diagonal)
+    )(index, jnp.asarray(coefficient_table()), own, across, pair)
 
 
 def update_kernel(got_ref, base_ref, scale_ref, cond_ref, lam_ref, *rest):
@@ -129,10 +129,9 @@
 
 def instance_mix(flat):
     i = lax.axis_index("iy") * 8 + lax.axis_index("ix") * 2 + lax.axis_index("ic")
-    mate = routed(flat, lambda s: s ^ 1)
     across = routed(flat, lambda s: s ^ 8)
-    diagonal = routed(across, lambda s: s ^ 1)
-    partials = partial_sums(jnp.reshape(i, (1,)).astype(jnp.int32), flat, mate, across, diagonal)
+    pair = routed(jnp.stack([flat, across]), lambda s: s ^ 1)
+    partials = partial_sums(jnp.reshape(i, (1,)).astype(jnp.int32), flat, across, pair)
     return partials, lax.all_to_all(partials, "ix", 0, 0)
 
 

time: 92.5 us -> 97.1 us (1.050)
  waiting for transfers between devices: 4.49 us -> 8.78 us
  starting transfers between devices: 51.1 us -> 48.1 us
  other arithmetic: 13.2 us -> 15.1 us
  local copies, waits for them, and re-layouts: 5.39 us -> 6.78 us
    ppermute x6 -> x4, waiting for transfers between devices: 3.6 us -> 8.04 us  [routed(): return lax.ppermute(block, INST, [(s, dest(s)) for s in range(NT)])]
    ppermute x6 -> x4, starting transfers between devices: 21.8 us -> 18.6 us  [routed(): return lax.ppermute(block, INST, [(s, dest(s)) for s in range(NT)])]
    another operation x0 -> x2, other arithmetic: none -> 2 us  [instance_mix(): pair = routed(jnp.stack([flat, across]), lambda s: s ^ 1)]
  transfers between devices with their start and end apart: 12 -> 10, of which waited for: 3 -> 3; matrix products, arithmetic and copies ran while one was open for 24% -> 25% of each run, Pallas kernels for 0% -> 0%
where the time goes in v14:
time: 97.1 us; the launch traced here: 95.6 us
  starting transfers between devices  48.1 us (50%)
  other arithmetic  15.1 us (16%)
  waiting for transfers between devices  8.78 us (9%)
  Pallas kernels  8.53 us (9%)
  matrix products  7.27 us (7%)
  local copies, waits for them, and re-layouts  6.78 us (7%)
  between operations  1.05 us (1%)
    ppermute x4, starting transfers between devices, shifted(): return lax.ppermute(block, axis, route)  20.8 us
    ppermute x4, starting transfers between devices, routed(): return lax.ppermute(block, INST, [(s, dest(s)) for s in range(NT)])  18.6 us
    all_to_all x2, starting transfers between devices, instance_mix(): return (partials, lax.all_to_all(partials, 'ix', 0, 0))  8.63 us
    ppermute x4, waiting for transfers between devices, routed(): return lax.ppermute(block, INST, [(s, dest(s)) for s in range(NT)])  8.04 us
    dot_general x2, matrix products, shards(): jnp.einsum('tnkri,tnkio->tnro', picked, jac, preferred_element_type=jnp.f...  5.12 us
    pallas_call x2, Pallas kernels, partial_sums(): pl.pallas_call(mix_kernel, grid_spec=pltpu.PrefetchScalarGridSpec(num_sca...  4.49 us
    pallas_call x2, Pallas kernels, updated(): pl.pallas_call(update_kernel, grid=(rows // block,), in_specs=[pl.BlockSp...  4.05 us
    gather x2, local copies, waits for them, and re-layouts, shards(): picked = lam_h[:, cols]  3.4 us
  transfers between devices with their start and end apart: 10, of which 3 were waited for; matrix products, arithmetic and copies ran while one was open for 25% of the time, Pallas kernels for 0%

profile of v14, /device:TPU:1, one launch (start us, length us, event | category | flops | bytes accessed | tf_op | source)
XLA Modules:
  0.0 95.6 jit_solution(16424495060509355507)
XLA Ops:
  0.8 1.2 %multiply_convert_fusion = (bf16[1,16,32,128]{3,2,1,0:T(8,128)(2,1)S(1)}, f32[1,16,32,128]{3,2,1,0:T(8,128)S(1)}) fusion(f32[1,16,32,128]{3,2,1,0:T(8,128)} %param.11, f32[16]{0:T(128)S(1)} %or_convert_fusion, f32[16,128]{1,0:T(8,128)} %cond_ref.3), kind=kLoop, calls=%fused_computation.12 | loop fusion | flops 196608 | bytes 663616 | tf_op jit(solution)/shard_map/convert_element_type | solution.py:153
  2.0 4.0 %collective-permute-start = (f32[512,128]{1,0:T(8,128)S(1)}, f32[512,128]{1,0:T(8,128)}, u32[]{:S(2)}, u32[]{:S(2)}) collective-permute-start(f32[512,128]{1,0:T(8,128)S(1)} %bitcast.68), channel_id=1, source_target_pairs={{0,256},{32,288},{64,320},{96,352},{128,384},{160,416},{192,448},{... | collective-permute-start | bytes 786440 | tf_op jit(solution)/shard_map/ppermute | solution.py:49
  6.8 1.1 %fusion.12 = f32[4,32,128]{2,1,0:T(8,128)S(1)} fusion(bf16[1,4,128,128]{3,2,1,0:T(8,128)(2,1)} %param.16, bf16[1,16,32,128]{3,2,1,0:T(8,128)(2,1)S(1)} %get-tuple-element.12), kind=kOutput, calls=%fused_computation.18 | convolution fusion | flops 4194304 | bytes 229376 | tf_op jit(solution)/shard_map/tjri,tjio->tjro/dot_general | solution.py:155
  9.9 1.0 %pad_maximum_fusion = f32[2,512,128]{2,1,0:T(8,128)S(1)} fusion(f32[1,512,128]{2,1,0:T(8,128)} %bitcast.4, f32[1,512,128]{2,1,0:T(8,128)S(1)} %bitcast.69), kind=kLoop, calls=%fused_computation.8 | loop fusion | flops 131072 | bytes 1048576 | tf_op jit(solution)/shard_map/stack | solution.py:133
  10.9 9.3 %collective-permute-start.1 = (f32[2,512,128]{2,1,0:T(8,128)S(1)}, f32[2,512,128]{2,1,0:T(8,128)}, u32[]{:S(2)}, u32[]{:S(2)}) collective-permute-start(f32[2,512,128]{2,1,0:T(8,128)S(1)} %pad_maximum_fusion), channel_id=1, source_target_pairs={{0,32},{32,0},{64,96},{96,64},{128,160},{160,128},{192,224},{224,1... | collective-permute-start | bytes 1572872 | tf_op jit(solution)/shard_map/ppermute | solution.py:49
  20.8 1.2 %broadcast_subtract_fusion = f32[4]{0:T(128)} fusion(s32[1,4]{1,0:T(1,128)} %param.18), kind=kLoop, calls=%fused_computation.35 | loop fusion | flops 8 | bytes 32 | tf_op jit(solution)/shard_map/sub | solution.py:169
  22.0 1.4 %broadcast_multiply_fusion.scale_ref = f32[16,128]{1,0:T(8,128)} fusion(f32[16]{0:T(128)S(1)} %or_convert_fusion, f32[1,16,128]{2,1,0:T(8,128)} %param.13), kind=kLoop, calls=%fused_computation.32 | loop fusion | flops 2048 | bytes 16448 | tf_op jit(solution)/shard_map/mul | solution.py:150
  23.4 2.2 %shard_map.109 = f32[4,512,128]{2,1,0:T(8,128)} custom-call(s32[1]{0:T(128)} %bitcast.index_ref, f32[16,16]{1,0:T(8,128)} %constant.32.clone.coef_ref, f32[512,128]{1,0:T(8,128)} %bitcast.70, f32[512,128]{1,0:T(8,128)} %collective-permute-done.across_ref, f32[2,512,128]{2,1,0:T(8,128)} %collective-permute-done.1.pair_ref), custom_call_target="tpu_custom_call" | custom-call | tf_op jit(solution)/shard_map/pallas_call | solution.py:91
  25.6 4.4 %all-to-all-start = ((f32[4,512,128]{2,1,0:T(8,128)}), f32[4,512,128]{2,1,0:T(8,128)}, u32[]{:S(2)}, u32[]{:S(2)}) async-start(f32[4,512,128]{2,1,0:T(8,128)} %shard_map.109), calls=%async_computation | async-start | bytes 2097152 | tf_op jit(solution)/shard_map/all_to_all | solution.py:135
  30.0 1.9 %collective-permute-start.2 = (bf16[1,5,32,128]{3,2,1,0:T(8,128)(2,1)}, bf16[1,5,32,128]{3,2,1,0:T(8,128)(2,1)S(1)}, u32[]{:S(2)}, u32[]{:S(2)}) collective-permute-start(bf16[1,5,32,128]{3,2,1,0:T(8,128)(2,1)} %pad_maximum_fusion.2), channel_id=1, source_target_pairs={{31,0},{0,1},{1,2},{2,3},{3,4},{4,5},{5,6},{6,7},{7,8},{8,9},{9,10... | collective-permute-start | bytes 122888 | tf_op jit(solution)/shard_map/ppermute | solution.py:32
  32.6 10.0 %collective-permute-start.3 = (bf16[1,1,32,128]{3,2,1,0:T(8,128)(2,1)S(1)}, bf16[1,1,32,128]{3,2,1,0:T(8,128)(2,1)S(1)}, u32[]{:S(2)}, u32[]{:S(2)}) collective-permute-start(bf16[1,1,32,128]{3,2,1,0:T(8,128)(2,1)S(1)} %slice.33), channel_id=1, source_target_pairs={{1,0},{2,1},{3,2},{4,3},{5,4},{6,5},{7,6},{8,7},{9,8},{10,9},{11,1... | collective-permute-start | bytes 24584 | tf_op jit(solution)/shard_map/ppermute | solution.py:32
  42.7 1.2 %pad_clamp_fusion = s32[1024]{0:T(1024)} fusion(s32[96]{0:T(128)} %reshape.113), kind=kLoop, calls=%fused_computation.31 | loop fusion | flops 1024 | bytes 4480 | tf_op jit(solution)/shard_map/gather | solution.py:166
  44.5 0.9 maximum_bitcast_fusion
  45.4 1.7 %gather_fusion = bf16[96,32,128]{2,1,0:T(8,128)(2,1)} fusion(bf16[18,32,128]{2,1,0:T(8,128)(2,1)S(1)} %maximum_bitcast_fusion, s32[1024]{0:T(1024)} %pad_clamp_fusion), kind=kCustom, calls=%fused_computation | custom fusion | bytes 1573248 | tf_op jit(solution)/shard_map/gather | solution.py:166
  47.1 0.9 bitcast_add_fusion.1
  48.1 2.6 %multiply_add_fusion.1 = f32[1,16,32,128]{3,2,1,0:T(8,128)} fusion(f32[1,16,32,128]{3,2,1,0:T(8,128)S(1)} %copy-done.2, f32[1,4,32,128]{3,2,1,0:T(8,128)S(1)} %bitcast_add_fusion.1, f32[1,16,32,128]{3,2,1,0:T(8,128)} %param.11, f32[16,128]{1,0:T(8,128)} %bitcast.77, f32[16]{0:T(128)} %copy-done.10, bf16[16,6,32,128]{3,2,1,0:T(8,128)(2,1)} %bitcast.67, ...), kind=kOutput, calls=%fused_computation.11 | convolution fusion | flops 101056512 | bytes 4792384 | tf_op jit(solution)/shard_map/tnkri,tnkio->tnro/dot_general | solution.py:167
  50.7 2.1 %shard_map.110 = (f32[512,128]{1,0:T(8,128)}, f32[512,128]{1,0:T(8,128)}) custom-call(f32[4,512,128]{2,1,0:T(8,128)} %all-to-all-done.got_ref, f32[512,128]{1,0:T(8,128)} %bitcast.76, f32[16,128]{1,0:T(8,128)} %broadcast_multiply_fusion.scale_ref, f32[16,128]{1,0:T(8,128)} %cond_ref.3), custom_call_target="tpu_custom_call" | custom-call | tf_op jit(solution)/shard_map/pallas_call | solution.py:121
  52.7 2.3 %collective-permute-start.4 = (f32[512,128]{1,0:T(8,128)}, f32[512,128]{1,0:T(8,128)S(1)}, u32[]{:S(2)}, u32[]{:S(2)}) collective-permute-start(f32[512,128]{1,0:T(8,128)} %get-tuple-element.13.own_ref), channel_id=1, source_target_pairs={{0,256},{32,288},{64,320},{96,352},{128,384},{160,416},{192,448},{... | collective-permute-start | bytes 786440 | tf_op jit(solution)/shard_map/ppermute | solution.py:49
  55.0 7.4 %collective-permute-done.4.across_ref = f32[512,128]{1,0:T(8,128)S(1)} collective-permute-done((f32[512,128]{1,0:T(8,128)}, f32[512,128]{1,0:T(8,128)S(1)}, u32[]{:S(2)}, u32[]{:S(2)}) %collective-permute-start.4) | collective-permute-done | bytes 262176 | tf_op jit(solution)/shard_map/ppermute | solution.py:49
  63.1 1.0 %pad_maximum_fusion.1 = f32[2,512,128]{2,1,0:T(8,128)S(1)} fusion(f32[1,512,128]{2,1,0:T(8,128)S(1)} %bitcast.75, f32[1,512,128]{2,1,0:T(8,128)} %bitcast.74), kind=kLoop, calls=%fused_computation.9 | loop fusion | flops 131072 | bytes 1048576 | tf_op jit(solution)/shard_map/stack | solution.py:133
  64.1 3.1 %collective-permute-start.5 = (f32[2,512,128]{2,1,0:T(8,128)S(1)}, f32[2,512,128]{2,1,0:T(8,128)}, u32[]{:S(2)}, u32[]{:S(2)}) collective-permute-start(f32[2,512,128]{2,1,0:T(8,128)S(1)} %pad_maximum_fusion.1), channel_id=1, source_target_pairs={{0,32},{32,0},{64,96},{96,64},{128,160},{160,128},{192,224},{224,1... | collective-permute-start | bytes 1572872 | tf_op jit(solution)/shard_map/ppermute | solution.py:49
  67.2 1.0 %convert_element_type.52 = bf16[1,16,32,128]{3,2,1,0:T(8,128)(2,1)S(1)} convert(f32[1,16,32,128]{3,2,1,0:T(8,128)} %bitcast.72) | non-fusion elementwise | flops 65536 | bytes 393216 | tf_op jit(solution)/shard_map/convert_element_type | solution.py:153
  68.2 1.1 %fusion.10 = f32[4,32,128]{2,1,0:T(8,128)S(1)} fusion(bf16[1,4,128,128]{3,2,1,0:T(8,128)(2,1)} %param.16, bf16[1,16,32,128]{3,2,1,0:T(8,128)(2,1)S(1)} %convert_element_type.52), kind=kOutput, calls=%fused_computation.16 | convolution fusion | flops 4194304 | bytes 229376 | tf_op jit(solution)/shard_map/tjri,tjio->tjro/dot_general | solution.py:155
  70.6 2.2 %shard_map.111 = f32[4,512,128]{2,1,0:T(8,128)} custom-call(s32[1]{0:T(128)} %bitcast.index_ref, f32[16,16]{1,0:T(8,128)} %constant.32.clone.coef_ref, f32[512,128]{1,0:T(8,128)} %get-tuple-element.13.own_ref, f32[512,128]{1,0:T(8,128)} %copy-done.3, f32[2,512,128]{2,1,0:T(8,128)} %collective-permute-done.5.pair_ref), custom_call_target="tpu_custom_call" | custom-call | tf_op jit(solution)/shard_map/pallas_call | solution.py:91
  72.8 4.3 %all-to-all-start.1 = ((f32[4,512,128]{2,1,0:T(8,128)}), f32[4,512,128]{2,1,0:T(8,128)}, u32[]{:S(2)}, u32[]{:S(2)}) async-start(f32[4,512,128]{2,1,0:T(8,128)} %shard_map.111), calls=%async_computation.1 | async-start | bytes 2097152 | tf_op jit(solution)/shard_map/all_to_all | solution.py:135
  77.8 1.9 %collective-permute-start.6 = (bf16[1,5,32,128]{3,2,1,0:T(8,128)(2,1)S(1)}, bf16[1,5,32,128]{3,2,1,0:T(8,128)(2,1)S(1)}, u32[]{:S(2)}, u32[]{:S(2)}) collective-permute-start(bf16[1,5,32,128]{3,2,1,0:T(8,128)(2,1)S(1)} %pad_maximum_fusion.3), channel_id=1, source_target_pairs={{31,0},{0,1},{1,2},{2,3},{3,4},{4,5},{5,6},{6,7},{7,8},{8,9},{9,10... | collective-permute-start | bytes 122888 | tf_op jit(solution)/shard_map/ppermute | solution.py:32
  79.8 7.0 %collective-permute-start.7 = (bf16[1,1,32,128]{3,2,1,0:T(8,128)(2,1)S(1)}, bf16[1,1,32,128]{3,2,1,0:T(8,128)(2,1)S(1)}, u32[]{:S(2)}, u32[]{:S(2)}) collective-permute-start(bf16[1,1,32,128]{3,2,1,0:T(8,128)(2,1)S(1)} %slice.38), channel_id=1, source_target_pairs={{1,0},{2,1},{3,2},{4,3},{5,4},{6,5},{7,6},{8,7},{9,8},{10,9},{11,1... | collective-permute-start | bytes 24584 | tf_op jit(solution)/shard_map/ppermute | solution.py:32
  87.5 0.9 maximum_bitcast_fusion.1
  88.4 1.7 %gather_fusion.1 = bf16[96,32,128]{2,1,0:T(8,128)(2,1)} fusion(bf16[18,32,128]{2,1,0:T(8,128)(2,1)S(1)} %maximum_bitcast_fusion.1, s32[1024]{0:T(1024)} %pad_clamp_fusion), kind=kCustom, calls=%fused_computation.1 | custom fusion | bytes 1573248 | tf_op jit(solution)/shard_map/gather | solution.py:166
  90.1 0.9 bitcast_add_fusion
  91.1 2.6 %multiply_add_fusion = f32[1,16,32,128]{3,2,1,0:T(8,128)} fusion(f32[1,16,32,128]{3,2,1,0:T(8,128)} %bitcast.73, f32[1,16,32,128]{3,2,1,0:T(8,128)S(1)} %copy-done.2, f32[1,4,32,128]{3,2,1,0:T(8,128)S(1)} %bitcast_add_fusion, f32[16,128]{1,0:T(8,128)} %bitcast.78, f32[16]{0:T(128)} %copy-done.10, bf16[16,6,32,128]{3,2,1,0:T(8,128)(2,1)} %bitcast.66, ...), kind=kOutput, calls=%fused_computation.10 | convolution fusion | flops 100990976 | bytes 4792384 | tf_op jit(solution)/shard_map/tnkri,tnkio->tnro/dot_general | solution.py:167
  93.6 2.0 %shard_map.112 = f32[512,128]{1,0:T(8,128)} custom-call(f32[4,512,128]{2,1,0:T(8,128)} %all-to-all-done.1.got_ref, f32[512,128]{1,0:T(8,128)} %bitcast.71, f32[16,128]{1,0:T(8,128)} %broadcast_multiply_fusion.scale_ref, f32[16,128]{1,0:T(8,128)} %cond_ref.3), custom_call_target="tpu_custom_call" | custom-call | tf_op jit(solution)/shard_map/pallas_call | solution.py:121
  (50 shorter events, 8.3 us)
Async XLA Ops:
  0.0 48.1 %copy-start = (bf16[1,16,6,128,128]{4,3,2,1,0:T(8,128)(2,1)S(1)}, bf16[1,16,6,128,128]{4,3,2,1,0:T(8,128)(2,1)}, u32[]{:S(2)}) copy-start(bf16[1,16,6,128,128]{4,3,2,1,0:T(8,128)(2,1)} %param.15) | copy-start | bytes 9437188
  0.8 22.5 %copy-start.10 = (f32[16]{0:T(128)}, f32[16]{0:T(128)S(1)}, u32[]{:S(2)}) copy-start(f32[16]{0:T(128)S(1)} %or_convert_fusion) | copy-start | bytes 196
  2.0 6.5 %copy-start.5 = (bf16[1,16,32,128]{3,2,1,0:T(8,128)(2,1)}, bf16[1,16,32,128]{3,2,1,0:T(8,128)(2,1)S(1)}, u32[]{:S(2)}) copy-start(bf16[1,16,32,128]{3,2,1,0:T(8,128)(2,1)S(1)} %get-tuple-element.12) | copy-start | bytes 393220
  2.0 21.3 %copy-start.1 = (f32[1,16,32,128]{3,2,1,0:T(8,128)}, f32[1,16,32,128]{3,2,1,0:T(8,128)S(1)}, u32[]{:S(2)}) copy-start(f32[1,16,32,128]{3,2,1,0:T(8,128)S(1)} %get-tuple-element.18) | copy-start | bytes 786436
  2.0 7.9 %collective-permute-start = (f32[512,128]{1,0:T(8,128)S(1)}, f32[512,128]{1,0:T(8,128)}, u32[]{:S(2)}, u32[]{:S(2)}) collective-permute-start(f32[512,128]{1,0:T(8,128)S(1)} %bitcast.68), channel_id=1, source_target_pairs={{0,256},{32,288},{64,320},{96,352},{128,384},{160,416},{192,448},{... | collective-permute-start | bytes 786440 | tf_op jit(solution)/shard_map/ppermute | solution.py:49
  7.8 15.5 %copy-start.6 = (f32[4,32,128]{2,1,0:T(8,128)}, f32[4,32,128]{2,1,0:T(8,128)S(1)}, u32[]{:S(2)}) copy-start(f32[4,32,128]{2,1,0:T(8,128)S(1)} %fusion.12) | copy-start | bytes 196612
  8.5 14.9 %copy-start.11 = (f32[4]{0:T(128)}, f32[4]{0:T(128)S(1)}, u32[]{:S(2)}) copy-start(f32[4]{0:T(128)S(1)} %convert_bitcast_fusion) | copy-start | bytes 52
  10.9 12.4 %collective-permute-start.1 = (f32[2,512,128]{2,1,0:T(8,128)S(1)}, f32[2,512,128]{2,1,0:T(8,128)}, u32[]{:S(2)}, u32[]{:S(2)}) collective-permute-start(f32[2,512,128]{2,1,0:T(8,128)S(1)} %pad_maximum_fusion), channel_id=1, source_target_pairs={{0,32},{32,0},{64,96},{96,64},{128,160},{160,128},{192,224},{224,1... | collective-permute-start | bytes 1572872 | tf_op jit(solution)/shard_map/ppermute | solution.py:49
  25.6 22.5 %copy-start.2 = (f32[1,16,32,128]{3,2,1,0:T(8,128)S(1)}, f32[1,16,32,128]{3,2,1,0:T(8,128)}, u32[]{:S(2)}) copy-start(f32[1,16,32,128]{3,2,1,0:T(8,128)} %param.12) | copy-start | bytes 786436
  25.6 25.0 %all-to-all-start = ((f32[4,512,128]{2,1,0:T(8,128)}), f32[4,512,128]{2,1,0:T(8,128)}, u32[]{:S(2)}, u32[]{:S(2)}) async-start(f32[4,512,128]{2,1,0:T(8,128)} %shard_map.109), calls=%async_computation | async-start | bytes 2097152 | tf_op jit(solution)/shard_map/all_to_all | solution.py:135
  30.0 13.9 %collective-permute-start.2 = (bf16[1,5,32,128]{3,2,1,0:T(8,128)(2,1)}, bf16[1,5,32,128]{3,2,1,0:T(8,128)(2,1)S(1)}, u32[]{:S(2)}, u32[]{:S(2)}) collective-permute-start(bf16[1,5,32,128]{3,2,1,0:T(8,128)(2,1)} %pad_maximum_fusion.2), channel_id=1, source_target_pairs={{31,0},{0,1},{1,2},{2,3},{3,4},{4,5},{5,6},{6,7},{7,8},{8,9},{9,10... | collective-permute-start | bytes 122888 | tf_op jit(solution)/shard_map/ppermute | solution.py:32
  32.6 11.9 %collective-permute-start.3 = (bf16[1,1,32,128]{3,2,1,0:T(8,128)(2,1)S(1)}, bf16[1,1,32,128]{3,2,1,0:T(8,128)(2,1)S(1)}, u32[]{:S(2)}, u32[]{:S(2)}) collective-permute-start(bf16[1,1,32,128]{3,2,1,0:T(8,128)(2,1)S(1)} %slice.33), channel_id=1, source_target_pairs={{1,0},{2,1},{3,2},{4,3},{5,4},{6,5},{7,6},{8,7},{9,8},{10,9},{11,1... | collective-permute-start | bytes 24584 | tf_op jit(solution)/shard_map/ppermute | solution.py:32
  43.9 0.6 copy-start.8
  48.1 21.8 %copy-start.12 = (f32[4]{0:T(128)S(1)}, f32[4]{0:T(128)}, u32[]{:S(2)}) copy-start(f32[4]{0:T(128)} %copy-done.11) | copy-start | bytes 52
  52.7 9.7 %collective-permute-start.4 = (f32[512,128]{1,0:T(8,128)}, f32[512,128]{1,0:T(8,128)S(1)}, u32[]{:S(2)}, u32[]{:S(2)}) collective-permute-start(f32[512,128]{1,0:T(8,128)} %get-tuple-element.13.own_ref), channel_id=1, source_target_pairs={{0,256},{32,288},{64,320},{96,352},{128,384},{160,416},{192,448},{... | collective-permute-start | bytes 786440 | tf_op jit(solution)/shard_map/ppermute | solution.py:49
  62.4 0.7 copy-start.3
  64.1 6.5 %collective-permute-start.5 = (f32[2,512,128]{2,1,0:T(8,128)S(1)}, f32[2,512,128]{2,1,0:T(8,128)}, u32[]{:S(2)}, u32[]{:S(2)}) collective-permute-start(f32[2,512,128]{2,1,0:T(8,128)S(1)} %pad_maximum_fusion.1), channel_id=1, source_target_pairs={{0,32},{32,0},{64,96},{96,64},{128,160},{160,128},{192,224},{224,1... | collective-permute-start | bytes 1572872 | tf_op jit(solution)/shard_map/ppermute | solution.py:49
  68.1 18.6 %copy-start.4 = (bf16[1,16,32,128]{3,2,1,0:T(8,128)(2,1)}, bf16[1,16,32,128]{3,2,1,0:T(8,128)(2,1)S(1)}, u32[]{:S(2)}) copy-start(bf16[1,16,32,128]{3,2,1,0:T(8,128)(2,1)S(1)} %convert_element_type.52) | copy-start | bytes 393220
  69.2 0.6 copy-start.7
  72.8 20.8 %all-to-all-start.1 = ((f32[4,512,128]{2,1,0:T(8,128)}), f32[4,512,128]{2,1,0:T(8,128)}, u32[]{:S(2)}, u32[]{:S(2)}) async-start(f32[4,512,128]{2,1,0:T(8,128)} %shard_map.111), calls=%async_computation.1 | async-start | bytes 2097152 | tf_op jit(solution)/shard_map/all_to_all | solution.py:135
  77.8 8.9 %collective-permute-start.6 = (bf16[1,5,32,128]{3,2,1,0:T(8,128)(2,1)S(1)}, bf16[1,5,32,128]{3,2,1,0:T(8,128)(2,1)S(1)}, u32[]{:S(2)}, u32[]{:S(2)}) collective-permute-start(bf16[1,5,32,128]{3,2,1,0:T(8,128)(2,1)S(1)} %pad_maximum_fusion.3), channel_id=1, source_target_pairs={{31,0},{0,1},{1,2},{2,3},{3,4},{4,5},{5,6},{6,7},{7,8},{8,9},{9,10... | collective-permute-start | bytes 122888 | tf_op jit(solution)/shard_map/ppermute | solution.py:32
  79.8 7.8 %collective-permute-start.7 = (bf16[1,1,32,128]{3,2,1,0:T(8,128)(2,1)S(1)}, bf16[1,1,32,128]{3,2,1,0:T(8,128)(2,1)S(1)}, u32[]{:S(2)}, u32[]{:S(2)}) collective-permute-start(bf16[1,1,32,128]{3,2,1,0:T(8,128)(2,1)S(1)} %slice.38), channel_id=1, source_target_pairs={{1,0},{2,1},{3,2},{4,3},{5,4},{6,5},{7,6},{8,7},{9,8},{10,9},{11,1... | collective-permute-start | bytes 24584 | tf_op jit(solution)/shard_map/ppermute | solution.py:32
  86.8 0.8 copy-start.9

commit v15 on v12

--- a/solution.py
+++ b/solution.py
@@ -127,10 +127,12 @@
     )(got, base, scale, cond)
 
 
-def instance_mix(flat):
+def instance_mix(flat, hold=None):
     i = lax.axis_index("iy") * 8 + lax.axis_index("ix") * 2 + lax.axis_index("ic")
     mate = routed(flat, lambda s: s ^ 1)
     across = routed(flat, lambda s: s ^ 8)
+    if hold is not None:
+        across = lax.optimization_barrier((across, hold))[0]
     diagonal = routed(across, lambda s: s ^ 1)
     partials = partial_sums(jnp.reshape(i, (1,)).astype(jnp.int32), flat, mate, across, diagonal)
     return partials, lax.all_to_all(partials, "ix", 0, 0)
@@ -152,7 +154,6 @@
     weighted = (lam * cond_wide).reshape(-1, lanes)
     for sweep in range(SWEEPS):
         lam_b = lam.astype(jnp.bfloat16)
-        partials, got = instance_mix(weighted)
         records = jnp.einsum(
             "tjri,tjio->tjro",
             lam_b[:, rows - rotor_rows :],
@@ -160,9 +161,15 @@
             preferred_element_type=jnp.float32,
         )
         onward = jnp.concatenate([lam_b[:, rows - 1 :], (records * moving).astype(jnp.bfloat16)], axis=1)
-        onward, lam_b, _ = lax.optimization_barrier((onward, lam_b, partials))
-        onward = shifted(onward, "sector", 1)
-        head = shifted(lam_b[:, :1], "sector", -1)
+        if sweep == 0:
+            partials, got = instance_mix(weighted)
+            onward, lam_b, _ = lax.optimization_barrier((onward, lam_b, partials))
+            onward = shifted(onward, "sector", 1)
+            head = shifted(lam_b[:, :1], "sector", -1)
+        else:
+            onward = shifted(onward, "sector", 1)
+            head = shifted(lam_b[:, :1], "sector", -1)
+            partials, got = instance_mix(weighted, (onward, head))
         lam_h = jnp.concatenate([onward[:, :1], lam_b, head], axis=1)
         picked = lam_h[:, cols]
         stator = jnp.einsum("tnkri,tnkio->tnro", picked, jac, preferred_element_type=jnp.float32)

time: 92.5 us -> 95.7 us (1.035)
  waiting for transfers between devices: 4.49 us -> 10.5 us
  other arithmetic: 13.2 us -> 11.9 us
    all_to_all x2, waiting for transfers between devices: 0.01 us -> 8.73 us  [instance_mix(): return (partials, lax.all_to_all(partials, 'ix', 0, 0))]
    ppermute x6, waiting for transfers between devices: 3.6 us -> 1.64 us  [routed(): return lax.ppermute(block, INST, [(s, dest(s)) for s in range(NT)])]
  transfers between devices with their start and end apart: 12 -> 12, of which waited for: 3 -> 3; matrix products, arithmetic and copies ran while one was open for 24% -> 20% of each run, Pallas kernels for 0% -> 0%
where the time goes in v15:
time: 95.7 us; the launch traced here: 94.8 us
  starting transfers between devices  51.6 us (54%)
  other arithmetic  11.9 us (12%)
  waiting for transfers between devices  10.5 us (11%)
  Pallas kernels  8.57 us (9%)
  matrix products  6.34 us (7%)
  local copies, waits for them, and re-layouts  4.76 us (5%)
  between operations  1.11 us (1%)
    ppermute x6, starting transfers between devices, routed(): return lax.ppermute(block, INST, [(s, dest(s)) for s in range(NT)])  21.5 us
    ppermute x4, starting transfers between devices, shifted(): return lax.ppermute(block, axis, route)  21.3 us
    all_to_all x2, starting transfers between devices, instance_mix(): return (partials, lax.all_to_all(partials, 'ix', 0, 0))  8.77 us
    all_to_all x2, waiting for transfers between devices, instance_mix(): return (partials, lax.all_to_all(partials, 'ix', 0, 0))  8.73 us
    dot_general x2, matrix products, shards(): jnp.einsum('tnkri,tnkio->tnro', picked, jac, preferred_element_type=jnp.f...  5.15 us
    pallas_call x2, Pallas kernels, partial_sums(): pl.pallas_call(mix_kernel, grid_spec=pltpu.PrefetchScalarGridSpec(num_sca...  4.55 us
    pallas_call x2, Pallas kernels, updated(): pl.pallas_call(update_kernel, grid=(rows // block,), in_specs=[pl.BlockSp...  4.02 us
    gather x2, local copies, waits for them, and re-layouts, shards(): picked = lam_h[:, cols]  3.4 us
  transfers between devices with their start and end apart: 12, of which 3 were waited for; matrix products, arithmetic and copies ran while one was open for 20% of the time, Pallas kernels for 0%

profile of v15, /device:TPU:1, one launch (start us, length us, event | category | flops | bytes accessed | tf_op | source)
XLA Modules:
  0.0 94.8 jit_solution(11948407675535477174)
XLA Ops:
  0.8 1.9 %multiply_convert_fusion = (bf16[1,16,32,128]{3,2,1,0:T(8,128)(2,1)S(1)}, f32[1,16,32,128]{3,2,1,0:T(8,128)}) fusion(f32[1,16,32,128]{3,2,1,0:T(8,128)} %param.11, f32[16]{0:T(128)S(1)} %or_convert_fusion, f32[16,128]{1,0:T(8,128)} %cond_ref.3), kind=kLoop, calls=%fused_computation.10 | loop fusion | flops 196608 | bytes 663616 | tf_op jit(solution)/shard_map/convert_element_type | solution.py:156
  2.7 4.0 %collective-permute-start.1 = (f32[512,128]{1,0:T(8,128)}, f32[512,128]{1,0:T(8,128)}, u32[]{:S(2)}, u32[]{:S(2)}) collective-permute-start(f32[512,128]{1,0:T(8,128)} %bitcast.2.own_ref), channel_id=1, source_target_pairs={{0,256},{32,288},{64,320},{96,352},{128,384},{160,416},{192,448},{... | collective-permute-start | bytes 786440 | tf_op jit(solution)/shard_map/ppermute | solution.py:49
  6.8 6.7 %collective-permute-start = (f32[512,128]{1,0:T(8,128)}, f32[512,128]{1,0:T(8,128)}, u32[]{:S(2)}, u32[]{:S(2)}) collective-permute-start(f32[512,128]{1,0:T(8,128)} %bitcast.2.own_ref), channel_id=1, source_target_pairs={{0,32},{32,0},{64,96},{96,64},{128,160},{160,128},{192,224},{224,1... | collective-permute-start | bytes 786440 | tf_op jit(solution)/shard_map/ppermute | solution.py:49
  14.8 1.0 %fusion.12 = f32[4,32,128]{2,1,0:T(8,128)S(1)} fusion(bf16[1,4,128,128]{3,2,1,0:T(8,128)(2,1)} %param.16, bf16[1,16,32,128]{3,2,1,0:T(8,128)(2,1)S(1)} %get-tuple-element.11), kind=kOutput, calls=%fused_computation.16 | convolution fusion | flops 4194304 | bytes 229376 | tf_op jit(solution)/shard_map/tjri,tjio->tjro/dot_general | solution.py:157
  15.8 1.2 %broadcast_subtract_fusion = f32[4]{0:T(128)} fusion(s32[1,4]{1,0:T(1,128)} %param.18), kind=kLoop, calls=%fused_computation.33 | loop fusion | flops 8 | bytes 32 | tf_op jit(solution)/shard_map/sub | solution.py:177
  17.1 2.9 %collective-permute-start.2 = (f32[512,128]{1,0:T(8,128)}, f32[512,128]{1,0:T(8,128)}, u32[]{:S(2)}, u32[]{:S(2)}) collective-permute-start(f32[512,128]{1,0:T(8,128)} %collective-permute-done.1.across_ref), channel_id=1, source_target_pairs={{0,32},{32,0},{64,96},{96,64},{128,160},{160,128},{192,224},{224,1... | collective-permute-start | bytes 786440 | tf_op jit(solution)/shard_map/ppermute | solution.py:49
  20.9 1.4 %broadcast_multiply_fusion.scale_ref = f32[16,128]{1,0:T(8,128)} fusion(f32[16]{0:T(128)S(1)} %or_convert_fusion, f32[1,16,128]{2,1,0:T(8,128)} %param.13), kind=kLoop, calls=%fused_computation.30 | loop fusion | flops 2048 | bytes 16448 | tf_op jit(solution)/shard_map/mul | solution.py:153
  22.3 2.3 %shard_map.109 = f32[4,512,128]{2,1,0:T(8,128)} custom-call(s32[1]{0:T(128)} %bitcast.index_ref, f32[16,16]{1,0:T(8,128)} %constant.32.clone.coef_ref, f32[512,128]{1,0:T(8,128)} %bitcast.2.own_ref, f32[512,128]{1,0:T(8,128)} %collective-permute-done.mate_ref, f32[512,128]{1,0:T(8,128)} %collective-permute-done.1.across_ref, ...), custom_call_target="tpu_custom_call" | custom-call | tf_op jit(solution)/shard_map/pallas_call | solution.py:91
  24.6 4.3 %all-to-all-start = ((f32[4,512,128]{2,1,0:T(8,128)}), f32[4,512,128]{2,1,0:T(8,128)}, u32[]{:S(2)}, u32[]{:S(2)}) async-start(f32[4,512,128]{2,1,0:T(8,128)} %shard_map.109), calls=%async_computation | async-start | bytes 2097152 | tf_op jit(solution)/shard_map/all_to_all | solution.py:138
  28.8 1.9 %collective-permute-start.3 = (bf16[1,5,32,128]{3,2,1,0:T(8,128)(2,1)}, bf16[1,5,32,128]{3,2,1,0:T(8,128)(2,1)S(1)}, u32[]{:S(2)}, u32[]{:S(2)}) collective-permute-start(bf16[1,5,32,128]{3,2,1,0:T(8,128)(2,1)} %pad_maximum_fusion), channel_id=1, source_target_pairs={{31,0},{0,1},{1,2},{2,3},{3,4},{4,5},{5,6},{6,7},{7,8},{8,9},{9,10... | collective-permute-start | bytes 122888 | tf_op jit(solution)/shard_map/ppermute | solution.py:32
  30.8 10.1 %collective-permute-start.4 = (bf16[1,1,32,128]{3,2,1,0:T(8,128)(2,1)S(1)}, bf16[1,1,32,128]{3,2,1,0:T(8,128)(2,1)S(1)}, u32[]{:S(2)}, u32[]{:S(2)}) collective-permute-start(bf16[1,1,32,128]{3,2,1,0:T(8,128)(2,1)S(1)} %slice.33), channel_id=1, source_target_pairs={{1,0},{2,1},{3,2},{4,3},{5,4},{6,5},{7,6},{8,7},{9,8},{10,9},{11,1... | collective-permute-start | bytes 24584 | tf_op jit(solution)/shard_map/ppermute | solution.py:32
  42.0 0.9 maximum_bitcast_fusion
  43.0 1.7 %gather_fusion = bf16[96,32,128]{2,1,0:T(8,128)(2,1)} fusion(bf16[18,32,128]{2,1,0:T(8,128)(2,1)S(1)} %maximum_bitcast_fusion, s32[1024]{0:T(1024)} %pad_clamp_fusion), kind=kCustom, calls=%fused_computation | custom fusion | bytes 1573248 | tf_op jit(solution)/shard_map/gather | solution.py:174
  44.7 0.9 bitcast_add_fusion.1
  45.6 2.6 %multiply_add_fusion.1 = f32[1,16,32,128]{3,2,1,0:T(8,128)} fusion(f32[1,16,32,128]{3,2,1,0:T(8,128)S(1)} %copy-done.1, f32[1,4,32,128]{3,2,1,0:T(8,128)S(1)} %bitcast_add_fusion.1, f32[1,16,32,128]{3,2,1,0:T(8,128)} %param.11, f32[16,128]{1,0:T(8,128)} %bitcast.68, f32[16]{0:T(128)} %copy-done.10, bf16[16,6,32,128]{3,2,1,0:T(8,128)(2,1)} %bitcast.63, ...), kind=kOutput, calls=%fused_computation.9 | convolution fusion | flops 101056512 | bytes 4792384 | tf_op jit(solution)/shard_map/tnkri,tnkio->tnro/dot_general | solution.py:175
  48.2 2.0 %shard_map.110 = (f32[512,128]{1,0:T(8,128)}, f32[512,128]{1,0:T(8,128)}) custom-call(f32[4,512,128]{2,1,0:T(8,128)} %all-to-all-done.got_ref, f32[512,128]{1,0:T(8,128)} %bitcast.67, f32[16,128]{1,0:T(8,128)} %broadcast_multiply_fusion.scale_ref, f32[16,128]{1,0:T(8,128)} %cond_ref.3), custom_call_target="tpu_custom_call" | custom-call | tf_op jit(solution)/shard_map/pallas_call | solution.py:121
  50.3 1.0 %convert_element_type.52 = bf16[1,16,32,128]{3,2,1,0:T(8,128)(2,1)S(1)} convert(f32[1,16,32,128]{3,2,1,0:T(8,128)} %bitcast.65) | non-fusion elementwise | flops 65536 | bytes 393216 | tf_op jit(solution)/shard_map/convert_element_type | solution.py:156
  51.5 2.3 %collective-permute-start.6 = (f32[512,128]{1,0:T(8,128)}, f32[512,128]{1,0:T(8,128)S(1)}, u32[]{:S(2)}, u32[]{:S(2)}) collective-permute-start(f32[512,128]{1,0:T(8,128)} %get-tuple-element.12.own_ref), channel_id=1, source_target_pairs={{0,256},{32,288},{64,320},{96,352},{128,384},{160,416},{192,448},{... | collective-permute-start | bytes 786440 | tf_op jit(solution)/shard_map/ppermute | solution.py:49
  53.8 1.9 %collective-permute-start.7 = (bf16[1,5,32,128]{3,2,1,0:T(8,128)(2,1)S(1)}, bf16[1,5,32,128]{3,2,1,0:T(8,128)(2,1)S(1)}, u32[]{:S(2)}, u32[]{:S(2)}) collective-permute-start(bf16[1,5,32,128]{3,2,1,0:T(8,128)(2,1)S(1)} %pad_maximum_fusion.1), channel_id=1, source_target_pairs={{31,0},{0,1},{1,2},{2,3},{3,4},{4,5},{5,6},{6,7},{7,8},{8,9},{9,10... | collective-permute-start | bytes 122888 | tf_op jit(solution)/shard_map/ppermute | solution.py:32
  55.8 7.4 %collective-permute-start.8 = (bf16[1,1,32,128]{3,2,1,0:T(8,128)(2,1)S(1)}, bf16[1,1,32,128]{3,2,1,0:T(8,128)(2,1)S(1)}, u32[]{:S(2)}, u32[]{:S(2)}) collective-permute-start(bf16[1,1,32,128]{3,2,1,0:T(8,128)(2,1)S(1)} %get-tuple-element.17), channel_id=1, source_target_pairs={{1,0},{2,1},{3,2},{4,3},{5,4},{6,5},{7,6},{8,7},{9,8},{10,9},{11,1... | collective-permute-start | bytes 24584 | tf_op jit(solution)/shard_map/ppermute | solution.py:32
  63.2 3.7 %collective-permute-start.5 = (f32[512,128]{1,0:T(8,128)}, f32[512,128]{1,0:T(8,128)}, u32[]{:S(2)}, u32[]{:S(2)}) collective-permute-start(f32[512,128]{1,0:T(8,128)} %get-tuple-element.12.own_ref), channel_id=1, source_target_pairs={{0,32},{32,0},{64,96},{96,64},{128,160},{160,128},{192,224},{224,1... | collective-permute-start | bytes 786440 | tf_op jit(solution)/shard_map/ppermute | solution.py:49
  66.9 0.7 copy-done.7
  67.6 1.9 %collective-permute-start.9 = (f32[512,128]{1,0:T(8,128)S(1)}, f32[512,128]{1,0:T(8,128)}, u32[]{:S(2)}, u32[]{:S(2)}) collective-permute-start(f32[512,128]{1,0:T(8,128)S(1)} %collective-permute-done.6.across_ref), channel_id=1, source_target_pairs={{0,32},{32,0},{64,96},{96,64},{128,160},{160,128},{192,224},{224,1... | collective-permute-start | bytes 786440 | tf_op jit(solution)/shard_map/ppermute | solution.py:49
  69.5 1.6 %collective-permute-done.9.diagonal_ref = f32[512,128]{1,0:T(8,128)} collective-permute-done((f32[512,128]{1,0:T(8,128)S(1)}, f32[512,128]{1,0:T(8,128)}, u32[]{:S(2)}, u32[]{:S(2)}) %collective-permute-start.9) | collective-permute-done | bytes 262176 | tf_op jit(solution)/shard_map/ppermute | solution.py:49
  71.2 2.2 %shard_map.111 = f32[4,512,128]{2,1,0:T(8,128)} custom-call(s32[1]{0:T(128)} %bitcast.index_ref, f32[16,16]{1,0:T(8,128)} %constant.32.clone.coef_ref, f32[512,128]{1,0:T(8,128)} %get-tuple-element.12.own_ref, f32[512,128]{1,0:T(8,128)} %collective-permute-done.5.mate_ref, f32[512,128]{1,0:T(8,128)} %copy-done.7, f32[512,128]{1,0:T(8,128)} %collective-permute-done.9.diagonal_ref), custom_call_target="tpu_custom_call" | custom-call | tf_op jit(solution)/shard_map/pallas_call | solution.py:91
  73.4 4.5 %all-to-all-start.1 = ((f32[4,512,128]{2,1,0:T(8,128)}), f32[4,512,128]{2,1,0:T(8,128)}, u32[]{:S(2)}, u32[]{:S(2)}) async-start(f32[4,512,128]{2,1,0:T(8,128)} %shard_map.111), calls=%async_computation.1 | async-start | bytes 2097152 | tf_op jit(solution)/shard_map/all_to_all | solution.py:138
  77.9 0.9 maximum_bitcast_fusion.1
  78.9 1.7 %gather_fusion.1 = bf16[96,32,128]{2,1,0:T(8,128)(2,1)} fusion(bf16[18,32,128]{2,1,0:T(8,128)(2,1)S(1)} %maximum_bitcast_fusion.1, s32[1024]{0:T(1024)} %pad_clamp_fusion), kind=kCustom, calls=%fused_computation.1 | custom fusion | bytes 1573248 | tf_op jit(solution)/shard_map/gather | solution.py:174
  80.6 0.9 bitcast_add_fusion
  81.5 2.6 %multiply_add_fusion = f32[1,16,32,128]{3,2,1,0:T(8,128)} fusion(f32[1,16,32,128]{3,2,1,0:T(8,128)} %bitcast.66, f32[1,16,32,128]{3,2,1,0:T(8,128)S(1)} %copy-done.1, f32[1,4,32,128]{3,2,1,0:T(8,128)S(1)} %bitcast_add_fusion, f32[16,128]{1,0:T(8,128)} %bitcast.69, f32[16]{0:T(128)} %copy-done.10, bf16[16,6,32,128]{3,2,1,0:T(8,128)(2,1)} %bitcast.62, ...), kind=kOutput, calls=%fused_computation.8 | convolution fusion | flops 100990976 | bytes 4792384 | tf_op jit(solution)/shard_map/tnkri,tnkio->tnro/dot_general | solution.py:175
  84.1 8.7 %all-to-all-done.1.got_ref = f32[4,512,128]{2,1,0:T(8,128)} async-done(((f32[4,512,128]{2,1,0:T(8,128)}), f32[4,512,128]{2,1,0:T(8,128)}, u32[]{:S(2)}, u32[]{:S(2)}) %all-to-all-start.1) | async-done | bytes 1048608 | tf_op jit(solution)/shard_map/all_to_all | solution.py:138
  92.8 2.0 %shard_map.112 = f32[512,128]{1,0:T(8,128)} custom-call(f32[4,512,128]{2,1,0:T(8,128)} %all-to-all-done.1.got_ref, f32[512,128]{1,0:T(8,128)} %bitcast.64, f32[16,128]{1,0:T(8,128)} %broadcast_multiply_fusion.scale_ref, f32[16,128]{1,0:T(8,128)} %cond_ref.3), custom_call_target="tpu_custom_call" | custom-call | tf_op jit(solution)/shard_map/pallas_call | solution.py:121
  (53 shorter events, 3.7 us)
Async XLA Ops:
  0.0 45.6 %copy-start = (bf16[1,16,6,128,128]{4,3,2,1,0:T(8,128)(2,1)S(1)}, bf16[1,16,6,128,128]{4,3,2,1,0:T(8,128)(2,1)}, u32[]{:S(2)}) copy-start(bf16[1,16,6,128,128]{4,3,2,1,0:T(8,128)(2,1)} %param.15) | copy-start | bytes 9437188
  0.8 40.6 %copy-start.10 = (f32[16]{0:T(128)}, f32[16]{0:T(128)S(1)}, u32[]{:S(2)}) copy-start(f32[16]{0:T(128)S(1)} %or_convert_fusion) | copy-start | bytes 196
  2.7 38.7 %copy-start.3 = (bf16[1,16,32,128]{3,2,1,0:T(8,128)(2,1)}, bf16[1,16,32,128]{3,2,1,0:T(8,128)(2,1)S(1)}, u32[]{:S(2)}) copy-start(bf16[1,16,32,128]{3,2,1,0:T(8,128)(2,1)S(1)} %get-tuple-element.11) | copy-start | bytes 393220
  2.7 14.4 %collective-permute-start.1 = (f32[512,128]{1,0:T(8,128)}, f32[512,128]{1,0:T(8,128)}, u32[]{:S(2)}, u32[]{:S(2)}) collective-permute-start(f32[512,128]{1,0:T(8,128)} %bitcast.2.own_ref), channel_id=1, source_target_pairs={{0,256},{32,288},{64,320},{96,352},{128,384},{160,416},{192,448},{... | collective-permute-start | bytes 786440 | tf_op jit(solution)/shard_map/ppermute | solution.py:49
  6.8 15.5 %collective-permute-start = (f32[512,128]{1,0:T(8,128)}, f32[512,128]{1,0:T(8,128)}, u32[]{:S(2)}, u32[]{:S(2)}) collective-permute-start(f32[512,128]{1,0:T(8,128)} %bitcast.2.own_ref), channel_id=1, source_target_pairs={{0,32},{32,0},{64,96},{96,64},{128,160},{160,128},{192,224},{224,1... | collective-permute-start | bytes 786440 | tf_op jit(solution)/shard_map/ppermute | solution.py:49
  14.1 6.6 %copy-start.12 = (f32[4]{0:T(128)}, f32[4]{0:T(128)S(1)}, u32[]{:S(2)}) copy-start(f32[4]{0:T(128)S(1)} %convert_bitcast_fusion) | copy-start | bytes 52
  15.8 1.2 %copy-start.4 = (f32[4,32,128]{2,1,0:T(8,128)}, f32[4,32,128]{2,1,0:T(8,128)S(1)}, u32[]{:S(2)}) copy-start(f32[4,32,128]{2,1,0:T(8,128)S(1)} %fusion.12) | copy-start | bytes 196612
  17.1 5.1 %collective-permute-start.2 = (f32[512,128]{1,0:T(8,128)}, f32[512,128]{1,0:T(8,128)}, u32[]{:S(2)}, u32[]{:S(2)}) collective-permute-start(f32[512,128]{1,0:T(8,128)} %collective-permute-done.1.across_ref), channel_id=1, source_target_pairs={{0,32},{32,0},{64,96},{96,64},{128,160},{160,128},{192,224},{224,1... | collective-permute-start | bytes 786440 | tf_op jit(solution)/shard_map/ppermute | solution.py:49
  22.3 23.3 %copy-start.1 = (f32[1,16,32,128]{3,2,1,0:T(8,128)S(1)}, f32[1,16,32,128]{3,2,1,0:T(8,128)}, u32[]{:S(2)}) copy-start(f32[1,16,32,128]{3,2,1,0:T(8,128)} %param.12) | copy-start | bytes 786436
  24.6 23.7 %all-to-all-start = ((f32[4,512,128]{2,1,0:T(8,128)}), f32[4,512,128]{2,1,0:T(8,128)}, u32[]{:S(2)}, u32[]{:S(2)}) async-start(f32[4,512,128]{2,1,0:T(8,128)} %shard_map.109), calls=%async_computation | async-start | bytes 2097152 | tf_op jit(solution)/shard_map/all_to_all | solution.py:138
  28.8 12.6 %collective-permute-start.3 = (bf16[1,5,32,128]{3,2,1,0:T(8,128)(2,1)}, bf16[1,5,32,128]{3,2,1,0:T(8,128)(2,1)S(1)}, u32[]{:S(2)}, u32[]{:S(2)}) collective-permute-start(bf16[1,5,32,128]{3,2,1,0:T(8,128)(2,1)} %pad_maximum_fusion), channel_id=1, source_target_pairs={{31,0},{0,1},{1,2},{2,3},{3,4},{4,5},{5,6},{6,7},{7,8},{8,9},{9,10... | collective-permute-start | bytes 122888 | tf_op jit(solution)/shard_map/ppermute | solution.py:32
  30.8 10.8 %collective-permute-start.4 = (bf16[1,1,32,128]{3,2,1,0:T(8,128)(2,1)S(1)}, bf16[1,1,32,128]{3,2,1,0:T(8,128)(2,1)S(1)}, u32[]{:S(2)}, u32[]{:S(2)}) collective-permute-start(bf16[1,1,32,128]{3,2,1,0:T(8,128)(2,1)S(1)} %slice.33), channel_id=1, source_target_pairs={{1,0},{2,1},{3,2},{4,3},{5,4},{6,5},{7,6},{8,7},{9,8},{10,9},{11,1... | collective-permute-start | bytes 24584 | tf_op jit(solution)/shard_map/ppermute | solution.py:32
  41.4 0.6 copy-start.9
  45.6 5.6 %copy-start.6 = (bf16[1,4,128,128]{3,2,1,0:T(8,128)(2,1)S(1)}, bf16[1,4,128,128]{3,2,1,0:T(8,128)(2,1)}, u32[]{:S(2)}) copy-start(bf16[1,4,128,128]{3,2,1,0:T(8,128)(2,1)} %param.16) | copy-start | bytes 393220
  45.6 5.8 %copy-start.13 = (f32[4]{0:T(128)S(1)}, f32[4]{0:T(128)}, u32[]{:S(2)}) copy-start(f32[4]{0:T(128)} %copy-done.12) | copy-start | bytes 52
  51.2 2.5 %copy-start.2 = (bf16[1,16,32,128]{3,2,1,0:T(8,128)(2,1)}, bf16[1,16,32,128]{3,2,1,0:T(8,128)(2,1)S(1)}, u32[]{:S(2)}) copy-start(bf16[1,16,32,128]{3,2,1,0:T(8,128)(2,1)S(1)} %convert_element_type.52) | copy-start | bytes 393220
  51.4 2.4 %copy-start.5 = (f32[4,32,128]{2,1,0:T(8,128)}, f32[4,32,128]{2,1,0:T(8,128)S(1)}, u32[]{:S(2)}) copy-start(f32[4,32,128]{2,1,0:T(8,128)S(1)} %fusion.10) | copy-start | bytes 196612
  51.5 15.4 %collective-permute-start.6 = (f32[512,128]{1,0:T(8,128)}, f32[512,128]{1,0:T(8,128)S(1)}, u32[]{:S(2)}, u32[]{:S(2)}) collective-permute-start(f32[512,128]{1,0:T(8,128)} %get-tuple-element.12.own_ref), channel_id=1, source_target_pairs={{0,256},{32,288},{64,320},{96,352},{128,384},{160,416},{192,448},{... | collective-permute-start | bytes 786440 | tf_op jit(solution)/shard_map/ppermute | solution.py:49
  53.8 13.0 %collective-permute-start.7 = (bf16[1,5,32,128]{3,2,1,0:T(8,128)(2,1)S(1)}, bf16[1,5,32,128]{3,2,1,0:T(8,128)(2,1)S(1)}, u32[]{:S(2)}, u32[]{:S(2)}) collective-permute-start(bf16[1,5,32,128]{3,2,1,0:T(8,128)(2,1)S(1)} %pad_maximum_fusion.1), channel_id=1, source_target_pairs={{31,0},{0,1},{1,2},{2,3},{3,4},{4,5},{5,6},{6,7},{7,8},{8,9},{9,10... | collective-permute-start | bytes 122888 | tf_op jit(solution)/shard_map/ppermute | solution.py:32
  55.8 11.1 %collective-permute-start.8 = (bf16[1,1,32,128]{3,2,1,0:T(8,128)(2,1)S(1)}, bf16[1,1,32,128]{3,2,1,0:T(8,128)(2,1)S(1)}, u32[]{:S(2)}, u32[]{:S(2)}) collective-permute-start(bf16[1,1,32,128]{3,2,1,0:T(8,128)(2,1)S(1)} %get-tuple-element.17), channel_id=1, source_target_pairs={{1,0},{2,1},{3,2},{4,3},{5,4},{6,5},{7,6},{8,7},{9,8},{10,9},{11,1... | collective-permute-start | bytes 24584 | tf_op jit(solution)/shard_map/ppermute | solution.py:32
  63.2 6.3 %collective-permute-start.5 = (f32[512,128]{1,0:T(8,128)}, f32[512,128]{1,0:T(8,128)}, u32[]{:S(2)}, u32[]{:S(2)}) collective-permute-start(f32[512,128]{1,0:T(8,128)} %get-tuple-element.12.own_ref), channel_id=1, source_target_pairs={{0,32},{32,0},{64,96},{96,64},{128,160},{160,128},{192,224},{224,1... | collective-permute-start | bytes 786440 | tf_op jit(solution)/shard_map/ppermute | solution.py:49
  66.9 11.1 %copy-start.11 = (bf16[1,1,32,128]{3,2,1,0:T(8,128)(2,1)}, bf16[1,1,32,128]{3,2,1,0:T(8,128)(2,1)S(1)}, u32[]{:S(2)}) copy-start(bf16[1,1,32,128]{3,2,1,0:T(8,128)(2,1)S(1)} %collective-permute-done.8) | copy-start | bytes 24580
  66.9 11.0 %copy-start.8 = (bf16[1,5,32,128]{3,2,1,0:T(8,128)(2,1)}, bf16[1,5,32,128]{3,2,1,0:T(8,128)(2,1)S(1)}, u32[]{:S(2)}) copy-start(bf16[1,5,32,128]{3,2,1,0:T(8,128)(2,1)S(1)} %collective-permute-done.7) | copy-start | bytes 122884
  66.9 0.7 copy-start.7
  67.6 3.5 %collective-permute-start.9 = (f32[512,128]{1,0:T(8,128)S(1)}, f32[512,128]{1,0:T(8,128)}, u32[]{:S(2)}, u32[]{:S(2)}) collective-permute-start(f32[512,128]{1,0:T(8,128)S(1)} %collective-permute-done.6.across_ref), channel_id=1, source_target_pairs={{0,32},{32,0},{64,96},{96,64},{128,160},{160,128},{192,224},{224,1... | collective-permute-start | bytes 786440 | tf_op jit(solution)/shard_map/ppermute | solution.py:49
  73.4 19.4 %all-to-all-start.1 = ((f32[4,512,128]{2,1,0:T(8,128)}), f32[4,512,128]{2,1,0:T(8,128)}, u32[]{:S(2)}, u32[]{:S(2)}) async-start(f32[4,512,128]{2,1,0:T(8,128)} %shard_map.111), calls=%async_computation.1 | async-start | bytes 2097152 | tf_op jit(solution)/shard_map/all_to_all | solution.py:138

commit v16 on v12

--- a/solution.py
+++ b/solution.py
@@ -150,6 +150,7 @@
     cond_wide = cond[None, :, None, :]
     scale = relax[0] * live[0, :, 0]
     weighted = (lam * cond_wide).reshape(-1, lanes)
+    select = (cols[:, :, None] == jnp.arange(rows + 2)[None, None, :]).astype(jnp.bfloat16)
     for sweep in range(SWEEPS):
         lam_b = lam.astype(jnp.bfloat16)
         partials, got = instance_mix(weighted)
@@ -164,7 +165,7 @@
         onward = shifted(onward, "sector", 1)
         head = shifted(lam_b[:, :1], "sector", -1)
         lam_h = jnp.concatenate([onward[:, :1], lam_b, head], axis=1)
-        picked = lam_h[:, cols]
+        picked = jnp.einsum("nkm,tmri->tnkri", select, lam_h, preferred_element_type=jnp.float32).astype(jnp.bfloat16)
         stator = jnp.einsum("tnkri,tnkio->tnro", picked, jac, preferred_element_type=jnp.float32)
         arrived = onward[:, 1:].astype(jnp.float32)
         rotor = records * (1.0 - moving) + arrived

time: 92.5 us -> 107 us (1.16)
  waiting for transfers between devices: 4.49 us -> 19.7 us
  starting transfers between devices: 51.1 us -> 54.7 us
  local copies, waits for them, and re-layouts: 5.39 us -> 2.63 us
  other arithmetic: 13.2 us -> 11.4 us
    all_to_all x2, waiting for transfers between devices: 0.01 us -> 18.7 us  [instance_mix(): return (partials, lax.all_to_all(partials, 'ix', 0, 0))]
    ppermute x6, starting transfers between devices: 21.8 us -> 25.3 us  [routed(): return lax.ppermute(block, INST, [(s, dest(s)) for s in range(NT)])]
    gather x2 -> x0, local copies, waits for them, and re-layouts: 3.4 us -> none  [shards(): picked = lam_h[:, cols]]
    ppermute x6, waiting for transfers between devices: 3.6 us -> 1 us  [routed(): return lax.ppermute(block, INST, [(s, dest(s)) for s in range(NT)])]
    concatenate x2 -> x0, other arithmetic: 1.85 us -> none  [shards(): lam_h = jnp.concatenate([onward[:, :1], lam_b, head], axis=1)]
    unnamed x26 -> x16, local copies, waits for them, and re-layouts: 1.81 us -> 0.03 us
    another operation x0 -> x2, other arithmetic: none -> 1.44 us
    slice x2, local copies, waits for them, and re-layouts: 0.01 us -> 1.4 us  [shards(): lam_h = jnp.concatenate([onward[:, :1], lam_b, head], axis=1)]
  transfers between devices with their start and end apart: 12 -> 12, of which waited for: 3 -> 3; matrix products, arithmetic and copies ran while one was open for 24% -> 19% of each run, Pallas kernels for 0% -> 0%
where the time goes in v16:
time: 107 us; the launch traced here: 106 us
  starting transfers between devices  54.7 us (51%)
  waiting for transfers between devices  19.7 us (18%)
  other arithmetic  11.4 us (11%)
  Pallas kernels  8.53 us (8%)
  matrix products  7.9 us (7%)
  local copies, waits for them, and re-layouts  2.63 us (2%)
    ppermute x6, starting transfers between devices, routed(): return lax.ppermute(block, INST, [(s, dest(s)) for s in range(NT)])  25.3 us
    ppermute x4, starting transfers between devices, shifted(): return lax.ppermute(block, axis, route)  20.8 us
    all_to_all x2, waiting for transfers between devices, instance_mix(): return (partials, lax.all_to_all(partials, 'ix', 0, 0))  18.7 us
    all_to_all x2, starting transfers between devices, instance_mix(): return (partials, lax.all_to_all(partials, 'ix', 0, 0))  8.53 us
    dot_general x2, matrix products, shards(): jnp.einsum('tnkri,tnkio->tnro', picked, jac, preferred_element_type=jnp.f...  4.98 us
    pallas_call x2, Pallas kernels, partial_sums(): pl.pallas_call(mix_kernel, grid_spec=pltpu.PrefetchScalarGridSpec(num_sca...  4.53 us
    pallas_call x2, Pallas kernels, updated(): pl.pallas_call(update_kernel, grid=(rows // block,), in_specs=[pl.BlockSp...  4.01 us
    convert_element_type x2, other arithmetic, shards(): lam_b = lam.astype(jnp.bfloat16)  2.87 us
  transfers between devices with their start and end apart: 12, of which 3 were waited for; matrix products, arithmetic and copies ran while one was open for 19% of the time, Pallas kernels for 0%

profile of v16, /device:TPU:1, one launch (start us, length us, event | category | flops | bytes accessed | tf_op | source)
XLA Modules:
  0.0 105.8 jit_solution(15129210929530337448)
XLA Ops:
  0.8 1.9 %multiply_convert_fusion = (bf16[1,16,32,128]{3,2,1,0:T(8,128)(2,1)S(1)}, f32[1,16,32,128]{3,2,1,0:T(8,128)}) fusion(f32[1,16,32,128]{3,2,1,0:T(8,128)} %param.11, f32[16]{0:T(128)S(1)} %or_convert_fusion, f32[16,128]{1,0:T(8,128)} %cond_ref.3), kind=kLoop, calls=%fused_computation.14 | loop fusion | flops 196608 | bytes 663616 | tf_op jit(solution)/shard_map/convert_element_type | solution.py:155
  2.7 4.2 %collective-permute-start.1 = (f32[512,128]{1,0:T(8,128)}, f32[512,128]{1,0:T(8,128)}, u32[]{:S(2)}, u32[]{:S(2)}) collective-permute-start(f32[512,128]{1,0:T(8,128)} %bitcast.2.own_ref), channel_id=1, source_target_pairs={{0,256},{32,288},{64,320},{96,352},{128,384},{160,416},{192,448},{... | collective-permute-start | bytes 786440 | tf_op jit(solution)/shard_map/ppermute | solution.py:49
  6.9 6.7 %collective-permute-start = (f32[512,128]{1,0:T(8,128)}, f32[512,128]{1,0:T(8,128)}, u32[]{:S(2)}, u32[]{:S(2)}) collective-permute-start(f32[512,128]{1,0:T(8,128)} %bitcast.2.own_ref), channel_id=1, source_target_pairs={{0,32},{32,0},{64,96},{96,64},{128,160},{160,128},{192,224},{224,1... | collective-permute-start | bytes 786440 | tf_op jit(solution)/shard_map/ppermute | solution.py:49
  13.6 1.1 fusion.18
  15.4 4.8 %collective-permute-start.2 = (f32[512,128]{1,0:T(8,128)}, f32[512,128]{1,0:T(8,128)}, u32[]{:S(2)}, u32[]{:S(2)}) collective-permute-start(f32[512,128]{1,0:T(8,128)} %collective-permute-done.1.across_ref), channel_id=1, source_target_pairs={{0,32},{32,0},{64,96},{96,64},{128,160},{160,128},{192,224},{224,1... | collective-permute-start | bytes 786440 | tf_op jit(solution)/shard_map/ppermute | solution.py:49
  20.9 1.4 %broadcast_multiply_fusion.scale_ref = f32[16,128]{1,0:T(8,128)} fusion(f32[16]{0:T(128)S(1)} %or_convert_fusion, f32[1,16,128]{2,1,0:T(8,128)} %param.13), kind=kLoop, calls=%fused_computation.38 | loop fusion | flops 2048 | bytes 16448 | tf_op jit(solution)/shard_map/mul | solution.py:151
  22.2 2.3 %shard_map.109 = f32[4,512,128]{2,1,0:T(8,128)} custom-call(s32[1]{0:T(128)} %bitcast.index_ref, f32[16,16]{1,0:T(8,128)} %constant.28.clone.coef_ref, f32[512,128]{1,0:T(8,128)} %bitcast.2.own_ref, f32[512,128]{1,0:T(8,128)} %collective-permute-done.mate_ref, f32[512,128]{1,0:T(8,128)} %collective-permute-done.1.across_ref, ...), custom_call_target="tpu_custom_call" | custom-call | tf_op jit(solution)/shard_map/pallas_call | solution.py:91
  24.5 1.9 %collective-permute-start.3 = (bf16[1,5,32,128]{3,2,1,0:T(8,128)(2,1)}, bf16[1,5,32,128]{3,2,1,0:T(8,128)(2,1)}, u32[]{:S(2)}, u32[]{:S(2)}) collective-permute-start(bf16[1,5,32,128]{3,2,1,0:T(8,128)(2,1)} %pad_maximum_fusion), channel_id=1, source_target_pairs={{31,0},{0,1},{1,2},{2,3},{3,4},{4,5},{5,6},{6,7},{7,8},{8,9},{9,10... | collective-permute-start | bytes 122888 | tf_op jit(solution)/shard_map/ppermute | solution.py:32
  27.0 10.0 %collective-permute-start.4 = (bf16[1,1,32,128]{3,2,1,0:T(8,128)(2,1)}, bf16[1,1,32,128]{3,2,1,0:T(8,128)(2,1)}, u32[]{:S(2)}, u32[]{:S(2)}) collective-permute-start(bf16[1,1,32,128]{3,2,1,0:T(8,128)(2,1)} %slice.33), channel_id=1, source_target_pairs={{1,0},{2,1},{3,2},{4,3},{5,4},{6,5},{7,6},{8,7},{9,8},{10,9},{11,1... | collective-permute-start | bytes 24584 | tf_op jit(solution)/shard_map/ppermute | solution.py:32
  37.1 1.2 %broadcast_subtract_fusion = f32[4]{0:T(128)} fusion(s32[1,4]{1,0:T(1,128)} %param.18), kind=kLoop, calls=%fused_computation.41 | loop fusion | flops 8 | bytes 32 | tf_op jit(solution)/shard_map/sub | solution.py:171
  38.2 4.3 %all-to-all-start = ((f32[4,512,128]{2,1,0:T(8,128)}), f32[4,512,128]{2,1,0:T(8,128)}, u32[]{:S(2)}, u32[]{:S(2)}) async-start(f32[4,512,128]{2,1,0:T(8,128)} %shard_map.109), calls=%async_computation | async-start | bytes 2097152 | tf_op jit(solution)/shard_map/all_to_all | solution.py:136
  42.5 0.7 slice.42
  43.2 0.7 maximum_bitcast_fusion
  43.9 0.9 bitcast_add_fusion.1
  45.3 2.5 %multiply_add_fusion.1 = f32[1,16,32,128]{3,2,1,0:T(8,128)} fusion(f32[1,16,32,128]{3,2,1,0:T(8,128)S(1)} %copy-done.1, f32[1,4,32,128]{3,2,1,0:T(8,128)S(1)} %bitcast_add_fusion.1, f32[1,16,32,128]{3,2,1,0:T(8,128)} %param.11, f32[16,128]{1,0:T(8,128)S(1)} %bitcast.82, f32[16]{0:T(128)S(1)} %or_convert_fusion, ...), kind=kOutput, calls=%fused_computation.13 | convolution fusion | flops 101056512 | bytes 4792384 | tf_op jit(solution)/shard_map/tnkri,tnkio->tnro/dot_general | solution.py:169
  47.8 9.6 %all-to-all-done.got_ref = f32[4,512,128]{2,1,0:T(8,128)} async-done(((f32[4,512,128]{2,1,0:T(8,128)}), f32[4,512,128]{2,1,0:T(8,128)}, u32[]{:S(2)}, u32[]{:S(2)}) %all-to-all-start) | async-done | bytes 1048608 | tf_op jit(solution)/shard_map/all_to_all | solution.py:136
  57.4 2.0 %shard_map.110 = (f32[512,128]{1,0:T(8,128)}, f32[512,128]{1,0:T(8,128)}) custom-call(f32[4,512,128]{2,1,0:T(8,128)} %all-to-all-done.got_ref, f32[512,128]{1,0:T(8,128)} %bitcast.81, f32[16,128]{1,0:T(8,128)} %broadcast_multiply_fusion.scale_ref, f32[16,128]{1,0:T(8,128)} %cond_ref.3), custom_call_target="tpu_custom_call" | custom-call | tf_op jit(solution)/shard_map/pallas_call | solution.py:121
  59.5 2.3 %collective-permute-start.6 = (f32[512,128]{1,0:T(8,128)}, f32[512,128]{1,0:T(8,128)S(1)}, u32[]{:S(2)}, u32[]{:S(2)}) collective-permute-start(f32[512,128]{1,0:T(8,128)} %get-tuple-element.13.own_ref), channel_id=1, source_target_pairs={{0,256},{32,288},{64,320},{96,352},{128,384},{160,416},{192,448},{... | collective-permute-start | bytes 786440 | tf_op jit(solution)/shard_map/ppermute | solution.py:49
  61.8 3.4 %collective-permute-start.5 = (f32[512,128]{1,0:T(8,128)}, f32[512,128]{1,0:T(8,128)}, u32[]{:S(2)}, u32[]{:S(2)}) collective-permute-start(f32[512,128]{1,0:T(8,128)} %get-tuple-element.13.own_ref), channel_id=1, source_target_pairs={{0,32},{32,0},{64,96},{96,64},{128,160},{160,128},{192,224},{224,1... | collective-permute-start | bytes 786440 | tf_op jit(solution)/shard_map/ppermute | solution.py:49
  65.2 1.0 convert_element_type.74
  66.1 1.1 fusion.16
  67.2 1.0 collective-permute-done.6.across_ref
  68.2 4.0 %collective-permute-start.7 = (f32[512,128]{1,0:T(8,128)S(1)}, f32[512,128]{1,0:T(8,128)}, u32[]{:S(2)}, u32[]{:S(2)}) collective-permute-start(f32[512,128]{1,0:T(8,128)S(1)} %collective-permute-done.6.across_ref), channel_id=1, source_target_pairs={{0,32},{32,0},{64,96},{96,64},{128,160},{160,128},{192,224},{224,1... | collective-permute-start | bytes 786440 | tf_op jit(solution)/shard_map/ppermute | solution.py:49
  73.5 2.3 %shard_map.111 = f32[4,512,128]{2,1,0:T(8,128)} custom-call(s32[1]{0:T(128)} %bitcast.index_ref, f32[16,16]{1,0:T(8,128)} %constant.28.clone.coef_ref, f32[512,128]{1,0:T(8,128)} %get-tuple-element.13.own_ref, f32[512,128]{1,0:T(8,128)} %collective-permute-done.5.mate_ref, f32[512,128]{1,0:T(8,128)} %copy-done.4, f32[512,128]{1,0:T(8,128)} %collective-permute-done.7.diagonal_ref), custom_call_target="tpu_custom_call" | custom-call | tf_op jit(solution)/shard_map/pallas_call | solution.py:91
  75.8 1.9 %collective-permute-start.8 = (bf16[1,5,32,128]{3,2,1,0:T(8,128)(2,1)}, bf16[1,5,32,128]{3,2,1,0:T(8,128)(2,1)}, u32[]{:S(2)}, u32[]{:S(2)}) collective-permute-start(bf16[1,5,32,128]{3,2,1,0:T(8,128)(2,1)} %pad_maximum_fusion.1), channel_id=1, source_target_pairs={{31,0},{0,1},{1,2},{2,3},{3,4},{4,5},{5,6},{6,7},{7,8},{8,9},{9,10... | collective-permute-start | bytes 122888 | tf_op jit(solution)/shard_map/ppermute | solution.py:32
  78.3 7.0 %collective-permute-start.9 = (bf16[1,1,32,128]{3,2,1,0:T(8,128)(2,1)}, bf16[1,1,32,128]{3,2,1,0:T(8,128)(2,1)}, u32[]{:S(2)}, u32[]{:S(2)}) collective-permute-start(bf16[1,1,32,128]{3,2,1,0:T(8,128)(2,1)} %slice.38), channel_id=1, source_target_pairs={{1,0},{2,1},{3,2},{4,3},{5,4},{6,5},{7,6},{8,7},{9,8},{10,9},{11,1... | collective-permute-start | bytes 24584 | tf_op jit(solution)/shard_map/ppermute | solution.py:32
  85.3 4.3 %all-to-all-start.1 = ((f32[4,512,128]{2,1,0:T(8,128)}), f32[4,512,128]{2,1,0:T(8,128)}, u32[]{:S(2)}, u32[]{:S(2)}) async-start(f32[4,512,128]{2,1,0:T(8,128)} %shard_map.111), calls=%async_computation.1 | async-start | bytes 2097152 | tf_op jit(solution)/shard_map/all_to_all | solution.py:136
  90.3 0.7 maximum_bitcast_fusion.1
  91.0 0.9 bitcast_add_fusion
  92.3 2.5 %multiply_add_fusion = f32[1,16,32,128]{3,2,1,0:T(8,128)} fusion(f32[1,16,32,128]{3,2,1,0:T(8,128)} %bitcast.80, f32[1,16,32,128]{3,2,1,0:T(8,128)S(1)} %copy-done.1, f32[1,4,32,128]{3,2,1,0:T(8,128)S(1)} %bitcast_add_fusion, f32[16,128]{1,0:T(8,128)S(1)} %bitcast.83, f32[16]{0:T(128)S(1)} %or_convert_fusion, bf16[1,16,6,128,128]{4,3,2,1,0:T(8,128)(2,1)S(1)} %copy-done, ...), kind=kOutput, calls=%fused_computation.12 | convolution fusion | flops 100990976 | bytes 4792384 | tf_op jit(solution)/shard_map/tnkri,tnkio->tnro/dot_general | solution.py:169
  94.8 9.1 %all-to-all-done.1.got_ref = f32[4,512,128]{2,1,0:T(8,128)} async-done(((f32[4,512,128]{2,1,0:T(8,128)}), f32[4,512,128]{2,1,0:T(8,128)}, u32[]{:S(2)}, u32[]{:S(2)}) %all-to-all-start.1) | async-done | bytes 1048608 | tf_op jit(solution)/shard_map/all_to_all | solution.py:136
  103.9 2.0 %shard_map.112 = f32[512,128]{1,0:T(8,128)} custom-call(f32[4,512,128]{2,1,0:T(8,128)} %all-to-all-done.1.got_ref, f32[512,128]{1,0:T(8,128)} %bitcast.78, f32[16,128]{1,0:T(8,128)} %broadcast_multiply_fusion.scale_ref, f32[16,128]{1,0:T(8,128)} %cond_ref.3), custom_call_target="tpu_custom_call" | custom-call | tf_op jit(solution)/shard_map/pallas_call | solution.py:121
  (38 shorter events, 5.4 us)
Async XLA Ops:
  0.0 45.3 %copy-start = (bf16[1,16,6,128,128]{4,3,2,1,0:T(8,128)(2,1)S(1)}, bf16[1,16,6,128,128]{4,3,2,1,0:T(8,128)(2,1)}, u32[]{:S(2)}) copy-start(bf16[1,16,6,128,128]{4,3,2,1,0:T(8,128)(2,1)} %param.15) | copy-start | bytes 9437188
  0.0 44.9 %copy-start.6 = (s32[16,6]{0,1:T(8,128)S(1)}, s32[16,6]{0,1:T(8,128)}, u32[]{:S(2)}) copy-start(s32[16,6]{0,1:T(8,128)} %param.17) | copy-start | bytes 1156
  2.7 42.6 %copy-start.1 = (f32[1,16,32,128]{3,2,1,0:T(8,128)S(1)}, f32[1,16,32,128]{3,2,1,0:T(8,128)}, u32[]{:S(2)}) copy-start(f32[1,16,32,128]{3,2,1,0:T(8,128)} %param.12) | copy-start | bytes 786436
  2.7 42.6 %copy-start.5 = (f32[1,16,128]{2,1,0:T(8,128)S(1)}, f32[1,16,128]{2,1,0:T(8,128)}, u32[]{:S(2)}) copy-start(f32[1,16,128]{2,1,0:T(8,128)} %param.13) | copy-start | bytes 24580
  2.7 12.6 %collective-permute-start.1 = (f32[512,128]{1,0:T(8,128)}, f32[512,128]{1,0:T(8,128)}, u32[]{:S(2)}, u32[]{:S(2)}) collective-permute-start(f32[512,128]{1,0:T(8,128)} %bitcast.2.own_ref), channel_id=1, source_target_pairs={{0,256},{32,288},{64,320},{96,352},{128,384},{160,416},{192,448},{... | collective-permute-start | bytes 786440 | tf_op jit(solution)/shard_map/ppermute | solution.py:49
  6.9 15.3 %collective-permute-start = (f32[512,128]{1,0:T(8,128)}, f32[512,128]{1,0:T(8,128)}, u32[]{:S(2)}, u32[]{:S(2)}) collective-permute-start(f32[512,128]{1,0:T(8,128)} %bitcast.2.own_ref), channel_id=1, source_target_pairs={{0,32},{32,0},{64,96},{96,64},{128,160},{160,128},{192,224},{224,1... | collective-permute-start | bytes 786440 | tf_op jit(solution)/shard_map/ppermute | solution.py:49
  14.6 0.7 copy-start.2
  15.3 5.5 %copy-start.7 = (f32[4]{0:T(128)}, f32[4]{0:T(128)S(1)}, u32[]{:S(2)}) copy-start(f32[4]{0:T(128)S(1)} %convert_bitcast_fusion) | copy-start | bytes 52
  15.4 6.8 %collective-permute-start.2 = (f32[512,128]{1,0:T(8,128)}, f32[512,128]{1,0:T(8,128)}, u32[]{:S(2)}, u32[]{:S(2)}) collective-permute-start(f32[512,128]{1,0:T(8,128)} %collective-permute-done.1.across_ref), channel_id=1, source_target_pairs={{0,32},{32,0},{64,96},{96,64},{128,160},{160,128},{192,224},{224,1... | collective-permute-start | bytes 786440 | tf_op jit(solution)/shard_map/ppermute | solution.py:49
  24.5 18.0 %collective-permute-start.3 = (bf16[1,5,32,128]{3,2,1,0:T(8,128)(2,1)}, bf16[1,5,32,128]{3,2,1,0:T(8,128)(2,1)}, u32[]{:S(2)}, u32[]{:S(2)}) collective-permute-start(bf16[1,5,32,128]{3,2,1,0:T(8,128)(2,1)} %pad_maximum_fusion), channel_id=1, source_target_pairs={{31,0},{0,1},{1,2},{2,3},{3,4},{4,5},{5,6},{6,7},{7,8},{8,9},{9,10... | collective-permute-start | bytes 122888 | tf_op jit(solution)/shard_map/ppermute | solution.py:32
  27.0 16.2 %collective-permute-start.4 = (bf16[1,1,32,128]{3,2,1,0:T(8,128)(2,1)}, bf16[1,1,32,128]{3,2,1,0:T(8,128)(2,1)}, u32[]{:S(2)}, u32[]{:S(2)}) collective-permute-start(bf16[1,1,32,128]{3,2,1,0:T(8,128)(2,1)} %slice.33), channel_id=1, source_target_pairs={{1,0},{2,1},{3,2},{4,3},{5,4},{6,5},{7,6},{8,7},{9,8},{10,9},{11,1... | collective-permute-start | bytes 24584 | tf_op jit(solution)/shard_map/ppermute | solution.py:32
  38.2 19.2 %all-to-all-start = ((f32[4,512,128]{2,1,0:T(8,128)}), f32[4,512,128]{2,1,0:T(8,128)}, u32[]{:S(2)}, u32[]{:S(2)}) async-start(f32[4,512,128]{2,1,0:T(8,128)} %shard_map.109), calls=%async_computation | async-start | bytes 2097152 | tf_op jit(solution)/shard_map/all_to_all | solution.py:136
  59.5 8.7 %collective-permute-start.6 = (f32[512,128]{1,0:T(8,128)}, f32[512,128]{1,0:T(8,128)S(1)}, u32[]{:S(2)}, u32[]{:S(2)}) collective-permute-start(f32[512,128]{1,0:T(8,128)} %get-tuple-element.13.own_ref), channel_id=1, source_target_pairs={{0,256},{32,288},{64,320},{96,352},{128,384},{160,416},{192,448},{... | collective-permute-start | bytes 786440 | tf_op jit(solution)/shard_map/ppermute | solution.py:49
  61.8 11.7 %collective-permute-start.5 = (f32[512,128]{1,0:T(8,128)}, f32[512,128]{1,0:T(8,128)}, u32[]{:S(2)}, u32[]{:S(2)}) collective-permute-start(f32[512,128]{1,0:T(8,128)} %get-tuple-element.13.own_ref), channel_id=1, source_target_pairs={{0,32},{32,0},{64,96},{96,64},{128,160},{160,128},{192,224},{224,1... | collective-permute-start | bytes 786440 | tf_op jit(solution)/shard_map/ppermute | solution.py:49
  67.2 5.0 %copy-start.3 = (f32[4,32,128]{2,1,0:T(8,128)}, f32[4,32,128]{2,1,0:T(8,128)S(1)}, u32[]{:S(2)}) copy-start(f32[4,32,128]{2,1,0:T(8,128)S(1)} %fusion.16) | copy-start | bytes 196612
  68.2 4.7 %copy-start.4 = (f32[512,128]{1,0:T(8,128)}, f32[512,128]{1,0:T(8,128)S(1)}, u32[]{:S(2)}) copy-start(f32[512,128]{1,0:T(8,128)S(1)} %collective-permute-done.6.across_ref) | copy-start | bytes 786436
  68.2 5.3 %collective-permute-start.7 = (f32[512,128]{1,0:T(8,128)S(1)}, f32[512,128]{1,0:T(8,128)}, u32[]{:S(2)}, u32[]{:S(2)}) collective-permute-start(f32[512,128]{1,0:T(8,128)S(1)} %collective-permute-done.6.across_ref), channel_id=1, source_target_pairs={{0,32},{32,0},{64,96},{96,64},{128,160},{160,128},{192,224},{224,1... | collective-permute-start | bytes 786440 | tf_op jit(solution)/shard_map/ppermute | solution.py:49
  75.8 13.8 %collective-permute-start.8 = (bf16[1,5,32,128]{3,2,1,0:T(8,128)(2,1)}, bf16[1,5,32,128]{3,2,1,0:T(8,128)(2,1)}, u32[]{:S(2)}, u32[]{:S(2)}) collective-permute-start(bf16[1,5,32,128]{3,2,1,0:T(8,128)(2,1)} %pad_maximum_fusion.1), channel_id=1, source_target_pairs={{31,0},{0,1},{1,2},{2,3},{3,4},{4,5},{5,6},{6,7},{7,8},{8,9},{9,10... | collective-permute-start | bytes 122888 | tf_op jit(solution)/shard_map/ppermute | solution.py:32
  78.3 12.0 %collective-permute-start.9 = (bf16[1,1,32,128]{3,2,1,0:T(8,128)(2,1)}, bf16[1,1,32,128]{3,2,1,0:T(8,128)(2,1)}, u32[]{:S(2)}, u32[]{:S(2)}) collective-permute-start(bf16[1,1,32,128]{3,2,1,0:T(8,128)(2,1)} %slice.38), channel_id=1, source_target_pairs={{1,0},{2,1},{3,2},{4,3},{5,4},{6,5},{7,6},{8,7},{9,8},{10,9},{11,1... | collective-permute-start | bytes 24584 | tf_op jit(solution)/shard_map/ppermute | solution.py:32
  85.3 18.6 %all-to-all-start.1 = ((f32[4,512,128]{2,1,0:T(8,128)}), f32[4,512,128]{2,1,0:T(8,128)}, u32[]{:S(2)}, u32[]{:S(2)}) async-start(f32[4,512,128]{2,1,0:T(8,128)} %shard_map.111), calls=%async_computation.1 | async-start | bytes 2097152 | tf_op jit(solution)/shard_map/all_to_all | solution.py:136

commit v17 on v12

--- a/solution.py
+++ b/solution.py
@@ -149,7 +149,8 @@
     relax_wide = relax[:, :, None, :]
     cond_wide = cond[None, :, None, :]
     scale = relax[0] * live[0, :, 0]
-    weighted = (lam * cond_wide).reshape(-1, lanes)
+    weighted = (lam_init * (live * cond_wide)).reshape(-1, lanes)
+    lam = lax.optimization_barrier((lam_init, weighted))[0] * live
     for sweep in range(SWEEPS):
         lam_b = lam.astype(jnp.bfloat16)
         partials, got = instance_mix(weighted)

time: 92.5 us -> 93.6 us (1.012)
  other arithmetic: 13.2 us -> 14.2 us
    mul x0 -> x1, other arithmetic: none -> 1.68 us  [shards(): weighted = (lam_init * (live * cond_wide)).reshape(-1, lanes)]
where the time goes in v17:
time: 93.6 us; the launch traced here: 92.2 us
  starting transfers between devices  51.2 us (55%)
  other arithmetic  14.2 us (15%)
  Pallas kernels  8.53 us (9%)
  matrix products  7.22 us (8%)
  local copies, waits for them, and re-layouts  5.38 us (6%)
  waiting for transfers between devices  4.5 us (5%)
  between operations  1.09 us (1%)
    ppermute x6, starting transfers between devices, routed(): return lax.ppermute(block, INST, [(s, dest(s)) for s in range(NT)])  21.9 us
    ppermute x4, starting transfers between devices, shifted(): return lax.ppermute(block, axis, route)  20.9 us
    all_to_all x2, starting transfers between devices, instance_mix(): return (partials, lax.all_to_all(partials, 'ix', 0, 0))  8.48 us
    dot_general x2, matrix products, shards(): jnp.einsum('tnkri,tnkio->tnro', picked, jac, preferred_element_type=jnp.f...  5.12 us
    pallas_call x2, Pallas kernels, partial_sums(): pl.pallas_call(mix_kernel, grid_spec=pltpu.PrefetchScalarGridSpec(num_sca...  4.5 us
    pallas_call x2, Pallas kernels, updated(): pl.pallas_call(update_kernel, grid=(rows // block,), in_specs=[pl.BlockSp...  4.03 us
    ppermute x6, waiting for transfers between devices, routed(): return lax.ppermute(block, INST, [(s, dest(s)) for s in range(NT)])  3.6 us
    gather x2, local copies, waits for them, and re-layouts, shards(): picked = lam_h[:, cols]  3.39 us
  transfers between devices with their start and end apart: 12, of which 3 were waited for; matrix products, arithmetic and copies ran while one was open for 24% of the time, Pallas kernels for 0%

profile of v17, /device:TPU:1, one launch (start us, length us, event | category | flops | bytes accessed | tf_op | source)
XLA Modules:
  0.0 92.2 jit_solution(3403815986178906981)
XLA Ops:
  0.8 1.5 %broadcast_multiply_fusion.1 = (f32[16,128]{1,0:T(8,128)}, f32[16,128]{1,0:T(8,128)S(1)}) fusion(f32[16]{0:T(128)S(1)} %or_convert_fusion, f32[1,16,128]{2,1,0:T(8,128)} %param.13, f32[16,128]{1,0:T(8,128)} %cond_ref.3), kind=kLoop, calls=%fused_computation.30 | loop fusion | flops 4096 | bytes 32832 | tf_op jit(solution)/shard_map/mul | solution.py:151
  2.3 1.7 %broadcast_multiply_fusion = f32[1,16,32,128]{3,2,1,0:T(8,128)} fusion(f32[1,16,32,128]{3,2,1,0:T(8,128)} %param.11, f32[16,128]{1,0:T(8,128)S(1)} %get-tuple-element.20), kind=kLoop, calls=%fused_computation.17 | loop fusion | flops 65536 | bytes 532480 | tf_op jit(solution)/shard_map/mul | solution.py:152
  4.0 4.0 %collective-permute-start.1 = (f32[512,128]{1,0:T(8,128)}, f32[512,128]{1,0:T(8,128)}, u32[]{:S(2)}, u32[]{:S(2)}) collective-permute-start(f32[512,128]{1,0:T(8,128)} %bitcast.2.own_ref), channel_id=1, source_target_pairs={{0,256},{32,288},{64,320},{96,352},{128,384},{160,416},{192,448},{... | collective-permute-start | bytes 786440 | tf_op jit(solution)/shard_map/ppermute | solution.py:49
  8.1 6.7 %collective-permute-start = (f32[512,128]{1,0:T(8,128)}, f32[512,128]{1,0:T(8,128)}, u32[]{:S(2)}, u32[]{:S(2)}) collective-permute-start(f32[512,128]{1,0:T(8,128)} %bitcast.2.own_ref), channel_id=1, source_target_pairs={{0,32},{32,0},{64,96},{96,64},{128,160},{160,128},{192,224},{224,1... | collective-permute-start | bytes 786440 | tf_op jit(solution)/shard_map/ppermute | solution.py:49
  14.7 1.0 %multiply_convert_fusion = bf16[1,16,32,128]{3,2,1,0:T(8,128)(2,1)S(1)} fusion(f32[1,16,32,128]{3,2,1,0:T(8,128)} %param.11, f32[16]{0:T(128)S(1)} %or_convert_fusion), kind=kLoop, calls=%fused_computation.10 | loop fusion | flops 131072 | bytes 393280 | tf_op jit(solution)/shard_map/convert_element_type | solution.py:155
  16.5 1.0 %fusion.12 = f32[4,32,128]{2,1,0:T(8,128)S(1)} fusion(bf16[1,4,128,128]{3,2,1,0:T(8,128)(2,1)} %param.16, bf16[1,16,32,128]{3,2,1,0:T(8,128)(2,1)S(1)} %multiply_convert_fusion), kind=kOutput, calls=%fused_computation.15 | convolution fusion | flops 4194304 | bytes 229376 | tf_op jit(solution)/shard_map/tjri,tjio->tjro/dot_general | solution.py:157
  18.3 3.0 %collective-permute-start.2 = (f32[512,128]{1,0:T(8,128)}, f32[512,128]{1,0:T(8,128)}, u32[]{:S(2)}, u32[]{:S(2)}) collective-permute-start(f32[512,128]{1,0:T(8,128)} %collective-permute-done.1.across_ref), channel_id=1, source_target_pairs={{0,32},{32,0},{64,96},{96,64},{128,160},{160,128},{192,224},{224,1... | collective-permute-start | bytes 786440 | tf_op jit(solution)/shard_map/ppermute | solution.py:49
  22.2 1.2 %broadcast_subtract_fusion = f32[4]{0:T(128)} fusion(s32[1,4]{1,0:T(1,128)} %param.18), kind=kLoop, calls=%fused_computation.34 | loop fusion | flops 8 | bytes 32 | tf_op jit(solution)/shard_map/sub | solution.py:171
  23.4 2.2 %shard_map.109 = f32[4,512,128]{2,1,0:T(8,128)} custom-call(s32[1]{0:T(128)} %bitcast.index_ref, f32[16,16]{1,0:T(8,128)} %constant.32.clone.coef_ref, f32[512,128]{1,0:T(8,128)} %bitcast.2.own_ref, f32[512,128]{1,0:T(8,128)} %collective-permute-done.mate_ref, f32[512,128]{1,0:T(8,128)} %collective-permute-done.1.across_ref, ...), custom_call_target="tpu_custom_call" | custom-call | tf_op jit(solution)/shard_map/pallas_call | solution.py:91
  25.6 4.2 %all-to-all-start = ((f32[4,512,128]{2,1,0:T(8,128)}), f32[4,512,128]{2,1,0:T(8,128)}, u32[]{:S(2)}, u32[]{:S(2)}) async-start(f32[4,512,128]{2,1,0:T(8,128)} %shard_map.109), calls=%async_computation | async-start | bytes 2097152 | tf_op jit(solution)/shard_map/all_to_all | solution.py:136
  29.9 1.9 %collective-permute-start.3 = (bf16[1,5,32,128]{3,2,1,0:T(8,128)(2,1)}, bf16[1,5,32,128]{3,2,1,0:T(8,128)(2,1)S(1)}, u32[]{:S(2)}, u32[]{:S(2)}) collective-permute-start(bf16[1,5,32,128]{3,2,1,0:T(8,128)(2,1)} %pad_maximum_fusion), channel_id=1, source_target_pairs={{31,0},{0,1},{1,2},{2,3},{3,4},{4,5},{5,6},{6,7},{7,8},{8,9},{9,10... | collective-permute-start | bytes 122888 | tf_op jit(solution)/shard_map/ppermute | solution.py:32
  31.8 10.1 %collective-permute-start.4 = (bf16[1,1,32,128]{3,2,1,0:T(8,128)(2,1)S(1)}, bf16[1,1,32,128]{3,2,1,0:T(8,128)(2,1)S(1)}, u32[]{:S(2)}, u32[]{:S(2)}) collective-permute-start(bf16[1,1,32,128]{3,2,1,0:T(8,128)(2,1)S(1)} %slice.33), channel_id=1, source_target_pairs={{1,0},{2,1},{3,2},{4,3},{5,4},{6,5},{7,6},{8,7},{9,8},{10,9},{11,1... | collective-permute-start | bytes 24584 | tf_op jit(solution)/shard_map/ppermute | solution.py:32
  43.1 0.9 %maximum_bitcast_fusion = bf16[18,32,128]{2,1,0:T(8,128)(2,1)S(1)} fusion(bf16[1,1,32,128]{3,2,1,0:T(8,128)(2,1)S(1)} %collective-permute-done.4, bf16[1,16,32,128]{3,2,1,0:T(8,128)(2,1)} %copy-done.4, bf16[1,1,32,128]{3,2,1,0:T(8,128)(2,1)S(1)} %slice.46), kind=kLoop, calls=%fused_computation.11 | loop fusion | flops 147456 | bytes 294912 | tf_op jit(solution)/shard_map/concatenate | solution.py:167
  44.0 1.7 %gather_fusion = bf16[96,32,128]{2,1,0:T(8,128)(2,1)} fusion(bf16[18,32,128]{2,1,0:T(8,128)(2,1)S(1)} %maximum_bitcast_fusion, s32[1024]{0:T(1024)} %pad_clamp_fusion), kind=kCustom, calls=%fused_computation | custom fusion | bytes 1573248 | tf_op jit(solution)/shard_map/gather | solution.py:168
  45.7 0.9 %bitcast_add_fusion.1 = f32[1,4,32,128]{3,2,1,0:T(8,128)S(1)} fusion(f32[4,32,128]{2,1,0:T(8,128)} %copy-done.5, bf16[1,5,32,128]{3,2,1,0:T(8,128)(2,1)} %copy-done.9, f32[4]{0:T(128)} %broadcast_subtract_fusion), kind=kLoop, calls=%fused_computation.19 | loop fusion | flops 49152 | bytes 163856 | tf_op jit(solution)/shard_map/add | solution.py:171
  46.7 2.6 %multiply_add_fusion.1 = f32[1,16,32,128]{3,2,1,0:T(8,128)} fusion(f32[1,16,32,128]{3,2,1,0:T(8,128)} %param.12, f32[1,4,32,128]{3,2,1,0:T(8,128)S(1)} %bitcast_add_fusion.1, f32[1,16,32,128]{3,2,1,0:T(8,128)S(1)} %copy-done.1, f32[16,128]{1,0:T(8,128)} %bitcast.68, f32[16]{0:T(128)} %copy-done.11, bf16[16,6,32,128]{3,2,1,0:T(8,128)(2,1)} %bitcast.63, ...), kind=kOutput, calls=%fused_computation.9 | convolution fusion | flops 101056512 | bytes 4792384 | tf_op jit(solution)/shard_map/tnkri,tnkio->tnro/dot_general | solution.py:169
  49.3 2.0 %shard_map.110 = (f32[512,128]{1,0:T(8,128)}, f32[512,128]{1,0:T(8,128)}) custom-call(f32[4,512,128]{2,1,0:T(8,128)} %all-to-all-done.got_ref, f32[512,128]{1,0:T(8,128)} %bitcast.67, f32[16,128]{1,0:T(8,128)} %get-tuple-element.19.scale_ref, f32[16,128]{1,0:T(8,128)} %cond_ref.3), custom_call_target="tpu_custom_call" | custom-call | tf_op jit(solution)/shard_map/pallas_call | solution.py:121
  51.3 2.3 %collective-permute-start.6 = (f32[512,128]{1,0:T(8,128)}, f32[512,128]{1,0:T(8,128)S(1)}, u32[]{:S(2)}, u32[]{:S(2)}) collective-permute-start(f32[512,128]{1,0:T(8,128)} %get-tuple-element.15.own_ref), channel_id=1, source_target_pairs={{0,256},{32,288},{64,320},{96,352},{128,384},{160,416},{192,448},{... | collective-permute-start | bytes 786440 | tf_op jit(solution)/shard_map/ppermute | solution.py:49
  53.6 2.6 %collective-permute-start.5 = (f32[512,128]{1,0:T(8,128)}, f32[512,128]{1,0:T(8,128)S(1)}, u32[]{:S(2)}, u32[]{:S(2)}) collective-permute-start(f32[512,128]{1,0:T(8,128)} %get-tuple-element.15.own_ref), channel_id=1, source_target_pairs={{0,32},{32,0},{64,96},{96,64},{128,160},{160,128},{192,224},{224,1... | collective-permute-start | bytes 786440 | tf_op jit(solution)/shard_map/ppermute | solution.py:49
  56.2 1.0 %convert_element_type.51 = bf16[1,16,32,128]{3,2,1,0:T(8,128)(2,1)S(1)} convert(f32[1,16,32,128]{3,2,1,0:T(8,128)} %bitcast.65) | non-fusion elementwise | flops 65536 | bytes 393216 | tf_op jit(solution)/shard_map/convert_element_type | solution.py:155
  57.2 3.6 %collective-permute-done.6.across_ref = f32[512,128]{1,0:T(8,128)S(1)} collective-permute-done((f32[512,128]{1,0:T(8,128)}, f32[512,128]{1,0:T(8,128)S(1)}, u32[]{:S(2)}, u32[]{:S(2)}) %collective-permute-start.6) | collective-permute-done | bytes 262176 | tf_op jit(solution)/shard_map/ppermute | solution.py:49
  60.8 3.2 %collective-permute-start.7 = (f32[512,128]{1,0:T(8,128)S(1)}, f32[512,128]{1,0:T(8,128)}, u32[]{:S(2)}, u32[]{:S(2)}) collective-permute-start(f32[512,128]{1,0:T(8,128)S(1)} %collective-permute-done.6.across_ref), channel_id=1, source_target_pairs={{0,32},{32,0},{64,96},{96,64},{128,160},{160,128},{192,224},{224,1... | collective-permute-start | bytes 786440 | tf_op jit(solution)/shard_map/ppermute | solution.py:49
  64.0 1.1 %fusion.10 = f32[4,32,128]{2,1,0:T(8,128)S(1)} fusion(bf16[1,4,128,128]{3,2,1,0:T(8,128)(2,1)} %param.16, bf16[1,16,32,128]{3,2,1,0:T(8,128)(2,1)S(1)} %convert_element_type.51), kind=kOutput, calls=%fused_computation.13 | convolution fusion | flops 4194304 | bytes 229376 | tf_op jit(solution)/shard_map/tjri,tjio->tjro/dot_general | solution.py:157
  67.1 2.2 %shard_map.111 = f32[4,512,128]{2,1,0:T(8,128)} custom-call(s32[1]{0:T(128)} %bitcast.index_ref, f32[16,16]{1,0:T(8,128)} %constant.32.clone.coef_ref, f32[512,128]{1,0:T(8,128)} %get-tuple-element.15.own_ref, f32[512,128]{1,0:T(8,128)} %copy-done.8, f32[512,128]{1,0:T(8,128)} %copy-done.7, f32[512,128]{1,0:T(8,128)} %collective-permute-done.7.diagonal_ref), custom_call_target="tpu_custom_call" | custom-call | tf_op jit(solution)/shard_map/pallas_call | solution.py:91
  69.3 4.2 %all-to-all-start.1 = ((f32[4,512,128]{2,1,0:T(8,128)}), f32[4,512,128]{2,1,0:T(8,128)}, u32[]{:S(2)}, u32[]{:S(2)}) async-start(f32[4,512,128]{2,1,0:T(8,128)} %shard_map.111), calls=%async_computation.1 | async-start | bytes 2097152 | tf_op jit(solution)/shard_map/all_to_all | solution.py:136
  74.4 1.9 %collective-permute-start.8 = (bf16[1,5,32,128]{3,2,1,0:T(8,128)(2,1)S(1)}, bf16[1,5,32,128]{3,2,1,0:T(8,128)(2,1)S(1)}, u32[]{:S(2)}, u32[]{:S(2)}) collective-permute-start(bf16[1,5,32,128]{3,2,1,0:T(8,128)(2,1)S(1)} %pad_maximum_fusion.1), channel_id=1, source_target_pairs={{31,0},{0,1},{1,2},{2,3},{3,4},{4,5},{5,6},{6,7},{7,8},{8,9},{9,10... | collective-permute-start | bytes 122888 | tf_op jit(solution)/shard_map/ppermute | solution.py:32
  76.3 7.0 %collective-permute-start.9 = (bf16[1,1,32,128]{3,2,1,0:T(8,128)(2,1)S(1)}, bf16[1,1,32,128]{3,2,1,0:T(8,128)(2,1)S(1)}, u32[]{:S(2)}, u32[]{:S(2)}) collective-permute-start(bf16[1,1,32,128]{3,2,1,0:T(8,128)(2,1)S(1)} %slice.38), channel_id=1, source_target_pairs={{1,0},{2,1},{3,2},{4,3},{5,4},{6,5},{7,6},{8,7},{9,8},{10,9},{11,1... | collective-permute-start | bytes 24584 | tf_op jit(solution)/shard_map/ppermute | solution.py:32
  84.0 0.9 %maximum_bitcast_fusion.1 = bf16[18,32,128]{2,1,0:T(8,128)(2,1)S(1)} fusion(bf16[1,1,32,128]{3,2,1,0:T(8,128)(2,1)S(1)} %collective-permute-done.9, bf16[1,16,32,128]{3,2,1,0:T(8,128)(2,1)} %copy-done.3, bf16[1,1,32,128]{3,2,1,0:T(8,128)(2,1)S(1)} %slice.50), kind=kLoop, calls=%fused_computation.12 | loop fusion | flops 147456 | bytes 294912 | tf_op jit(solution)/shard_map/concatenate | solution.py:167
  85.0 1.7 %gather_fusion.1 = bf16[96,32,128]{2,1,0:T(8,128)(2,1)} fusion(bf16[18,32,128]{2,1,0:T(8,128)(2,1)S(1)} %maximum_bitcast_fusion.1, s32[1024]{0:T(1024)} %pad_clamp_fusion), kind=kCustom, calls=%fused_computation.1 | custom fusion | bytes 1573248 | tf_op jit(solution)/shard_map/gather | solution.py:168
  86.7 0.9 %bitcast_add_fusion = f32[1,4,32,128]{3,2,1,0:T(8,128)S(1)} fusion(f32[4,32,128]{2,1,0:T(8,128)} %copy-done.6, bf16[1,5,32,128]{3,2,1,0:T(8,128)(2,1)} %copy-done.10, f32[4]{0:T(128)} %broadcast_subtract_fusion), kind=kLoop, calls=%fused_computation.18 | loop fusion | flops 49152 | bytes 163856 | tf_op jit(solution)/shard_map/add | solution.py:171
  87.6 2.6 %multiply_add_fusion = f32[1,16,32,128]{3,2,1,0:T(8,128)} fusion(f32[1,16,32,128]{3,2,1,0:T(8,128)} %bitcast.66, f32[1,16,32,128]{3,2,1,0:T(8,128)S(1)} %copy-done.2, f32[1,4,32,128]{3,2,1,0:T(8,128)S(1)} %bitcast_add_fusion, f32[16,128]{1,0:T(8,128)} %bitcast.69, f32[16]{0:T(128)} %copy-done.11, bf16[16,6,32,128]{3,2,1,0:T(8,128)(2,1)} %bitcast.62, ...), kind=kOutput, calls=%fused_computation.8 | convolution fusion | flops 100990976 | bytes 4792384 | tf_op jit(solution)/shard_map/tnkri,tnkio->tnro/dot_general | solution.py:169
  90.2 2.0 %shard_map.112 = f32[512,128]{1,0:T(8,128)} custom-call(f32[4,512,128]{2,1,0:T(8,128)} %all-to-all-done.1.got_ref, f32[512,128]{1,0:T(8,128)} %bitcast.64, f32[16,128]{1,0:T(8,128)} %get-tuple-element.19.scale_ref, f32[16,128]{1,0:T(8,128)} %cond_ref.3), custom_call_target="tpu_custom_call" | custom-call | tf_op jit(solution)/shard_map/pallas_call | solution.py:121
  (55 shorter events, 7.0 us)
Async XLA Ops:
  0.0 46.7 %copy-start = (bf16[1,16,6,128,128]{4,3,2,1,0:T(8,128)(2,1)S(1)}, bf16[1,16,6,128,128]{4,3,2,1,0:T(8,128)(2,1)}, u32[]{:S(2)}) copy-start(bf16[1,16,6,128,128]{4,3,2,1,0:T(8,128)(2,1)} %param.15) | copy-start | bytes 9437188
  0.8 15.0 %copy-start.11 = (f32[16]{0:T(128)}, f32[16]{0:T(128)S(1)}, u32[]{:S(2)}) copy-start(f32[16]{0:T(128)S(1)} %or_convert_fusion) | copy-start | bytes 196
  4.0 14.3 %collective-permute-start.1 = (f32[512,128]{1,0:T(8,128)}, f32[512,128]{1,0:T(8,128)}, u32[]{:S(2)}, u32[]{:S(2)}) collective-permute-start(f32[512,128]{1,0:T(8,128)} %bitcast.2.own_ref), channel_id=1, source_target_pairs={{0,256},{32,288},{64,320},{96,352},{128,384},{160,416},{192,448},{... | collective-permute-start | bytes 786440 | tf_op jit(solution)/shard_map/ppermute | solution.py:49
  8.1 15.3 %collective-permute-start = (f32[512,128]{1,0:T(8,128)}, f32[512,128]{1,0:T(8,128)}, u32[]{:S(2)}, u32[]{:S(2)}) collective-permute-start(f32[512,128]{1,0:T(8,128)} %bitcast.2.own_ref), channel_id=1, source_target_pairs={{0,32},{32,0},{64,96},{96,64},{128,160},{160,128},{192,224},{224,1... | collective-permute-start | bytes 786440 | tf_op jit(solution)/shard_map/ppermute | solution.py:49
  15.8 26.7 %copy-start.4 = (bf16[1,16,32,128]{3,2,1,0:T(8,128)(2,1)}, bf16[1,16,32,128]{3,2,1,0:T(8,128)(2,1)S(1)}, u32[]{:S(2)}) copy-start(bf16[1,16,32,128]{3,2,1,0:T(8,128)(2,1)S(1)} %multiply_convert_fusion) | copy-start | bytes 393220
  17.6 0.7 copy-start.5
  18.2 3.8 %copy-start.12 = (f32[4]{0:T(128)}, f32[4]{0:T(128)S(1)}, u32[]{:S(2)}) copy-start(f32[4]{0:T(128)S(1)} %convert_bitcast_fusion) | copy-start | bytes 52
  18.3 5.1 %collective-permute-start.2 = (f32[512,128]{1,0:T(8,128)}, f32[512,128]{1,0:T(8,128)}, u32[]{:S(2)}, u32[]{:S(2)}) collective-permute-start(f32[512,128]{1,0:T(8,128)} %collective-permute-done.1.across_ref), channel_id=1, source_target_pairs={{0,32},{32,0},{64,96},{96,64},{128,160},{160,128},{192,224},{224,1... | collective-permute-start | bytes 786440 | tf_op jit(solution)/shard_map/ppermute | solution.py:49
  22.2 24.5 %copy-start.1 = (f32[1,16,32,128]{3,2,1,0:T(8,128)S(1)}, f32[1,16,32,128]{3,2,1,0:T(8,128)}, u32[]{:S(2)}) copy-start(f32[1,16,32,128]{3,2,1,0:T(8,128)} %param.11) | copy-start | bytes 786436
  25.6 23.6 %all-to-all-start = ((f32[4,512,128]{2,1,0:T(8,128)}), f32[4,512,128]{2,1,0:T(8,128)}, u32[]{:S(2)}, u32[]{:S(2)}) async-start(f32[4,512,128]{2,1,0:T(8,128)} %shard_map.109), calls=%async_computation | async-start | bytes 2097152 | tf_op jit(solution)/shard_map/all_to_all | solution.py:136
  29.9 12.6 %collective-permute-start.3 = (bf16[1,5,32,128]{3,2,1,0:T(8,128)(2,1)}, bf16[1,5,32,128]{3,2,1,0:T(8,128)(2,1)S(1)}, u32[]{:S(2)}, u32[]{:S(2)}) collective-permute-start(bf16[1,5,32,128]{3,2,1,0:T(8,128)(2,1)} %pad_maximum_fusion), channel_id=1, source_target_pairs={{31,0},{0,1},{1,2},{2,3},{3,4},{4,5},{5,6},{6,7},{7,8},{8,9},{9,10... | collective-permute-start | bytes 122888 | tf_op jit(solution)/shard_map/ppermute | solution.py:32
  31.8 10.8 %collective-permute-start.4 = (bf16[1,1,32,128]{3,2,1,0:T(8,128)(2,1)S(1)}, bf16[1,1,32,128]{3,2,1,0:T(8,128)(2,1)S(1)}, u32[]{:S(2)}, u32[]{:S(2)}) collective-permute-start(bf16[1,1,32,128]{3,2,1,0:T(8,128)(2,1)S(1)} %slice.33), channel_id=1, source_target_pairs={{1,0},{2,1},{3,2},{4,3},{5,4},{6,5},{7,6},{8,7},{9,8},{10,9},{11,1... | collective-permute-start | bytes 24584 | tf_op jit(solution)/shard_map/ppermute | solution.py:32
  42.5 0.6 copy-start.9
  46.7 19.0 %copy-start.13 = (f32[4]{0:T(128)S(1)}, f32[4]{0:T(128)}, u32[]{:S(2)}) copy-start(f32[4]{0:T(128)} %copy-done.12) | copy-start | bytes 52
  51.3 9.5 %collective-permute-start.6 = (f32[512,128]{1,0:T(8,128)}, f32[512,128]{1,0:T(8,128)S(1)}, u32[]{:S(2)}, u32[]{:S(2)}) collective-permute-start(f32[512,128]{1,0:T(8,128)} %get-tuple-element.15.own_ref), channel_id=1, source_target_pairs={{0,256},{32,288},{64,320},{96,352},{128,384},{160,416},{192,448},{... | collective-permute-start | bytes 786440 | tf_op jit(solution)/shard_map/ppermute | solution.py:49
  53.6 12.8 %collective-permute-start.5 = (f32[512,128]{1,0:T(8,128)}, f32[512,128]{1,0:T(8,128)S(1)}, u32[]{:S(2)}, u32[]{:S(2)}) collective-permute-start(f32[512,128]{1,0:T(8,128)} %get-tuple-element.15.own_ref), channel_id=1, source_target_pairs={{0,32},{32,0},{64,96},{96,64},{128,160},{160,128},{192,224},{224,1... | collective-permute-start | bytes 786440 | tf_op jit(solution)/shard_map/ppermute | solution.py:49
  57.2 26.1 %copy-start.3 = (bf16[1,16,32,128]{3,2,1,0:T(8,128)(2,1)}, bf16[1,16,32,128]{3,2,1,0:T(8,128)(2,1)S(1)}, u32[]{:S(2)}) copy-start(bf16[1,16,32,128]{3,2,1,0:T(8,128)(2,1)S(1)} %convert_element_type.51) | copy-start | bytes 393220
  60.8 5.6 %copy-start.7 = (f32[512,128]{1,0:T(8,128)}, f32[512,128]{1,0:T(8,128)S(1)}, u32[]{:S(2)}) copy-start(f32[512,128]{1,0:T(8,128)S(1)} %collective-permute-done.6.across_ref) | copy-start | bytes 786436
  60.8 6.3 %collective-permute-start.7 = (f32[512,128]{1,0:T(8,128)S(1)}, f32[512,128]{1,0:T(8,128)}, u32[]{:S(2)}, u32[]{:S(2)}) collective-permute-start(f32[512,128]{1,0:T(8,128)S(1)} %collective-permute-done.6.across_ref), channel_id=1, source_target_pairs={{0,32},{32,0},{64,96},{96,64},{128,160},{160,128},{192,224},{224,1... | collective-permute-start | bytes 786440 | tf_op jit(solution)/shard_map/ppermute | solution.py:49
  65.1 0.6 copy-start.6
  66.4 21.2 %copy-start.2 = (f32[1,16,32,128]{3,2,1,0:T(8,128)S(1)}, f32[1,16,32,128]{3,2,1,0:T(8,128)}, u32[]{:S(2)}) copy-start(f32[1,16,32,128]{3,2,1,0:T(8,128)} %param.12) | copy-start | bytes 786436
  66.4 0.7 copy-start.8
  69.3 20.8 %all-to-all-start.1 = ((f32[4,512,128]{2,1,0:T(8,128)}), f32[4,512,128]{2,1,0:T(8,128)}, u32[]{:S(2)}, u32[]{:S(2)}) async-start(f32[4,512,128]{2,1,0:T(8,128)} %shard_map.111), calls=%async_computation.1 | async-start | bytes 2097152 | tf_op jit(solution)/shard_map/all_to_all | solution.py:136
  74.4 8.9 %collective-permute-start.8 = (bf16[1,5,32,128]{3,2,1,0:T(8,128)(2,1)S(1)}, bf16[1,5,32,128]{3,2,1,0:T(8,128)(2,1)S(1)}, u32[]{:S(2)}, u32[]{:S(2)}) collective-permute-start(bf16[1,5,32,128]{3,2,1,0:T(8,128)(2,1)S(1)} %pad_maximum_fusion.1), channel_id=1, source_target_pairs={{31,0},{0,1},{1,2},{2,3},{3,4},{4,5},{5,6},{6,7},{7,8},{8,9},{9,10... | collective-permute-start | bytes 122888 | tf_op jit(solution)/shard_map/ppermute | solution.py:32
  76.3 7.8 %collective-permute-start.9 = (bf16[1,1,32,128]{3,2,1,0:T(8,128)(2,1)S(1)}, bf16[1,1,32,128]{3,2,1,0:T(8,128)(2,1)S(1)}, u32[]{:S(2)}, u32[]{:S(2)}) collective-permute-start(bf16[1,1,32,128]{3,2,1,0:T(8,128)(2,1)S(1)} %slice.38), channel_id=1, source_target_pairs={{1,0},{2,1},{3,2},{4,3},{5,4},{6,5},{7,6},{8,7},{9,8},{10,9},{11,1... | collective-permute-start | bytes 24584 | tf_op jit(solution)/shard_map/ppermute | solution.py:32
  83.3 0.8 copy-start.10

commit v18 on v12

--- a/solution.py
+++ b/solution.py
@@ -100,20 +100,20 @@
     )(index, jnp.asarray(coefficient_table()), own, mate, across, diagonal)
 
 
-def update_kernel(got_ref, base_ref, scale_ref, cond_ref, lam_ref, *rest):
-    rows, lanes = base_ref.shape
+def update_kernel(got_ref, lam_ref, rhs_ref, local_ref, scale_ref, cond_ref, out_ref, *rest):
+    rows, lanes = lam_ref.shape
     groups = scale_ref.shape[0]
     spec = (got_ref[0] + got_ref[1]) + (got_ref[2] + got_ref[3])
     scale = jnp.broadcast_to(scale_ref[...][:, None, :], (groups, rows // groups, lanes)).reshape(rows, lanes)
-    lam = base_ref[...] - scale * spec
-    lam_ref[...] = lam
+    lam = lam_ref[...] + scale * (rhs_ref[...] - (local_ref[...] + spec))
+    out_ref[...] = lam
     for weighted_ref in rest:
         cond = jnp.broadcast_to(cond_ref[...][:, None, :], (groups, rows // groups, lanes)).reshape(rows, lanes)
         weighted_ref[...] = lam * cond
 
 
-def updated(got, base, scale, cond, outputs):
-    rows, lanes = base.shape
+def updated(got, lam, rhs, local, scale, cond, outputs):
+    rows, lanes = lam.shape
     block = 256
     groups = block * scale.shape[0] // rows
     flat = pl.BlockSpec((block, lanes), lambda r: (r, 0))
@@ -121,10 +121,10 @@
     return pl.pallas_call(
         update_kernel,
         grid=(rows // block,),
-        in_specs=[pl.BlockSpec((4, block, lanes), lambda r: (0, r, 0)), flat, narrow, narrow],
+        in_specs=[pl.BlockSpec((4, block, lanes), lambda r: (0, r, 0)), flat, flat, flat, narrow, narrow],
         out_specs=[flat] * outputs,
-        out_shape=[jax.ShapeDtypeStruct(base.shape, jnp.float32)] * outputs,
-    )(got, base, scale, cond)
+        out_shape=[jax.ShapeDtypeStruct(lam.shape, jnp.float32)] * outputs,
+    )(got, lam, rhs, local, scale, cond)
 
 
 def instance_mix(flat):
@@ -172,8 +172,10 @@
             [jnp.zeros((local_inst, rows - rotor_rows) + rotor.shape[2:], jnp.float32), rotor],
             axis=1,
         )
-        base = lam + relax_wide * (rhs - (stator + rotor_full)) * live
-        fresh = updated(got, base.reshape(-1, lanes), scale, cond, 2 if sweep + 1 < SWEEPS else 1)
+        local = (stator + rotor_full).reshape(-1, lanes)
+        fresh = updated(
+            got, lam.reshape(-1, lanes), rhs.reshape(-1, lanes), local, scale, cond, 2 if sweep + 1 < SWEEPS else 1
+        )
         lam = fresh[0].reshape(shape)
         weighted = fresh[-1]
     return lam

time: 92.5 us -> 95.3 us (1.030)
  waiting for transfers between devices: 4.49 us -> 10.1 us
  other arithmetic: 13.2 us -> 10.9 us
  starting transfers between devices: 51.1 us -> 53.2 us
  local copies, waits for them, and re-layouts: 5.39 us -> 4.09 us
  matrix products: 7.23 us -> 6.09 us
    ppermute x4, waiting for transfers between devices: 0.89 us -> 6.81 us  [shifted(): return lax.ppermute(block, axis, route)]
    ppermute x6, starting transfers between devices: 21.8 us -> 23.8 us  [routed(): return lax.ppermute(block, INST, [(s, dest(s)) for s in range(NT)])]
    mul x0 -> x1, other arithmetic: none -> 1.47 us  [shards(): weighted = (lam * cond_wide).reshape(-1, lanes)]
    unnamed x26 -> x24, local copies, waits for them, and re-layouts: 1.81 us -> 0.64 us
    ppermute x6, waiting for transfers between devices: 3.6 us -> 2.5 us  [routed(): return lax.ppermute(block, INST, [(s, dest(s)) for s in range(NT)])]
  transfers between devices with their start and end apart: 12 -> 12, of which waited for: 3 -> 5; matrix products, arithmetic and copies ran while one was open for 24% -> 19% of each run, Pallas kernels for 0% -> 0%
where the time goes in v18:
time: 95.3 us; the launch traced here: 94.3 us
  starting transfers between devices  53.2 us (56%)
  other arithmetic  10.9 us (11%)
  waiting for transfers between devices  10.1 us (11%)
  Pallas kernels  8.88 us (9%)
  matrix products  6.09 us (6%)
  local copies, waits for them, and re-layouts  4.09 us (4%)
  between operations  1.09 us (1%)
    ppermute x6, starting transfers between devices, routed(): return lax.ppermute(block, INST, [(s, dest(s)) for s in range(NT)])  23.8 us
    ppermute x4, starting transfers between devices, shifted(): return lax.ppermute(block, axis, route)  20.9 us
    all_to_all x2, starting transfers between devices, instance_mix(): return (partials, lax.all_to_all(partials, 'ix', 0, 0))  8.47 us
    ppermute x4, waiting for transfers between devices, shifted(): return lax.ppermute(block, axis, route)  6.81 us
    dot_general x2, matrix products, shards(): jnp.einsum('tnkri,tnkio->tnro', picked, jac, preferred_element_type=jnp.f...  4.9 us
    pallas_call x2, Pallas kernels, partial_sums(): pl.pallas_call(mix_kernel, grid_spec=pltpu.PrefetchScalarGridSpec(num_sca...  4.48 us
    pallas_call x2, Pallas kernels, updated(): pl.pallas_call(update_kernel, grid=(rows // block,), in_specs=[pl.BlockSp...  4.4 us
    gather x2, local copies, waits for them, and re-layouts, shards(): picked = lam_h[:, cols]  3.27 us
  transfers between devices with their start and end apart: 12, of which 5 were waited for; matrix products, arithmetic and copies ran while one was open for 19% of the time, Pallas kernels for 0%

profile of v18, /device:TPU:1, one launch (start us, length us, event | category | flops | bytes accessed | tf_op | source)
XLA Modules:
  0.0 94.3 jit_solution(2796021333942706608)
XLA Ops:
  0.8 1.2 %fusion.16 = (bf16[1,16,32,128]{3,2,1,0:T(8,128)(2,1)S(1)}, f32[1,16,32,128]{3,2,1,0:T(8,128)S(1)}) fusion(f32[1,16,32,128]{3,2,1,0:T(8,128)} %param.11, f32[16]{0:T(128)S(1)} %or_convert_fusion), kind=kLoop, calls=%fused_computation.34 | loop fusion | flops 131072 | bytes 655424 | tf_op jit(solution)/shard_map/convert_element_type | solution.py:154
  2.0 1.5 %broadcast_multiply_fusion = f32[1,16,32,128]{3,2,1,0:T(8,128)} fusion(f32[1,16,32,128]{3,2,1,0:T(8,128)S(1)} %get-tuple-element.18, f32[16,128]{1,0:T(8,128)} %cond_ref.3), kind=kLoop, calls=%fused_computation.16 | loop fusion | flops 65536 | bytes 532480 | tf_op jit(solution)/shard_map/mul | solution.py:152
  3.5 4.0 %collective-permute-start.1 = (f32[512,128]{1,0:T(8,128)}, f32[512,128]{1,0:T(8,128)}, u32[]{:S(2)}, u32[]{:S(2)}) collective-permute-start(f32[512,128]{1,0:T(8,128)} %bitcast.2.own_ref), channel_id=1, source_target_pairs={{0,256},{32,288},{64,320},{96,352},{128,384},{160,416},{192,448},{... | collective-permute-start | bytes 786440 | tf_op jit(solution)/shard_map/ppermute | solution.py:49
  7.5 6.7 %collective-permute-start = (f32[512,128]{1,0:T(8,128)}, f32[512,128]{1,0:T(8,128)}, u32[]{:S(2)}, u32[]{:S(2)}) collective-permute-start(f32[512,128]{1,0:T(8,128)} %bitcast.2.own_ref), channel_id=1, source_target_pairs={{0,32},{32,0},{64,96},{96,64},{128,160},{160,128},{192,224},{224,1... | collective-permute-start | bytes 786440 | tf_op jit(solution)/shard_map/ppermute | solution.py:49
  14.2 1.2 %broadcast_subtract_fusion = f32[4]{0:T(128)} fusion(s32[1,4]{1,0:T(1,128)} %param.18), kind=kLoop, calls=%fused_computation.33 | loop fusion | flops 8 | bytes 32 | tf_op jit(solution)/shard_map/sub | solution.py:170
  16.1 1.0 %fusion.12 = f32[4,32,128]{2,1,0:T(8,128)S(1)} fusion(bf16[1,4,128,128]{3,2,1,0:T(8,128)(2,1)} %param.16, bf16[1,16,32,128]{3,2,1,0:T(8,128)(2,1)S(1)} %get-tuple-element.12), kind=kOutput, calls=%fused_computation.14 | convolution fusion | flops 4194304 | bytes 229376 | tf_op jit(solution)/shard_map/tjri,tjio->tjro/dot_general | solution.py:156
  18.0 2.9 %collective-permute-start.2 = (f32[512,128]{1,0:T(8,128)}, f32[512,128]{1,0:T(8,128)}, u32[]{:S(2)}, u32[]{:S(2)}) collective-permute-start(f32[512,128]{1,0:T(8,128)} %collective-permute-done.1.across_ref), channel_id=1, source_target_pairs={{0,32},{32,0},{64,96},{96,64},{128,160},{160,128},{192,224},{224,1... | collective-permute-start | bytes 786440 | tf_op jit(solution)/shard_map/ppermute | solution.py:49
  21.7 1.4 %bitcast_multiply_fusion.scale_ref = f32[16,128]{1,0:T(8,128)} fusion(f32[1,16,128]{2,1,0:T(8,128)} %param.13, f32[16]{0:T(128)} %copy-done.11), kind=kLoop, calls=%fused_computation.29 | loop fusion | flops 2048 | bytes 16448 | tf_op jit(solution)/shard_map/mul | solution.py:151
  23.1 2.2 %shard_map.109 = f32[4,512,128]{2,1,0:T(8,128)} custom-call(s32[1]{0:T(128)} %bitcast.index_ref, f32[16,16]{1,0:T(8,128)} %constant.32.clone.coef_ref, f32[512,128]{1,0:T(8,128)} %bitcast.2.own_ref, f32[512,128]{1,0:T(8,128)} %collective-permute-done.mate_ref, f32[512,128]{1,0:T(8,128)} %collective-permute-done.1.across_ref, ...), custom_call_target="tpu_custom_call" | custom-call | tf_op jit(solution)/shard_map/pallas_call | solution.py:91
  25.3 4.2 %all-to-all-start = ((f32[4,512,128]{2,1,0:T(8,128)}), f32[4,512,128]{2,1,0:T(8,128)}, u32[]{:S(2)}, u32[]{:S(2)}) async-start(f32[4,512,128]{2,1,0:T(8,128)} %shard_map.109), calls=%async_computation | async-start | bytes 2097152 | tf_op jit(solution)/shard_map/all_to_all | solution.py:136
  29.5 10.1 %collective-permute-start.4 = (bf16[1,1,32,128]{3,2,1,0:T(8,128)(2,1)S(1)}, bf16[1,1,32,128]{3,2,1,0:T(8,128)(2,1)S(1)}, u32[]{:S(2)}, u32[]{:S(2)}) collective-permute-start(bf16[1,1,32,128]{3,2,1,0:T(8,128)(2,1)S(1)} %slice.33), channel_id=1, source_target_pairs={{1,0},{2,1},{3,2},{4,3},{5,4},{6,5},{7,6},{8,7},{9,8},{10,9},{11,1... | collective-permute-start | bytes 24584 | tf_op jit(solution)/shard_map/ppermute | solution.py:32
  39.6 1.9 %collective-permute-start.3 = (bf16[1,5,32,128]{3,2,1,0:T(8,128)(2,1)}, bf16[1,5,32,128]{3,2,1,0:T(8,128)(2,1)S(1)}, u32[]{:S(2)}, u32[]{:S(2)}) collective-permute-start(bf16[1,5,32,128]{3,2,1,0:T(8,128)(2,1)} %pad_maximum_fusion), channel_id=1, source_target_pairs={{31,0},{0,1},{1,2},{2,3},{3,4},{4,5},{5,6},{6,7},{7,8},{8,9},{9,10... | collective-permute-start | bytes 122888 | tf_op jit(solution)/shard_map/ppermute | solution.py:32
  42.1 6.1 %collective-permute-done.3 = bf16[1,5,32,128]{3,2,1,0:T(8,128)(2,1)S(1)} collective-permute-done((bf16[1,5,32,128]{3,2,1,0:T(8,128)(2,1)}, bf16[1,5,32,128]{3,2,1,0:T(8,128)(2,1)S(1)}, u32[]{:S(2)}, u32[]{:S(2)}) %collective-permute-start.3) | collective-permute-done | bytes 40992 | tf_op jit(solution)/shard_map/ppermute | solution.py:32
  48.8 0.9 maximum_bitcast_fusion
  49.7 1.7 %gather_fusion = bf16[96,32,128]{2,1,0:T(8,128)(2,1)} fusion(bf16[18,32,128]{2,1,0:T(8,128)(2,1)S(1)} %maximum_bitcast_fusion, s32[1024]{0:T(1024)} %pad_clamp_fusion), kind=kCustom, calls=%fused_computation | custom fusion | bytes 1573248 | tf_op jit(solution)/shard_map/gather | solution.py:167
  51.4 0.9 bitcast_add_fusion.1
  52.4 2.5 %pad_add_fusion.1 = f32[1,16,32,128]{3,2,1,0:T(8,128)} fusion(f32[1,4,32,128]{3,2,1,0:T(8,128)S(1)} %bitcast_add_fusion.1, bf16[16,6,32,128]{3,2,1,0:T(8,128)(2,1)} %bitcast.65, bf16[1,16,6,128,128]{4,3,2,1,0:T(8,128)(2,1)S(1)} %copy-done), kind=kOutput, calls=%fused_computation.9 | convolution fusion | flops 100728832 | bytes 4259840 | tf_op jit(solution)/shard_map/tnkri,tnkio->tnro/dot_general | solution.py:168
  54.8 2.2 %shard_map.110 = (f32[512,128]{1,0:T(8,128)}, f32[512,128]{1,0:T(8,128)}) custom-call(f32[4,512,128]{2,1,0:T(8,128)} %all-to-all-done.got_ref, f32[512,128]{1,0:T(8,128)} %bitcast.66, f32[512,128]{1,0:T(8,128)} %bitcast.68, f32[512,128]{1,0:T(8,128)} %bitcast.67, f32[16,128]{1,0:T(8,128)} %bitcast_multiply_fusion.scale_ref, f32[16,128]{1,0:T(8,128)} %cond_ref.3), custom_call_target="tpu_custom_call" | custom-call | tf_op jit(solution)/shard_map/pallas_call | solution.py:121
  57.1 2.3 %collective-permute-start.6 = (f32[512,128]{1,0:T(8,128)}, f32[512,128]{1,0:T(8,128)S(1)}, u32[]{:S(2)}, u32[]{:S(2)}) collective-permute-start(f32[512,128]{1,0:T(8,128)} %get-tuple-element.13.own_ref), channel_id=1, source_target_pairs={{0,256},{32,288},{64,320},{96,352},{128,384},{160,416},{192,448},{... | collective-permute-start | bytes 786440 | tf_op jit(solution)/shard_map/ppermute | solution.py:49
  59.4 3.7 %collective-permute-start.5 = (f32[512,128]{1,0:T(8,128)}, f32[512,128]{1,0:T(8,128)}, u32[]{:S(2)}, u32[]{:S(2)}) collective-permute-start(f32[512,128]{1,0:T(8,128)} %get-tuple-element.13.own_ref), channel_id=1, source_target_pairs={{0,32},{32,0},{64,96},{96,64},{128,160},{160,128},{192,224},{224,1... | collective-permute-start | bytes 786440 | tf_op jit(solution)/shard_map/ppermute | solution.py:49
  63.1 1.0 %convert_element_type.55 = bf16[512,128]{1,0:T(8,128)(2,1)S(1)} convert(f32[512,128]{1,0:T(8,128)} %get-tuple-element.14.lam_ref) | non-fusion elementwise | flops 65536 | bytes 393216 | tf_op jit(solution)/shard_map/convert_element_type | solution.py:154
  64.0 1.5 %collective-permute-done.6.across_ref = f32[512,128]{1,0:T(8,128)S(1)} collective-permute-done((f32[512,128]{1,0:T(8,128)}, f32[512,128]{1,0:T(8,128)S(1)}, u32[]{:S(2)}, u32[]{:S(2)}) %collective-permute-start.6) | collective-permute-done | bytes 262176 | tf_op jit(solution)/shard_map/ppermute | solution.py:49
  65.5 4.3 %collective-permute-start.7 = (f32[512,128]{1,0:T(8,128)S(1)}, f32[512,128]{1,0:T(8,128)}, u32[]{:S(2)}, u32[]{:S(2)}) collective-permute-start(f32[512,128]{1,0:T(8,128)S(1)} %collective-permute-done.6.across_ref), channel_id=1, source_target_pairs={{0,32},{32,0},{64,96},{96,64},{128,160},{160,128},{192,224},{224,1... | collective-permute-start | bytes 786440 | tf_op jit(solution)/shard_map/ppermute | solution.py:49
  70.1 1.0 %collective-permute-done.7.diagonal_ref = f32[512,128]{1,0:T(8,128)} collective-permute-done((f32[512,128]{1,0:T(8,128)S(1)}, f32[512,128]{1,0:T(8,128)}, u32[]{:S(2)}, u32[]{:S(2)}) %collective-permute-start.7) | collective-permute-done | bytes 262176 | tf_op jit(solution)/shard_map/ppermute | solution.py:49
  71.1 2.3 %shard_map.111 = f32[4,512,128]{2,1,0:T(8,128)} custom-call(s32[1]{0:T(128)} %bitcast.index_ref, f32[16,16]{1,0:T(8,128)} %constant.32.clone.coef_ref, f32[512,128]{1,0:T(8,128)} %get-tuple-element.13.own_ref, f32[512,128]{1,0:T(8,128)} %collective-permute-done.5.mate_ref, f32[512,128]{1,0:T(8,128)} %copy-done.5, f32[512,128]{1,0:T(8,128)} %collective-permute-done.7.diagonal_ref), custom_call_target="tpu_custom_call" | custom-call | tf_op jit(solution)/shard_map/pallas_call | solution.py:91
  73.3 4.2 %all-to-all-start.1 = ((f32[4,512,128]{2,1,0:T(8,128)}), f32[4,512,128]{2,1,0:T(8,128)}, u32[]{:S(2)}, u32[]{:S(2)}) async-start(f32[4,512,128]{2,1,0:T(8,128)} %shard_map.111), calls=%async_computation.1 | async-start | bytes 2097152 | tf_op jit(solution)/shard_map/all_to_all | solution.py:136
  77.6 1.9 %collective-permute-start.8 = (bf16[1,5,32,128]{3,2,1,0:T(8,128)(2,1)S(1)}, bf16[1,5,32,128]{3,2,1,0:T(8,128)(2,1)S(1)}, u32[]{:S(2)}, u32[]{:S(2)}) collective-permute-start(bf16[1,5,32,128]{3,2,1,0:T(8,128)(2,1)S(1)} %pad_maximum_fusion.1), channel_id=1, source_target_pairs={{31,0},{0,1},{1,2},{2,3},{3,4},{4,5},{5,6},{6,7},{7,8},{8,9},{9,10... | collective-permute-start | bytes 122888 | tf_op jit(solution)/shard_map/ppermute | solution.py:32
  79.5 7.0 %collective-permute-start.9 = (bf16[1,1,32,128]{3,2,1,0:T(8,128)(2,1)S(1)}, bf16[1,1,32,128]{3,2,1,0:T(8,128)(2,1)S(1)}, u32[]{:S(2)}, u32[]{:S(2)}) collective-permute-start(bf16[1,1,32,128]{3,2,1,0:T(8,128)(2,1)S(1)} %slice.38), channel_id=1, source_target_pairs={{1,0},{2,1},{3,2},{4,3},{5,4},{6,5},{7,6},{8,7},{9,8},{10,9},{11,1... | collective-permute-start | bytes 24584 | tf_op jit(solution)/shard_map/ppermute | solution.py:32
  86.5 0.8 collective-permute-done.9
  87.3 1.6 %gather_fusion.1 = bf16[96,32,128]{2,1,0:T(8,128)(2,1)} fusion(bf16[18,32,128]{2,1,0:T(8,128)(2,1)S(1)} %maximum_bitcast_fusion.1, s32[1024]{0:T(1024)S(1)} %copy-done.6), kind=kCustom, calls=%fused_computation.1 | custom fusion | bytes 1573248 | tf_op jit(solution)/shard_map/gather | solution.py:167
  89.0 2.4 %pad_add_fusion = f32[1,16,32,128]{3,2,1,0:T(8,128)} fusion(f32[1,4,32,128]{3,2,1,0:T(8,128)S(1)} %bitcast_add_fusion, bf16[16,6,32,128]{3,2,1,0:T(8,128)(2,1)} %bitcast.64, bf16[1,16,6,128,128]{4,3,2,1,0:T(8,128)(2,1)S(1)} %copy-done), kind=kOutput, calls=%fused_computation.8 | convolution fusion | flops 100728832 | bytes 4259840 | tf_op jit(solution)/shard_map/tnkri,tnkio->tnro/dot_general | solution.py:168
  92.2 2.2 %shard_map.112 = f32[512,128]{1,0:T(8,128)} custom-call(f32[4,512,128]{2,1,0:T(8,128)} %all-to-all-done.1.got_ref, f32[512,128]{1,0:T(8,128)} %get-tuple-element.14.lam_ref, f32[512,128]{1,0:T(8,128)} %bitcast.69, f32[512,128]{1,0:T(8,128)} %bitcast.70, f32[16,128]{1,0:T(8,128)} %bitcast_multiply_fusion.scale_ref, f32[16,128]{1,0:T(8,128)} %cond_ref.3), custom_call_target="tpu_custom_call" | custom-call | tf_op jit(solution)/shard_map/pallas_call | solution.py:121
  (51 shorter events, 4.6 us)
Async XLA Ops:
  0.0 52.4 %copy-start = (bf16[1,16,6,128,128]{4,3,2,1,0:T(8,128)(2,1)S(1)}, bf16[1,16,6,128,128]{4,3,2,1,0:T(8,128)(2,1)}, u32[]{:S(2)}) copy-start(bf16[1,16,6,128,128]{4,3,2,1,0:T(8,128)(2,1)} %param.15) | copy-start | bytes 9437188
  0.8 16.4 %copy-start.11 = (f32[16]{0:T(128)}, f32[16]{0:T(128)S(1)}, u32[]{:S(2)}) copy-start(f32[16]{0:T(128)S(1)} %or_convert_fusion) | copy-start | bytes 196
  2.0 46.2 %copy-start.2 = (bf16[1,16,32,128]{3,2,1,0:T(8,128)(2,1)}, bf16[1,16,32,128]{3,2,1,0:T(8,128)(2,1)S(1)}, u32[]{:S(2)}) copy-start(bf16[1,16,32,128]{3,2,1,0:T(8,128)(2,1)S(1)} %get-tuple-element.12) | copy-start | bytes 393220
  2.0 49.4 %copy-start.1 = (f32[1,16,32,128]{3,2,1,0:T(8,128)}, f32[1,16,32,128]{3,2,1,0:T(8,128)S(1)}, u32[]{:S(2)}) copy-start(f32[1,16,32,128]{3,2,1,0:T(8,128)S(1)} %get-tuple-element.18) | copy-start | bytes 786436
  3.5 14.4 %collective-permute-start.1 = (f32[512,128]{1,0:T(8,128)}, f32[512,128]{1,0:T(8,128)}, u32[]{:S(2)}, u32[]{:S(2)}) collective-permute-start(f32[512,128]{1,0:T(8,128)} %bitcast.2.own_ref), channel_id=1, source_target_pairs={{0,256},{32,288},{64,320},{96,352},{128,384},{160,416},{192,448},{... | collective-permute-start | bytes 786440 | tf_op jit(solution)/shard_map/ppermute | solution.py:49
  7.5 15.5 %collective-permute-start = (f32[512,128]{1,0:T(8,128)}, f32[512,128]{1,0:T(8,128)}, u32[]{:S(2)}, u32[]{:S(2)}) collective-permute-start(f32[512,128]{1,0:T(8,128)} %bitcast.2.own_ref), channel_id=1, source_target_pairs={{0,32},{32,0},{64,96},{96,64},{128,160},{160,128},{192,224},{224,1... | collective-permute-start | bytes 786440 | tf_op jit(solution)/shard_map/ppermute | solution.py:49
  17.2 0.7 copy-start.3
  17.9 30.3 %copy-start.9 = (f32[4]{0:T(128)}, f32[4]{0:T(128)S(1)}, u32[]{:S(2)}) copy-start(f32[4]{0:T(128)S(1)} %convert_bitcast_fusion) | copy-start | bytes 52
  18.0 5.1 %collective-permute-start.2 = (f32[512,128]{1,0:T(8,128)}, f32[512,128]{1,0:T(8,128)}, u32[]{:S(2)}, u32[]{:S(2)}) collective-permute-start(f32[512,128]{1,0:T(8,128)} %collective-permute-done.1.across_ref), channel_id=1, source_target_pairs={{0,32},{32,0},{64,96},{96,64},{128,160},{160,128},{192,224},{224,1... | collective-permute-start | bytes 786440 | tf_op jit(solution)/shard_map/ppermute | solution.py:49
  25.3 29.6 %all-to-all-start = ((f32[4,512,128]{2,1,0:T(8,128)}), f32[4,512,128]{2,1,0:T(8,128)}, u32[]{:S(2)}, u32[]{:S(2)}) async-start(f32[4,512,128]{2,1,0:T(8,128)} %shard_map.109), calls=%async_computation | async-start | bytes 2097152 | tf_op jit(solution)/shard_map/all_to_all | solution.py:136
  29.5 18.6 %collective-permute-start.4 = (bf16[1,1,32,128]{3,2,1,0:T(8,128)(2,1)S(1)}, bf16[1,1,32,128]{3,2,1,0:T(8,128)(2,1)S(1)}, u32[]{:S(2)}, u32[]{:S(2)}) collective-permute-start(bf16[1,1,32,128]{3,2,1,0:T(8,128)(2,1)S(1)} %slice.33), channel_id=1, source_target_pairs={{1,0},{2,1},{3,2},{4,3},{5,4},{6,5},{7,6},{8,7},{9,8},{10,9},{11,1... | collective-permute-start | bytes 24584 | tf_op jit(solution)/shard_map/ppermute | solution.py:32
  39.6 8.6 %collective-permute-start.3 = (bf16[1,5,32,128]{3,2,1,0:T(8,128)(2,1)}, bf16[1,5,32,128]{3,2,1,0:T(8,128)(2,1)S(1)}, u32[]{:S(2)}, u32[]{:S(2)}) collective-permute-start(bf16[1,5,32,128]{3,2,1,0:T(8,128)(2,1)} %pad_maximum_fusion), channel_id=1, source_target_pairs={{31,0},{0,1},{1,2},{2,3},{3,4},{4,5},{5,6},{6,7},{7,8},{8,9},{9,10... | collective-permute-start | bytes 122888 | tf_op jit(solution)/shard_map/ppermute | solution.py:32
  48.2 0.6 copy-start.7
  52.4 17.5 %copy-start.4 = (bf16[1,4,128,128]{3,2,1,0:T(8,128)(2,1)S(1)}, bf16[1,4,128,128]{3,2,1,0:T(8,128)(2,1)}, u32[]{:S(2)}) copy-start(bf16[1,4,128,128]{3,2,1,0:T(8,128)(2,1)} %param.16) | copy-start | bytes 393220
  52.4 17.6 %copy-start.10 = (f32[4]{0:T(128)S(1)}, f32[4]{0:T(128)}, u32[]{:S(2)}) copy-start(f32[4]{0:T(128)} %copy-done.9) | copy-start | bytes 52
  54.8 32.5 %copy-start.6 = (s32[1024]{0:T(1024)S(1)}, s32[1024]{0:T(1024)}, u32[]{:S(2)}) copy-start(s32[1024]{0:T(1024)} %pad_clamp_fusion) | copy-start | bytes 12292
  57.1 8.4 %collective-permute-start.6 = (f32[512,128]{1,0:T(8,128)}, f32[512,128]{1,0:T(8,128)S(1)}, u32[]{:S(2)}, u32[]{:S(2)}) collective-permute-start(f32[512,128]{1,0:T(8,128)} %get-tuple-element.13.own_ref), channel_id=1, source_target_pairs={{0,256},{32,288},{64,320},{96,352},{128,384},{160,416},{192,448},{... | collective-permute-start | bytes 786440 | tf_op jit(solution)/shard_map/ppermute | solution.py:49
  59.4 10.7 %collective-permute-start.5 = (f32[512,128]{1,0:T(8,128)}, f32[512,128]{1,0:T(8,128)}, u32[]{:S(2)}, u32[]{:S(2)}) collective-permute-start(f32[512,128]{1,0:T(8,128)} %get-tuple-element.13.own_ref), channel_id=1, source_target_pairs={{0,32},{32,0},{64,96},{96,64},{128,160},{160,128},{192,224},{224,1... | collective-permute-start | bytes 786440 | tf_op jit(solution)/shard_map/ppermute | solution.py:49
  65.5 4.5 %copy-start.5 = (f32[512,128]{1,0:T(8,128)}, f32[512,128]{1,0:T(8,128)S(1)}, u32[]{:S(2)}) copy-start(f32[512,128]{1,0:T(8,128)S(1)} %collective-permute-done.6.across_ref) | copy-start | bytes 786436
  65.5 5.6 %collective-permute-start.7 = (f32[512,128]{1,0:T(8,128)S(1)}, f32[512,128]{1,0:T(8,128)}, u32[]{:S(2)}, u32[]{:S(2)}) collective-permute-start(f32[512,128]{1,0:T(8,128)S(1)} %collective-permute-done.6.across_ref), channel_id=1, source_target_pairs={{0,32},{32,0},{64,96},{96,64},{128,160},{160,128},{192,224},{224,1... | collective-permute-start | bytes 786440 | tf_op jit(solution)/shard_map/ppermute | solution.py:49
  70.0 18.9 %copy-start.8 = (f32[4]{0:T(128)S(1)}, f32[4]{0:T(128)}, u32[]{:S(2)}) copy-start(f32[4]{0:T(128)} %broadcast_subtract_fusion) | copy-start | bytes 52
  73.3 18.8 %all-to-all-start.1 = ((f32[4,512,128]{2,1,0:T(8,128)}), f32[4,512,128]{2,1,0:T(8,128)}, u32[]{:S(2)}, u32[]{:S(2)}) async-start(f32[4,512,128]{2,1,0:T(8,128)} %shard_map.111), calls=%async_computation.1 | async-start | bytes 2097152 | tf_op jit(solution)/shard_map/all_to_all | solution.py:136
  77.6 8.9 %collective-permute-start.8 = (bf16[1,5,32,128]{3,2,1,0:T(8,128)(2,1)S(1)}, bf16[1,5,32,128]{3,2,1,0:T(8,128)(2,1)S(1)}, u32[]{:S(2)}, u32[]{:S(2)}) collective-permute-start(bf16[1,5,32,128]{3,2,1,0:T(8,128)(2,1)S(1)} %pad_maximum_fusion.1), channel_id=1, source_target_pairs={{31,0},{0,1},{1,2},{2,3},{3,4},{4,5},{5,6},{6,7},{7,8},{8,9},{9,10... | collective-permute-start | bytes 122888 | tf_op jit(solution)/shard_map/ppermute | solution.py:32
  79.5 7.8 %collective-permute-start.9 = (bf16[1,1,32,128]{3,2,1,0:T(8,128)(2,1)S(1)}, bf16[1,1,32,128]{3,2,1,0:T(8,128)(2,1)S(1)}, u32[]{:S(2)}, u32[]{:S(2)}) collective-permute-start(bf16[1,1,32,128]{3,2,1,0:T(8,128)(2,1)S(1)} %slice.38), channel_id=1, source_target_pairs={{1,0},{2,1},{3,2},{4,3},{5,4},{6,5},{7,6},{8,7},{9,8},{10,9},{11,1... | collective-permute-start | bytes 24584 | tf_op jit(solution)/shard_map/ppermute | solution.py:32

commit v19 on v12

--- a/solution.py
+++ b/solution.py
@@ -86,7 +86,7 @@
 
 def partial_sums(index, own, mate, across, diagonal):
     rows, lanes = own.shape
-    block = 256
+    block = 128
     flat = pl.BlockSpec((block, lanes), lambda r, index: (r, 0))
     return pl.pallas_call(
         mix_kernel,

time: 92.5 us -> 95.3 us (1.030)
  Pallas kernels: 8.6 us -> 11.1 us
    pallas_call x2, Pallas kernels: 4.56 us -> 7.02 us  [partial_sums(): pl.pallas_call(mix_kernel, grid_spec=pltpu.PrefetchScalarGridSpec(num_sca...]
where the time goes in v19:
time: 95.3 us; the launch traced here: 93.6 us
  starting transfers between devices  51.1 us (54%)
  other arithmetic  13.2 us (14%)
  Pallas kernels  11.1 us (12%)
  matrix products  7.23 us (8%)
  local copies, waits for them, and re-layouts  5.39 us (6%)
  waiting for transfers between devices  4.49 us (5%)
  between operations  1.06 us (1%)
    ppermute x6, starting transfers between devices, routed(): return lax.ppermute(block, INST, [(s, dest(s)) for s in range(NT)])  21.8 us
    ppermute x4, starting transfers between devices, shifted(): return lax.ppermute(block, axis, route)  20.9 us
    all_to_all x2, starting transfers between devices, instance_mix(): return (partials, lax.all_to_all(partials, 'ix', 0, 0))  8.49 us
    pallas_call x2, Pallas kernels, partial_sums(): pl.pallas_call(mix_kernel, grid_spec=pltpu.PrefetchScalarGridSpec(num_sca...  7.02 us
    dot_general x2, matrix products, shards(): jnp.einsum('tnkri,tnkio->tnro', picked, jac, preferred_element_type=jnp.f...  5.13 us
    pallas_call x2, Pallas kernels, updated(): pl.pallas_call(update_kernel, grid=(rows // block,), in_specs=[pl.BlockSp...  4.03 us
    ppermute x6, waiting for transfers between devices, routed(): return lax.ppermute(block, INST, [(s, dest(s)) for s in range(NT)])  3.6 us
    gather x2, local copies, waits for them, and re-layouts, shards(): picked = lam_h[:, cols]  3.4 us
  transfers between devices with their start and end apart: 12, of which 3 were waited for; matrix products, arithmetic and copies ran while one was open for 24% of the time, Pallas kernels for 0%

profile of v19, /device:TPU:1, one launch (start us, length us, event | category | flops | bytes accessed | tf_op | source)
XLA Modules:
  0.0 93.6 jit_solution(11085278112854591794)
XLA Ops:
  0.8 1.9 %multiply_convert_fusion = (bf16[1,16,32,128]{3,2,1,0:T(8,128)(2,1)S(1)}, f32[1,16,32,128]{3,2,1,0:T(8,128)}) fusion(f32[1,16,32,128]{3,2,1,0:T(8,128)} %param.11, f32[16]{0:T(128)S(1)} %or_convert_fusion, f32[16,128]{1,0:T(8,128)} %cond_ref.3), kind=kLoop, calls=%fused_computation.10 | loop fusion | flops 196608 | bytes 663616 | tf_op jit(solution)/shard_map/convert_element_type | solution.py:154
  2.7 4.0 %collective-permute-start.1 = (f32[512,128]{1,0:T(8,128)}, f32[512,128]{1,0:T(8,128)}, u32[]{:S(2)}, u32[]{:S(2)}) collective-permute-start(f32[512,128]{1,0:T(8,128)} %bitcast.2.own_ref), channel_id=1, source_target_pairs={{0,256},{32,288},{64,320},{96,352},{128,384},{160,416},{192,448},{... | collective-permute-start | bytes 786440 | tf_op jit(solution)/shard_map/ppermute | solution.py:49
  6.8 6.7 %collective-permute-start = (f32[512,128]{1,0:T(8,128)}, f32[512,128]{1,0:T(8,128)}, u32[]{:S(2)}, u32[]{:S(2)}) collective-permute-start(f32[512,128]{1,0:T(8,128)} %bitcast.2.own_ref), channel_id=1, source_target_pairs={{0,32},{32,0},{64,96},{96,64},{128,160},{160,128},{192,224},{224,1... | collective-permute-start | bytes 786440 | tf_op jit(solution)/shard_map/ppermute | solution.py:49
  14.8 1.0 %fusion.12 = f32[4,32,128]{2,1,0:T(8,128)S(1)} fusion(bf16[1,4,128,128]{3,2,1,0:T(8,128)(2,1)} %param.16, bf16[1,16,32,128]{3,2,1,0:T(8,128)(2,1)S(1)} %get-tuple-element.12), kind=kOutput, calls=%fused_computation.16 | convolution fusion | flops 4194304 | bytes 229376 | tf_op jit(solution)/shard_map/tjri,tjio->tjro/dot_general | solution.py:156
  15.8 1.2 %broadcast_subtract_fusion = f32[4]{0:T(128)} fusion(s32[1,4]{1,0:T(1,128)} %param.18), kind=kLoop, calls=%fused_computation.33 | loop fusion | flops 8 | bytes 32 | tf_op jit(solution)/shard_map/sub | solution.py:170
  17.1 2.9 %collective-permute-start.2 = (f32[512,128]{1,0:T(8,128)}, f32[512,128]{1,0:T(8,128)}, u32[]{:S(2)}, u32[]{:S(2)}) collective-permute-start(f32[512,128]{1,0:T(8,128)} %collective-permute-done.1.across_ref), channel_id=1, source_target_pairs={{0,32},{32,0},{64,96},{96,64},{128,160},{160,128},{192,224},{224,1... | collective-permute-start | bytes 786440 | tf_op jit(solution)/shard_map/ppermute | solution.py:49
  20.9 1.4 %broadcast_multiply_fusion.scale_ref = f32[16,128]{1,0:T(8,128)} fusion(f32[16]{0:T(128)S(1)} %or_convert_fusion, f32[1,16,128]{2,1,0:T(8,128)} %param.13), kind=kLoop, calls=%fused_computation.30 | loop fusion | flops 2048 | bytes 16448 | tf_op jit(solution)/shard_map/mul | solution.py:151
  22.3 3.5 %shard_map.109 = f32[4,512,128]{2,1,0:T(8,128)} custom-call(s32[1]{0:T(128)} %bitcast.index_ref, f32[16,16]{1,0:T(8,128)} %constant.32.clone.coef_ref, f32[512,128]{1,0:T(8,128)} %bitcast.2.own_ref, f32[512,128]{1,0:T(8,128)} %collective-permute-done.mate_ref, f32[512,128]{1,0:T(8,128)} %collective-permute-done.1.across_ref, ...), custom_call_target="tpu_custom_call" | custom-call | tf_op jit(solution)/shard_map/pallas_call | solution.py:91
  25.8 4.2 %all-to-all-start = ((f32[4,512,128]{2,1,0:T(8,128)}), f32[4,512,128]{2,1,0:T(8,128)}, u32[]{:S(2)}, u32[]{:S(2)}) async-start(f32[4,512,128]{2,1,0:T(8,128)} %shard_map.109), calls=%async_computation | async-start | bytes 2097152 | tf_op jit(solution)/shard_map/all_to_all | solution.py:136
  30.0 1.9 %collective-permute-start.3 = (bf16[1,5,32,128]{3,2,1,0:T(8,128)(2,1)}, bf16[1,5,32,128]{3,2,1,0:T(8,128)(2,1)S(1)}, u32[]{:S(2)}, u32[]{:S(2)}) collective-permute-start(bf16[1,5,32,128]{3,2,1,0:T(8,128)(2,1)} %pad_maximum_fusion), channel_id=1, source_target_pairs={{31,0},{0,1},{1,2},{2,3},{3,4},{4,5},{5,6},{6,7},{7,8},{8,9},{9,10... | collective-permute-start | bytes 122888 | tf_op jit(solution)/shard_map/ppermute | solution.py:32
  32.0 10.1 %collective-permute-start.4 = (bf16[1,1,32,128]{3,2,1,0:T(8,128)(2,1)S(1)}, bf16[1,1,32,128]{3,2,1,0:T(8,128)(2,1)S(1)}, u32[]{:S(2)}, u32[]{:S(2)}) collective-permute-start(bf16[1,1,32,128]{3,2,1,0:T(8,128)(2,1)S(1)} %slice.33), channel_id=1, source_target_pairs={{1,0},{2,1},{3,2},{4,3},{5,4},{6,5},{7,6},{8,7},{9,8},{10,9},{11,1... | collective-permute-start | bytes 24584 | tf_op jit(solution)/shard_map/ppermute | solution.py:32
  43.3 0.9 maximum_bitcast_fusion
  44.2 1.7 %gather_fusion = bf16[96,32,128]{2,1,0:T(8,128)(2,1)} fusion(bf16[18,32,128]{2,1,0:T(8,128)(2,1)S(1)} %maximum_bitcast_fusion, s32[1024]{0:T(1024)} %pad_clamp_fusion), kind=kCustom, calls=%fused_computation | custom fusion | bytes 1573248 | tf_op jit(solution)/shard_map/gather | solution.py:167
  45.9 0.9 bitcast_add_fusion.1
  46.8 2.6 %multiply_add_fusion.1 = f32[1,16,32,128]{3,2,1,0:T(8,128)} fusion(f32[1,16,32,128]{3,2,1,0:T(8,128)S(1)} %copy-done.1, f32[1,4,32,128]{3,2,1,0:T(8,128)S(1)} %bitcast_add_fusion.1, f32[1,16,32,128]{3,2,1,0:T(8,128)} %param.11, f32[16,128]{1,0:T(8,128)} %bitcast.68, f32[16]{0:T(128)} %copy-done.10, bf16[16,6,32,128]{3,2,1,0:T(8,128)(2,1)} %bitcast.63, ...), kind=kOutput, calls=%fused_computation.9 | convolution fusion | flops 101056512 | bytes 4792384 | tf_op jit(solution)/shard_map/tnkri,tnkio->tnro/dot_general | solution.py:168
  49.4 2.0 %shard_map.110 = (f32[512,128]{1,0:T(8,128)}, f32[512,128]{1,0:T(8,128)}) custom-call(f32[4,512,128]{2,1,0:T(8,128)} %all-to-all-done.got_ref, f32[512,128]{1,0:T(8,128)} %bitcast.67, f32[16,128]{1,0:T(8,128)} %broadcast_multiply_fusion.scale_ref, f32[16,128]{1,0:T(8,128)} %cond_ref.3), custom_call_target="tpu_custom_call" | custom-call | tf_op jit(solution)/shard_map/pallas_call | solution.py:121
  51.5 2.3 %collective-permute-start.6 = (f32[512,128]{1,0:T(8,128)}, f32[512,128]{1,0:T(8,128)S(1)}, u32[]{:S(2)}, u32[]{:S(2)}) collective-permute-start(f32[512,128]{1,0:T(8,128)} %get-tuple-element.13.own_ref), channel_id=1, source_target_pairs={{0,256},{32,288},{64,320},{96,352},{128,384},{160,416},{192,448},{... | collective-permute-start | bytes 786440 | tf_op jit(solution)/shard_map/ppermute | solution.py:49
  53.8 2.6 %collective-permute-start.5 = (f32[512,128]{1,0:T(8,128)}, f32[512,128]{1,0:T(8,128)S(1)}, u32[]{:S(2)}, u32[]{:S(2)}) collective-permute-start(f32[512,128]{1,0:T(8,128)} %get-tuple-element.13.own_ref), channel_id=1, source_target_pairs={{0,32},{32,0},{64,96},{96,64},{128,160},{160,128},{192,224},{224,1... | collective-permute-start | bytes 786440 | tf_op jit(solution)/shard_map/ppermute | solution.py:49
  56.4 1.0 %convert_element_type.52 = bf16[1,16,32,128]{3,2,1,0:T(8,128)(2,1)S(1)} convert(f32[1,16,32,128]{3,2,1,0:T(8,128)} %bitcast.65) | non-fusion elementwise | flops 65536 | bytes 393216 | tf_op jit(solution)/shard_map/convert_element_type | solution.py:154
  57.4 3.6 %collective-permute-done.6.across_ref = f32[512,128]{1,0:T(8,128)S(1)} collective-permute-done((f32[512,128]{1,0:T(8,128)}, f32[512,128]{1,0:T(8,128)S(1)}, u32[]{:S(2)}, u32[]{:S(2)}) %collective-permute-start.6) | collective-permute-done | bytes 262176 | tf_op jit(solution)/shard_map/ppermute | solution.py:49
  61.0 3.2 %collective-permute-start.7 = (f32[512,128]{1,0:T(8,128)S(1)}, f32[512,128]{1,0:T(8,128)}, u32[]{:S(2)}, u32[]{:S(2)}) collective-permute-start(f32[512,128]{1,0:T(8,128)S(1)} %collective-permute-done.6.across_ref), channel_id=1, source_target_pairs={{0,32},{32,0},{64,96},{96,64},{128,160},{160,128},{192,224},{224,1... | collective-permute-start | bytes 786440 | tf_op jit(solution)/shard_map/ppermute | solution.py:49
  64.2 1.1 %fusion.10 = f32[4,32,128]{2,1,0:T(8,128)S(1)} fusion(bf16[1,4,128,128]{3,2,1,0:T(8,128)(2,1)} %param.16, bf16[1,16,32,128]{3,2,1,0:T(8,128)(2,1)S(1)} %convert_element_type.52), kind=kOutput, calls=%fused_computation.14 | convolution fusion | flops 4194304 | bytes 229376 | tf_op jit(solution)/shard_map/tjri,tjio->tjro/dot_general | solution.py:156
  67.3 3.5 %shard_map.111 = f32[4,512,128]{2,1,0:T(8,128)} custom-call(s32[1]{0:T(128)} %bitcast.index_ref, f32[16,16]{1,0:T(8,128)} %constant.32.clone.coef_ref, f32[512,128]{1,0:T(8,128)} %get-tuple-element.13.own_ref, f32[512,128]{1,0:T(8,128)} %copy-done.7, f32[512,128]{1,0:T(8,128)} %copy-done.6, f32[512,128]{1,0:T(8,128)} %collective-permute-done.7.diagonal_ref), custom_call_target="tpu_custom_call" | custom-call | tf_op jit(solution)/shard_map/pallas_call | solution.py:91
  70.8 4.2 %all-to-all-start.1 = ((f32[4,512,128]{2,1,0:T(8,128)}), f32[4,512,128]{2,1,0:T(8,128)}, u32[]{:S(2)}, u32[]{:S(2)}) async-start(f32[4,512,128]{2,1,0:T(8,128)} %shard_map.111), calls=%async_computation.1 | async-start | bytes 2097152 | tf_op jit(solution)/shard_map/all_to_all | solution.py:136
  75.0 0.8 pad_maximum_fusion.1
  75.8 1.9 %collective-permute-start.8 = (bf16[1,5,32,128]{3,2,1,0:T(8,128)(2,1)S(1)}, bf16[1,5,32,128]{3,2,1,0:T(8,128)(2,1)S(1)}, u32[]{:S(2)}, u32[]{:S(2)}) collective-permute-start(bf16[1,5,32,128]{3,2,1,0:T(8,128)(2,1)S(1)} %pad_maximum_fusion.1), channel_id=1, source_target_pairs={{31,0},{0,1},{1,2},{2,3},{3,4},{4,5},{5,6},{6,7},{7,8},{8,9},{9,10... | collective-permute-start | bytes 122888 | tf_op jit(solution)/shard_map/ppermute | solution.py:32
  77.7 7.0 %collective-permute-start.9 = (bf16[1,1,32,128]{3,2,1,0:T(8,128)(2,1)S(1)}, bf16[1,1,32,128]{3,2,1,0:T(8,128)(2,1)S(1)}, u32[]{:S(2)}, u32[]{:S(2)}) collective-permute-start(bf16[1,1,32,128]{3,2,1,0:T(8,128)(2,1)S(1)} %slice.38), channel_id=1, source_target_pairs={{1,0},{2,1},{3,2},{4,3},{5,4},{6,5},{7,6},{8,7},{9,8},{10,9},{11,1... | collective-permute-start | bytes 24584 | tf_op jit(solution)/shard_map/ppermute | solution.py:32
  85.5 0.9 maximum_bitcast_fusion.1
  86.4 1.7 %gather_fusion.1 = bf16[96,32,128]{2,1,0:T(8,128)(2,1)} fusion(bf16[18,32,128]{2,1,0:T(8,128)(2,1)S(1)} %maximum_bitcast_fusion.1, s32[1024]{0:T(1024)} %pad_clamp_fusion), kind=kCustom, calls=%fused_computation.1 | custom fusion | bytes 1573248 | tf_op jit(solution)/shard_map/gather | solution.py:167
  88.1 0.9 bitcast_add_fusion
  89.0 2.6 %multiply_add_fusion = f32[1,16,32,128]{3,2,1,0:T(8,128)} fusion(f32[1,16,32,128]{3,2,1,0:T(8,128)} %bitcast.66, f32[1,16,32,128]{3,2,1,0:T(8,128)S(1)} %copy-done.1, f32[1,4,32,128]{3,2,1,0:T(8,128)S(1)} %bitcast_add_fusion, f32[16,128]{1,0:T(8,128)} %bitcast.69, f32[16]{0:T(128)} %copy-done.10, bf16[16,6,32,128]{3,2,1,0:T(8,128)(2,1)} %bitcast.62, ...), kind=kOutput, calls=%fused_computation.8 | convolution fusion | flops 100990976 | bytes 4792384 | tf_op jit(solution)/shard_map/tnkri,tnkio->tnro/dot_general | solution.py:168
  91.6 2.0 %shard_map.112 = f32[512,128]{1,0:T(8,128)} custom-call(f32[4,512,128]{2,1,0:T(8,128)} %all-to-all-done.1.got_ref, f32[512,128]{1,0:T(8,128)} %bitcast.64, f32[16,128]{1,0:T(8,128)} %broadcast_multiply_fusion.scale_ref, f32[16,128]{1,0:T(8,128)} %cond_ref.3), custom_call_target="tpu_custom_call" | custom-call | tf_op jit(solution)/shard_map/pallas_call | solution.py:121
  (52 shorter events, 6.2 us)
Async XLA Ops:
  0.0 46.8 %copy-start = (bf16[1,16,6,128,128]{4,3,2,1,0:T(8,128)(2,1)S(1)}, bf16[1,16,6,128,128]{4,3,2,1,0:T(8,128)(2,1)}, u32[]{:S(2)}) copy-start(bf16[1,16,6,128,128]{4,3,2,1,0:T(8,128)(2,1)} %param.15) | copy-start | bytes 9437188
  0.8 41.8 %copy-start.10 = (f32[16]{0:T(128)}, f32[16]{0:T(128)S(1)}, u32[]{:S(2)}) copy-start(f32[16]{0:T(128)S(1)} %or_convert_fusion) | copy-start | bytes 196
  2.7 39.9 %copy-start.3 = (bf16[1,16,32,128]{3,2,1,0:T(8,128)(2,1)}, bf16[1,16,32,128]{3,2,1,0:T(8,128)(2,1)S(1)}, u32[]{:S(2)}) copy-start(bf16[1,16,32,128]{3,2,1,0:T(8,128)(2,1)S(1)} %get-tuple-element.12) | copy-start | bytes 393220
  2.7 14.4 %collective-permute-start.1 = (f32[512,128]{1,0:T(8,128)}, f32[512,128]{1,0:T(8,128)}, u32[]{:S(2)}, u32[]{:S(2)}) collective-permute-start(f32[512,128]{1,0:T(8,128)} %bitcast.2.own_ref), channel_id=1, source_target_pairs={{0,256},{32,288},{64,320},{96,352},{128,384},{160,416},{192,448},{... | collective-permute-start | bytes 786440 | tf_op jit(solution)/shard_map/ppermute | solution.py:49
  6.8 15.5 %collective-permute-start = (f32[512,128]{1,0:T(8,128)}, f32[512,128]{1,0:T(8,128)}, u32[]{:S(2)}, u32[]{:S(2)}) collective-permute-start(f32[512,128]{1,0:T(8,128)} %bitcast.2.own_ref), channel_id=1, source_target_pairs={{0,32},{32,0},{64,96},{96,64},{128,160},{160,128},{192,224},{224,1... | collective-permute-start | bytes 786440 | tf_op jit(solution)/shard_map/ppermute | solution.py:49
  14.1 6.6 %copy-start.11 = (f32[4]{0:T(128)}, f32[4]{0:T(128)S(1)}, u32[]{:S(2)}) copy-start(f32[4]{0:T(128)S(1)} %convert_bitcast_fusion) | copy-start | bytes 52
  15.8 1.2 %copy-start.4 = (f32[4,32,128]{2,1,0:T(8,128)}, f32[4,32,128]{2,1,0:T(8,128)S(1)}, u32[]{:S(2)}) copy-start(f32[4,32,128]{2,1,0:T(8,128)S(1)} %fusion.12) | copy-start | bytes 196612
  17.1 5.1 %collective-permute-start.2 = (f32[512,128]{1,0:T(8,128)}, f32[512,128]{1,0:T(8,128)}, u32[]{:S(2)}, u32[]{:S(2)}) collective-permute-start(f32[512,128]{1,0:T(8,128)} %collective-permute-done.1.across_ref), channel_id=1, source_target_pairs={{0,32},{32,0},{64,96},{96,64},{128,160},{160,128},{192,224},{224,1... | collective-permute-start | bytes 786440 | tf_op jit(solution)/shard_map/ppermute | solution.py:49
  22.3 24.6 %copy-start.1 = (f32[1,16,32,128]{3,2,1,0:T(8,128)S(1)}, f32[1,16,32,128]{3,2,1,0:T(8,128)}, u32[]{:S(2)}) copy-start(f32[1,16,32,128]{3,2,1,0:T(8,128)} %param.12) | copy-start | bytes 786436
  25.8 23.6 %all-to-all-start = ((f32[4,512,128]{2,1,0:T(8,128)}), f32[4,512,128]{2,1,0:T(8,128)}, u32[]{:S(2)}, u32[]{:S(2)}) async-start(f32[4,512,128]{2,1,0:T(8,128)} %shard_map.109), calls=%async_computation | async-start | bytes 2097152 | tf_op jit(solution)/shard_map/all_to_all | solution.py:136
  30.0 12.6 %collective-permute-start.3 = (bf16[1,5,32,128]{3,2,1,0:T(8,128)(2,1)}, bf16[1,5,32,128]{3,2,1,0:T(8,128)(2,1)S(1)}, u32[]{:S(2)}, u32[]{:S(2)}) collective-permute-start(bf16[1,5,32,128]{3,2,1,0:T(8,128)(2,1)} %pad_maximum_fusion), channel_id=1, source_target_pairs={{31,0},{0,1},{1,2},{2,3},{3,4},{4,5},{5,6},{6,7},{7,8},{8,9},{9,10... | collective-permute-start | bytes 122888 | tf_op jit(solution)/shard_map/ppermute | solution.py:32
  32.0 10.8 %collective-permute-start.4 = (bf16[1,1,32,128]{3,2,1,0:T(8,128)(2,1)S(1)}, bf16[1,1,32,128]{3,2,1,0:T(8,128)(2,1)S(1)}, u32[]{:S(2)}, u32[]{:S(2)}) collective-permute-start(bf16[1,1,32,128]{3,2,1,0:T(8,128)(2,1)S(1)} %slice.33), channel_id=1, source_target_pairs={{1,0},{2,1},{3,2},{4,3},{5,4},{6,5},{7,6},{8,7},{9,8},{10,9},{11,1... | collective-permute-start | bytes 24584 | tf_op jit(solution)/shard_map/ppermute | solution.py:32
  42.6 0.6 copy-start.8
  46.8 19.0 %copy-start.12 = (f32[4]{0:T(128)S(1)}, f32[4]{0:T(128)}, u32[]{:S(2)}) copy-start(f32[4]{0:T(128)} %copy-done.11) | copy-start | bytes 52
  51.5 9.5 %collective-permute-start.6 = (f32[512,128]{1,0:T(8,128)}, f32[512,128]{1,0:T(8,128)S(1)}, u32[]{:S(2)}, u32[]{:S(2)}) collective-permute-start(f32[512,128]{1,0:T(8,128)} %get-tuple-element.13.own_ref), channel_id=1, source_target_pairs={{0,256},{32,288},{64,320},{96,352},{128,384},{160,416},{192,448},{... | collective-permute-start | bytes 786440 | tf_op jit(solution)/shard_map/ppermute | solution.py:49
  53.8 12.8 %collective-permute-start.5 = (f32[512,128]{1,0:T(8,128)}, f32[512,128]{1,0:T(8,128)S(1)}, u32[]{:S(2)}, u32[]{:S(2)}) collective-permute-start(f32[512,128]{1,0:T(8,128)} %get-tuple-element.13.own_ref), channel_id=1, source_target_pairs={{0,32},{32,0},{64,96},{96,64},{128,160},{160,128},{192,224},{224,1... | collective-permute-start | bytes 786440 | tf_op jit(solution)/shard_map/ppermute | solution.py:49
  57.4 27.3 %copy-start.2 = (bf16[1,16,32,128]{3,2,1,0:T(8,128)(2,1)}, bf16[1,16,32,128]{3,2,1,0:T(8,128)(2,1)S(1)}, u32[]{:S(2)}) copy-start(bf16[1,16,32,128]{3,2,1,0:T(8,128)(2,1)S(1)} %convert_element_type.52) | copy-start | bytes 393220
  61.0 5.6 %copy-start.6 = (f32[512,128]{1,0:T(8,128)}, f32[512,128]{1,0:T(8,128)S(1)}, u32[]{:S(2)}) copy-start(f32[512,128]{1,0:T(8,128)S(1)} %collective-permute-done.6.across_ref) | copy-start | bytes 786436
  61.0 6.3 %collective-permute-start.7 = (f32[512,128]{1,0:T(8,128)S(1)}, f32[512,128]{1,0:T(8,128)}, u32[]{:S(2)}, u32[]{:S(2)}) collective-permute-start(f32[512,128]{1,0:T(8,128)S(1)} %collective-permute-done.6.across_ref), channel_id=1, source_target_pairs={{0,32},{32,0},{64,96},{96,64},{128,160},{160,128},{192,224},{224,1... | collective-permute-start | bytes 786440 | tf_op jit(solution)/shard_map/ppermute | solution.py:49
  65.2 0.6 copy-start.5
  66.6 0.7 copy-start.7
  70.8 20.8 %all-to-all-start.1 = ((f32[4,512,128]{2,1,0:T(8,128)}), f32[4,512,128]{2,1,0:T(8,128)}, u32[]{:S(2)}, u32[]{:S(2)}) async-start(f32[4,512,128]{2,1,0:T(8,128)} %shard_map.111), calls=%async_computation.1 | async-start | bytes 2097152 | tf_op jit(solution)/shard_map/all_to_all | solution.py:136
  75.8 8.9 %collective-permute-start.8 = (bf16[1,5,32,128]{3,2,1,0:T(8,128)(2,1)S(1)}, bf16[1,5,32,128]{3,2,1,0:T(8,128)(2,1)S(1)}, u32[]{:S(2)}, u32[]{:S(2)}) collective-permute-start(bf16[1,5,32,128]{3,2,1,0:T(8,128)(2,1)S(1)} %pad_maximum_fusion.1), channel_id=1, source_target_pairs={{31,0},{0,1},{1,2},{2,3},{3,4},{4,5},{5,6},{6,7},{7,8},{8,9},{9,10... | collective-permute-start | bytes 122888 | tf_op jit(solution)/shard_map/ppermute | solution.py:32
  77.7 7.8 %collective-permute-start.9 = (bf16[1,1,32,128]{3,2,1,0:T(8,128)(2,1)S(1)}, bf16[1,1,32,128]{3,2,1,0:T(8,128)(2,1)S(1)}, u32[]{:S(2)}, u32[]{:S(2)}) collective-permute-start(bf16[1,1,32,128]{3,2,1,0:T(8,128)(2,1)S(1)} %slice.38), channel_id=1, source_target_pairs={{1,0},{2,1},{3,2},{4,3},{5,4},{6,5},{7,6},{8,7},{9,8},{10,9},{11,1... | collective-permute-start | bytes 24584 | tf_op jit(solution)/shard_map/ppermute | solution.py:32
  84.7 0.8 copy-start.9

commit v20 on v12

--- a/solution.py
+++ b/solution.py
@@ -107,9 +107,10 @@
     scale = jnp.broadcast_to(scale_ref[...][:, None, :], (groups, rows // groups, lanes)).reshape(rows, lanes)
     lam = base_ref[...] - scale * spec
     lam_ref[...] = lam
-    for weighted_ref in rest:
+    if rest:
         cond = jnp.broadcast_to(cond_ref[...][:, None, :], (groups, rows // groups, lanes)).reshape(rows, lanes)
-        weighted_ref[...] = lam * cond
+        rest[0][...] = lam * cond
+        rest[1][...] = lam.astype(jnp.bfloat16)
 
 
 def updated(got, base, scale, cond, outputs):
@@ -123,7 +124,8 @@
         grid=(rows // block,),
         in_specs=[pl.BlockSpec((4, block, lanes), lambda r: (0, r, 0)), flat, narrow, narrow],
         out_specs=[flat] * outputs,
-        out_shape=[jax.ShapeDtypeStruct(base.shape, jnp.float32)] * outputs,
+        out_shape=[jax.ShapeDtypeStruct(base.shape, jnp.float32)] * min(outputs, 2)
+        + [jax.ShapeDtypeStruct(base.shape, jnp.bfloat16)] * (outputs - 2),
     )(got, base, scale, cond)
 
 
@@ -150,8 +152,8 @@
     cond_wide = cond[None, :, None, :]
     scale = relax[0] * live[0, :, 0]
     weighted = (lam * cond_wide).reshape(-1, lanes)
+    lam_b = lam.astype(jnp.bfloat16)
     for sweep in range(SWEEPS):
-        lam_b = lam.astype(jnp.bfloat16)
         partials, got = instance_mix(weighted)
         records = jnp.einsum(
             "tjri,tjio->tjro",
@@ -173,9 +175,11 @@
             axis=1,
         )
         base = lam + relax_wide * (rhs - (stator + rotor_full)) * live
-        fresh = updated(got, base.reshape(-1, lanes), scale, cond, 2 if sweep + 1 < SWEEPS else 1)
+        fresh = updated(got, base.reshape(-1, lanes), scale, cond, 3 if sweep + 1 < SWEEPS else 1)
         lam = fresh[0].reshape(shape)
-        weighted = fresh[-1]
+        if len(fresh) > 1:
+            weighted = fresh[1]
+            lam_b = fresh[2].reshape(shape)
     return lam
 
 

time: 92.5 us -> 97.4 us (1.053)
  waiting for transfers between devices: 4.49 us -> 10.8 us
  matrix products: 7.23 us -> 6.23 us
    all_to_all x2, waiting for transfers between devices: 0.01 us -> 7.15 us  [instance_mix(): return (partials, lax.all_to_all(partials, 'ix', 0, 0))]
    convert_element_type x2 -> x1, other arithmetic: 2.86 us -> 1.89 us  [shards(): lam_b = lam.astype(jnp.bfloat16)]
  transfers between devices with their start and end apart: 12 -> 12, of which waited for: 3 -> 4; matrix products, arithmetic and copies ran while one was open for 24% -> 22% of each run, Pallas kernels for 0% -> 0%
where the time goes in v20:
time: 97.4 us; the launch traced here: 96.4 us
  starting transfers between devices  51.2 us (53%)
  other arithmetic  12.4 us (13%)
  waiting for transfers between devices  10.8 us (11%)
  Pallas kernels  8.66 us (9%)
  matrix products  6.23 us (6%)
  local copies, waits for them, and re-layouts  6.07 us (6%)
  between operations  1.09 us (1%)
    ppermute x6, starting transfers between devices, routed(): return lax.ppermute(block, INST, [(s, dest(s)) for s in range(NT)])  21.8 us
    ppermute x4, starting transfers between devices, shifted(): return lax.ppermute(block, axis, route)  20.8 us
    all_to_all x2, starting transfers between devices, instance_mix(): return (partials, lax.all_to_all(partials, 'ix', 0, 0))  8.51 us
    all_to_all x2, waiting for transfers between devices, instance_mix(): return (partials, lax.all_to_all(partials, 'ix', 0, 0))  7.15 us
    pallas_call x2, Pallas kernels, partial_sums(): pl.pallas_call(mix_kernel, grid_spec=pltpu.PrefetchScalarGridSpec(num_sca...  4.6 us
    dot_general x2, matrix products, shards(): jnp.einsum('tnkri,tnkio->tnro', picked, jac, preferred_element_type=jnp.f...  4.28 us
    pallas_call x2, Pallas kernels, updated(): pl.pallas_call(update_kernel, grid=(rows // block,), in_specs=[pl.BlockSp...  4.06 us
    ppermute x6, waiting for transfers between devices, routed(): return lax.ppermute(block, INST, [(s, dest(s)) for s in range(NT)])  3.53 us
  transfers between devices with their start and end apart: 12, of which 4 were waited for; matrix products, arithmetic and copies ran while one was open for 22% of the time, Pallas kernels for 0%

profile of v20, /device:TPU:1, one launch (start us, length us, event | category | flops | bytes accessed | tf_op | source)
XLA Modules:
  0.0 96.4 jit_solution(8613086592689119724)
XLA Ops:
  0.8 1.9 %multiply_convert_fusion = (bf16[1,16,32,128]{3,2,1,0:T(8,128)(2,1)S(1)}, f32[1,16,32,128]{3,2,1,0:T(8,128)}) fusion(f32[1,16,32,128]{3,2,1,0:T(8,128)} %param.11, f32[16]{0:T(128)S(1)} %or_convert_fusion, f32[16,128]{1,0:T(8,128)} %cond_ref.3), kind=kLoop, calls=%fused_computation.10 | loop fusion | flops 196608 | bytes 663616 | tf_op jit(solution)/shard_map/convert_element_type | solution.py:155
  2.7 4.0 %collective-permute-start.1 = (f32[512,128]{1,0:T(8,128)}, f32[512,128]{1,0:T(8,128)}, u32[]{:S(2)}, u32[]{:S(2)}) collective-permute-start(f32[512,128]{1,0:T(8,128)} %bitcast.2.own_ref), channel_id=1, source_target_pairs={{0,256},{32,288},{64,320},{96,352},{128,384},{160,416},{192,448},{... | collective-permute-start | bytes 786440 | tf_op jit(solution)/shard_map/ppermute | solution.py:49
  6.8 6.7 %collective-permute-start = (f32[512,128]{1,0:T(8,128)}, f32[512,128]{1,0:T(8,128)}, u32[]{:S(2)}, u32[]{:S(2)}) collective-permute-start(f32[512,128]{1,0:T(8,128)} %bitcast.2.own_ref), channel_id=1, source_target_pairs={{0,32},{32,0},{64,96},{96,64},{128,160},{160,128},{192,224},{224,1... | collective-permute-start | bytes 786440 | tf_op jit(solution)/shard_map/ppermute | solution.py:49
  14.8 1.0 %fusion.12 = f32[4,32,128]{2,1,0:T(8,128)S(1)} fusion(bf16[1,4,128,128]{3,2,1,0:T(8,128)(2,1)} %param.16, bf16[1,16,32,128]{3,2,1,0:T(8,128)(2,1)S(1)} %get-tuple-element.13), kind=kOutput, calls=%fused_computation.16 | convolution fusion | flops 4194304 | bytes 229376 | tf_op jit(solution)/shard_map/tjri,tjio->tjro/dot_general | solution.py:158
  15.8 1.1 %broadcast_subtract_fusion = f32[4]{0:T(128)} fusion(s32[1,4]{1,0:T(1,128)} %param.18), kind=kLoop, calls=%fused_computation.33 | loop fusion | flops 8 | bytes 32 | tf_op jit(solution)/shard_map/sub | solution.py:172
  17.1 3.0 %collective-permute-start.2 = (f32[512,128]{1,0:T(8,128)}, f32[512,128]{1,0:T(8,128)}, u32[]{:S(2)}, u32[]{:S(2)}) collective-permute-start(f32[512,128]{1,0:T(8,128)} %collective-permute-done.1.across_ref), channel_id=1, source_target_pairs={{0,32},{32,0},{64,96},{96,64},{128,160},{160,128},{192,224},{224,1... | collective-permute-start | bytes 786440 | tf_op jit(solution)/shard_map/ppermute | solution.py:49
  20.9 1.4 %broadcast_multiply_fusion.scale_ref = f32[16,128]{1,0:T(8,128)} fusion(f32[16]{0:T(128)S(1)} %or_convert_fusion, f32[1,16,128]{2,1,0:T(8,128)} %param.13), kind=kLoop, calls=%fused_computation.30 | loop fusion | flops 2048 | bytes 16448 | tf_op jit(solution)/shard_map/mul | solution.py:153
  22.3 2.3 %shard_map.109 = f32[4,512,128]{2,1,0:T(8,128)} custom-call(s32[1]{0:T(128)} %bitcast.index_ref, f32[16,16]{1,0:T(8,128)} %constant.32.clone.coef_ref, f32[512,128]{1,0:T(8,128)} %bitcast.2.own_ref, f32[512,128]{1,0:T(8,128)} %collective-permute-done.mate_ref, f32[512,128]{1,0:T(8,128)} %collective-permute-done.1.across_ref, ...), custom_call_target="tpu_custom_call" | custom-call | tf_op jit(solution)/shard_map/pallas_call | solution.py:91
  24.6 4.2 %all-to-all-start = ((f32[4,512,128]{2,1,0:T(8,128)}), f32[4,512,128]{2,1,0:T(8,128)}, u32[]{:S(2)}, u32[]{:S(2)}) async-start(f32[4,512,128]{2,1,0:T(8,128)} %shard_map.109), calls=%async_computation | async-start | bytes 2097152 | tf_op jit(solution)/shard_map/all_to_all | solution.py:138
  28.9 1.9 %collective-permute-start.3 = (bf16[1,5,32,128]{3,2,1,0:T(8,128)(2,1)}, bf16[1,5,32,128]{3,2,1,0:T(8,128)(2,1)S(1)}, u32[]{:S(2)}, u32[]{:S(2)}) collective-permute-start(bf16[1,5,32,128]{3,2,1,0:T(8,128)(2,1)} %pad_maximum_fusion), channel_id=1, source_target_pairs={{31,0},{0,1},{1,2},{2,3},{3,4},{4,5},{5,6},{6,7},{7,8},{8,9},{9,10... | collective-permute-start | bytes 122888 | tf_op jit(solution)/shard_map/ppermute | solution.py:32
  30.8 10.1 %collective-permute-start.4 = (bf16[1,1,32,128]{3,2,1,0:T(8,128)(2,1)S(1)}, bf16[1,1,32,128]{3,2,1,0:T(8,128)(2,1)S(1)}, u32[]{:S(2)}, u32[]{:S(2)}) collective-permute-start(bf16[1,1,32,128]{3,2,1,0:T(8,128)(2,1)S(1)} %slice.33), channel_id=1, source_target_pairs={{1,0},{2,1},{3,2},{4,3},{5,4},{6,5},{7,6},{8,7},{9,8},{10,9},{11,1... | collective-permute-start | bytes 24584 | tf_op jit(solution)/shard_map/ppermute | solution.py:32
  42.1 0.9 maximum_bitcast_fusion
  43.0 1.7 %gather_fusion = bf16[96,32,128]{2,1,0:T(8,128)(2,1)} fusion(bf16[18,32,128]{2,1,0:T(8,128)(2,1)S(1)} %maximum_bitcast_fusion, s32[1024]{0:T(1024)} %pad_clamp_fusion), kind=kCustom, calls=%fused_computation | custom fusion | bytes 1573248 | tf_op jit(solution)/shard_map/gather | solution.py:169
  44.7 1.0 %bitcast_add_fusion.1 = f32[1,4,32,128]{3,2,1,0:T(8,128)S(1)} fusion(f32[4,32,128]{2,1,0:T(8,128)} %copy-done.4, bf16[1,5,32,128]{3,2,1,0:T(8,128)(2,1)} %copy-done.11, f32[4]{0:T(128)} %broadcast_subtract_fusion), kind=kLoop, calls=%fused_computation.19 | loop fusion | flops 49152 | bytes 163856 | tf_op jit(solution)/shard_map/add | solution.py:172
  45.7 2.6 %multiply_add_fusion.1 = f32[1,16,32,128]{3,2,1,0:T(8,128)} fusion(f32[1,16,32,128]{3,2,1,0:T(8,128)} %param.12, f32[1,4,32,128]{3,2,1,0:T(8,128)S(1)} %bitcast_add_fusion.1, f32[1,16,32,128]{3,2,1,0:T(8,128)S(1)} %copy-done.1, f32[16,128]{1,0:T(8,128)} %bitcast.70, f32[16]{0:T(128)} %copy-done.12, bf16[16,6,32,128]{3,2,1,0:T(8,128)(2,1)} %bitcast.62, ...), kind=kOutput, calls=%fused_computation.9 | convolution fusion | flops 101056512 | bytes 4792384 | tf_op jit(solution)/shard_map/tnkri,tnkio->tnro/dot_general | solution.py:170
  48.3 2.1 %shard_map.110 = (f32[512,128]{1,0:T(8,128)}, f32[512,128]{1,0:T(8,128)}, bf16[512,128]{1,0:T(8,128)(2,1)}) custom-call(f32[4,512,128]{2,1,0:T(8,128)} %all-to-all-done.got_ref, f32[512,128]{1,0:T(8,128)} %bitcast.63, f32[16,128]{1,0:T(8,128)} %broadcast_multiply_fusion.scale_ref, f32[16,128]{1,0:T(8,128)} %cond_ref.3), custom_call_target="tpu_custom_call" | custom-call | tf_op jit(solution)/shard_map/pallas_call | solution.py:122
  50.4 2.3 %collective-permute-start.6 = (f32[512,128]{1,0:T(8,128)}, f32[512,128]{1,0:T(8,128)S(1)}, u32[]{:S(2)}, u32[]{:S(2)}) collective-permute-start(f32[512,128]{1,0:T(8,128)} %get-tuple-element.14.own_ref), channel_id=1, source_target_pairs={{0,256},{32,288},{64,320},{96,352},{128,384},{160,416},{192,448},{... | collective-permute-start | bytes 786440 | tf_op jit(solution)/shard_map/ppermute | solution.py:49
  52.7 2.6 %collective-permute-start.5 = (f32[512,128]{1,0:T(8,128)}, f32[512,128]{1,0:T(8,128)}, u32[]{:S(2)}, u32[]{:S(2)}) collective-permute-start(f32[512,128]{1,0:T(8,128)} %get-tuple-element.14.own_ref), channel_id=1, source_target_pairs={{0,32},{32,0},{64,96},{96,64},{128,160},{160,128},{192,224},{224,1... | collective-permute-start | bytes 786440 | tf_op jit(solution)/shard_map/ppermute | solution.py:49
  56.0 0.9 fusion.10
  56.9 3.0 %collective-permute-done.6.across_ref = f32[512,128]{1,0:T(8,128)S(1)} collective-permute-done((f32[512,128]{1,0:T(8,128)}, f32[512,128]{1,0:T(8,128)S(1)}, u32[]{:S(2)}, u32[]{:S(2)}) %collective-permute-start.6) | collective-permute-done | bytes 262176 | tf_op jit(solution)/shard_map/ppermute | solution.py:49
  59.9 3.2 %collective-permute-start.7 = (f32[512,128]{1,0:T(8,128)S(1)}, f32[512,128]{1,0:T(8,128)}, u32[]{:S(2)}, u32[]{:S(2)}) collective-permute-start(f32[512,128]{1,0:T(8,128)S(1)} %collective-permute-done.6.across_ref), channel_id=1, source_target_pairs={{0,32},{32,0},{64,96},{96,64},{128,160},{160,128},{192,224},{224,1... | collective-permute-start | bytes 786440 | tf_op jit(solution)/shard_map/ppermute | solution.py:49
  64.4 2.3 %shard_map.111 = f32[4,512,128]{2,1,0:T(8,128)} custom-call(s32[1]{0:T(128)} %bitcast.index_ref, f32[16,16]{1,0:T(8,128)} %constant.32.clone.coef_ref, f32[512,128]{1,0:T(8,128)} %get-tuple-element.14.own_ref, f32[512,128]{1,0:T(8,128)} %collective-permute-done.5.mate_ref, f32[512,128]{1,0:T(8,128)} %copy-done.7, f32[512,128]{1,0:T(8,128)} %collective-permute-done.7.diagonal_ref), custom_call_target="tpu_custom_call" | custom-call | tf_op jit(solution)/shard_map/pallas_call | solution.py:91
  66.6 1.9 %collective-permute-start.8 = (bf16[1,5,32,128]{3,2,1,0:T(8,128)(2,1)S(1)}, bf16[1,5,32,128]{3,2,1,0:T(8,128)(2,1)S(1)}, u32[]{:S(2)}, u32[]{:S(2)}) collective-permute-start(bf16[1,5,32,128]{3,2,1,0:T(8,128)(2,1)S(1)} %pad_maximum_fusion.1), channel_id=1, source_target_pairs={{31,0},{0,1},{1,2},{2,3},{3,4},{4,5},{5,6},{6,7},{7,8},{8,9},{9,10... | collective-permute-start | bytes 122888 | tf_op jit(solution)/shard_map/ppermute | solution.py:32
  69.2 7.0 %collective-permute-start.9 = (bf16[1,1,32,128]{3,2,1,0:T(8,128)(2,1)S(1)}, bf16[1,1,32,128]{3,2,1,0:T(8,128)(2,1)}, u32[]{:S(2)}, u32[]{:S(2)}) collective-permute-start(bf16[1,1,32,128]{3,2,1,0:T(8,128)(2,1)S(1)} %slice.38), channel_id=1, source_target_pairs={{1,0},{2,1},{3,2},{4,3},{5,4},{6,5},{7,6},{8,7},{9,8},{10,9},{11,1... | collective-permute-start | bytes 24584 | tf_op jit(solution)/shard_map/ppermute | solution.py:32
  76.2 4.3 %all-to-all-start.1 = ((f32[4,512,128]{2,1,0:T(8,128)}), f32[4,512,128]{2,1,0:T(8,128)}, u32[]{:S(2)}, u32[]{:S(2)}) async-start(f32[4,512,128]{2,1,0:T(8,128)} %shard_map.111), calls=%async_computation.1 | async-start | bytes 2097152 | tf_op jit(solution)/shard_map/all_to_all | solution.py:138
  81.1 0.9 maximum_bitcast_fusion.1
  82.1 1.7 %gather_fusion.1 = bf16[96,32,128]{2,1,0:T(8,128)(2,1)} fusion(bf16[18,32,128]{2,1,0:T(8,128)(2,1)S(1)} %maximum_bitcast_fusion.1, s32[1024]{0:T(1024)} %pad_clamp_fusion), kind=kCustom, calls=%fused_computation.1 | custom fusion | bytes 1573248 | tf_op jit(solution)/shard_map/gather | solution.py:169
  83.8 1.0 %bitcast_add_fusion = f32[1,4,32,128]{3,2,1,0:T(8,128)S(1)} fusion(f32[4,32,128]{2,1,0:T(8,128)} %copy-done.5, bf16[1,5,32,128]{3,2,1,0:T(8,128)(2,1)} %copy-done.10, f32[4]{0:T(128)} %broadcast_subtract_fusion), kind=kLoop, calls=%fused_computation.18 | loop fusion | flops 49152 | bytes 163856 | tf_op jit(solution)/shard_map/add | solution.py:172
  84.7 1.7 %fusion.7 = f32[1,16,32,128]{3,2,1,0:T(8,128)S(1)} fusion(bf16[16,6,32,128]{3,2,1,0:T(8,128)(2,1)} %bitcast.61, bf16[1,16,6,128,128]{4,3,2,1,0:T(8,128)(2,1)S(1)} %copy-done), kind=kOutput, calls=%fused_computation.7 | convolution fusion | flops 100663296 | bytes 4194304 | tf_op jit(solution)/shard_map/tnkri,tnkio->tnro/dot_general | solution.py:170
  86.5 0.8 multiply_add_fusion
  87.3 7.1 %all-to-all-done.1.got_ref = f32[4,512,128]{2,1,0:T(8,128)} async-done(((f32[4,512,128]{2,1,0:T(8,128)}), f32[4,512,128]{2,1,0:T(8,128)}, u32[]{:S(2)}, u32[]{:S(2)}) %all-to-all-start.1) | async-done | bytes 1048608 | tf_op jit(solution)/shard_map/all_to_all | solution.py:138
  94.5 2.0 %shard_map.112 = f32[512,128]{1,0:T(8,128)} custom-call(f32[4,512,128]{2,1,0:T(8,128)} %all-to-all-done.1.got_ref, f32[512,128]{1,0:T(8,128)} %bitcast.64, f32[16,128]{1,0:T(8,128)} %broadcast_multiply_fusion.scale_ref, f32[16,128]{1,0:T(8,128)} %cond_ref.3), custom_call_target="tpu_custom_call" | custom-call | tf_op jit(solution)/shard_map/pallas_call | solution.py:122
  (56 shorter events, 6.7 us)
Async XLA Ops:
  0.0 45.7 %copy-start = (bf16[1,16,6,128,128]{4,3,2,1,0:T(8,128)(2,1)S(1)}, bf16[1,16,6,128,128]{4,3,2,1,0:T(8,128)(2,1)}, u32[]{:S(2)}) copy-start(bf16[1,16,6,128,128]{4,3,2,1,0:T(8,128)(2,1)} %param.15) | copy-start | bytes 9437188
  0.8 40.7 %copy-start.12 = (f32[16]{0:T(128)}, f32[16]{0:T(128)S(1)}, u32[]{:S(2)}) copy-start(f32[16]{0:T(128)S(1)} %or_convert_fusion) | copy-start | bytes 196
  2.7 38.8 %copy-start.3 = (bf16[1,16,32,128]{3,2,1,0:T(8,128)(2,1)}, bf16[1,16,32,128]{3,2,1,0:T(8,128)(2,1)S(1)}, u32[]{:S(2)}) copy-start(bf16[1,16,32,128]{3,2,1,0:T(8,128)(2,1)S(1)} %get-tuple-element.13) | copy-start | bytes 393220
  2.7 14.3 %collective-permute-start.1 = (f32[512,128]{1,0:T(8,128)}, f32[512,128]{1,0:T(8,128)}, u32[]{:S(2)}, u32[]{:S(2)}) collective-permute-start(f32[512,128]{1,0:T(8,128)} %bitcast.2.own_ref), channel_id=1, source_target_pairs={{0,256},{32,288},{64,320},{96,352},{128,384},{160,416},{192,448},{... | collective-permute-start | bytes 786440 | tf_op jit(solution)/shard_map/ppermute | solution.py:49
  6.8 15.5 %collective-permute-start = (f32[512,128]{1,0:T(8,128)}, f32[512,128]{1,0:T(8,128)}, u32[]{:S(2)}, u32[]{:S(2)}) collective-permute-start(f32[512,128]{1,0:T(8,128)} %bitcast.2.own_ref), channel_id=1, source_target_pairs={{0,32},{32,0},{64,96},{96,64},{128,160},{160,128},{192,224},{224,1... | collective-permute-start | bytes 786440 | tf_op jit(solution)/shard_map/ppermute | solution.py:49
  14.1 6.6 %copy-start.14 = (f32[4]{0:T(128)}, f32[4]{0:T(128)S(1)}, u32[]{:S(2)}) copy-start(f32[4]{0:T(128)S(1)} %convert_bitcast_fusion) | copy-start | bytes 52
  15.8 1.1 %copy-start.4 = (f32[4,32,128]{2,1,0:T(8,128)}, f32[4,32,128]{2,1,0:T(8,128)S(1)}, u32[]{:S(2)}) copy-start(f32[4,32,128]{2,1,0:T(8,128)S(1)} %fusion.12) | copy-start | bytes 196612
  17.1 5.2 %collective-permute-start.2 = (f32[512,128]{1,0:T(8,128)}, f32[512,128]{1,0:T(8,128)}, u32[]{:S(2)}, u32[]{:S(2)}) collective-permute-start(f32[512,128]{1,0:T(8,128)} %collective-permute-done.1.across_ref), channel_id=1, source_target_pairs={{0,32},{32,0},{64,96},{96,64},{128,160},{160,128},{192,224},{224,1... | collective-permute-start | bytes 786440 | tf_op jit(solution)/shard_map/ppermute | solution.py:49
  22.3 23.4 %copy-start.1 = (f32[1,16,32,128]{3,2,1,0:T(8,128)S(1)}, f32[1,16,32,128]{3,2,1,0:T(8,128)}, u32[]{:S(2)}) copy-start(f32[1,16,32,128]{3,2,1,0:T(8,128)} %param.11) | copy-start | bytes 786436
  24.6 23.6 %all-to-all-start = ((f32[4,512,128]{2,1,0:T(8,128)}), f32[4,512,128]{2,1,0:T(8,128)}, u32[]{:S(2)}, u32[]{:S(2)}) async-start(f32[4,512,128]{2,1,0:T(8,128)} %shard_map.109), calls=%async_computation | async-start | bytes 2097152 | tf_op jit(solution)/shard_map/all_to_all | solution.py:138
  28.9 12.6 %collective-permute-start.3 = (bf16[1,5,32,128]{3,2,1,0:T(8,128)(2,1)}, bf16[1,5,32,128]{3,2,1,0:T(8,128)(2,1)S(1)}, u32[]{:S(2)}, u32[]{:S(2)}) collective-permute-start(bf16[1,5,32,128]{3,2,1,0:T(8,128)(2,1)} %pad_maximum_fusion), channel_id=1, source_target_pairs={{31,0},{0,1},{1,2},{2,3},{3,4},{4,5},{5,6},{6,7},{7,8},{8,9},{9,10... | collective-permute-start | bytes 122888 | tf_op jit(solution)/shard_map/ppermute | solution.py:32
  30.8 10.8 %collective-permute-start.4 = (bf16[1,1,32,128]{3,2,1,0:T(8,128)(2,1)S(1)}, bf16[1,1,32,128]{3,2,1,0:T(8,128)(2,1)S(1)}, u32[]{:S(2)}, u32[]{:S(2)}) collective-permute-start(bf16[1,1,32,128]{3,2,1,0:T(8,128)(2,1)S(1)} %slice.33), channel_id=1, source_target_pairs={{1,0},{2,1},{3,2},{4,3},{5,4},{6,5},{7,6},{8,7},{9,8},{10,9},{11,1... | collective-permute-start | bytes 24584 | tf_op jit(solution)/shard_map/ppermute | solution.py:32
  41.5 0.6 copy-start.11
  44.7 11.3 %copy-start.6 = (bf16[1,4,128,128]{3,2,1,0:T(8,128)(2,1)S(1)}, bf16[1,4,128,128]{3,2,1,0:T(8,128)(2,1)}, u32[]{:S(2)}) copy-start(bf16[1,4,128,128]{3,2,1,0:T(8,128)(2,1)} %param.16) | copy-start | bytes 393220
  50.4 9.5 %collective-permute-start.6 = (f32[512,128]{1,0:T(8,128)}, f32[512,128]{1,0:T(8,128)S(1)}, u32[]{:S(2)}, u32[]{:S(2)}) collective-permute-start(f32[512,128]{1,0:T(8,128)} %get-tuple-element.14.own_ref), channel_id=1, source_target_pairs={{0,256},{32,288},{64,320},{96,352},{128,384},{160,416},{192,448},{... | collective-permute-start | bytes 786440 | tf_op jit(solution)/shard_map/ppermute | solution.py:49
  52.7 11.1 %collective-permute-start.5 = (f32[512,128]{1,0:T(8,128)}, f32[512,128]{1,0:T(8,128)}, u32[]{:S(2)}, u32[]{:S(2)}) collective-permute-start(f32[512,128]{1,0:T(8,128)} %get-tuple-element.14.own_ref), channel_id=1, source_target_pairs={{0,32},{32,0},{64,96},{96,64},{128,160},{160,128},{192,224},{224,1... | collective-permute-start | bytes 786440 | tf_op jit(solution)/shard_map/ppermute | solution.py:49
  56.9 6.2 %copy-start.5 = (f32[4,32,128]{2,1,0:T(8,128)}, f32[4,32,128]{2,1,0:T(8,128)S(1)}, u32[]{:S(2)}) copy-start(f32[4,32,128]{2,1,0:T(8,128)S(1)} %fusion.10) | copy-start | bytes 196612
  59.9 4.5 %copy-start.7 = (f32[512,128]{1,0:T(8,128)}, f32[512,128]{1,0:T(8,128)S(1)}, u32[]{:S(2)}) copy-start(f32[512,128]{1,0:T(8,128)S(1)} %collective-permute-done.6.across_ref) | copy-start | bytes 786436
  59.9 4.5 %collective-permute-start.7 = (f32[512,128]{1,0:T(8,128)S(1)}, f32[512,128]{1,0:T(8,128)}, u32[]{:S(2)}, u32[]{:S(2)}) collective-permute-start(f32[512,128]{1,0:T(8,128)S(1)} %collective-permute-done.6.across_ref), channel_id=1, source_target_pairs={{0,32},{32,0},{64,96},{96,64},{128,160},{160,128},{192,224},{224,1... | collective-permute-start | bytes 786440 | tf_op jit(solution)/shard_map/ppermute | solution.py:49
  66.6 13.9 %collective-permute-start.8 = (bf16[1,5,32,128]{3,2,1,0:T(8,128)(2,1)S(1)}, bf16[1,5,32,128]{3,2,1,0:T(8,128)(2,1)S(1)}, u32[]{:S(2)}, u32[]{:S(2)}) collective-permute-start(bf16[1,5,32,128]{3,2,1,0:T(8,128)(2,1)S(1)} %pad_maximum_fusion.1), channel_id=1, source_target_pairs={{31,0},{0,1},{1,2},{2,3},{3,4},{4,5},{5,6},{6,7},{7,8},{8,9},{9,10... | collective-permute-start | bytes 122888 | tf_op jit(solution)/shard_map/ppermute | solution.py:32
  69.2 11.9 %collective-permute-start.9 = (bf16[1,1,32,128]{3,2,1,0:T(8,128)(2,1)S(1)}, bf16[1,1,32,128]{3,2,1,0:T(8,128)(2,1)}, u32[]{:S(2)}, u32[]{:S(2)}) collective-permute-start(bf16[1,1,32,128]{3,2,1,0:T(8,128)(2,1)S(1)} %slice.38), channel_id=1, source_target_pairs={{1,0},{2,1},{3,2},{4,3},{5,4},{6,5},{7,6},{8,7},{9,8},{10,9},{11,1... | collective-permute-start | bytes 24584 | tf_op jit(solution)/shard_map/ppermute | solution.py:32
  76.2 18.3 %all-to-all-start.1 = ((f32[4,512,128]{2,1,0:T(8,128)}), f32[4,512,128]{2,1,0:T(8,128)}, u32[]{:S(2)}, u32[]{:S(2)}) async-start(f32[4,512,128]{2,1,0:T(8,128)} %shard_map.111), calls=%async_computation.1 | async-start | bytes 2097152 | tf_op jit(solution)/shard_map/all_to_all | solution.py:138
  80.5 6.0 %copy-start.2 = (f32[1,16,32,128]{3,2,1,0:T(8,128)S(1)}, f32[1,16,32,128]{3,2,1,0:T(8,128)}, u32[]{:S(2)}) copy-start(f32[1,16,32,128]{3,2,1,0:T(8,128)} %param.12) | copy-start | bytes 786436
  80.5 0.6 copy-start.10
  83.8 2.7 %copy-start.8 = (f32[512,128]{1,0:T(8,128)S(1)}, f32[512,128]{1,0:T(8,128)}, u32[]{:S(2)}) copy-start(f32[512,128]{1,0:T(8,128)} %get-tuple-element.15) | copy-start | bytes 786436
  83.8 2.7 %copy-start.9 = (f32[1,16,128]{2,1,0:T(8,128)S(1)}, f32[1,16,128]{2,1,0:T(8,128)}, u32[]{:S(2)}) copy-start(f32[1,16,128]{2,1,0:T(8,128)} %param.13) | copy-start | bytes 24580
  83.8 2.7 %copy-start.13 = (f32[16]{0:T(128)S(1)}, f32[16]{0:T(128)}, u32[]{:S(2)}) copy-start(f32[16]{0:T(128)} %copy-done.12) | copy-start | bytes 196

commit v21 on v12

--- a/solution.py
+++ b/solution.py
@@ -69,7 +69,7 @@
 def mix_kernel(index_ref, coef_ref, own_ref, mate_ref, across_ref, diagonal_ref, o_ref):
     me = index_ref[0]
     coef = [[coef_ref[me, slot * 4 + m] for m in range(4)] for slot in range(4)]
-    chunk = 32
+    chunk = 64
 
     def step(c, carry):
         rows = pl.ds(pl.multiple_of(c * chunk, chunk), chunk)

time: 92.5 us -> 92.5 us (level)
  no operation moved by 1% of the time
where the time goes in v21:
time: 92.5 us; the launch traced here: 91.1 us
  starting transfers between devices  51.1 us (55%)
  other arithmetic  13.2 us (14%)
  Pallas kernels  8.59 us (9%)
  matrix products  7.22 us (8%)
  local copies, waits for them, and re-layouts  5.39 us (6%)
  waiting for transfers between devices  4.49 us (5%)
  between operations  1.06 us (1%)
    ppermute x6, starting transfers between devices, routed(): return lax.ppermute(block, INST, [(s, dest(s)) for s in range(NT)])  21.8 us
    ppermute x4, starting transfers between devices, shifted(): return lax.ppermute(block, axis, route)  20.9 us
    all_to_all x2, starting transfers between devices, instance_mix(): return (partials, lax.all_to_all(partials, 'ix', 0, 0))  8.49 us
    dot_general x2, matrix products, shards(): jnp.einsum('tnkri,tnkio->tnro', picked, jac, preferred_element_type=jnp.f...  5.12 us
    pallas_call x2, Pallas kernels, partial_sums(): pl.pallas_call(mix_kernel, grid_spec=pltpu.PrefetchScalarGridSpec(num_sca...  4.56 us
    pallas_call x2, Pallas kernels, updated(): pl.pallas_call(update_kernel, grid=(rows // block,), in_specs=[pl.BlockSp...  4.03 us
    ppermute x6, waiting for transfers between devices, routed(): return lax.ppermute(block, INST, [(s, dest(s)) for s in range(NT)])  3.6 us
    gather x2, local copies, waits for them, and re-layouts, shards(): picked = lam_h[:, cols]  3.4 us
  transfers between devices with their start and end apart: 12, of which 3 were waited for; matrix products, arithmetic and copies ran while one was open for 24% of the time, Pallas kernels for 0%

profile of v21, /device:TPU:1, one launch (start us, length us, event | category | flops | bytes accessed | tf_op | source)
XLA Modules:
  0.0 91.1 jit_solution(17050081145103577576)
XLA Ops:
  0.8 1.9 %multiply_convert_fusion = (bf16[1,16,32,128]{3,2,1,0:T(8,128)(2,1)S(1)}, f32[1,16,32,128]{3,2,1,0:T(8,128)}) fusion(f32[1,16,32,128]{3,2,1,0:T(8,128)} %param.11, f32[16]{0:T(128)S(1)} %or_convert_fusion, f32[16,128]{1,0:T(8,128)} %cond_ref.3), kind=kLoop, calls=%fused_computation.10 | loop fusion | flops 196608 | bytes 663616 | tf_op jit(solution)/shard_map/convert_element_type | solution.py:154
  2.7 4.0 %collective-permute-start.1 = (f32[512,128]{1,0:T(8,128)}, f32[512,128]{1,0:T(8,128)}, u32[]{:S(2)}, u32[]{:S(2)}) collective-permute-start(f32[512,128]{1,0:T(8,128)} %bitcast.2.own_ref), channel_id=1, source_target_pairs={{0,256},{32,288},{64,320},{96,352},{128,384},{160,416},{192,448},{... | collective-permute-start | bytes 786440 | tf_op jit(solution)/shard_map/ppermute | solution.py:49
  6.8 6.7 %collective-permute-start = (f32[512,128]{1,0:T(8,128)}, f32[512,128]{1,0:T(8,128)}, u32[]{:S(2)}, u32[]{:S(2)}) collective-permute-start(f32[512,128]{1,0:T(8,128)} %bitcast.2.own_ref), channel_id=1, source_target_pairs={{0,32},{32,0},{64,96},{96,64},{128,160},{160,128},{192,224},{224,1... | collective-permute-start | bytes 786440 | tf_op jit(solution)/shard_map/ppermute | solution.py:49
  14.8 1.0 %fusion.12 = f32[4,32,128]{2,1,0:T(8,128)S(1)} fusion(bf16[1,4,128,128]{3,2,1,0:T(8,128)(2,1)} %param.16, bf16[1,16,32,128]{3,2,1,0:T(8,128)(2,1)S(1)} %get-tuple-element.12), kind=kOutput, calls=%fused_computation.16 | convolution fusion | flops 4194304 | bytes 229376 | tf_op jit(solution)/shard_map/tjri,tjio->tjro/dot_general | solution.py:156
  15.8 1.2 %broadcast_subtract_fusion = f32[4]{0:T(128)} fusion(s32[1,4]{1,0:T(1,128)} %param.18), kind=kLoop, calls=%fused_computation.33 | loop fusion | flops 8 | bytes 32 | tf_op jit(solution)/shard_map/sub | solution.py:170
  17.1 2.9 %collective-permute-start.2 = (f32[512,128]{1,0:T(8,128)}, f32[512,128]{1,0:T(8,128)}, u32[]{:S(2)}, u32[]{:S(2)}) collective-permute-start(f32[512,128]{1,0:T(8,128)} %collective-permute-done.1.across_ref), channel_id=1, source_target_pairs={{0,32},{32,0},{64,96},{96,64},{128,160},{160,128},{192,224},{224,1... | collective-permute-start | bytes 786440 | tf_op jit(solution)/shard_map/ppermute | solution.py:49
  20.9 1.4 %broadcast_multiply_fusion.scale_ref = f32[16,128]{1,0:T(8,128)} fusion(f32[16]{0:T(128)S(1)} %or_convert_fusion, f32[1,16,128]{2,1,0:T(8,128)} %param.13), kind=kLoop, calls=%fused_computation.30 | loop fusion | flops 2048 | bytes 16448 | tf_op jit(solution)/shard_map/mul | solution.py:151
  22.3 2.3 %shard_map.109 = f32[4,512,128]{2,1,0:T(8,128)} custom-call(s32[1]{0:T(128)} %bitcast.index_ref, f32[16,16]{1,0:T(8,128)} %constant.32.clone.coef_ref, f32[512,128]{1,0:T(8,128)} %bitcast.2.own_ref, f32[512,128]{1,0:T(8,128)} %collective-permute-done.mate_ref, f32[512,128]{1,0:T(8,128)} %collective-permute-done.1.across_ref, ...), custom_call_target="tpu_custom_call" | custom-call | tf_op jit(solution)/shard_map/pallas_call | solution.py:91
  24.6 4.2 %all-to-all-start = ((f32[4,512,128]{2,1,0:T(8,128)}), f32[4,512,128]{2,1,0:T(8,128)}, u32[]{:S(2)}, u32[]{:S(2)}) async-start(f32[4,512,128]{2,1,0:T(8,128)} %shard_map.109), calls=%async_computation | async-start | bytes 2097152 | tf_op jit(solution)/shard_map/all_to_all | solution.py:136
  28.8 1.9 %collective-permute-start.3 = (bf16[1,5,32,128]{3,2,1,0:T(8,128)(2,1)}, bf16[1,5,32,128]{3,2,1,0:T(8,128)(2,1)S(1)}, u32[]{:S(2)}, u32[]{:S(2)}) collective-permute-start(bf16[1,5,32,128]{3,2,1,0:T(8,128)(2,1)} %pad_maximum_fusion), channel_id=1, source_target_pairs={{31,0},{0,1},{1,2},{2,3},{3,4},{4,5},{5,6},{6,7},{7,8},{8,9},{9,10... | collective-permute-start | bytes 122888 | tf_op jit(solution)/shard_map/ppermute | solution.py:32
  30.8 10.1 %collective-permute-start.4 = (bf16[1,1,32,128]{3,2,1,0:T(8,128)(2,1)S(1)}, bf16[1,1,32,128]{3,2,1,0:T(8,128)(2,1)S(1)}, u32[]{:S(2)}, u32[]{:S(2)}) collective-permute-start(bf16[1,1,32,128]{3,2,1,0:T(8,128)(2,1)S(1)} %slice.33), channel_id=1, source_target_pairs={{1,0},{2,1},{3,2},{4,3},{5,4},{6,5},{7,6},{8,7},{9,8},{10,9},{11,1... | collective-permute-start | bytes 24584 | tf_op jit(solution)/shard_map/ppermute | solution.py:32
  42.0 0.9 %maximum_bitcast_fusion = bf16[18,32,128]{2,1,0:T(8,128)(2,1)S(1)} fusion(bf16[1,1,32,128]{3,2,1,0:T(8,128)(2,1)S(1)} %collective-permute-done.4, bf16[1,16,32,128]{3,2,1,0:T(8,128)(2,1)} %copy-done.3, bf16[1,1,32,128]{3,2,1,0:T(8,128)(2,1)S(1)} %slice.46), kind=kLoop, calls=%fused_computation.12 | loop fusion | flops 147456 | bytes 294912 | tf_op jit(solution)/shard_map/concatenate | solution.py:166
  43.0 1.7 %gather_fusion = bf16[96,32,128]{2,1,0:T(8,128)(2,1)} fusion(bf16[18,32,128]{2,1,0:T(8,128)(2,1)S(1)} %maximum_bitcast_fusion, s32[1024]{0:T(1024)} %pad_clamp_fusion), kind=kCustom, calls=%fused_computation | custom fusion | bytes 1573248 | tf_op jit(solution)/shard_map/gather | solution.py:167
  44.7 0.9 %bitcast_add_fusion.1 = f32[1,4,32,128]{3,2,1,0:T(8,128)S(1)} fusion(f32[4,32,128]{2,1,0:T(8,128)} %copy-done.4, bf16[1,5,32,128]{3,2,1,0:T(8,128)(2,1)} %copy-done.8, f32[4]{0:T(128)} %broadcast_subtract_fusion), kind=kLoop, calls=%fused_computation.19 | loop fusion | flops 49152 | bytes 163856 | tf_op jit(solution)/shard_map/add | solution.py:170
  45.6 2.6 %multiply_add_fusion.1 = f32[1,16,32,128]{3,2,1,0:T(8,128)} fusion(f32[1,16,32,128]{3,2,1,0:T(8,128)S(1)} %copy-done.1, f32[1,4,32,128]{3,2,1,0:T(8,128)S(1)} %bitcast_add_fusion.1, f32[1,16,32,128]{3,2,1,0:T(8,128)} %param.11, f32[16,128]{1,0:T(8,128)} %bitcast.68, f32[16]{0:T(128)} %copy-done.10, bf16[16,6,32,128]{3,2,1,0:T(8,128)(2,1)} %bitcast.63, ...), kind=kOutput, calls=%fused_computation.9 | convolution fusion | flops 101056512 | bytes 4792384 | tf_op jit(solution)/shard_map/tnkri,tnkio->tnro/dot_general | solution.py:168
  48.2 2.0 %shard_map.110 = (f32[512,128]{1,0:T(8,128)}, f32[512,128]{1,0:T(8,128)}) custom-call(f32[4,512,128]{2,1,0:T(8,128)} %all-to-all-done.got_ref, f32[512,128]{1,0:T(8,128)} %bitcast.67, f32[16,128]{1,0:T(8,128)} %broadcast_multiply_fusion.scale_ref, f32[16,128]{1,0:T(8,128)} %cond_ref.3), custom_call_target="tpu_custom_call" | custom-call | tf_op jit(solution)/shard_map/pallas_call | solution.py:121
  50.2 2.3 %collective-permute-start.6 = (f32[512,128]{1,0:T(8,128)}, f32[512,128]{1,0:T(8,128)S(1)}, u32[]{:S(2)}, u32[]{:S(2)}) collective-permute-start(f32[512,128]{1,0:T(8,128)} %get-tuple-element.13.own_ref), channel_id=1, source_target_pairs={{0,256},{32,288},{64,320},{96,352},{128,384},{160,416},{192,448},{... | collective-permute-start | bytes 786440 | tf_op jit(solution)/shard_map/ppermute | solution.py:49
  52.5 2.6 %collective-permute-start.5 = (f32[512,128]{1,0:T(8,128)}, f32[512,128]{1,0:T(8,128)S(1)}, u32[]{:S(2)}, u32[]{:S(2)}) collective-permute-start(f32[512,128]{1,0:T(8,128)} %get-tuple-element.13.own_ref), channel_id=1, source_target_pairs={{0,32},{32,0},{64,96},{96,64},{128,160},{160,128},{192,224},{224,1... | collective-permute-start | bytes 786440 | tf_op jit(solution)/shard_map/ppermute | solution.py:49
  55.2 1.0 %convert_element_type.52 = bf16[1,16,32,128]{3,2,1,0:T(8,128)(2,1)S(1)} convert(f32[1,16,32,128]{3,2,1,0:T(8,128)} %bitcast.65) | non-fusion elementwise | flops 65536 | bytes 393216 | tf_op jit(solution)/shard_map/convert_element_type | solution.py:154
  56.2 3.6 %collective-permute-done.6.across_ref = f32[512,128]{1,0:T(8,128)S(1)} collective-permute-done((f32[512,128]{1,0:T(8,128)}, f32[512,128]{1,0:T(8,128)S(1)}, u32[]{:S(2)}, u32[]{:S(2)}) %collective-permute-start.6) | collective-permute-done | bytes 262176 | tf_op jit(solution)/shard_map/ppermute | solution.py:49
  59.8 3.2 %collective-permute-start.7 = (f32[512,128]{1,0:T(8,128)S(1)}, f32[512,128]{1,0:T(8,128)}, u32[]{:S(2)}, u32[]{:S(2)}) collective-permute-start(f32[512,128]{1,0:T(8,128)S(1)} %collective-permute-done.6.across_ref), channel_id=1, source_target_pairs={{0,32},{32,0},{64,96},{96,64},{128,160},{160,128},{192,224},{224,1... | collective-permute-start | bytes 786440 | tf_op jit(solution)/shard_map/ppermute | solution.py:49
  63.0 1.1 %fusion.10 = f32[4,32,128]{2,1,0:T(8,128)S(1)} fusion(bf16[1,4,128,128]{3,2,1,0:T(8,128)(2,1)} %param.16, bf16[1,16,32,128]{3,2,1,0:T(8,128)(2,1)S(1)} %convert_element_type.52), kind=kOutput, calls=%fused_computation.14 | convolution fusion | flops 4194304 | bytes 229376 | tf_op jit(solution)/shard_map/tjri,tjio->tjro/dot_general | solution.py:156
  66.0 2.3 %shard_map.111 = f32[4,512,128]{2,1,0:T(8,128)} custom-call(s32[1]{0:T(128)} %bitcast.index_ref, f32[16,16]{1,0:T(8,128)} %constant.32.clone.coef_ref, f32[512,128]{1,0:T(8,128)} %get-tuple-element.13.own_ref, f32[512,128]{1,0:T(8,128)} %copy-done.7, f32[512,128]{1,0:T(8,128)} %copy-done.6, f32[512,128]{1,0:T(8,128)} %collective-permute-done.7.diagonal_ref), custom_call_target="tpu_custom_call" | custom-call | tf_op jit(solution)/shard_map/pallas_call | solution.py:91
  68.3 4.2 %all-to-all-start.1 = ((f32[4,512,128]{2,1,0:T(8,128)}), f32[4,512,128]{2,1,0:T(8,128)}, u32[]{:S(2)}, u32[]{:S(2)}) async-start(f32[4,512,128]{2,1,0:T(8,128)} %shard_map.111), calls=%async_computation.1 | async-start | bytes 2097152 | tf_op jit(solution)/shard_map/all_to_all | solution.py:136
  72.5 0.8 pad_maximum_fusion.1
  73.3 1.9 %collective-permute-start.8 = (bf16[1,5,32,128]{3,2,1,0:T(8,128)(2,1)S(1)}, bf16[1,5,32,128]{3,2,1,0:T(8,128)(2,1)S(1)}, u32[]{:S(2)}, u32[]{:S(2)}) collective-permute-start(bf16[1,5,32,128]{3,2,1,0:T(8,128)(2,1)S(1)} %pad_maximum_fusion.1), channel_id=1, source_target_pairs={{31,0},{0,1},{1,2},{2,3},{3,4},{4,5},{5,6},{6,7},{7,8},{8,9},{9,10... | collective-permute-start | bytes 122888 | tf_op jit(solution)/shard_map/ppermute | solution.py:32
  75.2 7.0 %collective-permute-start.9 = (bf16[1,1,32,128]{3,2,1,0:T(8,128)(2,1)S(1)}, bf16[1,1,32,128]{3,2,1,0:T(8,128)(2,1)S(1)}, u32[]{:S(2)}, u32[]{:S(2)}) collective-permute-start(bf16[1,1,32,128]{3,2,1,0:T(8,128)(2,1)S(1)} %slice.38), channel_id=1, source_target_pairs={{1,0},{2,1},{3,2},{4,3},{5,4},{6,5},{7,6},{8,7},{9,8},{10,9},{11,1... | collective-permute-start | bytes 24584 | tf_op jit(solution)/shard_map/ppermute | solution.py:32
  83.0 0.9 %maximum_bitcast_fusion.1 = bf16[18,32,128]{2,1,0:T(8,128)(2,1)S(1)} fusion(bf16[1,1,32,128]{3,2,1,0:T(8,128)(2,1)S(1)} %collective-permute-done.9, bf16[1,16,32,128]{3,2,1,0:T(8,128)(2,1)} %copy-done.2, bf16[1,1,32,128]{3,2,1,0:T(8,128)(2,1)S(1)} %slice.50), kind=kLoop, calls=%fused_computation.13 | loop fusion | flops 147456 | bytes 294912 | tf_op jit(solution)/shard_map/concatenate | solution.py:166
  83.9 1.7 %gather_fusion.1 = bf16[96,32,128]{2,1,0:T(8,128)(2,1)} fusion(bf16[18,32,128]{2,1,0:T(8,128)(2,1)S(1)} %maximum_bitcast_fusion.1, s32[1024]{0:T(1024)} %pad_clamp_fusion), kind=kCustom, calls=%fused_computation.1 | custom fusion | bytes 1573248 | tf_op jit(solution)/shard_map/gather | solution.py:167
  85.6 0.9 %bitcast_add_fusion = f32[1,4,32,128]{3,2,1,0:T(8,128)S(1)} fusion(f32[4,32,128]{2,1,0:T(8,128)} %copy-done.5, bf16[1,5,32,128]{3,2,1,0:T(8,128)(2,1)} %copy-done.9, f32[4]{0:T(128)} %broadcast_subtract_fusion), kind=kLoop, calls=%fused_computation.18 | loop fusion | flops 49152 | bytes 163856 | tf_op jit(solution)/shard_map/add | solution.py:170
  86.6 2.6 %multiply_add_fusion = f32[1,16,32,128]{3,2,1,0:T(8,128)} fusion(f32[1,16,32,128]{3,2,1,0:T(8,128)} %bitcast.66, f32[1,16,32,128]{3,2,1,0:T(8,128)S(1)} %copy-done.1, f32[1,4,32,128]{3,2,1,0:T(8,128)S(1)} %bitcast_add_fusion, f32[16,128]{1,0:T(8,128)} %bitcast.69, f32[16]{0:T(128)} %copy-done.10, bf16[16,6,32,128]{3,2,1,0:T(8,128)(2,1)} %bitcast.62, ...), kind=kOutput, calls=%fused_computation.8 | convolution fusion | flops 100990976 | bytes 4792384 | tf_op jit(solution)/shard_map/tnkri,tnkio->tnro/dot_general | solution.py:168
  89.1 2.0 %shard_map.112 = f32[512,128]{1,0:T(8,128)} custom-call(f32[4,512,128]{2,1,0:T(8,128)} %all-to-all-done.1.got_ref, f32[512,128]{1,0:T(8,128)} %bitcast.64, f32[16,128]{1,0:T(8,128)} %broadcast_multiply_fusion.scale_ref, f32[16,128]{1,0:T(8,128)} %cond_ref.3), custom_call_target="tpu_custom_call" | custom-call | tf_op jit(solution)/shard_map/pallas_call | solution.py:121
  (52 shorter events, 6.2 us)
Async XLA Ops:
  0.0 45.6 %copy-start = (bf16[1,16,6,128,128]{4,3,2,1,0:T(8,128)(2,1)S(1)}, bf16[1,16,6,128,128]{4,3,2,1,0:T(8,128)(2,1)}, u32[]{:S(2)}) copy-start(bf16[1,16,6,128,128]{4,3,2,1,0:T(8,128)(2,1)} %param.15) | copy-start | bytes 9437188
  0.8 40.6 %copy-start.10 = (f32[16]{0:T(128)}, f32[16]{0:T(128)S(1)}, u32[]{:S(2)}) copy-start(f32[16]{0:T(128)S(1)} %or_convert_fusion) | copy-start | bytes 196
  2.7 38.7 %copy-start.3 = (bf16[1,16,32,128]{3,2,1,0:T(8,128)(2,1)}, bf16[1,16,32,128]{3,2,1,0:T(8,128)(2,1)S(1)}, u32[]{:S(2)}) copy-start(bf16[1,16,32,128]{3,2,1,0:T(8,128)(2,1)S(1)} %get-tuple-element.12) | copy-start | bytes 393220
  2.7 14.4 %collective-permute-start.1 = (f32[512,128]{1,0:T(8,128)}, f32[512,128]{1,0:T(8,128)}, u32[]{:S(2)}, u32[]{:S(2)}) collective-permute-start(f32[512,128]{1,0:T(8,128)} %bitcast.2.own_ref), channel_id=1, source_target_pairs={{0,256},{32,288},{64,320},{96,352},{128,384},{160,416},{192,448},{... | collective-permute-start | bytes 786440 | tf_op jit(solution)/shard_map/ppermute | solution.py:49
  6.8 15.5 %collective-permute-start = (f32[512,128]{1,0:T(8,128)}, f32[512,128]{1,0:T(8,128)}, u32[]{:S(2)}, u32[]{:S(2)}) collective-permute-start(f32[512,128]{1,0:T(8,128)} %bitcast.2.own_ref), channel_id=1, source_target_pairs={{0,32},{32,0},{64,96},{96,64},{128,160},{160,128},{192,224},{224,1... | collective-permute-start | bytes 786440 | tf_op jit(solution)/shard_map/ppermute | solution.py:49
  14.1 6.6 %copy-start.11 = (f32[4]{0:T(128)}, f32[4]{0:T(128)S(1)}, u32[]{:S(2)}) copy-start(f32[4]{0:T(128)S(1)} %convert_bitcast_fusion) | copy-start | bytes 52
  15.8 1.2 %copy-start.4 = (f32[4,32,128]{2,1,0:T(8,128)}, f32[4,32,128]{2,1,0:T(8,128)S(1)}, u32[]{:S(2)}) copy-start(f32[4,32,128]{2,1,0:T(8,128)S(1)} %fusion.12) | copy-start | bytes 196612
  17.1 5.1 %collective-permute-start.2 = (f32[512,128]{1,0:T(8,128)}, f32[512,128]{1,0:T(8,128)}, u32[]{:S(2)}, u32[]{:S(2)}) collective-permute-start(f32[512,128]{1,0:T(8,128)} %collective-permute-done.1.across_ref), channel_id=1, source_target_pairs={{0,32},{32,0},{64,96},{96,64},{128,160},{160,128},{192,224},{224,1... | collective-permute-start | bytes 786440 | tf_op jit(solution)/shard_map/ppermute | solution.py:49
  22.3 23.4 %copy-start.1 = (f32[1,16,32,128]{3,2,1,0:T(8,128)S(1)}, f32[1,16,32,128]{3,2,1,0:T(8,128)}, u32[]{:S(2)}) copy-start(f32[1,16,32,128]{3,2,1,0:T(8,128)} %param.12) | copy-start | bytes 786436
  24.6 23.6 %all-to-all-start = ((f32[4,512,128]{2,1,0:T(8,128)}), f32[4,512,128]{2,1,0:T(8,128)}, u32[]{:S(2)}, u32[]{:S(2)}) async-start(f32[4,512,128]{2,1,0:T(8,128)} %shard_map.109), calls=%async_computation | async-start | bytes 2097152 | tf_op jit(solution)/shard_map/all_to_all | solution.py:136
  28.8 12.6 %collective-permute-start.3 = (bf16[1,5,32,128]{3,2,1,0:T(8,128)(2,1)}, bf16[1,5,32,128]{3,2,1,0:T(8,128)(2,1)S(1)}, u32[]{:S(2)}, u32[]{:S(2)}) collective-permute-start(bf16[1,5,32,128]{3,2,1,0:T(8,128)(2,1)} %pad_maximum_fusion), channel_id=1, source_target_pairs={{31,0},{0,1},{1,2},{2,3},{3,4},{4,5},{5,6},{6,7},{7,8},{8,9},{9,10... | collective-permute-start | bytes 122888 | tf_op jit(solution)/shard_map/ppermute | solution.py:32
  30.8 10.8 %collective-permute-start.4 = (bf16[1,1,32,128]{3,2,1,0:T(8,128)(2,1)S(1)}, bf16[1,1,32,128]{3,2,1,0:T(8,128)(2,1)S(1)}, u32[]{:S(2)}, u32[]{:S(2)}) collective-permute-start(bf16[1,1,32,128]{3,2,1,0:T(8,128)(2,1)S(1)} %slice.33), channel_id=1, source_target_pairs={{1,0},{2,1},{3,2},{4,3},{5,4},{6,5},{7,6},{8,7},{9,8},{10,9},{11,1... | collective-permute-start | bytes 24584 | tf_op jit(solution)/shard_map/ppermute | solution.py:32
  41.4 0.6 copy-start.8
  45.6 19.0 %copy-start.12 = (f32[4]{0:T(128)S(1)}, f32[4]{0:T(128)}, u32[]{:S(2)}) copy-start(f32[4]{0:T(128)} %copy-done.11) | copy-start | bytes 52
  50.2 9.5 %collective-permute-start.6 = (f32[512,128]{1,0:T(8,128)}, f32[512,128]{1,0:T(8,128)S(1)}, u32[]{:S(2)}, u32[]{:S(2)}) collective-permute-start(f32[512,128]{1,0:T(8,128)} %get-tuple-element.13.own_ref), channel_id=1, source_target_pairs={{0,256},{32,288},{64,320},{96,352},{128,384},{160,416},{192,448},{... | collective-permute-start | bytes 786440 | tf_op jit(solution)/shard_map/ppermute | solution.py:49
  52.5 12.8 %collective-permute-start.5 = (f32[512,128]{1,0:T(8,128)}, f32[512,128]{1,0:T(8,128)S(1)}, u32[]{:S(2)}, u32[]{:S(2)}) collective-permute-start(f32[512,128]{1,0:T(8,128)} %get-tuple-element.13.own_ref), channel_id=1, source_target_pairs={{0,32},{32,0},{64,96},{96,64},{128,160},{160,128},{192,224},{224,1... | collective-permute-start | bytes 786440 | tf_op jit(solution)/shard_map/ppermute | solution.py:49
  56.2 26.1 %copy-start.2 = (bf16[1,16,32,128]{3,2,1,0:T(8,128)(2,1)}, bf16[1,16,32,128]{3,2,1,0:T(8,128)(2,1)S(1)}, u32[]{:S(2)}) copy-start(bf16[1,16,32,128]{3,2,1,0:T(8,128)(2,1)S(1)} %convert_element_type.52) | copy-start | bytes 393220
  59.8 5.6 %copy-start.6 = (f32[512,128]{1,0:T(8,128)}, f32[512,128]{1,0:T(8,128)S(1)}, u32[]{:S(2)}) copy-start(f32[512,128]{1,0:T(8,128)S(1)} %collective-permute-done.6.across_ref) | copy-start | bytes 786436
  59.8 6.3 %collective-permute-start.7 = (f32[512,128]{1,0:T(8,128)S(1)}, f32[512,128]{1,0:T(8,128)}, u32[]{:S(2)}, u32[]{:S(2)}) collective-permute-start(f32[512,128]{1,0:T(8,128)S(1)} %collective-permute-done.6.across_ref), channel_id=1, source_target_pairs={{0,32},{32,0},{64,96},{96,64},{128,160},{160,128},{192,224},{224,1... | collective-permute-start | bytes 786440 | tf_op jit(solution)/shard_map/ppermute | solution.py:49
  64.0 0.6 copy-start.5
  65.3 0.7 copy-start.7
  68.3 20.8 %all-to-all-start.1 = ((f32[4,512,128]{2,1,0:T(8,128)}), f32[4,512,128]{2,1,0:T(8,128)}, u32[]{:S(2)}, u32[]{:S(2)}) async-start(f32[4,512,128]{2,1,0:T(8,128)} %shard_map.111), calls=%async_computation.1 | async-start | bytes 2097152 | tf_op jit(solution)/shard_map/all_to_all | solution.py:136
  73.3 8.9 %collective-permute-start.8 = (bf16[1,5,32,128]{3,2,1,0:T(8,128)(2,1)S(1)}, bf16[1,5,32,128]{3,2,1,0:T(8,128)(2,1)S(1)}, u32[]{:S(2)}, u32[]{:S(2)}) collective-permute-start(bf16[1,5,32,128]{3,2,1,0:T(8,128)(2,1)S(1)} %pad_maximum_fusion.1), channel_id=1, source_target_pairs={{31,0},{0,1},{1,2},{2,3},{3,4},{4,5},{5,6},{6,7},{7,8},{8,9},{9,10... | collective-permute-start | bytes 122888 | tf_op jit(solution)/shard_map/ppermute | solution.py:32
  75.2 7.8 %collective-permute-start.9 = (bf16[1,1,32,128]{3,2,1,0:T(8,128)(2,1)S(1)}, bf16[1,1,32,128]{3,2,1,0:T(8,128)(2,1)S(1)}, u32[]{:S(2)}, u32[]{:S(2)}) collective-permute-start(bf16[1,1,32,128]{3,2,1,0:T(8,128)(2,1)S(1)} %slice.38), channel_id=1, source_target_pairs={{1,0},{2,1},{3,2},{4,3},{5,4},{6,5},{7,6},{8,7},{9,8},{10,9},{11,1... | collective-permute-start | bytes 24584 | tf_op jit(solution)/shard_map/ppermute | solution.py:32
  82.2 0.8 copy-start.9

commit v22 on v21

--- a/solution.py
+++ b/solution.py
@@ -69,7 +69,7 @@
 def mix_kernel(index_ref, coef_ref, own_ref, mate_ref, across_ref, diagonal_ref, o_ref):
     me = index_ref[0]
     coef = [[coef_ref[me, slot * 4 + m] for m in range(4)] for slot in range(4)]
-    chunk = 64
+    chunk = 16
 
     def step(c, carry):
         rows = pl.ds(pl.multiple_of(c * chunk, chunk), chunk)

time: 92.5 us -> 92.5 us (level)
  no operation moved by 1% of the time
where the time goes in v22:
time: 92.5 us; the launch traced here: 91.1 us
  starting transfers between devices  51.1 us (55%)
  other arithmetic  13.2 us (14%)
  Pallas kernels  8.6 us (9%)
  matrix products  7.23 us (8%)
  local copies, waits for them, and re-layouts  5.39 us (6%)
  waiting for transfers between devices  4.49 us (5%)
  between operations  1.06 us (1%)
    ppermute x6, starting transfers between devices, routed(): return lax.ppermute(block, INST, [(s, dest(s)) for s in range(NT)])  21.8 us
    ppermute x4, starting transfers between devices, shifted(): return lax.ppermute(block, axis, route)  20.9 us
    all_to_all x2, starting transfers between devices, instance_mix(): return (partials, lax.all_to_all(partials, 'ix', 0, 0))  8.49 us
    dot_general x2, matrix products, shards(): jnp.einsum('tnkri,tnkio->tnro', picked, jac, preferred_element_type=jnp.f...  5.13 us
    pallas_call x2, Pallas kernels, partial_sums(): pl.pallas_call(mix_kernel, grid_spec=pltpu.PrefetchScalarGridSpec(num_sca...  4.56 us
    pallas_call x2, Pallas kernels, updated(): pl.pallas_call(update_kernel, grid=(rows // block,), in_specs=[pl.BlockSp...  4.03 us
    ppermute x6, waiting for transfers between devices, routed(): return lax.ppermute(block, INST, [(s, dest(s)) for s in range(NT)])  3.6 us
    gather x2, local copies, waits for them, and re-layouts, shards(): picked = lam_h[:, cols]  3.4 us
  transfers between devices with their start and end apart: 12, of which 3 were waited for; matrix products, arithmetic and copies ran while one was open for 24% of the time, Pallas kernels for 0%

profile of v22, /device:TPU:1, one launch (start us, length us, event | category | flops | bytes accessed | tf_op | source)
XLA Modules:
  0.0 91.1 jit_solution(7944982320210578177)
XLA Ops:
  0.8 1.9 %multiply_convert_fusion = (bf16[1,16,32,128]{3,2,1,0:T(8,128)(2,1)S(1)}, f32[1,16,32,128]{3,2,1,0:T(8,128)}) fusion(f32[1,16,32,128]{3,2,1,0:T(8,128)} %param.11, f32[16]{0:T(128)S(1)} %or_convert_fusion, f32[16,128]{1,0:T(8,128)} %cond_ref.3), kind=kLoop, calls=%fused_computation.10 | loop fusion | flops 196608 | bytes 663616 | tf_op jit(solution)/shard_map/convert_element_type | solution.py:154
  2.7 4.0 %collective-permute-start.1 = (f32[512,128]{1,0:T(8,128)}, f32[512,128]{1,0:T(8,128)}, u32[]{:S(2)}, u32[]{:S(2)}) collective-permute-start(f32[512,128]{1,0:T(8,128)} %bitcast.2.own_ref), channel_id=1, source_target_pairs={{0,256},{32,288},{64,320},{96,352},{128,384},{160,416},{192,448},{... | collective-permute-start | bytes 786440 | tf_op jit(solution)/shard_map/ppermute | solution.py:49
  6.8 6.7 %collective-permute-start = (f32[512,128]{1,0:T(8,128)}, f32[512,128]{1,0:T(8,128)}, u32[]{:S(2)}, u32[]{:S(2)}) collective-permute-start(f32[512,128]{1,0:T(8,128)} %bitcast.2.own_ref), channel_id=1, source_target_pairs={{0,32},{32,0},{64,96},{96,64},{128,160},{160,128},{192,224},{224,1... | collective-permute-start | bytes 786440 | tf_op jit(solution)/shard_map/ppermute | solution.py:49
  14.8 1.0 %fusion.12 = f32[4,32,128]{2,1,0:T(8,128)S(1)} fusion(bf16[1,4,128,128]{3,2,1,0:T(8,128)(2,1)} %param.16, bf16[1,16,32,128]{3,2,1,0:T(8,128)(2,1)S(1)} %get-tuple-element.12), kind=kOutput, calls=%fused_computation.16 | convolution fusion | flops 4194304 | bytes 229376 | tf_op jit(solution)/shard_map/tjri,tjio->tjro/dot_general | solution.py:156
  15.8 1.2 %broadcast_subtract_fusion = f32[4]{0:T(128)} fusion(s32[1,4]{1,0:T(1,128)} %param.18), kind=kLoop, calls=%fused_computation.33 | loop fusion | flops 8 | bytes 32 | tf_op jit(solution)/shard_map/sub | solution.py:170
  17.1 2.9 %collective-permute-start.2 = (f32[512,128]{1,0:T(8,128)}, f32[512,128]{1,0:T(8,128)}, u32[]{:S(2)}, u32[]{:S(2)}) collective-permute-start(f32[512,128]{1,0:T(8,128)} %collective-permute-done.1.across_ref), channel_id=1, source_target_pairs={{0,32},{32,0},{64,96},{96,64},{128,160},{160,128},{192,224},{224,1... | collective-permute-start | bytes 786440 | tf_op jit(solution)/shard_map/ppermute | solution.py:49
  20.9 1.4 %broadcast_multiply_fusion.scale_ref = f32[16,128]{1,0:T(8,128)} fusion(f32[16]{0:T(128)S(1)} %or_convert_fusion, f32[1,16,128]{2,1,0:T(8,128)} %param.13), kind=kLoop, calls=%fused_computation.30 | loop fusion | flops 2048 | bytes 16448 | tf_op jit(solution)/shard_map/mul | solution.py:151
  22.3 2.3 %shard_map.109 = f32[4,512,128]{2,1,0:T(8,128)} custom-call(s32[1]{0:T(128)} %bitcast.index_ref, f32[16,16]{1,0:T(8,128)} %constant.32.clone.coef_ref, f32[512,128]{1,0:T(8,128)} %bitcast.2.own_ref, f32[512,128]{1,0:T(8,128)} %collective-permute-done.mate_ref, f32[512,128]{1,0:T(8,128)} %collective-permute-done.1.across_ref, ...), custom_call_target="tpu_custom_call" | custom-call | tf_op jit(solution)/shard_map/pallas_call | solution.py:91
  24.6 4.2 %all-to-all-start = ((f32[4,512,128]{2,1,0:T(8,128)}), f32[4,512,128]{2,1,0:T(8,128)}, u32[]{:S(2)}, u32[]{:S(2)}) async-start(f32[4,512,128]{2,1,0:T(8,128)} %shard_map.109), calls=%async_computation | async-start | bytes 2097152 | tf_op jit(solution)/shard_map/all_to_all | solution.py:136
  28.8 1.9 %collective-permute-start.3 = (bf16[1,5,32,128]{3,2,1,0:T(8,128)(2,1)}, bf16[1,5,32,128]{3,2,1,0:T(8,128)(2,1)S(1)}, u32[]{:S(2)}, u32[]{:S(2)}) collective-permute-start(bf16[1,5,32,128]{3,2,1,0:T(8,128)(2,1)} %pad_maximum_fusion), channel_id=1, source_target_pairs={{31,0},{0,1},{1,2},{2,3},{3,4},{4,5},{5,6},{6,7},{7,8},{8,9},{9,10... | collective-permute-start | bytes 122888 | tf_op jit(solution)/shard_map/ppermute | solution.py:32
  30.8 10.1 %collective-permute-start.4 = (bf16[1,1,32,128]{3,2,1,0:T(8,128)(2,1)S(1)}, bf16[1,1,32,128]{3,2,1,0:T(8,128)(2,1)S(1)}, u32[]{:S(2)}, u32[]{:S(2)}) collective-permute-start(bf16[1,1,32,128]{3,2,1,0:T(8,128)(2,1)S(1)} %slice.33), channel_id=1, source_target_pairs={{1,0},{2,1},{3,2},{4,3},{5,4},{6,5},{7,6},{8,7},{9,8},{10,9},{11,1... | collective-permute-start | bytes 24584 | tf_op jit(solution)/shard_map/ppermute | solution.py:32
  42.0 0.9 %maximum_bitcast_fusion = bf16[18,32,128]{2,1,0:T(8,128)(2,1)S(1)} fusion(bf16[1,1,32,128]{3,2,1,0:T(8,128)(2,1)S(1)} %collective-permute-done.4, bf16[1,16,32,128]{3,2,1,0:T(8,128)(2,1)} %copy-done.3, bf16[1,1,32,128]{3,2,1,0:T(8,128)(2,1)S(1)} %slice.46), kind=kLoop, calls=%fused_computation.12 | loop fusion | flops 147456 | bytes 294912 | tf_op jit(solution)/shard_map/concatenate | solution.py:166
  43.0 1.7 %gather_fusion = bf16[96,32,128]{2,1,0:T(8,128)(2,1)} fusion(bf16[18,32,128]{2,1,0:T(8,128)(2,1)S(1)} %maximum_bitcast_fusion, s32[1024]{0:T(1024)} %pad_clamp_fusion), kind=kCustom, calls=%fused_computation | custom fusion | bytes 1573248 | tf_op jit(solution)/shard_map/gather | solution.py:167
  44.7 0.9 %bitcast_add_fusion.1 = f32[1,4,32,128]{3,2,1,0:T(8,128)S(1)} fusion(f32[4,32,128]{2,1,0:T(8,128)} %copy-done.4, bf16[1,5,32,128]{3,2,1,0:T(8,128)(2,1)} %copy-done.8, f32[4]{0:T(128)} %broadcast_subtract_fusion), kind=kLoop, calls=%fused_computation.19 | loop fusion | flops 49152 | bytes 163856 | tf_op jit(solution)/shard_map/add | solution.py:170
  45.6 2.6 %multiply_add_fusion.1 = f32[1,16,32,128]{3,2,1,0:T(8,128)} fusion(f32[1,16,32,128]{3,2,1,0:T(8,128)S(1)} %copy-done.1, f32[1,4,32,128]{3,2,1,0:T(8,128)S(1)} %bitcast_add_fusion.1, f32[1,16,32,128]{3,2,1,0:T(8,128)} %param.11, f32[16,128]{1,0:T(8,128)} %bitcast.68, f32[16]{0:T(128)} %copy-done.10, bf16[16,6,32,128]{3,2,1,0:T(8,128)(2,1)} %bitcast.63, ...), kind=kOutput, calls=%fused_computation.9 | convolution fusion | flops 101056512 | bytes 4792384 | tf_op jit(solution)/shard_map/tnkri,tnkio->tnro/dot_general | solution.py:168
  48.2 2.0 %shard_map.110 = (f32[512,128]{1,0:T(8,128)}, f32[512,128]{1,0:T(8,128)}) custom-call(f32[4,512,128]{2,1,0:T(8,128)} %all-to-all-done.got_ref, f32[512,128]{1,0:T(8,128)} %bitcast.67, f32[16,128]{1,0:T(8,128)} %broadcast_multiply_fusion.scale_ref, f32[16,128]{1,0:T(8,128)} %cond_ref.3), custom_call_target="tpu_custom_call" | custom-call | tf_op jit(solution)/shard_map/pallas_call | solution.py:121
  50.2 2.3 %collective-permute-start.6 = (f32[512,128]{1,0:T(8,128)}, f32[512,128]{1,0:T(8,128)S(1)}, u32[]{:S(2)}, u32[]{:S(2)}) collective-permute-start(f32[512,128]{1,0:T(8,128)} %get-tuple-element.13.own_ref), channel_id=1, source_target_pairs={{0,256},{32,288},{64,320},{96,352},{128,384},{160,416},{192,448},{... | collective-permute-start | bytes 786440 | tf_op jit(solution)/shard_map/ppermute | solution.py:49
  52.5 2.6 %collective-permute-start.5 = (f32[512,128]{1,0:T(8,128)}, f32[512,128]{1,0:T(8,128)S(1)}, u32[]{:S(2)}, u32[]{:S(2)}) collective-permute-start(f32[512,128]{1,0:T(8,128)} %get-tuple-element.13.own_ref), channel_id=1, source_target_pairs={{0,32},{32,0},{64,96},{96,64},{128,160},{160,128},{192,224},{224,1... | collective-permute-start | bytes 786440 | tf_op jit(solution)/shard_map/ppermute | solution.py:49
  55.2 1.0 %convert_element_type.52 = bf16[1,16,32,128]{3,2,1,0:T(8,128)(2,1)S(1)} convert(f32[1,16,32,128]{3,2,1,0:T(8,128)} %bitcast.65) | non-fusion elementwise | flops 65536 | bytes 393216 | tf_op jit(solution)/shard_map/convert_element_type | solution.py:154
  56.2 3.6 %collective-permute-done.6.across_ref = f32[512,128]{1,0:T(8,128)S(1)} collective-permute-done((f32[512,128]{1,0:T(8,128)}, f32[512,128]{1,0:T(8,128)S(1)}, u32[]{:S(2)}, u32[]{:S(2)}) %collective-permute-start.6) | collective-permute-done | bytes 262176 | tf_op jit(solution)/shard_map/ppermute | solution.py:49
  59.8 3.2 %collective-permute-start.7 = (f32[512,128]{1,0:T(8,128)S(1)}, f32[512,128]{1,0:T(8,128)}, u32[]{:S(2)}, u32[]{:S(2)}) collective-permute-start(f32[512,128]{1,0:T(8,128)S(1)} %collective-permute-done.6.across_ref), channel_id=1, source_target_pairs={{0,32},{32,0},{64,96},{96,64},{128,160},{160,128},{192,224},{224,1... | collective-permute-start | bytes 786440 | tf_op jit(solution)/shard_map/ppermute | solution.py:49
  63.0 1.1 %fusion.10 = f32[4,32,128]{2,1,0:T(8,128)S(1)} fusion(bf16[1,4,128,128]{3,2,1,0:T(8,128)(2,1)} %param.16, bf16[1,16,32,128]{3,2,1,0:T(8,128)(2,1)S(1)} %convert_element_type.52), kind=kOutput, calls=%fused_computation.14 | convolution fusion | flops 4194304 | bytes 229376 | tf_op jit(solution)/shard_map/tjri,tjio->tjro/dot_general | solution.py:156
  66.0 2.3 %shard_map.111 = f32[4,512,128]{2,1,0:T(8,128)} custom-call(s32[1]{0:T(128)} %bitcast.index_ref, f32[16,16]{1,0:T(8,128)} %constant.32.clone.coef_ref, f32[512,128]{1,0:T(8,128)} %get-tuple-element.13.own_ref, f32[512,128]{1,0:T(8,128)} %copy-done.7, f32[512,128]{1,0:T(8,128)} %copy-done.6, f32[512,128]{1,0:T(8,128)} %collective-permute-done.7.diagonal_ref), custom_call_target="tpu_custom_call" | custom-call | tf_op jit(solution)/shard_map/pallas_call | solution.py:91
  68.3 4.2 %all-to-all-start.1 = ((f32[4,512,128]{2,1,0:T(8,128)}), f32[4,512,128]{2,1,0:T(8,128)}, u32[]{:S(2)}, u32[]{:S(2)}) async-start(f32[4,512,128]{2,1,0:T(8,128)} %shard_map.111), calls=%async_computation.1 | async-start | bytes 2097152 | tf_op jit(solution)/shard_map/all_to_all | solution.py:136
  72.6 0.8 pad_maximum_fusion.1
  73.3 1.9 %collective-permute-start.8 = (bf16[1,5,32,128]{3,2,1,0:T(8,128)(2,1)S(1)}, bf16[1,5,32,128]{3,2,1,0:T(8,128)(2,1)S(1)}, u32[]{:S(2)}, u32[]{:S(2)}) collective-permute-start(bf16[1,5,32,128]{3,2,1,0:T(8,128)(2,1)S(1)} %pad_maximum_fusion.1), channel_id=1, source_target_pairs={{31,0},{0,1},{1,2},{2,3},{3,4},{4,5},{5,6},{6,7},{7,8},{8,9},{9,10... | collective-permute-start | bytes 122888 | tf_op jit(solution)/shard_map/ppermute | solution.py:32
  75.2 7.0 %collective-permute-start.9 = (bf16[1,1,32,128]{3,2,1,0:T(8,128)(2,1)S(1)}, bf16[1,1,32,128]{3,2,1,0:T(8,128)(2,1)S(1)}, u32[]{:S(2)}, u32[]{:S(2)}) collective-permute-start(bf16[1,1,32,128]{3,2,1,0:T(8,128)(2,1)S(1)} %slice.38), channel_id=1, source_target_pairs={{1,0},{2,1},{3,2},{4,3},{5,4},{6,5},{7,6},{8,7},{9,8},{10,9},{11,1... | collective-permute-start | bytes 24584 | tf_op jit(solution)/shard_map/ppermute | solution.py:32
  83.0 0.9 %maximum_bitcast_fusion.1 = bf16[18,32,128]{2,1,0:T(8,128)(2,1)S(1)} fusion(bf16[1,1,32,128]{3,2,1,0:T(8,128)(2,1)S(1)} %collective-permute-done.9, bf16[1,16,32,128]{3,2,1,0:T(8,128)(2,1)} %copy-done.2, bf16[1,1,32,128]{3,2,1,0:T(8,128)(2,1)S(1)} %slice.50), kind=kLoop, calls=%fused_computation.13 | loop fusion | flops 147456 | bytes 294912 | tf_op jit(solution)/shard_map/concatenate | solution.py:166
  83.9 1.7 %gather_fusion.1 = bf16[96,32,128]{2,1,0:T(8,128)(2,1)} fusion(bf16[18,32,128]{2,1,0:T(8,128)(2,1)S(1)} %maximum_bitcast_fusion.1, s32[1024]{0:T(1024)} %pad_clamp_fusion), kind=kCustom, calls=%fused_computation.1 | custom fusion | bytes 1573248 | tf_op jit(solution)/shard_map/gather | solution.py:167
  85.6 0.9 %bitcast_add_fusion = f32[1,4,32,128]{3,2,1,0:T(8,128)S(1)} fusion(f32[4,32,128]{2,1,0:T(8,128)} %copy-done.5, bf16[1,5,32,128]{3,2,1,0:T(8,128)(2,1)} %copy-done.9, f32[4]{0:T(128)} %broadcast_subtract_fusion), kind=kLoop, calls=%fused_computation.18 | loop fusion | flops 49152 | bytes 163856 | tf_op jit(solution)/shard_map/add | solution.py:170
  86.6 2.6 %multiply_add_fusion = f32[1,16,32,128]{3,2,1,0:T(8,128)} fusion(f32[1,16,32,128]{3,2,1,0:T(8,128)} %bitcast.66, f32[1,16,32,128]{3,2,1,0:T(8,128)S(1)} %copy-done.1, f32[1,4,32,128]{3,2,1,0:T(8,128)S(1)} %bitcast_add_fusion, f32[16,128]{1,0:T(8,128)} %bitcast.69, f32[16]{0:T(128)} %copy-done.10, bf16[16,6,32,128]{3,2,1,0:T(8,128)(2,1)} %bitcast.62, ...), kind=kOutput, calls=%fused_computation.8 | convolution fusion | flops 100990976 | bytes 4792384 | tf_op jit(solution)/shard_map/tnkri,tnkio->tnro/dot_general | solution.py:168
  89.1 2.0 %shard_map.112 = f32[512,128]{1,0:T(8,128)} custom-call(f32[4,512,128]{2,1,0:T(8,128)} %all-to-all-done.1.got_ref, f32[512,128]{1,0:T(8,128)} %bitcast.64, f32[16,128]{1,0:T(8,128)} %broadcast_multiply_fusion.scale_ref, f32[16,128]{1,0:T(8,128)} %cond_ref.3), custom_call_target="tpu_custom_call" | custom-call | tf_op jit(solution)/shard_map/pallas_call | solution.py:121
  (52 shorter events, 6.2 us)
Async XLA Ops:
  0.0 45.6 %copy-start = (bf16[1,16,6,128,128]{4,3,2,1,0:T(8,128)(2,1)S(1)}, bf16[1,16,6,128,128]{4,3,2,1,0:T(8,128)(2,1)}, u32[]{:S(2)}) copy-start(bf16[1,16,6,128,128]{4,3,2,1,0:T(8,128)(2,1)} %param.15) | copy-start | bytes 9437188
  0.8 40.6 %copy-start.10 = (f32[16]{0:T(128)}, f32[16]{0:T(128)S(1)}, u32[]{:S(2)}) copy-start(f32[16]{0:T(128)S(1)} %or_convert_fusion) | copy-start | bytes 196
  2.7 38.7 %copy-start.3 = (bf16[1,16,32,128]{3,2,1,0:T(8,128)(2,1)}, bf16[1,16,32,128]{3,2,1,0:T(8,128)(2,1)S(1)}, u32[]{:S(2)}) copy-start(bf16[1,16,32,128]{3,2,1,0:T(8,128)(2,1)S(1)} %get-tuple-element.12) | copy-start | bytes 393220
  2.7 14.4 %collective-permute-start.1 = (f32[512,128]{1,0:T(8,128)}, f32[512,128]{1,0:T(8,128)}, u32[]{:S(2)}, u32[]{:S(2)}) collective-permute-start(f32[512,128]{1,0:T(8,128)} %bitcast.2.own_ref), channel_id=1, source_target_pairs={{0,256},{32,288},{64,320},{96,352},{128,384},{160,416},{192,448},{... | collective-permute-start | bytes 786440 | tf_op jit(solution)/shard_map/ppermute | solution.py:49
  6.8 15.5 %collective-permute-start = (f32[512,128]{1,0:T(8,128)}, f32[512,128]{1,0:T(8,128)}, u32[]{:S(2)}, u32[]{:S(2)}) collective-permute-start(f32[512,128]{1,0:T(8,128)} %bitcast.2.own_ref), channel_id=1, source_target_pairs={{0,32},{32,0},{64,96},{96,64},{128,160},{160,128},{192,224},{224,1... | collective-permute-start | bytes 786440 | tf_op jit(solution)/shard_map/ppermute | solution.py:49
  14.1 6.6 %copy-start.11 = (f32[4]{0:T(128)}, f32[4]{0:T(128)S(1)}, u32[]{:S(2)}) copy-start(f32[4]{0:T(128)S(1)} %convert_bitcast_fusion) | copy-start | bytes 52
  15.8 1.2 %copy-start.4 = (f32[4,32,128]{2,1,0:T(8,128)}, f32[4,32,128]{2,1,0:T(8,128)S(1)}, u32[]{:S(2)}) copy-start(f32[4,32,128]{2,1,0:T(8,128)S(1)} %fusion.12) | copy-start | bytes 196612
  17.1 5.1 %collective-permute-start.2 = (f32[512,128]{1,0:T(8,128)}, f32[512,128]{1,0:T(8,128)}, u32[]{:S(2)}, u32[]{:S(2)}) collective-permute-start(f32[512,128]{1,0:T(8,128)} %collective-permute-done.1.across_ref), channel_id=1, source_target_pairs={{0,32},{32,0},{64,96},{96,64},{128,160},{160,128},{192,224},{224,1... | collective-permute-start | bytes 786440 | tf_op jit(solution)/shard_map/ppermute | solution.py:49
  22.3 23.4 %copy-start.1 = (f32[1,16,32,128]{3,2,1,0:T(8,128)S(1)}, f32[1,16,32,128]{3,2,1,0:T(8,128)}, u32[]{:S(2)}) copy-start(f32[1,16,32,128]{3,2,1,0:T(8,128)} %param.12) | copy-start | bytes 786436
  24.6 23.6 %all-to-all-start = ((f32[4,512,128]{2,1,0:T(8,128)}), f32[4,512,128]{2,1,0:T(8,128)}, u32[]{:S(2)}, u32[]{:S(2)}) async-start(f32[4,512,128]{2,1,0:T(8,128)} %shard_map.109), calls=%async_computation | async-start | bytes 2097152 | tf_op jit(solution)/shard_map/all_to_all | solution.py:136
  28.8 12.6 %collective-permute-start.3 = (bf16[1,5,32,128]{3,2,1,0:T(8,128)(2,1)}, bf16[1,5,32,128]{3,2,1,0:T(8,128)(2,1)S(1)}, u32[]{:S(2)}, u32[]{:S(2)}) collective-permute-start(bf16[1,5,32,128]{3,2,1,0:T(8,128)(2,1)} %pad_maximum_fusion), channel_id=1, source_target_pairs={{31,0},{0,1},{1,2},{2,3},{3,4},{4,5},{5,6},{6,7},{7,8},{8,9},{9,10... | collective-permute-start | bytes 122888 | tf_op jit(solution)/shard_map/ppermute | solution.py:32
  30.8 10.8 %collective-permute-start.4 = (bf16[1,1,32,128]{3,2,1,0:T(8,128)(2,1)S(1)}, bf16[1,1,32,128]{3,2,1,0:T(8,128)(2,1)S(1)}, u32[]{:S(2)}, u32[]{:S(2)}) collective-permute-start(bf16[1,1,32,128]{3,2,1,0:T(8,128)(2,1)S(1)} %slice.33), channel_id=1, source_target_pairs={{1,0},{2,1},{3,2},{4,3},{5,4},{6,5},{7,6},{8,7},{9,8},{10,9},{11,1... | collective-permute-start | bytes 24584 | tf_op jit(solution)/shard_map/ppermute | solution.py:32
  41.4 0.6 copy-start.8
  45.6 19.0 %copy-start.12 = (f32[4]{0:T(128)S(1)}, f32[4]{0:T(128)}, u32[]{:S(2)}) copy-start(f32[4]{0:T(128)} %copy-done.11) | copy-start | bytes 52
  50.2 9.5 %collective-permute-start.6 = (f32[512,128]{1,0:T(8,128)}, f32[512,128]{1,0:T(8,128)S(1)}, u32[]{:S(2)}, u32[]{:S(2)}) collective-permute-start(f32[512,128]{1,0:T(8,128)} %get-tuple-element.13.own_ref), channel_id=1, source_target_pairs={{0,256},{32,288},{64,320},{96,352},{128,384},{160,416},{192,448},{... | collective-permute-start | bytes 786440 | tf_op jit(solution)/shard_map/ppermute | solution.py:49
  52.5 12.8 %collective-permute-start.5 = (f32[512,128]{1,0:T(8,128)}, f32[512,128]{1,0:T(8,128)S(1)}, u32[]{:S(2)}, u32[]{:S(2)}) collective-permute-start(f32[512,128]{1,0:T(8,128)} %get-tuple-element.13.own_ref), channel_id=1, source_target_pairs={{0,32},{32,0},{64,96},{96,64},{128,160},{160,128},{192,224},{224,1... | collective-permute-start | bytes 786440 | tf_op jit(solution)/shard_map/ppermute | solution.py:49
  56.2 26.1 %copy-start.2 = (bf16[1,16,32,128]{3,2,1,0:T(8,128)(2,1)}, bf16[1,16,32,128]{3,2,1,0:T(8,128)(2,1)S(1)}, u32[]{:S(2)}) copy-start(bf16[1,16,32,128]{3,2,1,0:T(8,128)(2,1)S(1)} %convert_element_type.52) | copy-start | bytes 393220
  59.8 5.6 %copy-start.6 = (f32[512,128]{1,0:T(8,128)}, f32[512,128]{1,0:T(8,128)S(1)}, u32[]{:S(2)}) copy-start(f32[512,128]{1,0:T(8,128)S(1)} %collective-permute-done.6.across_ref) | copy-start | bytes 786436
  59.8 6.3 %collective-permute-start.7 = (f32[512,128]{1,0:T(8,128)S(1)}, f32[512,128]{1,0:T(8,128)}, u32[]{:S(2)}, u32[]{:S(2)}) collective-permute-start(f32[512,128]{1,0:T(8,128)S(1)} %collective-permute-done.6.across_ref), channel_id=1, source_target_pairs={{0,32},{32,0},{64,96},{96,64},{128,160},{160,128},{192,224},{224,1... | collective-permute-start | bytes 786440 | tf_op jit(solution)/shard_map/ppermute | solution.py:49
  64.0 0.6 copy-start.5
  65.3 0.7 copy-start.7
  68.3 20.8 %all-to-all-start.1 = ((f32[4,512,128]{2,1,0:T(8,128)}), f32[4,512,128]{2,1,0:T(8,128)}, u32[]{:S(2)}, u32[]{:S(2)}) async-start(f32[4,512,128]{2,1,0:T(8,128)} %shard_map.111), calls=%async_computation.1 | async-start | bytes 2097152 | tf_op jit(solution)/shard_map/all_to_all | solution.py:136
  73.3 8.9 %collective-permute-start.8 = (bf16[1,5,32,128]{3,2,1,0:T(8,128)(2,1)S(1)}, bf16[1,5,32,128]{3,2,1,0:T(8,128)(2,1)S(1)}, u32[]{:S(2)}, u32[]{:S(2)}) collective-permute-start(bf16[1,5,32,128]{3,2,1,0:T(8,128)(2,1)S(1)} %pad_maximum_fusion.1), channel_id=1, source_target_pairs={{31,0},{0,1},{1,2},{2,3},{3,4},{4,5},{5,6},{6,7},{7,8},{8,9},{9,10... | collective-permute-start | bytes 122888 | tf_op jit(solution)/shard_map/ppermute | solution.py:32
  75.2 7.8 %collective-permute-start.9 = (bf16[1,1,32,128]{3,2,1,0:T(8,128)(2,1)S(1)}, bf16[1,1,32,128]{3,2,1,0:T(8,128)(2,1)S(1)}, u32[]{:S(2)}, u32[]{:S(2)}) collective-permute-start(bf16[1,1,32,128]{3,2,1,0:T(8,128)(2,1)S(1)} %slice.38), channel_id=1, source_target_pairs={{1,0},{2,1},{3,2},{4,3},{5,4},{6,5},{7,6},{8,7},{9,8},{10,9},{11,1... | collective-permute-start | bytes 24584 | tf_op jit(solution)/shard_map/ppermute | solution.py:32
  82.2 0.8 copy-start.9
